TPU v7x, 128 devices: a whole 4x4x4 slice. The times are simulated.
128 devices in a mesh: ctx: 32 (over x, z, core), head: 4 (over y).
Axes of the slice: x: 4, y: 4, z: 4, core: 2. Of those that a mesh axis runs over, the one named last changes fastest.
Arguments:
- queries: bfloat16 [16384, 4096], P('ctx', 'head'), may hold values from -200 to 200
- keys_values: bfloat16 [2, 16384, 4096], P(None, 'ctx', 'head'), may hold values from -7 to 7
- w_out: bfloat16 [4096, 4096], P('head'), may hold values from -0.09375 to 0.09375
- doc_index: int32 [16384], replicated, may hold values from 0 to 31, never falling along the last dimension, each value on 1 to 1152 neighbouring positions
Outputs:
- mixed: bfloat16 [16384, 4096], P(('ctx', 'head'))
Inputs may be any that keep to these rules, and one draw needn't show every extreme that they name: `doc_index`: ids never fall along the pack; each document is a run of 1 to 1152 tokens and one has exactly 1152.
All inputs are finite; a program needn't handle non-finite values.
Results may differ from a plain program's by a relative error of at most 0.0095.
Values may be sent and summed in bfloat16 or wider, within the bound.
A program may use at most 64 MiB of HBM per device.

v0:
```python
import jax
import jax.numpy as jnp
from jax import lax
from jax.sharding import PartitionSpec as P

HD = 128
SPAN = 3


def from_behind(shard, axis, by):
    peers = lax.axis_size(axis)
    pairs = [(i, i + by) for i in range(peers) if 0 <= i + by < peers]
    return lax.ppermute(shard, axis, pairs)


def masked_scores(query_head, key_head, allowed):
    raw = lax.dot_general(
        query_head, key_head, (((1,), (1,)), ((), ())), preferred_element_type=jnp.float32
    ) * HD ** (-0.5)
    return jnp.where(allowed, raw, jnp.float32(-1e30))


def weighted_values(probs, value_head):
    return jnp.dot(probs, value_head, preferred_element_type=jnp.float32)


def per_device(queries, keys_values, w_out, doc_index):
    shard_rows = queries.shape[0]
    my_index = lax.axis_index("ctx")
    first_row = my_index * shard_rows
    offsets = jnp.arange(shard_rows, dtype=jnp.int32)
    query_docs = lax.dynamic_slice_in_dim(doc_index, first_row, shard_rows)
    query_place = first_row + offsets
    earlier = [from_behind(keys_values, "ctx", distance) for distance in range(1, SPAN + 1)]
    blocks = [keys_values] + earlier
    masks = []
    live_flags = []
    for distance in range(SPAN + 1):
        start = first_row - distance * shard_rows
        safe_start = jnp.maximum(start, 0)
        docs_here = lax.dynamic_slice_in_dim(doc_index, safe_start, shard_rows)
        docs_here = jnp.where(start >= 0, docs_here, -1)
        key_place = safe_start + offsets
        masks.append(
            (docs_here[None, :] == query_docs[:, None])
            & (key_place[None, :] <= query_place[:, None])
        )
        live_flags.append(docs_here[shard_rows - 1] == query_docs[0])
    head_count = queries.shape[1] // HD

    def one_head(head):
        query_head = lax.dynamic_slice_in_dim(queries, head * HD, HD, 1)
        score_list = []
        value_list = []
        for number, block in enumerate(blocks):
            key_head = lax.dynamic_slice_in_dim(block[0], head * HD, HD, 1)
            value_list.append(lax.dynamic_slice_in_dim(block[1], head * HD, HD, 1))
            score_list.append(masked_scores(query_head, key_head, masks[number]))
        top = jnp.max(jnp.stack([jnp.max(entry, axis=1) for entry in score_list]), axis=0)[:, None]
        total = jnp.zeros((shard_rows, 1), jnp.float32)
        summed = jnp.zeros((shard_rows, HD), jnp.float32)
        for number, entry in enumerate(score_list):
            weights = jnp.exp(entry - top)
            total = total + jnp.sum(weights, axis=1, keepdims=True)
            probs = weights.astype(jnp.bfloat16)
            summed = summed + weighted_values(probs, value_list[number])
        return summed / total

    per_head = lax.map(one_head, jnp.arange(head_count, dtype=jnp.int32))
    attended = (
        jnp.transpose(per_head, (1, 0, 2)).reshape(shard_rows, head_count * HD).astype(jnp.bfloat16)
    )
    term = jnp.dot(attended, w_out, preferred_element_type=jnp.float32).astype(jnp.bfloat16)
    return lax.psum_scatter(
        lax.optimization_barrier(term).astype(jnp.float32).astype(jnp.bfloat16),
        "head",
        scatter_dimension=0,
        tiled=True,
    )


def solution(mesh):
    in_specs = (P("ctx", "head"), P(None, "ctx", "head"), P("head", None), P())
    out_specs = P(("ctx", "head"), None)
    return jax.shard_map(
        per_device, mesh=mesh, in_specs=in_specs, out_specs=out_specs, check_vma=False
    )
```

profile of v0, /device:TPU:98, one launch (start us, length us, event | category | flops | bytes accessed | tf_op | source)
XLA Modules:
  0.0 282.3 jit_solution(5526711160969116241)
XLA Ops:
  6.5 1.9 collective-permute-start
  8.5 2.0 collective-permute-start.1
  10.5 5.2 %collective-permute-start.2 = (bf16[2,512,1024]{2,1,0:T(8,128)(2,1)}, bf16[2,512,1024]{2,1,0:T(8,128)(2,1)}, u32[]{:S(2)}, u32[]{:S(2)}) collective-permute-start(bf16[2,512,1024]{2,1,0:T(8,128)(2,1)} %param.7), channel_id=1, source_target_pairs={{0,12},{4,16},{8,20},{12,24},{16,28},{20,32},{24,36},{28,40},{32,4... | collective-permute-start | bytes 6291464 | tf_op jit(solution)/shard_map/ppermute | solution.py:13
  15.7 0.9 dynamic-slice_select_fusion
  16.7 59.8 %collective-permute-done = bf16[2,512,1024]{2,1,0:T(8,128)(2,1)S(1)} collective-permute-done((bf16[2,512,1024]{2,1,0:T(8,128)(2,1)}, bf16[2,512,1024]{2,1,0:T(8,128)(2,1)S(1)}, u32[]{:S(2)}, u32[]{:S(2)}) %collective-permute-start) | collective-permute-done | bytes 2097184 | tf_op jit(solution)/shard_map/ppermute | solution.py:13
  76.5 5.2 %collective-permute-done.1 = bf16[2,512,1024]{2,1,0:T(8,128)(2,1)} collective-permute-done((bf16[2,512,1024]{2,1,0:T(8,128)(2,1)}, bf16[2,512,1024]{2,1,0:T(8,128)(2,1)}, u32[]{:S(2)}, u32[]{:S(2)}) %collective-permute-start.1) | collective-permute-done | bytes 2097184 | tf_op jit(solution)/shard_map/ppermute | solution.py:13
  81.7 42.5 %collective-permute-done.2 = bf16[2,512,1024]{2,1,0:T(8,128)(2,1)} collective-permute-done((bf16[2,512,1024]{2,1,0:T(8,128)(2,1)}, bf16[2,512,1024]{2,1,0:T(8,128)(2,1)}, u32[]{:S(2)}, u32[]{:S(2)}) %collective-permute-start.2) | collective-permute-done | bytes 2097184 | tf_op jit(solution)/shard_map/ppermute | solution.py:13
  124.2 72.2 %while.12 = (s32[]{:T(128)}, bf16[8,512,128]{1,2,0:T(8,128)(2,1)S(1)}, s32[8]{0:T(128)S(1)}, bf16[512,1024]{1,0:T(8,128)(2,1)}, bf16[2,512,1024]{2,1,0:T(8,128)(...) while((s32[]{:T(128)}, ...), condition=%wide.region_9.10_spmd.clone.clone, body=%wide.region_0.9_spmd.clone.clone.sunk | while | flops 547683328 | bytes 45830472 | solution.py:69
  125.5 2.7 fusion.96
  129.0 0.8 copy-done
  134.5 2.7 fusion.96
  138.0 0.8 copy-done
  143.5 2.7 fusion.96
  147.0 0.8 copy-done
  152.5 2.7 fusion.96
  156.1 0.8 copy-done
  161.6 2.7 fusion.96
  165.1 0.8 copy-done
  170.6 2.7 fusion.96
  179.7 2.7 fusion.96
  188.7 2.7 fusion.96
  192.2 0.8 copy-done
  196.5 9.5 %convolution_convert_fusion = bf16[512,4096]{1,0:T(8,128)(2,1)} fusion(bf16[512,1024]{0,1:T(8,128)(2,1)S(1)} %bitcast.60, bf16[1024,4096]{1,0:T(8,128)(2,1)} %param.8), kind=kOutput, calls=%fused_computation.65 | convolution fusion | flops 4297064448 | bytes 13631488 | tf_op jit(solution)/shard_map/dot_general | solution.py:73
  206.0 69.4 %reduce-scatter.2.cloned.1.call-done = bf16[128,4096]{1,0:T(8,128)(2,1)} async-done(((bf16[512,4096]{1,0:T(8,128)(2,1)}), bf16[128,4096]{1,0:T(8,128)(2,1)}) %reduce-scatter.2.cloned.1.call-update) | async-done | bytes 1048592 | tf_op jit(solution)/shard_map/reduce_scatter | solution.py:74
  (152 shorter events, 40.2 us)
Async XLA Ops:
  6.5 268.9 %reduce-scatter.2.cloned.1.call-start = ((), (), s32[]{:S(2)}) async-start(), calls=%async_computation.1 | async-start | bytes 5242880 | tf_op jit(solution)/shard_map/reduce_scatter | solution.py:74
  6.5 69.9 %collective-permute-start = (bf16[2,512,1024]{2,1,0:T(8,128)(2,1)}, bf16[2,512,1024]{2,1,0:T(8,128)(2,1)S(1)}, u32[]{:S(2)}, u32[]{:S(2)}) collective-permute-start(bf16[2,512,1024]{2,1,0:T(8,128)(2,1)} %param.7), channel_id=1, source_target_pairs={{0,4},{4,8},{8,12},{12,16},{16,20},{20,24},{24,28},{28,32},{32,36}... | collective-permute-start | bytes 6291464 | tf_op jit(solution)/shard_map/ppermute | solution.py:13
  8.5 73.2 %collective-permute-start.1 = (bf16[2,512,1024]{2,1,0:T(8,128)(2,1)}, bf16[2,512,1024]{2,1,0:T(8,128)(2,1)}, u32[]{:S(2)}, u32[]{:S(2)}) collective-permute-start(bf16[2,512,1024]{2,1,0:T(8,128)(2,1)} %param.7), channel_id=1, source_target_pairs={{0,8},{4,12},{8,16},{12,20},{16,24},{20,28},{24,32},{28,36},{32,40... | collective-permute-start | bytes 6291464 | tf_op jit(solution)/shard_map/ppermute | solution.py:13
  10.5 113.7 %collective-permute-start.2 = (bf16[2,512,1024]{2,1,0:T(8,128)(2,1)}, bf16[2,512,1024]{2,1,0:T(8,128)(2,1)}, u32[]{:S(2)}, u32[]{:S(2)}) collective-permute-start(bf16[2,512,1024]{2,1,0:T(8,128)(2,1)} %param.7), channel_id=1, source_target_pairs={{0,12},{4,16},{8,20},{12,24},{16,28},{20,32},{24,36},{28,40},{32,4... | collective-permute-start | bytes 6291464 | tf_op jit(solution)/shard_map/ppermute | solution.py:13
  125.5 2.7 copy-start.1
  128.2 1.6 copy-start
  134.5 2.7 copy-start.1
  137.2 1.6 copy-start
  143.5 2.7 copy-start.1
  146.2 1.6 copy-start
  152.5 2.7 copy-start.1
  155.3 1.6 copy-start
  161.6 2.7 copy-start.1
  164.3 1.6 copy-start
  170.6 2.7 copy-start.1
  173.3 1.6 copy-start
  179.6 2.7 copy-start.1
  182.4 1.6 copy-start
  188.7 2.7 copy-start.1
  191.4 1.6 copy-start
Sparse Core Ops, SparseCore 0:
  206.1 69.2 reduce-scatter.1
where the time goes:
time: 285 us; the launch traced here: 282 us
  waiting for transfers between devices  177 us (62%)
  local copies, waits for them, and re-layouts  37.3 us (13%)
  matrix products  33.9 us (12%)
  between operations  13.5 us (5%)
  starting transfers between devices  9.12 us (3%)
  loops' own time  5.82 us (2%)
  other arithmetic  5.66 us (2%)
    ppermute x3, waiting for transfers between devices, from_behind(): return lax.ppermute(shard, axis, pairs)  108 us
    reduce_scatter x1, waiting for transfers between devices, per_device(): lax.psum_scatter(lax.optimization_barrier(term).astype(jnp.float32).astyp...  69.4 us
    slice x16, local copies, waits for them, and re-layouts, one_head(): value_list.append(lax.dynamic_slice_in_dim(block[1], head * HD, HD, 1))  25.3 us
    dot_general x32, matrix products, masked_scores(): lax.dot_general(query_head, key_head, (((1,), (1,)), ((), ())), preferred...  12.9 us
    dot_general x32, matrix products, weighted_values(): return jnp.dot(probs, value_head, preferred_element_type=jnp.float32)  11.5 us
    dot_general x1, matrix products, per_device(): jnp.dot(attended, w_out, preferred_element_type=jnp.float32)  9.48 us
    ppermute x3, starting transfers between devices, from_behind(): return lax.ppermute(shard, axis, pairs)  9.12 us
    while x32, local copies, waits for them, and re-layouts  6.2 us
  transfers between devices with their start and end apart: 4, of which 4 were waited for; matrix products, arithmetic and copies ran while one was open for 0% of the time, Pallas kernels for 0%

commit v1 on v0

v1 whole, which is shorter than its diff:
```python
import jax
import jax.numpy as jnp
from jax import lax
from jax.sharding import PartitionSpec as P

HD = 128
SPAN = 3
DOC_MOST = 1152
CHUNK = 128


def shift_up(x, axis):
    peers = lax.axis_size(axis)
    return lax.ppermute(x, axis, [(i, i + 1) for i in range(peers - 1)])


def rotate(x, axis, by):
    peers = lax.axis_size(axis)
    return lax.ppermute(x, axis, [(i, (i + by) % peers) for i in range(peers)])


def per_device(queries, keys_values, w_out, doc_index):
    rows, width = queries.shape
    heads = width // HD
    groups = lax.axis_size("head")
    me = lax.axis_index("ctx")
    h = lax.axis_index("head")
    first_row = me * rows
    tail = DOC_MOST - 2 * rows
    r1 = shift_up(keys_values, "ctx")
    r2 = shift_up(r1, "ctx")
    r3 = shift_up(r2[:, rows - tail:], "ctx")
    window = jnp.concatenate([r3, r2, r1, keys_values], axis=1)
    padded_docs = jnp.concatenate([jnp.full((DOC_MOST,), -1, jnp.int32), doc_index])
    span = DOC_MOST + CHUNK
    scale = HD ** (-0.5)

    def chunk_part(c):
        start = c * CHUNK
        q = lax.dynamic_slice_in_dim(queries, start, CHUNK, 0).reshape(CHUNK, heads, HD)
        kv = lax.dynamic_slice_in_dim(window, start, span, 1)
        k = kv[0].reshape(span, heads, HD)
        v = kv[1].reshape(span, heads, HD)
        q_docs = lax.dynamic_slice_in_dim(doc_index, first_row + start, CHUNK)
        k_docs = lax.dynamic_slice_in_dim(padded_docs, first_row + start, span)
        q_place = start + jnp.arange(CHUNK, dtype=jnp.int32)
        k_place = start - DOC_MOST + jnp.arange(span, dtype=jnp.int32)
        allowed = (k_docs[None, :] == q_docs[:, None]) & (k_place[None, :] <= q_place[:, None])
        raw = jnp.einsum("qhd,khd->hqk", q, k, preferred_element_type=jnp.float32) * scale
        scores = jnp.where(allowed[None], raw, jnp.float32(-1e30))
        top = jnp.max(scores, axis=2, keepdims=True)
        weights = jnp.exp(scores - top)
        total = jnp.sum(weights, axis=2)
        probs = weights.astype(jnp.bfloat16)
        summed = jnp.einsum("hqk,khd->qhd", probs, v, preferred_element_type=jnp.float32)
        attended = (summed / jnp.transpose(total)[:, :, None]).astype(jnp.bfloat16)
        attended = attended.reshape(CHUNK, heads * HD)
        return jnp.dot(attended, w_out, preferred_element_type=jnp.float32).astype(jnp.bfloat16)

    total_out = None
    for step in range(groups):
        by = (step + 1) % groups
        part = chunk_part((h + by) % groups)
        if by:
            part = rotate(part, "head", by)
        part = part.astype(jnp.float32)
        total_out = part if total_out is None else total_out + part
    return total_out.astype(jnp.bfloat16)


def solution(mesh):
    in_specs = (P("ctx", "head"), P(None, "ctx", "head"), P("head", None), P())
    out_specs = P(("ctx", "head"), None)
    return jax.shard_map(
        per_device, mesh=mesh, in_specs=in_specs, out_specs=out_specs, check_vma=False
    )
```

time: 285 us -> 146 us (0.51)
  waiting for transfers between devices: 177 us -> 91.5 us
  local copies, waits for them, and re-layouts: 37.3 us -> 13 us
  matrix products: 33.9 us -> 17.6 us
  between operations: 13.5 us -> 0.42 us
  loops' own time: 5.82 us -> 0 us
  other arithmetic: 5.66 us -> 9.14 us
  starting transfers between devices: 9.12 us -> 12.2 us
    reduce_scatter x1 -> x0, waiting for transfers between devices: 69.4 us -> none  [per_device(): lax.psum_scatter(lax.optimization_barrier(term).astype(jnp.float32).astyp...]
    slice x16 -> x2, local copies, waits for them, and re-layouts: 25.3 us -> 7.58 us  [the longest x1 6.5 us: chunk_part(): k = kv[0].reshape(span, heads, HD)]
    dot_general x65 -> x12, matrix products: 33.9 us -> 17.6 us  [the longest x4 7.17 us: chunk_part(): jnp.einsum('qhd,khd->hqk', q, k, preferred_element_type=jnp.float32) * scale]
    ppermute x3 -> x6, waiting for transfers between devices: 108 us -> 91.5 us  [the longest x3 56 us: shift_up(): return lax.ppermute(x, axis, [(i, i + 1) for i in range(peers - 1)])]
    while x32 -> x0, local copies, waits for them, and re-layouts: 6.2 us -> none
    another operation x1 -> x0, loops' own time: 5.82 us -> none  [per_device(): per_head = lax.map(one_head, jnp.arange(head_count, dtype=jnp.int32))]
    unnamed x0 -> x29, local copies, waits for them, and re-layouts: none -> 3.92 us
    concatenate x0 -> x1, other arithmetic: none -> 3.63 us  [per_device(): window = jnp.concatenate([r3, r2, r1, keys_values], axis=1)]
  transfers between devices with their start and end apart: 4 -> 6, of which waited for: 4 -> 6; matrix products, arithmetic and copies ran while one was open for 0% -> 11% of each run, Pallas kernels for 0% -> 0%
where the time goes in v1:
time: 146 us; the launch traced here: 144 us
  waiting for transfers between devices  91.5 us (63%)
  matrix products  17.6 us (12%)
  local copies, waits for them, and re-layouts  13 us (9%)
  starting transfers between devices  12.2 us (8%)
  other arithmetic  9.14 us (6%)
    ppermute x3, waiting for transfers between devices, shift_up(): return lax.ppermute(x, axis, [(i, i + 1) for i in range(peers - 1)])  56 us
    ppermute x3, waiting for transfers between devices, rotate(): return lax.ppermute(x, axis, [(i, (i + by) % peers) for i in range(peers)])  35.5 us
    dot_general x4, matrix products, chunk_part(): jnp.einsum('qhd,khd->hqk', q, k, preferred_element_type=jnp.float32) * scale  7.17 us
    slice x1, local copies, waits for them, and re-layouts, chunk_part(): k = kv[0].reshape(span, heads, HD)  6.5 us
    dot_general x4, matrix products, chunk_part(): jnp.dot(attended, w_out, preferred_element_type=jnp.float32)  6.48 us
    ppermute x3, starting transfers between devices, rotate(): return lax.ppermute(x, axis, [(i, (i + by) % peers) for i in range(peers)])  6.44 us
    ppermute x3, starting transfers between devices, shift_up(): return lax.ppermute(x, axis, [(i, i + 1) for i in range(peers - 1)])  5.75 us
    reduce_sum x4, other arithmetic, chunk_part(): total = jnp.sum(weights, axis=2)  4.05 us
  transfers between devices with their start and end apart: 6, of which 6 were waited for; matrix products, arithmetic and copies ran while one was open for 11% of the time, Pallas kernels for 0%

profile of v1, /device:TPU:98, one launch (start us, length us, event | category | flops | bytes accessed | tf_op | source)
XLA Modules:
  0.0 143.9 jit_solution(12601005901014974497)
XLA Ops:
  0.0 2.9 %copy.9 = bf16[2,512,1024]{1,2,0:T(8,128)(2,1)S(1)} copy(bf16[2,512,1024]{2,1,0:T(8,128)(2,1)} %param.5) | data formatting | bytes 4194304 | tf_op args[1]
  2.9 1.9 %collective-permute-start = (bf16[2,512,1024]{1,2,0:T(8,128)(2,1)S(1)}, bf16[2,512,1024]{1,2,0:T(8,128)(2,1)}, u32[]{:S(2)}, u32[]{:S(2)}) collective-permute-start(bf16[2,512,1024]{1,2,0:T(8,128)(2,1)S(1)} %copy.9), channel_id=1, source_target_pairs={{0,4},{4,8},{8,12},{12,16},{16,20},{20,24},{24,28},{28,32},{32,36}... | collective-permute-start | bytes 6291464 | tf_op jit(solution)/shard_map/ppermute | solution.py:14
  4.8 25.5 %collective-permute-done = bf16[2,512,1024]{1,2,0:T(8,128)(2,1)} collective-permute-done((bf16[2,512,1024]{1,2,0:T(8,128)(2,1)S(1)}, bf16[2,512,1024]{1,2,0:T(8,128)(2,1)}, u32[]{:S(2)}, u32[]{:S(2)}) %collective-permute-start) | collective-permute-done | bytes 2097184 | tf_op jit(solution)/shard_map/ppermute | solution.py:14
  30.4 1.9 %collective-permute-start.1 = (bf16[2,512,1024]{1,2,0:T(8,128)(2,1)}, bf16[2,512,1024]{1,2,0:T(8,128)(2,1)}, u32[]{:S(2)}, u32[]{:S(2)}) collective-permute-start(bf16[2,512,1024]{1,2,0:T(8,128)(2,1)} %collective-permute-done), channel_id=1, source_target_pairs={{0,4},{4,8},{8,12},{12,16},{16,20},{20,24},{24,28},{28,32},{32,36}... | collective-permute-start | bytes 6291464 | tf_op jit(solution)/shard_map/ppermute | solution.py:14
  32.4 1.3 constant_dynamic-slice_fusion.10
  35.0 23.0 %collective-permute-done.1 = bf16[2,512,1024]{1,2,0:T(8,128)(2,1)} collective-permute-done((bf16[2,512,1024]{1,2,0:T(8,128)(2,1)}, bf16[2,512,1024]{1,2,0:T(8,128)(2,1)}, u32[]{:S(2)}, u32[]{:S(2)}) %collective-permute-start.1) | collective-permute-done | bytes 2097184 | tf_op jit(solution)/shard_map/ppermute | solution.py:14
  59.1 1.9 %collective-permute-start.2 = (bf16[2,128,1024]{1,2,0:T(8,128)(2,1)S(1)}, bf16[2,128,1024]{1,2,0:T(8,128)(2,1)S(1)}, u32[]{:S(2)}, u32[]{:S(2)}) collective-permute-start(bf16[2,128,1024]{1,2,0:T(8,128)(2,1)S(1)} %slice.36), channel_id=1, source_target_pairs={{0,4},{4,8},{8,12},{12,16},{16,20},{20,24},{24,28},{28,32},{32,36}... | collective-permute-start | bytes 1572872 | tf_op jit(solution)/shard_map/ppermute | solution.py:14
  62.1 7.5 %collective-permute-done.2 = bf16[2,128,1024]{1,2,0:T(8,128)(2,1)S(1)} collective-permute-done((bf16[2,128,1024]{1,2,0:T(8,128)(2,1)S(1)}, bf16[2,128,1024]{1,2,0:T(8,128)(2,1)S(1)}, u32[]{:S(2)}, u32[]{:S(2)}) %collective-permute-start.2) | collective-permute-done | bytes 524320 | tf_op jit(solution)/shard_map/ppermute | solution.py:14
  69.6 3.6 %pad_maximum_fusion = bf16[2,1664,1024]{1,2,0:T(8,128)(2,1)S(1)} fusion(bf16[2,512,1024]{1,2,0:T(8,128)(2,1)} %copy-done.2, bf16[2,512,1024]{1,2,0:T(8,128)(2,1)} %collective-permute-done, bf16[2,512,1024]{1,2,0:T(8,128)(2,1)} %collective-permute-done.1, bf16[2,128,1024]{1,2,0:T(8,128)(2,1)S(1)} %collective-permute-done.2), kind=kLoop, calls=%fused_computation | loop fusion | flops 27262976 | bytes 13631488 | tf_op jit(solution)/shard_map/concatenate | solution.py:33
  73.3 6.5 %constant_dynamic-slice_fusion.11 = (bf16[1,1280,1024]{1,2,0:T(8,128)(2,1)}, bf16[1,1280,1024]{1,2,0:T(8,128)(2,1)}, bf16[1,1280,1024]{1,2,0:T(8,128)(2,1)}, bf1...) fusion(bf16[2,1664,1024]{1,2,0:T(8,128)(2,1)S(1)} %pad_maximum_, ...), kind=kLoop, calls=%fused_computation.66 | loop fusion | bytes 41943060 | tf_op jit(solution)/shard_map/slice | solution.py:42
  79.8 3.2 %fusion.61 = (f32[8,128]{1,0:T(8,128)S(1)}, f32[8,128,1280]{2,1,0:T(8,128)S(1)}) fusion(bf16[128,8,128]{0,2,1:T(8,128)(2,1)S(1)} %bitcast.77, bf16[1280,8,128]{0,2,1:T(8,128)(2,1)} %bitcast.69, pred[128,1280]{1,0:T(8,128)(4,1)S(1)} %copy-done.8), kind=kOutput, calls=%fused_computation.75 | convolution fusion | flops 339475456 | bytes 8294400 | tf_op jit(solution)/shard_map/qhd,khd->hqk/dot_general | solution.py:49
  85.3 1.3 convolution_convert_fusion.3
  86.6 1.8 %collective-permute-start.3 = (bf16[128,4096]{1,0:T(8,128)(2,1)S(1)}, bf16[128,4096]{1,0:T(8,128)(2,1)S(1)}, u32[]{:S(2)}, u32[]{:S(2)}) collective-permute-start(bf16[128,4096]{1,0:T(8,128)(2,1)S(1)} %convolution_convert_fusion.3), channel_id=1, source_target_pairs={{0,1},{1,2},{2,3},{3,0},{4,5},{5,6},{6,7},{7,4},{8,9},{9,10},{10,1... | collective-permute-start | bytes 3145736 | tf_op jit(solution)/shard_map/ppermute | solution.py:19
  88.4 1.3 fusion.60
  91.8 1.3 convolution_convert_fusion.2
  93.1 3.0 %collective-permute-start.4 = (bf16[128,4096]{1,0:T(8,128)(2,1)S(1)}, bf16[128,4096]{1,0:T(8,128)(2,1)S(1)}, u32[]{:S(2)}, u32[]{:S(2)}) collective-permute-start(bf16[128,4096]{1,0:T(8,128)(2,1)S(1)} %convolution_convert_fusion.2), channel_id=1, source_target_pairs={{0,2},{1,3},{2,0},{3,1},{4,6},{5,7},{6,4},{7,5},{8,10},{9,11},{10,... | collective-permute-start | bytes 3145736 | tf_op jit(solution)/shard_map/ppermute | solution.py:19
  96.1 1.3 fusion.59
  99.4 1.3 convolution_convert_fusion.1
  100.7 1.6 %collective-permute-start.5 = (bf16[128,4096]{1,0:T(8,128)(2,1)S(1)}, bf16[128,4096]{1,0:T(8,128)(2,1)S(1)}, u32[]{:S(2)}, u32[]{:S(2)}) collective-permute-start(bf16[128,4096]{1,0:T(8,128)(2,1)S(1)} %convolution_convert_fusion.1), channel_id=1, source_target_pairs={{0,3},{1,0},{2,1},{3,2},{4,7},{5,4},{6,5},{7,6},{8,11},{9,8},{10,9... | collective-permute-start | bytes 3145736 | tf_op jit(solution)/shard_map/ppermute | solution.py:19
  102.3 1.3 fusion.58
  105.7 7.3 %collective-permute-done.3 = bf16[128,4096]{1,0:T(8,128)(2,1)S(1)} collective-permute-done((bf16[128,4096]{1,0:T(8,128)(2,1)S(1)}, bf16[128,4096]{1,0:T(8,128)(2,1)S(1)}, u32[]{:S(2)}, u32[]{:S(2)}) %collective-permute-start.3) | collective-permute-done | bytes 1048608 | tf_op jit(solution)/shard_map/ppermute | solution.py:19
  113.0 23.8 %collective-permute-done.4 = bf16[128,4096]{1,0:T(8,128)(2,1)S(1)} collective-permute-done((bf16[128,4096]{1,0:T(8,128)(2,1)S(1)}, bf16[128,4096]{1,0:T(8,128)(2,1)S(1)}, u32[]{:S(2)}, u32[]{:S(2)}) %collective-permute-start.4) | collective-permute-done | bytes 1048608 | tf_op jit(solution)/shard_map/ppermute | solution.py:19
  136.8 4.4 %collective-permute-done.5 = bf16[128,4096]{1,0:T(8,128)(2,1)S(1)} collective-permute-done((bf16[128,4096]{1,0:T(8,128)(2,1)S(1)}, bf16[128,4096]{1,0:T(8,128)(2,1)S(1)}, u32[]{:S(2)}, u32[]{:S(2)}) %collective-permute-start.5) | collective-permute-done | bytes 1048608 | tf_op jit(solution)/shard_map/ppermute | solution.py:19
  141.2 2.6 %add_convert_fusion = bf16[128,4096]{1,0:T(8,128)(2,1)} fusion(bf16[128,4096]{1,0:T(8,128)(2,1)S(1)} %collective-permute-done.5, bf16[128,4096]{1,0:T(8,128)(2,1)S(1)} %collective-permute-done.4, bf16[128,4096]{1,0:T(8,128)(2,1)S(1)} %collective-permute-done.3, bf16[128,1024]{0,1:T(8,128)(2,1)S(1)} %bitcast.81, bf16[1024,4096]{1,0:T(8,128)(2,1)S(1)} %bitcast.65), kind=kOutput, calls=%fused_computation.30 | convolution fusion | flops 1078460416 | bytes 12845056 | tf_op jit(solution)/shard_map/dot_general | solution.py:58
  (50 shorter events, 11.7 us)
Async XLA Ops:
  0.0 34.4 %copy-start.9 = (s32[16384]{0:T(1024)S(1)}, s32[16384]{0:T(1024)}, u32[]{:S(2)}) copy-start(s32[16384]{0:T(1024)} %param.7) | copy-start | bytes 196612
  2.9 59.2 %copy-start.2 = (bf16[2,512,1024]{1,2,0:T(8,128)(2,1)}, bf16[2,512,1024]{1,2,0:T(8,128)(2,1)S(1)}, u32[]{:S(2)}) copy-start(bf16[2,512,1024]{1,2,0:T(8,128)(2,1)S(1)} %copy.9) | copy-start | bytes 6291460
  2.9 27.5 %collective-permute-start = (bf16[2,512,1024]{1,2,0:T(8,128)(2,1)S(1)}, bf16[2,512,1024]{1,2,0:T(8,128)(2,1)}, u32[]{:S(2)}, u32[]{:S(2)}) collective-permute-start(bf16[2,512,1024]{1,2,0:T(8,128)(2,1)S(1)} %copy.9), channel_id=1, source_target_pairs={{0,4},{4,8},{8,12},{12,16},{16,20},{20,24},{24,28},{28,32},{32,36}... | collective-permute-start | bytes 6291464 | tf_op jit(solution)/shard_map/ppermute | solution.py:14
  30.4 27.7 %collective-permute-start.1 = (bf16[2,512,1024]{1,2,0:T(8,128)(2,1)}, bf16[2,512,1024]{1,2,0:T(8,128)(2,1)}, u32[]{:S(2)}, u32[]{:S(2)}) collective-permute-start(bf16[2,512,1024]{1,2,0:T(8,128)(2,1)} %collective-permute-done), channel_id=1, source_target_pairs={{0,4},{4,8},{8,12},{12,16},{16,20},{20,24},{24,28},{28,32},{32,36}... | collective-permute-start | bytes 6291464 | tf_op jit(solution)/shard_map/ppermute | solution.py:14
  59.1 10.5 %collective-permute-start.2 = (bf16[2,128,1024]{1,2,0:T(8,128)(2,1)S(1)}, bf16[2,128,1024]{1,2,0:T(8,128)(2,1)S(1)}, u32[]{:S(2)}, u32[]{:S(2)}) collective-permute-start(bf16[2,128,1024]{1,2,0:T(8,128)(2,1)S(1)} %slice.36), channel_id=1, source_target_pairs={{0,4},{4,8},{8,12},{12,16},{16,20},{20,24},{24,28},{28,32},{32,36}... | collective-permute-start | bytes 1572872 | tf_op jit(solution)/shard_map/ppermute | solution.py:14
  73.2 6.5 %copy-start.8 = (pred[128,1280]{1,0:T(8,128)(4,1)S(1)}, pred[128,1280]{1,0:T(8,128)(4,1)}, u32[]{:S(2)}) copy-start(pred[128,1280]{1,0:T(8,128)(4,1)} %get-tuple-element.36) | copy-start | bytes 491524
  79.8 4.2 %copy-start.6 = (bf16[1,1280,1024]{1,2,0:T(8,128)(2,1)S(1)}, bf16[1,1280,1024]{1,2,0:T(8,128)(2,1)}, u32[]{:S(2)}) copy-start(bf16[1,1280,1024]{1,2,0:T(8,128)(2,1)} %get-tuple-element.9) | copy-start | bytes 7864324
  79.8 5.2 %slice-start = ((s8[8388608]{0:T(1024)(128)(4,1)}), s8[4194304]{0:T(1024)(128)(4,1)S(1)}, s32[]{:S(2)}) async-start(s8[8388608]{0:T(1024)(128)(4,1)} %bitcast.64), calls=%async_computation | async-start | bytes 8388608
  83.0 2.3 %slice-start.1 = ((s8[8388608]{0:T(1024)(128)(4,1)}), s8[4194304]{0:T(1024)(128)(4,1)S(1)}, s32[]{:S(2)}) async-start(s8[8388608]{0:T(1024)(128)(4,1)} %bitcast.64), calls=%async_computation.1 | async-start | bytes 8388608
  85.3 3.1 %copy-start.1 = (bf16[1,1280,1024]{1,2,0:T(8,128)(2,1)S(1)}, bf16[1,1280,1024]{1,2,0:T(8,128)(2,1)}, u32[]{:S(2)}) copy-start(bf16[1,1280,1024]{1,2,0:T(8,128)(2,1)} %get-tuple-element.12) | copy-start | bytes 7864324
  85.3 3.1 %copy-start.7 = (pred[128,1280]{1,0:T(8,128)(4,1)S(1)}, pred[128,1280]{1,0:T(8,128)(4,1)}, u32[]{:S(2)}) copy-start(pred[128,1280]{1,0:T(8,128)(4,1)} %get-tuple-element.35) | copy-start | bytes 491524
  86.6 26.4 %collective-permute-start.3 = (bf16[128,4096]{1,0:T(8,128)(2,1)S(1)}, bf16[128,4096]{1,0:T(8,128)(2,1)S(1)}, u32[]{:S(2)}, u32[]{:S(2)}) collective-permute-start(bf16[128,4096]{1,0:T(8,128)(2,1)S(1)} %convolution_convert_fusion.3), channel_id=1, source_target_pairs={{0,1},{1,2},{2,3},{3,0},{4,5},{5,6},{6,7},{7,4},{8,9},{9,10},{10,1... | collective-permute-start | bytes 3145736 | tf_op jit(solution)/shard_map/ppermute | solution.py:19
  88.4 2.4 %copy-start.5 = (bf16[1,1280,1024]{1,2,0:T(8,128)(2,1)S(1)}, bf16[1,1280,1024]{1,2,0:T(8,128)(2,1)}, u32[]{:S(2)}) copy-start(bf16[1,1280,1024]{1,2,0:T(8,128)(2,1)} %get-tuple-element.8) | copy-start | bytes 7864324
  91.8 4.3 %copy-start = (bf16[1,1280,1024]{1,2,0:T(8,128)(2,1)S(1)}, bf16[1,1280,1024]{1,2,0:T(8,128)(2,1)}, u32[]{:S(2)}) copy-start(bf16[1,1280,1024]{1,2,0:T(8,128)(2,1)} %get-tuple-element.11) | copy-start | bytes 7864324
  93.1 43.7 %collective-permute-start.4 = (bf16[128,4096]{1,0:T(8,128)(2,1)S(1)}, bf16[128,4096]{1,0:T(8,128)(2,1)S(1)}, u32[]{:S(2)}, u32[]{:S(2)}) collective-permute-start(bf16[128,4096]{1,0:T(8,128)(2,1)S(1)} %convolution_convert_fusion.2), channel_id=1, source_target_pairs={{0,2},{1,3},{2,0},{3,1},{4,6},{5,7},{6,4},{7,5},{8,10},{9,11},{10,... | collective-permute-start | bytes 3145736 | tf_op jit(solution)/shard_map/ppermute | solution.py:19
  96.1 2.4 %copy-start.4 = (bf16[1,1280,1024]{1,2,0:T(8,128)(2,1)S(1)}, bf16[1,1280,1024]{1,2,0:T(8,128)(2,1)}, u32[]{:S(2)}) copy-start(bf16[1,1280,1024]{1,2,0:T(8,128)(2,1)} %get-tuple-element.7) | copy-start | bytes 7864324
  100.7 40.5 %collective-permute-start.5 = (bf16[128,4096]{1,0:T(8,128)(2,1)S(1)}, bf16[128,4096]{1,0:T(8,128)(2,1)S(1)}, u32[]{:S(2)}, u32[]{:S(2)}) collective-permute-start(bf16[128,4096]{1,0:T(8,128)(2,1)S(1)} %convolution_convert_fusion.1), channel_id=1, source_target_pairs={{0,3},{1,0},{2,1},{3,2},{4,7},{5,4},{6,5},{7,6},{8,11},{9,8},{10,9... | collective-permute-start | bytes 3145736 | tf_op jit(solution)/shard_map/ppermute | solution.py:19
  102.3 2.4 %copy-start.3 = (bf16[1,1280,1024]{1,2,0:T(8,128)(2,1)S(1)}, bf16[1,1280,1024]{1,2,0:T(8,128)(2,1)}, u32[]{:S(2)}) copy-start(bf16[1,1280,1024]{1,2,0:T(8,128)(2,1)} %get-tuple-element.6) | copy-start | bytes 7864324

commit v2 on v1

--- a/solution.py
+++ b/solution.py
@@ -4,7 +4,6 @@
 from jax.sharding import PartitionSpec as P
 
 HD = 128
-SPAN = 3
 DOC_MOST = 1152
 CHUNK = 128
 
@@ -14,31 +13,35 @@
     return lax.ppermute(x, axis, [(i, i + 1) for i in range(peers - 1)])
 
 
-def rotate(x, axis, by):
-    peers = lax.axis_size(axis)
-    return lax.ppermute(x, axis, [(i, (i + by) % peers) for i in range(peers)])
-
-
 def per_device(queries, keys_values, w_out, doc_index):
     rows, width = queries.shape
     heads = width // HD
     groups = lax.axis_size("head")
+    chunks = rows // CHUNK
     me = lax.axis_index("ctx")
     h = lax.axis_index("head")
     first_row = me * rows
-    tail = DOC_MOST - 2 * rows
+    back = DOC_MOST // CHUNK
     r1 = shift_up(keys_values, "ctx")
-    r2 = shift_up(r1, "ctx")
-    r3 = shift_up(r2[:, rows - tail:], "ctx")
-    window = jnp.concatenate([r3, r2, r1, keys_values], axis=1)
+    own_pieces = [keys_values[:, i * CHUNK:(i + 1) * CHUNK] for i in range(chunks)]
+    r1_pieces = [r1[:, i * CHUNK:(i + 1) * CHUNK] for i in range(chunks)]
+    upper = shift_up(r1[:, rows - 2 * CHUNK:], "ctx")
+    r2_pieces = [None] * chunks
+    r2_pieces[chunks - 2] = upper[:, :CHUNK]
+    r2_pieces[chunks - 1] = upper[:, CHUNK:]
+    for i in range(chunks - 3, -1, -1):
+        r2_pieces[i] = shift_up(r1_pieces[i], "ctx")
+    r3_piece = shift_up(r2_pieces[chunks - 1], "ctx")
+    pieces = [r3_piece] + r2_pieces + r1_pieces + own_pieces
+    assert len(pieces) == back + chunks
     padded_docs = jnp.concatenate([jnp.full((DOC_MOST,), -1, jnp.int32), doc_index])
     span = DOC_MOST + CHUNK
     scale = HD ** (-0.5)
 
     def chunk_part(c):
         start = c * CHUNK
-        q = lax.dynamic_slice_in_dim(queries, start, CHUNK, 0).reshape(CHUNK, heads, HD)
-        kv = lax.dynamic_slice_in_dim(window, start, span, 1)
+        q = queries[start:start + CHUNK].reshape(CHUNK, heads, HD)
+        kv = jnp.concatenate(pieces[c:c + back + 1], axis=1)
         k = kv[0].reshape(span, heads, HD)
         v = kv[1].reshape(span, heads, HD)
         q_docs = lax.dynamic_slice_in_dim(doc_index, first_row + start, CHUNK)
@@ -58,13 +61,16 @@
         return jnp.dot(attended, w_out, preferred_element_type=jnp.float32).astype(jnp.bfloat16)
 
     total_out = None
-    for step in range(groups):
-        by = (step + 1) % groups
-        part = chunk_part((h + by) % groups)
-        if by:
-            part = rotate(part, "head", by)
-        part = part.astype(jnp.float32)
-        total_out = part if total_out is None else total_out + part
+    for c in range(chunks - 1, -1, -1):
+        part = chunk_part(c)
+        owner = c % groups
+        terms = [jnp.where(h == owner, part, jnp.zeros_like(part)).astype(jnp.float32)]
+        for by in range(1, groups):
+            src = (owner - by) % groups
+            got = lax.ppermute(part, "head", [(src, owner)])
+            terms.append(got.astype(jnp.float32))
+        for t in terms:
+            total_out = t if total_out is None else total_out + t
     return total_out.astype(jnp.bfloat16)
 
 

time: 146 us -> 178 us (1.22)
  starting transfers between devices: 12.2 us -> 36.7 us
  local copies, waits for them, and re-layouts: 13 us -> 22.8 us
  other arithmetic: 9.14 us -> 17.2 us
  waiting for transfers between devices: 91.5 us -> 84.5 us
  matrix products: 17.6 us -> 15.8 us
    ppermute x3 -> x5, waiting for transfers between devices: 56 us -> 28.4 us  [shift_up(): return lax.ppermute(x, axis, [(i, i + 1) for i in range(peers - 1)])]
    ppermute x3 -> x12, waiting for transfers between devices: 35.5 us -> 56.1 us  [per_device(): got = lax.ppermute(part, 'head', [(src, owner)])]
    ppermute x3 -> x12, starting transfers between devices: 6.44 us -> 24.6 us  [per_device(): got = lax.ppermute(part, 'head', [(src, owner)])]
    unnamed x29 -> x36, local copies, waits for them, and re-layouts: 3.92 us -> 13.7 us
    convert_element_type x0 -> x1, other arithmetic: none -> 6.73 us  [per_device(): return total_out.astype(jnp.bfloat16)]
    ppermute x3 -> x5, starting transfers between devices: 5.75 us -> 12.1 us  [shift_up(): return lax.ppermute(x, axis, [(i, i + 1) for i in range(peers - 1)])]
    slice x1 -> x5, local copies, waits for them, and re-layouts: 1.08 us -> 5.7 us  [the longest x1 2.09 us: per_device(): r1_pieces = [r1[:, i * CHUNK:(i + 1) * CHUNK] for i in range(chunks)]]
    slice x1 -> x3, local copies, waits for them, and re-layouts: 6.5 us -> 2.98 us  [chunk_part(): k = kv[0].reshape(span, heads, HD)]
  transfers between devices with their start and end apart: 6 -> 17, of which waited for: 6 -> 6; matrix products, arithmetic and copies ran while one was open for 11% -> 25% of each run, Pallas kernels for 0% -> 0%
where the time goes in v2:
time: 178 us; the launch traced here: 177 us
  waiting for transfers between devices  84.5 us (47%)
  starting transfers between devices  36.7 us (21%)
  local copies, waits for them, and re-layouts  22.8 us (13%)
  other arithmetic  17.2 us (10%)
  matrix products  15.8 us (9%)
    ppermute x12, waiting for transfers between devices, per_device(): got = lax.ppermute(part, 'head', [(src, owner)])  56.1 us
    ppermute x5, waiting for transfers between devices, shift_up(): return lax.ppermute(x, axis, [(i, i + 1) for i in range(peers - 1)])  28.4 us
    ppermute x12, starting transfers between devices, per_device(): got = lax.ppermute(part, 'head', [(src, owner)])  24.6 us
    unnamed x36, local copies, waits for them, and re-layouts  13.7 us
    ppermute x5, starting transfers between devices, shift_up(): return lax.ppermute(x, axis, [(i, i + 1) for i in range(peers - 1)])  12.1 us
    convert_element_type x1, other arithmetic, per_device(): return total_out.astype(jnp.bfloat16)  6.73 us
    dot_general x4, matrix products, chunk_part(): jnp.dot(attended, w_out, preferred_element_type=jnp.float32)  6.1 us
    dot_general x4, matrix products, chunk_part(): jnp.einsum('qhd,khd->hqk', q, k, preferred_element_type=jnp.float32) * scale  5.68 us
  transfers between devices with their start and end apart: 17, of which 6 were waited for; matrix products, arithmetic and copies ran while one was open for 25% of the time, Pallas kernels for 0%

profile of v2, /device:TPU:98, one launch (start us, length us, event | category | flops | bytes accessed | tf_op | source)
XLA Modules:
  0.0 177.4 jit_solution(12543243550808550055)
XLA Ops:
  0.0 2.9 %copy.13 = bf16[2,512,1024]{1,2,0:T(8,128)(2,1)S(1)} copy(bf16[2,512,1024]{2,1,0:T(8,128)(2,1)} %param.5) | data formatting | bytes 4194304 | tf_op args[1]
  3.0 1.9 %collective-permute-start = (bf16[2,512,1024]{1,2,0:T(8,128)(2,1)S(1)}, bf16[2,512,1024]{1,2,0:T(8,128)(2,1)}, u32[]{:S(2)}, u32[]{:S(2)}) collective-permute-start(bf16[2,512,1024]{1,2,0:T(8,128)(2,1)S(1)} %copy.13), channel_id=1, source_target_pairs={{0,4},{4,8},{8,12},{12,16},{16,20},{20,24},{24,28},{28,32},{32,36}... | collective-permute-start | bytes 6291464 | tf_op jit(solution)/shard_map/ppermute | solution.py:13
  8.3 1.8 %copy.48 = bf16[128,1024]{0,1:T(8,128)(2,1)} copy(bf16[128,1024]{1,0:T(8,128)(2,1)} %get-tuple-element.20) | data formatting | bytes 524288
  13.3 2.1 %fusion.56 = (pred[128,1280]{0,1:T(8,128)(4,1)}, pred[128,1280]{0,1:T(8,128)(4,1)S(1)}) fusion(s32[1280]{0:T(1024)S(1)} %iota_add_fusion, s32[128]{0:T(128)S(1)} %get-tuple-element.35, s32[1280]{0:T(1024)S(1)} %get-tuple-element.32, s32[128]{0:T(128)S(1)} %iota_add_fusion.4, s32[1280]{0:T(1024)S(1)} %iota_add_fusion.1, s32[128]{0:T(128)S(1)} %get-tuple-element.36, ...), kind=kLoop, calls=%fused_computation.45 | loop fusion | flops 983040 | bytes 349696 | tf_op jit(solution)/shard_map/and | solution.py:51
  15.3 15.1 %collective-permute-done = bf16[2,512,1024]{1,2,0:T(8,128)(2,1)} collective-permute-done((bf16[2,512,1024]{1,2,0:T(8,128)(2,1)S(1)}, bf16[2,512,1024]{1,2,0:T(8,128)(2,1)}, u32[]{:S(2)}, u32[]{:S(2)}) %collective-permute-start) | collective-permute-done | bytes 2097184 | tf_op jit(solution)/shard_map/ppermute | solution.py:13
  31.7 1.9 %collective-permute-start.1 = (bf16[2,256,1024]{1,2,0:T(8,128)(2,1)S(1)}, bf16[2,256,1024]{1,2,0:T(8,128)(2,1)S(1)}, u32[]{:S(2)}, u32[]{:S(2)}) collective-permute-start(bf16[2,256,1024]{1,2,0:T(8,128)(2,1)S(1)} %slice.91), channel_id=1, source_target_pairs={{0,4},{4,8},{8,12},{12,16},{16,20},{20,24},{24,28},{28,32},{32,36}... | collective-permute-start | bytes 3145736 | tf_op jit(solution)/shard_map/ppermute | solution.py:13
  33.7 2.1 %fusion.61 = (bf16[2,128,1024]{1,2,0:T(8,128)(2,1)S(1)}, bf16[2,128,1024]{1,2,0:T(8,128)(2,1)}) fusion(bf16[2,512,1024]{1,2,0:T(8,128)(2,1)} %collective-permute-done), kind=kLoop, calls=%fused_computation.74 | loop fusion | bytes 2097152 | tf_op jit(solution)/shard_map/slice | solution.py:27
  35.8 4.2 %collective-permute-start.5 = (bf16[2,128,1024]{1,2,0:T(8,128)(2,1)S(1)}, bf16[2,128,1024]{1,2,0:T(8,128)(2,1)S(1)}, u32[]{:S(2)}, u32[]{:S(2)}) collective-permute-start(bf16[2,128,1024]{1,2,0:T(8,128)(2,1)S(1)} %get-tuple-element.17), channel_id=1, source_target_pairs={{0,4},{4,8},{8,12},{12,16},{16,20},{20,24},{24,28},{28,32},{32,36}... | collective-permute-start | bytes 1572872 | tf_op jit(solution)/shard_map/ppermute | solution.py:13
  40.0 2.1 %compare_and_fusion.1 = (pred[128,1280]{0,1:T(8,128)(4,1)S(1)}, pred[128,1280]{0,1:T(8,128)(4,1)}) fusion(s32[128]{0:T(128)S(1)} %iota_add_fusion.5, s32[128]{0:T(128)S(1)} %get-tuple-element.34, s32[1280]{0:T(1024)S(1)} %iota_add_fusion.2, s32[1280]{0:T(1024)S(1)} %get-tuple-element.30, s32[128]{0:T(128)S(1)} %iota_add_fusion.6, ...), kind=kLoop, calls=%fused_computation.47 | loop fusion | flops 983040 | bytes 350208 | tf_op jit(solution)/shard_map/and | solution.py:51
  42.1 1.9 %collective-permute-start.9 = (bf16[2,128,1024]{1,2,0:T(8,128)(2,1)}, bf16[2,128,1024]{1,2,0:T(8,128)(2,1)}, u32[]{:S(2)}, u32[]{:S(2)}) collective-permute-start(bf16[2,128,1024]{1,2,0:T(8,128)(2,1)} %get-tuple-element.18), channel_id=1, source_target_pairs={{0,4},{4,8},{8,12},{12,16},{16,20},{20,24},{24,28},{28,32},{32,36}... | collective-permute-start | bytes 1572872 | tf_op jit(solution)/shard_map/ppermute | solution.py:13
  44.0 9.4 %collective-permute-done.5 = bf16[2,128,1024]{1,2,0:T(8,128)(2,1)S(1)} collective-permute-done((bf16[2,128,1024]{1,2,0:T(8,128)(2,1)S(1)}, bf16[2,128,1024]{1,2,0:T(8,128)(2,1)S(1)}, u32[]{:S(2)}, u32[]{:S(2)}) %collective-permute-start.5) | collective-permute-done | bytes 524320 | tf_op jit(solution)/shard_map/ppermute | solution.py:13
  53.5 3.5 %pad_maximum_fusion = (bf16[2,1280,1024]{1,2,0:T(8,128)(2,1)S(1)}, bf16[2,1280,1024]{1,2,0:T(8,128)(2,1)S(1)}) fusion(bf16[2,512,1024]{1,2,0:T(8,128)(2,1)S(1)} %copy.13, bf16[2,512,1024]{1,2,0:T(8,128)(2,1)} %collective-permute-done, bf16[2,256,1024]{1,2,0:T(8,128)(2,1)S(1)} %collective-permute-done.1, bf16[2,384,1024]{1,2,0:T(8,128)(2,1)S(1)} %copy-done, ...), kind=kLoop, calls=%fused_computation | loop fusion | flops 36700160 | bytes 17825792 | tf_op jit(solution)/shard_map/concatenate | solution.py:44
  63.5 6.7 %collective-permute-start.7 = (bf16[128,4096]{1,0:T(8,128)(2,1)S(1)}, bf16[128,4096]{1,0:T(8,128)(2,1)}, u32[]{:S(2)}, u32[]{:S(2)}) collective-permute-start(bf16[128,4096]{1,0:T(8,128)(2,1)S(1)} %convolution_convert_fusion.2), channel_id=1, source_target_pairs={{0,2},{4,6},{8,10},{12,14},{16,18},{20,22},{24,26},{28,30},{32,34}... | collective-permute-start | bytes 3145736 | tf_op jit(solution)/shard_map/ppermute | solution.py:70
  71.8 2.1 %collective-permute-start.13 = (bf16[2,128,1024]{1,2,0:T(8,128)(2,1)S(1)}, bf16[2,128,1024]{1,2,0:T(8,128)(2,1)S(1)}, u32[]{:S(2)}, u32[]{:S(2)}) collective-permute-start(bf16[2,128,1024]{1,2,0:T(8,128)(2,1)S(1)} %slice.102), channel_id=1, source_target_pairs={{0,4},{4,8},{8,12},{12,16},{16,20},{20,24},{24,28},{28,32},{32,36}... | collective-permute-start | bytes 1572872 | tf_op jit(solution)/shard_map/ppermute | solution.py:13
  78.4 3.9 %collective-permute-done.13 = bf16[2,128,1024]{1,2,0:T(8,128)(2,1)S(1)} collective-permute-done((bf16[2,128,1024]{1,2,0:T(8,128)(2,1)S(1)}, bf16[2,128,1024]{1,2,0:T(8,128)(2,1)S(1)}, u32[]{:S(2)}, u32[]{:S(2)}) %collective-permute-start.13) | collective-permute-done | bytes 524320 | tf_op jit(solution)/shard_map/ppermute | solution.py:13
  82.3 2.9 %collective-permute-start.4 = (bf16[128,4096]{1,0:T(8,128)(2,1)S(1)}, bf16[128,4096]{1,0:T(8,128)(2,1)}, u32[]{:S(2)}, u32[]{:S(2)}) collective-permute-start(bf16[128,4096]{1,0:T(8,128)(2,1)S(1)} %convolution_convert_fusion.3), channel_id=1, source_target_pairs={{0,3},{4,7},{8,11},{12,15},{16,19},{20,23},{24,27},{28,31},{32,35}... | collective-permute-start | bytes 3145736 | tf_op jit(solution)/shard_map/ppermute | solution.py:70
  88.7 1.9 %constant_dynamic-update-slice_fusion = (bf16[2,1280,1024]{1,2,0:T(8,128)(2,1)S(1)}, bf16[2,1280,1024]{1,2,0:T(8,128)(2,1)S(1)}) fusion(bf16[2,1280,1024]{1,2,0:T(8,128)(2,1)S(1)} %get-tuple-element.23, bf16[2,512,1024]{1,2,0:T(8,128)(2,1)} %collective-permute-done, bf16[2,1280,1024]{1,2,0:T(8,128)(2,1)S(1)} %get-tuple-element.24), kind=kLoop, calls=%fused_computation.54 | loop fusion | bytes 6291456
  90.7 1.9 %fusion.60 = (bf16[1,1280,1024]{1,2,0:T(8,128)(2,1)S(1)}, bf16[1,1280,1024]{1,2,0:T(8,128)(2,1)}) fusion(bf16[2,1280,1024]{1,2,0:T(8,128)(2,1)S(1)} %slice_dynamic-update-slice_fusion.1), kind=kLoop, calls=%fused_computation.73 | loop fusion | bytes 10485760 | tf_op jit(solution)/shard_map/slice | solution.py:45
  104.2 2.3 %convolution_convert_fusion.1 = bf16[128,4096]{1,0:T(8,128)(2,1)} fusion(bf16[128,1024]{0,1:T(8,128)(2,1)S(1)} %bitcast.89, bf16[1024,4096]{1,0:T(8,128)(2,1)S(1)} %bitcast.73), kind=kOutput, calls=%fused_computation.11 | convolution fusion | flops 1074266112 | bytes 9699328 | tf_op jit(solution)/shard_map/dot_general | solution.py:61
  107.7 21.5 %collective-permute-done.4 = bf16[128,4096]{1,0:T(8,128)(2,1)} collective-permute-done((bf16[128,4096]{1,0:T(8,128)(2,1)S(1)}, bf16[128,4096]{1,0:T(8,128)(2,1)}, u32[]{:S(2)}, u32[]{:S(2)}) %collective-permute-start.4) | collective-permute-done | bytes 1048608 | tf_op jit(solution)/shard_map/ppermute | solution.py:70
  133.8 2.3 %collective-permute-start.10 = (bf16[128,4096]{1,0:T(8,128)(2,1)}, bf16[128,4096]{1,0:T(8,128)(2,1)}, u32[]{:S(2)}, u32[]{:S(2)}) collective-permute-start(bf16[128,4096]{1,0:T(8,128)(2,1)} %convolution_convert_fusion.1), channel_id=1, source_target_pairs={{0,1},{4,5},{8,9},{12,13},{16,17},{20,21},{24,25},{28,29},{32,33},... | collective-permute-start | bytes 3145736 | tf_op jit(solution)/shard_map/ppermute | solution.py:70
  136.1 11.2 %collective-permute-done.15 = bf16[128,4096]{1,0:T(8,128)(2,1)} collective-permute-done((bf16[128,4096]{1,0:T(8,128)(2,1)S(1)}, bf16[128,4096]{1,0:T(8,128)(2,1)}, u32[]{:S(2)}, u32[]{:S(2)}) %collective-permute-start.15) | collective-permute-done | bytes 1048608 | tf_op jit(solution)/shard_map/ppermute | solution.py:70
  147.3 23.4 %collective-permute-done.14 = bf16[128,4096]{1,0:T(8,128)(2,1)} collective-permute-done((bf16[128,4096]{1,0:T(8,128)(2,1)S(1)}, bf16[128,4096]{1,0:T(8,128)(2,1)}, u32[]{:S(2)}, u32[]{:S(2)}) %collective-permute-start.14) | collective-permute-done | bytes 1048608 | tf_op jit(solution)/shard_map/ppermute | solution.py:70
  170.7 6.7 %add_convert_fusion = bf16[128,4096]{1,0:T(8,128)(2,1)} fusion(bf16[128,4096]{1,0:T(8,128)(2,1)} %collective-permute-done.16, bf16[128,4096]{1,0:T(8,128)(2,1)} %collective-permute-done.15, bf16[128,4096]{1,0:T(8,128)(2,1)} %collective-permute-done.14, bf16[128,4096]{1,0:T(8,128)(2,1)} %collective-permute-done.12, ...), kind=kLoop, calls=%fused_computation.30 | loop fusion | flops 18874368 | bytes 17825796 | tf_op jit(solution)/shard_map/convert_element_type | solution.py:74
  (86 shorter events, 41.4 us)
Async XLA Ops:
  0.0 13.0 %copy-start.10 = (s32[16384]{0:T(1024)S(1)}, s32[16384]{0:T(1024)}, u32[]{:S(2)}) copy-start(s32[16384]{0:T(1024)} %param.7) | copy-start | bytes 196612
  3.0 27.5 %collective-permute-start = (bf16[2,512,1024]{1,2,0:T(8,128)(2,1)S(1)}, bf16[2,512,1024]{1,2,0:T(8,128)(2,1)}, u32[]{:S(2)}, u32[]{:S(2)}) collective-permute-start(bf16[2,512,1024]{1,2,0:T(8,128)(2,1)S(1)} %copy.13), channel_id=1, source_target_pairs={{0,4},{4,8},{8,12},{12,16},{16,20},{20,24},{24,28},{28,32},{32,36}... | collective-permute-start | bytes 6291464 | tf_op jit(solution)/shard_map/ppermute | solution.py:13
  13.0 40.4 %copy-start = (bf16[2,384,1024]{1,2,0:T(8,128)(2,1)S(1)}, bf16[2,384,1024]{1,2,0:T(8,128)(2,1)}, u32[]{:S(2)}) copy-start(bf16[2,384,1024]{1,2,0:T(8,128)(2,1)} %slice.95) | copy-start | bytes 4718596
  31.7 21.7 %collective-permute-start.1 = (bf16[2,256,1024]{1,2,0:T(8,128)(2,1)S(1)}, bf16[2,256,1024]{1,2,0:T(8,128)(2,1)S(1)}, u32[]{:S(2)}, u32[]{:S(2)}) collective-permute-start(bf16[2,256,1024]{1,2,0:T(8,128)(2,1)S(1)} %slice.91), channel_id=1, source_target_pairs={{0,4},{4,8},{8,12},{12,16},{16,20},{20,24},{24,28},{28,32},{32,36}... | collective-permute-start | bytes 3145736 | tf_op jit(solution)/shard_map/ppermute | solution.py:13
  35.8 17.7 %collective-permute-start.5 = (bf16[2,128,1024]{1,2,0:T(8,128)(2,1)S(1)}, bf16[2,128,1024]{1,2,0:T(8,128)(2,1)S(1)}, u32[]{:S(2)}, u32[]{:S(2)}) collective-permute-start(bf16[2,128,1024]{1,2,0:T(8,128)(2,1)S(1)} %get-tuple-element.17), channel_id=1, source_target_pairs={{0,4},{4,8},{8,12},{12,16},{16,20},{20,24},{24,28},{28,32},{32,36}... | collective-permute-start | bytes 1572872 | tf_op jit(solution)/shard_map/ppermute | solution.py:13
  42.1 43.2 %collective-permute-start.9 = (bf16[2,128,1024]{1,2,0:T(8,128)(2,1)}, bf16[2,128,1024]{1,2,0:T(8,128)(2,1)}, u32[]{:S(2)}, u32[]{:S(2)}) collective-permute-start(bf16[2,128,1024]{1,2,0:T(8,128)(2,1)} %get-tuple-element.18), channel_id=1, source_target_pairs={{0,4},{4,8},{8,12},{12,16},{16,20},{20,24},{24,28},{28,32},{32,36}... | collective-permute-start | bytes 1572872 | tf_op jit(solution)/shard_map/ppermute | solution.py:13
  61.5 12.4 %copy-start.6 = (bf16[128,1024]{0,1:T(8,128)(2,1)S(1)}, bf16[128,1024]{0,1:T(8,128)(2,1)}, u32[]{:S(2)}) copy-start(bf16[128,1024]{0,1:T(8,128)(2,1)} %copy.46) | copy-start | bytes 786436
  61.5 12.5 %copy-start.9 = (pred[128,1280]{0,1:T(8,128)(4,1)S(1)}, pred[128,1280]{0,1:T(8,128)(4,1)}, u32[]{:S(2)}) copy-start(pred[128,1280]{0,1:T(8,128)(4,1)} %get-tuple-element.50) | copy-start | bytes 491524
  62.8 37.4 %collective-permute-start.8 = (bf16[128,4096]{1,0:T(8,128)(2,1)S(1)}, bf16[128,4096]{1,0:T(8,128)(2,1)S(1)}, u32[]{:S(2)}, u32[]{:S(2)}) collective-permute-start(bf16[128,4096]{1,0:T(8,128)(2,1)S(1)} %convolution_convert_fusion.2), channel_id=1, source_target_pairs={{3,2},{7,6},{11,10},{15,14},{19,18},{23,22},{27,26},{31,30},{35,34... | collective-permute-start | bytes 3145736 | tf_op jit(solution)/shard_map/ppermute | solution.py:70
  63.5 38.4 %collective-permute-start.7 = (bf16[128,4096]{1,0:T(8,128)(2,1)S(1)}, bf16[128,4096]{1,0:T(8,128)(2,1)}, u32[]{:S(2)}, u32[]{:S(2)}) collective-permute-start(bf16[128,4096]{1,0:T(8,128)(2,1)S(1)} %convolution_convert_fusion.2), channel_id=1, source_target_pairs={{0,2},{4,6},{8,10},{12,14},{16,18},{20,22},{24,26},{28,30},{32,34}... | collective-permute-start | bytes 3145736 | tf_op jit(solution)/shard_map/ppermute | solution.py:70
  70.2 36.3 %collective-permute-start.6 = (bf16[128,4096]{1,0:T(8,128)(2,1)S(1)}, bf16[128,4096]{1,0:T(8,128)(2,1)}, u32[]{:S(2)}, u32[]{:S(2)}) collective-permute-start(bf16[128,4096]{1,0:T(8,128)(2,1)S(1)} %convolution_convert_fusion.2), channel_id=1, source_target_pairs={{1,2},{5,6},{9,10},{13,14},{17,18},{21,22},{25,26},{29,30},{33,34}... | collective-permute-start | bytes 3145736 | tf_op jit(solution)/shard_map/ppermute | solution.py:70
  71.8 10.5 %collective-permute-start.13 = (bf16[2,128,1024]{1,2,0:T(8,128)(2,1)S(1)}, bf16[2,128,1024]{1,2,0:T(8,128)(2,1)S(1)}, u32[]{:S(2)}, u32[]{:S(2)}) collective-permute-start(bf16[2,128,1024]{1,2,0:T(8,128)(2,1)S(1)} %slice.102), channel_id=1, source_target_pairs={{0,4},{4,8},{8,12},{12,16},{16,20},{20,24},{24,28},{28,32},{32,36}... | collective-permute-start | bytes 1572872 | tf_op jit(solution)/shard_map/ppermute | solution.py:13
  78.4 21.8 %copy-start.1 = (bf16[128,4096]{1,0:T(8,128)(2,1)}, bf16[128,4096]{1,0:T(8,128)(2,1)S(1)}, u32[]{:S(2)}) copy-start(bf16[128,4096]{1,0:T(8,128)(2,1)S(1)} %convolution_convert_fusion.3) | copy-start | bytes 3145732
  82.3 46.9 %collective-permute-start.4 = (bf16[128,4096]{1,0:T(8,128)(2,1)S(1)}, bf16[128,4096]{1,0:T(8,128)(2,1)}, u32[]{:S(2)}, u32[]{:S(2)}) collective-permute-start(bf16[128,4096]{1,0:T(8,128)(2,1)S(1)} %convolution_convert_fusion.3), channel_id=1, source_target_pairs={{0,3},{4,7},{8,11},{12,15},{16,19},{20,23},{24,27},{28,31},{32,35}... | collective-permute-start | bytes 3145736 | tf_op jit(solution)/shard_map/ppermute | solution.py:70
  85.3 45.2 %collective-permute-start.3 = (bf16[128,4096]{1,0:T(8,128)(2,1)S(1)}, bf16[128,4096]{1,0:T(8,128)(2,1)}, u32[]{:S(2)}, u32[]{:S(2)}) collective-permute-start(bf16[128,4096]{1,0:T(8,128)(2,1)S(1)} %convolution_convert_fusion.3), channel_id=1, source_target_pairs={{1,3},{5,7},{9,11},{13,15},{17,19},{21,23},{25,27},{29,31},{33,35}... | collective-permute-start | bytes 3145736 | tf_op jit(solution)/shard_map/ppermute | solution.py:70
  100.2 6.2 %copy-start.4 = (bf16[128,4096]{1,0:T(8,128)(2,1)}, bf16[128,4096]{1,0:T(8,128)(2,1)S(1)}, u32[]{:S(2)}) copy-start(bf16[128,4096]{1,0:T(8,128)(2,1)S(1)} %collective-permute-done.8) | copy-start | bytes 3145732
  100.2 31.9 %collective-permute-start.2 = (bf16[128,4096]{1,0:T(8,128)(2,1)S(1)}, bf16[128,4096]{1,0:T(8,128)(2,1)}, u32[]{:S(2)}, u32[]{:S(2)}) collective-permute-start(bf16[128,4096]{1,0:T(8,128)(2,1)S(1)} %convolution_convert_fusion.3), channel_id=1, source_target_pairs={{2,3},{6,7},{10,11},{14,15},{18,19},{22,23},{26,27},{30,31},{34,35... | collective-permute-start | bytes 3145736 | tf_op jit(solution)/shard_map/ppermute | solution.py:70
  101.9 31.9 %collective-permute-start.16 = (bf16[128,4096]{1,0:T(8,128)(2,1)S(1)}, bf16[128,4096]{1,0:T(8,128)(2,1)}, u32[]{:S(2)}, u32[]{:S(2)}) collective-permute-start(bf16[128,4096]{1,0:T(8,128)(2,1)S(1)} %convolution_convert_fusion), channel_id=1, source_target_pairs={{1,0},{5,4},{9,8},{13,12},{17,16},{21,20},{25,24},{29,28},{33,32},... | collective-permute-start | bytes 3145736 | tf_op jit(solution)/shard_map/ppermute | solution.py:70
  104.2 66.5 %copy-start.2 = (bf16[128,4096]{1,0:T(8,128)(2,1)S(1)}, bf16[128,4096]{1,0:T(8,128)(2,1)}, u32[]{:S(2)}) copy-start(bf16[128,4096]{1,0:T(8,128)(2,1)} %copy-done.1) | copy-start | bytes 3145732
  106.5 40.8 %collective-permute-start.15 = (bf16[128,4096]{1,0:T(8,128)(2,1)S(1)}, bf16[128,4096]{1,0:T(8,128)(2,1)}, u32[]{:S(2)}, u32[]{:S(2)}) collective-permute-start(bf16[128,4096]{1,0:T(8,128)(2,1)S(1)} %convolution_convert_fusion), channel_id=1, source_target_pairs={{2,0},{6,4},{10,8},{14,12},{18,16},{22,20},{26,24},{30,28},{34,32}... | collective-permute-start | bytes 3145736 | tf_op jit(solution)/shard_map/ppermute | solution.py:70
  129.2 41.5 %collective-permute-start.14 = (bf16[128,4096]{1,0:T(8,128)(2,1)S(1)}, bf16[128,4096]{1,0:T(8,128)(2,1)}, u32[]{:S(2)}, u32[]{:S(2)}) collective-permute-start(bf16[128,4096]{1,0:T(8,128)(2,1)S(1)} %convolution_convert_fusion), channel_id=1, source_target_pairs={{3,0},{7,4},{11,8},{15,12},{19,16},{23,20},{27,24},{31,28},{35,32}... | collective-permute-start | bytes 3145736 | tf_op jit(solution)/shard_map/ppermute | solution.py:70
  130.5 40.2 %collective-permute-start.12 = (bf16[128,4096]{1,0:T(8,128)(2,1)}, bf16[128,4096]{1,0:T(8,128)(2,1)}, u32[]{:S(2)}, u32[]{:S(2)}) collective-permute-start(bf16[128,4096]{1,0:T(8,128)(2,1)} %convolution_convert_fusion.1), channel_id=1, source_target_pairs={{2,1},{6,5},{10,9},{14,13},{18,17},{22,21},{26,25},{30,29},{34,33}... | collective-permute-start | bytes 3145736 | tf_op jit(solution)/shard_map/ppermute | solution.py:70
  132.2 38.5 %collective-permute-start.11 = (bf16[128,4096]{1,0:T(8,128)(2,1)}, bf16[128,4096]{1,0:T(8,128)(2,1)}, u32[]{:S(2)}, u32[]{:S(2)}) collective-permute-start(bf16[128,4096]{1,0:T(8,128)(2,1)} %convolution_convert_fusion.1), channel_id=1, source_target_pairs={{3,1},{7,5},{11,9},{15,13},{19,17},{23,21},{27,25},{31,29},{35,33}... | collective-permute-start | bytes 3145736 | tf_op jit(solution)/shard_map/ppermute | solution.py:70
  133.8 36.9 %collective-permute-start.10 = (bf16[128,4096]{1,0:T(8,128)(2,1)}, bf16[128,4096]{1,0:T(8,128)(2,1)}, u32[]{:S(2)}, u32[]{:S(2)}) collective-permute-start(bf16[128,4096]{1,0:T(8,128)(2,1)} %convolution_convert_fusion.1), channel_id=1, source_target_pairs={{0,1},{4,5},{8,9},{12,13},{16,17},{20,21},{24,25},{28,29},{32,33},... | collective-permute-start | bytes 3145736 | tf_op jit(solution)/shard_map/ppermute | solution.py:70
  (6 other events, 16.9 us)

commit v3 on v1

v3 whole, which is shorter than its diff:
```python
import functools

import jax
import jax.numpy as jnp
from jax import lax
from jax.experimental import pallas as pl
from jax.experimental.pallas import tpu as pltpu
from jax.sharding import PartitionSpec as P

HD = 128
DOC_MOST = 1152
CHUNK = 128
NEG = -1e30


def shift_up(x, axis):
    peers = lax.axis_size(axis)
    return lax.ppermute(x, axis, [(i, i + 1) for i in range(peers - 1)])


def rotate(x, axis, by):
    peers = lax.axis_size(axis)
    return lax.ppermute(x, axis, [(i, (i + by) % peers) for i in range(peers)])


def attend_kernel(heads, steps, sp, q_ref, qdoc_ref, kdoc_ref, tail_ref, win_ref, o_ref, m_sc, l_sc, acc_sc):
    t = pl.program_id(0)
    c = sp[0]
    lo = sp[1]
    kb = c + t

    @pl.when(t == 0)
    def _():
        m_sc[...] = jnp.full_like(m_sc, NEG)
        l_sc[...] = jnp.zeros_like(l_sc)
        acc_sc[...] = jnp.zeros_like(acc_sc)

    def body(kv_ref):
        q_place = c * CHUNK + lax.broadcasted_iota(jnp.int32, (CHUNK, CHUNK), 0)
        k_place = kb * CHUNK - DOC_MOST + lax.broadcasted_iota(jnp.int32, (CHUNK, CHUNK), 1)
        allowed = (kdoc_ref[...] == qdoc_ref[...]) & (k_place <= q_place)
        for hh in range(heads):
            cols = slice(hh * HD, (hh + 1) * HD)
            raw = lax.dot_general(
                q_ref[:, cols], kv_ref[0, :, cols], (((1,), (1,)), ((), ())),
                preferred_element_type=jnp.float32,
            ) * HD ** (-0.5)
            s = jnp.where(allowed, raw, jnp.float32(NEG))
            m_old = m_sc[hh]
            m_new = jnp.maximum(m_old, jnp.max(s, axis=1, keepdims=True))
            alpha = jnp.exp(m_old - m_new)
            p = jnp.exp(s - m_new)
            l_sc[hh] = alpha * l_sc[hh] + jnp.sum(p, axis=1, keepdims=True)
            acc_sc[hh] = alpha * acc_sc[hh] + jnp.dot(
                p.astype(jnp.bfloat16), kv_ref[1, :, cols], preferred_element_type=jnp.float32
            )
            m_sc[hh] = m_new

    @pl.when((kb >= lo) & (kb == 0))
    def _():
        body(tail_ref)

    @pl.when((kb >= lo) & (kb > 0))
    def _():
        body(win_ref)

    @pl.when(t == steps - 1)
    def _():
        for hh in range(heads):
            o_ref[:, hh * HD:(hh + 1) * HD] = (acc_sc[hh] / l_sc[hh]).astype(o_ref.dtype)


def attend_chunk(sp, queries, q_docs, k_docs, tail, window):
    rows, width = queries.shape
    heads = width // HD
    steps = DOC_MOST // CHUNK + 1
    blocks = window.shape[1] // CHUNK

    def win_map(t, sp):
        return (0, jnp.clip(jnp.maximum(sp[0] + t, sp[1]) - 1, 0, blocks - 1), 0)

    def kdoc_map(t, sp):
        return (0, jnp.maximum(sp[0] + t, sp[1]))

    return pl.pallas_call(
        functools.partial(attend_kernel, heads, steps),
        out_shape=jax.ShapeDtypeStruct((CHUNK, width), jnp.bfloat16),
        grid_spec=pltpu.PrefetchScalarGridSpec(
            num_scalar_prefetch=1,
            grid=(steps,),
            in_specs=[
                pl.BlockSpec((CHUNK, width), lambda t, sp: (sp[0], 0)),
                pl.BlockSpec((CHUNK, 1), lambda t, sp: (sp[0], 0)),
                pl.BlockSpec((1, CHUNK), kdoc_map),
                pl.BlockSpec((2, CHUNK, width), lambda t, sp: (0, 0, 0)),
                pl.BlockSpec((2, CHUNK, width), win_map),
            ],
            out_specs=pl.BlockSpec((CHUNK, width), lambda t, sp: (0, 0)),
            scratch_shapes=[
                pltpu.VMEM((heads, CHUNK, 1), jnp.float32),
                pltpu.VMEM((heads, CHUNK, 1), jnp.float32),
                pltpu.VMEM((heads, CHUNK, HD), jnp.float32),
            ],
        ),
        compiler_params=pltpu.CompilerParams(dimension_semantics=("arbitrary",)),
        cost_estimate=pl.CostEstimate(
            flops=4 * CHUNK * (DOC_MOST + CHUNK) * width,
            transcendentals=CHUNK * (DOC_MOST + CHUNK) * heads,
            bytes_accessed=2 * 2 * (DOC_MOST + CHUNK) * width + 4 * CHUNK * width,
        ),
    )(sp, queries, q_docs, k_docs, tail, window)


def per_device(queries, keys_values, w_out, doc_index):
    rows, width = queries.shape
    groups = lax.axis_size("head")
    me = lax.axis_index("ctx")
    h = lax.axis_index("head")
    first_row = me * rows
    tail_rows = DOC_MOST - 2 * rows
    r1 = shift_up(keys_values, "ctx")
    r2 = shift_up(r1, "ctx")
    r3 = shift_up(r2[:, rows - tail_rows:], "ctx")
    window = jnp.concatenate([r2, r1, keys_values], axis=1)
    padded_docs = jnp.concatenate([jnp.full((DOC_MOST,), -1, jnp.int32), doc_index])
    k_docs = lax.dynamic_slice_in_dim(padded_docs, first_row, DOC_MOST + rows).reshape(1, -1)
    q_docs = lax.dynamic_slice_in_dim(doc_index, first_row, rows).reshape(rows, 1)

    total_out = None
    for step in range(groups):
        by = (step + 1) % groups
        c = (h + by) % groups
        first_doc = doc_index[first_row + c * CHUNK]
        doc_start = jnp.sum((doc_index < first_doc).astype(jnp.int32))
        lo = jnp.clip((doc_start - first_row + DOC_MOST) // CHUNK, c, c + DOC_MOST // CHUNK)
        sp = jnp.stack([c, lo]).astype(jnp.int32)
        attended = attend_chunk(sp, queries, q_docs, k_docs, r3, window)
        part = jnp.dot(attended, w_out, preferred_element_type=jnp.float32).astype(jnp.bfloat16)
        if by:
            part = rotate(part, "head", by)
        part = part.astype(jnp.float32)
        total_out = part if total_out is None else total_out + part
    return total_out.astype(jnp.bfloat16)


def solution(mesh):
    in_specs = (P("ctx", "head"), P(None, "ctx", "head"), P("head", None), P())
    out_specs = P(("ctx", "head"), None)
    return jax.shard_map(
        per_device, mesh=mesh, in_specs=in_specs, out_specs=out_specs, check_vma=False
    )
```

time: 146 us -> 212 us (1.45)
  the two profiles are of different devices: /device:TPU:98 before, /device:TPU:31 now
where the time goes in v3:
time: 212 us; the launch traced here: 211 us
  Pallas kernels  90.9 us (43%)
  waiting for transfers between devices  61 us (29%)
  matrix products  23.2 us (11%)
  starting transfers between devices  15.4 us (7%)
  local copies, waits for them, and re-layouts  11.6 us (5%)
  other arithmetic  6.53 us (3%)
  between operations  2.8 us (1%)
    pallas_call x4, Pallas kernels, attend_chunk(): pl.pallas_call(functools.partial(attend_kernel, heads, steps), out_shape=...  90.9 us
    ppermute x3, waiting for transfers between devices, shift_up(): return lax.ppermute(x, axis, [(i, i + 1) for i in range(peers - 1)])  36.9 us
    ppermute x3, waiting for transfers between devices, rotate(): return lax.ppermute(x, axis, [(i, (i + by) % peers) for i in range(peers)])  24.1 us
    dot_general x4, matrix products, per_device(): jnp.dot(attended, w_out, preferred_element_type=jnp.float32)  23.2 us
    ppermute x3, starting transfers between devices, shift_up(): return lax.ppermute(x, axis, [(i, i + 1) for i in range(peers - 1)])  12.8 us
    unnamed x6, local copies, waits for them, and re-layouts  5.48 us
  transfers between devices with their start and end apart: 6, of which 3 were waited for; matrix products, arithmetic and copies ran while one was open for 8% of the time, Pallas kernels for 4%

profile of v3, /device:TPU:31, one launch (start us, length us, event | category | flops | bytes accessed | tf_op | source)
XLA Modules:
  0.0 211.4 jit_solution(18269879473442134978)
XLA Ops:
  0.0 4.1 %collective-permute-start = (bf16[2,512,1024]{2,1,0:T(8,128)(2,1)}, bf16[2,512,1024]{2,1,0:T(8,128)(2,1)}, u32[]{:S(2)}, u32[]{:S(2)}) collective-permute-start(bf16[2,512,1024]{2,1,0:T(8,128)(2,1)} %param.5), channel_id=1, source_target_pairs={{0,4},{4,8},{8,12},{12,16},{16,20},{20,24},{24,28},{28,32},{32,36}... | collective-permute-start | bytes 6291464 | tf_op jit(solution)/shard_map/ppermute | solution.py:18
  4.1 23.3 %collective-permute-done = bf16[2,512,1024]{2,1,0:T(8,128)(2,1)} collective-permute-done((bf16[2,512,1024]{2,1,0:T(8,128)(2,1)}, bf16[2,512,1024]{2,1,0:T(8,128)(2,1)}, u32[]{:S(2)}, u32[]{:S(2)}) %collective-permute-start) | collective-permute-done | bytes 2097184 | tf_op jit(solution)/shard_map/ppermute | solution.py:18
  27.4 4.4 %collective-permute-start.1 = (bf16[2,512,1024]{2,1,0:T(8,128)(2,1)}, bf16[2,512,1024]{2,1,0:T(8,128)(2,1)S(1)}, u32[]{:S(2)}, u32[]{:S(2)}) collective-permute-start(bf16[2,512,1024]{2,1,0:T(8,128)(2,1)} %collective-permute-done), channel_id=1, source_target_pairs={{0,4},{4,8},{8,12},{12,16},{16,20},{20,24},{24,28},{28,32},{32,36}... | collective-permute-start | bytes 6291464 | tf_op jit(solution)/shard_map/ppermute | solution.py:18
  31.8 1.5 fusion.1
  33.3 4.0 %convert_reduce_fusion.3 = (s32[]{:T(128)}, s32[]{:T(128)}, s32[]{:T(128)}, s32[]{:T(128)}) fusion(s32[16384]{0:T(1024)} %param.7, s32[]{:T(128)} %bitcast.1, s32[]{:T(128)} %bitcast.8, s32[]{:T(128)} %bitcast.5, s32[]{:T(128)} %bitcast.11), kind=kLoop, calls=%fused_computation.10 | loop fusion | flops 196604 | bytes 65568 | tf_op jit(solution)/shard_map/reduce_sum | solution.py:134
  40.6 0.8 pad_dynamic-slice_fusion
  41.4 13.6 %collective-permute-done.1 = bf16[2,512,1024]{2,1,0:T(8,128)(2,1)S(1)} collective-permute-done((bf16[2,512,1024]{2,1,0:T(8,128)(2,1)}, bf16[2,512,1024]{2,1,0:T(8,128)(2,1)S(1)}, u32[]{:S(2)}, u32[]{:S(2)}) %collective-permute-start.1) | collective-permute-done | bytes 2097184 | tf_op jit(solution)/shard_map/ppermute | solution.py:18
  55.1 4.3 %collective-permute-start.2 = (bf16[2,128,1024]{2,1,0:T(8,128)(2,1)S(1)}, bf16[2,128,1024]{2,1,0:T(8,128)(2,1)S(1)}, u32[]{:S(2)}, u32[]{:S(2)}) collective-permute-start(bf16[2,128,1024]{2,1,0:T(8,128)(2,1)S(1)} %slice.4), channel_id=1, source_target_pairs={{0,4},{4,8},{8,12},{12,16},{16,20},{20,24},{24,28},{28,32},{32,36}... | collective-permute-start | bytes 1572872 | tf_op jit(solution)/shard_map/ppermute | solution.py:18
  60.0 0.8 dynamic_slice.19
  61.3 0.9 copy.5.qdoc_ref
  62.2 1.5 constant_dynamic-update-slice_fusion.2
  63.7 3.2 %constant_dynamic-update-slice_fusion.1 = bf16[2,1536,1024]{2,1,0:T(8,128)(2,1)} fusion(bf16[2,1536,1024]{2,1,0:T(8,128)(2,1)} %constant_dynamic-update-slice_fusion.2, bf16[2,512,1024]{2,1,0:T(8,128)(2,1)} %collective-permute-done), kind=kLoop, calls=%fused_computation.12 | loop fusion | bytes 4194304
  66.9 1.5 constant_dynamic-update-slice_fusion.win_ref
  68.4 0.8 copy-done
  69.2 24.7 %shard_map.46 = bf16[128,1024]{1,0:T(8,128)(2,1)} custom-call(s32[2]{0:T(128)} %pad_add_fusion.sp, bf16[512,1024]{1,0:T(8,128)(2,1)} %q_ref.7, s32[512,1]{1,0:T(8,128)} %copy.5.qdoc_ref, s32[1,1664]{1,0:T(1,128)} %reshape.7.kdoc_ref, bf16[2,128,1024]{2,1,0:T(8,128)(2,1)} %copy-done, bf16[2,1536,1024]{2,1,0:T(8,128)(2,1)} %constant_dynamic-update-slice_fusion.win_ref), custom_call_target="tpu_custom_call" | custom-call | flops 671088640 | bytes 5767168 | tf_op jit(solution)/shard_map/pallas_call | solution.py:85
  93.9 5.8 %convolution_convert_fusion.3 = bf16[128,4096]{1,0:T(8,128)(2,1)} fusion(bf16[128,1024]{1,0:T(8,128)(2,1)} %shard_map.46, bf16[1024,4096]{1,0:T(8,128)(2,1)} %param.6), kind=kOutput, calls=%fused_computation.4 | convolution fusion | flops 1074266112 | bytes 9699328 | tf_op jit(solution)/shard_map/dot_general | solution.py:138
  99.6 27.3 %shard_map.47 = bf16[128,1024]{1,0:T(8,128)(2,1)} custom-call(s32[2]{0:T(128)} %pad_add_fusion.1.sp, bf16[512,1024]{1,0:T(8,128)(2,1)} %q_ref.7, s32[512,1]{1,0:T(8,128)} %copy.5.qdoc_ref, s32[1,1664]{1,0:T(1,128)} %reshape.7.kdoc_ref, bf16[2,128,1024]{2,1,0:T(8,128)(2,1)} %copy-done, bf16[2,1536,1024]{2,1,0:T(8,128)(2,1)} %constant_dynamic-update-slice_fusion.win_ref), custom_call_target="tpu_custom_call" | custom-call | flops 671088640 | bytes 5767168 | tf_op jit(solution)/shard_map/pallas_call | solution.py:85
  126.9 5.7 %convolution_convert_fusion.2 = bf16[128,4096]{1,0:T(8,128)(2,1)} fusion(bf16[128,1024]{1,0:T(8,128)(2,1)} %shard_map.47, bf16[1024,4096]{1,0:T(8,128)(2,1)} %param.6), kind=kOutput, calls=%fused_computation.3 | convolution fusion | flops 1074266112 | bytes 9699328 | tf_op jit(solution)/shard_map/dot_general | solution.py:138
  132.6 29.9 %shard_map.48 = bf16[128,1024]{1,0:T(8,128)(2,1)} custom-call(s32[2]{0:T(128)} %pad_add_fusion.2.sp, bf16[512,1024]{1,0:T(8,128)(2,1)} %q_ref.7, s32[512,1]{1,0:T(8,128)} %copy.5.qdoc_ref, s32[1,1664]{1,0:T(1,128)} %reshape.7.kdoc_ref, bf16[2,128,1024]{2,1,0:T(8,128)(2,1)} %copy-done, bf16[2,1536,1024]{2,1,0:T(8,128)(2,1)} %constant_dynamic-update-slice_fusion.win_ref), custom_call_target="tpu_custom_call" | custom-call | flops 671088640 | bytes 5767168 | tf_op jit(solution)/shard_map/pallas_call | solution.py:85
  162.5 5.7 %convolution_convert_fusion.1 = bf16[128,4096]{1,0:T(8,128)(2,1)} fusion(bf16[128,1024]{1,0:T(8,128)(2,1)} %shard_map.48, bf16[1024,4096]{1,0:T(8,128)(2,1)} %param.6), kind=kOutput, calls=%fused_computation.2 | convolution fusion | flops 1074266112 | bytes 9699328 | tf_op jit(solution)/shard_map/dot_general | solution.py:138
  168.3 2.7 %collective-permute-start.3 = (bf16[128,4096]{1,0:T(8,128)(2,1)}, bf16[128,4096]{1,0:T(8,128)(2,1)S(1)}, u32[]{:S(2)}, u32[]{:S(2)}) collective-permute-start(bf16[128,4096]{1,0:T(8,128)(2,1)} %convolution_convert_fusion.3), channel_id=1, source_target_pairs={{0,1},{1,2},{2,3},{3,0},{4,5},{5,6},{6,7},{7,4},{8,9},{9,10},{10,1... | collective-permute-start | bytes 3145736 | tf_op jit(solution)/shard_map/ppermute | solution.py:23
  172.3 9.0 %shard_map.49 = bf16[128,1024]{1,0:T(8,128)(2,1)} custom-call(s32[2]{0:T(128)} %pad_add_fusion.3.sp, bf16[512,1024]{1,0:T(8,128)(2,1)} %q_ref.7, s32[512,1]{1,0:T(8,128)} %copy.5.qdoc_ref, s32[1,1664]{1,0:T(1,128)} %reshape.7.kdoc_ref, bf16[2,128,1024]{2,1,0:T(8,128)(2,1)} %copy-done, bf16[2,1536,1024]{2,1,0:T(8,128)(2,1)} %constant_dynamic-update-slice_fusion.win_ref), custom_call_target="tpu_custom_call" | custom-call | flops 671088640 | bytes 5767168 | tf_op jit(solution)/shard_map/pallas_call | solution.py:85
  181.2 24.1 %collective-permute-done.5 = bf16[128,4096]{1,0:T(8,128)(2,1)S(1)} collective-permute-done((bf16[128,4096]{1,0:T(8,128)(2,1)}, bf16[128,4096]{1,0:T(8,128)(2,1)S(1)}, u32[]{:S(2)}, u32[]{:S(2)}) %collective-permute-start.5) | collective-permute-done | bytes 1048608 | tf_op jit(solution)/shard_map/ppermute | solution.py:23
  205.4 6.0 %add_convert_fusion = bf16[128,4096]{1,0:T(8,128)(2,1)} fusion(bf16[128,4096]{1,0:T(8,128)(2,1)S(1)} %collective-permute-done.5, bf16[128,4096]{1,0:T(8,128)(2,1)S(1)} %collective-permute-done.4, bf16[128,4096]{1,0:T(8,128)(2,1)S(1)} %collective-permute-done.3, bf16[128,1024]{1,0:T(8,128)(2,1)} %shard_map.49, bf16[1024,4096]{1,0:T(8,128)(2,1)} %param.6), kind=kOutput, calls=%fused_computation.5 | convolution fusion | flops 1078460416 | bytes 12845056 | tf_op jit(solution)/shard_map/dot_general | solution.py:138
  (14 shorter events, 3.2 us)
Async XLA Ops:
  0.0 27.4 %collective-permute-start = (bf16[2,512,1024]{2,1,0:T(8,128)(2,1)}, bf16[2,512,1024]{2,1,0:T(8,128)(2,1)}, u32[]{:S(2)}, u32[]{:S(2)}) collective-permute-start(bf16[2,512,1024]{2,1,0:T(8,128)(2,1)} %param.5), channel_id=1, source_target_pairs={{0,4},{4,8},{8,12},{12,16},{16,20},{20,24},{24,28},{28,32},{32,36}... | collective-permute-start | bytes 6291464 | tf_op jit(solution)/shard_map/ppermute | solution.py:18
  27.4 27.7 %collective-permute-start.1 = (bf16[2,512,1024]{2,1,0:T(8,128)(2,1)}, bf16[2,512,1024]{2,1,0:T(8,128)(2,1)S(1)}, u32[]{:S(2)}, u32[]{:S(2)}) collective-permute-start(bf16[2,512,1024]{2,1,0:T(8,128)(2,1)} %collective-permute-done), channel_id=1, source_target_pairs={{0,4},{4,8},{8,12},{12,16},{16,20},{20,24},{24,28},{28,32},{32,36}... | collective-permute-start | bytes 6291464 | tf_op jit(solution)/shard_map/ppermute | solution.py:18
  55.1 13.3 %collective-permute-start.2 = (bf16[2,128,1024]{2,1,0:T(8,128)(2,1)S(1)}, bf16[2,128,1024]{2,1,0:T(8,128)(2,1)S(1)}, u32[]{:S(2)}, u32[]{:S(2)}) collective-permute-start(bf16[2,128,1024]{2,1,0:T(8,128)(2,1)S(1)} %slice.4), channel_id=1, source_target_pairs={{0,4},{4,8},{8,12},{12,16},{16,20},{20,24},{24,28},{28,32},{32,36}... | collective-permute-start | bytes 1572872 | tf_op jit(solution)/shard_map/ppermute | solution.py:18
  62.2 4.6 %copy-start.1 = (bf16[2,512,1024]{2,1,0:T(8,128)(2,1)S(1)}, bf16[2,512,1024]{2,1,0:T(8,128)(2,1)}, u32[]{:S(2)}) copy-start(bf16[2,512,1024]{2,1,0:T(8,128)(2,1)} %param.5) | copy-start | bytes 6291460
  68.4 0.8 copy-start
  168.3 37.1 %collective-permute-start.5 = (bf16[128,4096]{1,0:T(8,128)(2,1)}, bf16[128,4096]{1,0:T(8,128)(2,1)S(1)}, u32[]{:S(2)}, u32[]{:S(2)}) collective-permute-start(bf16[128,4096]{1,0:T(8,128)(2,1)} %convolution_convert_fusion.1), channel_id=1, source_target_pairs={{0,3},{1,0},{2,1},{3,2},{4,7},{5,4},{6,5},{7,6},{8,11},{9,8},{10,9... | collective-permute-start | bytes 3145736 | tf_op jit(solution)/shard_map/ppermute | solution.py:23
  168.3 37.1 %collective-permute-start.4 = (bf16[128,4096]{1,0:T(8,128)(2,1)}, bf16[128,4096]{1,0:T(8,128)(2,1)S(1)}, u32[]{:S(2)}, u32[]{:S(2)}) collective-permute-start(bf16[128,4096]{1,0:T(8,128)(2,1)} %convolution_convert_fusion.2), channel_id=1, source_target_pairs={{0,2},{1,3},{2,0},{3,1},{4,6},{5,7},{6,4},{7,5},{8,10},{9,11},{10,... | collective-permute-start | bytes 3145736 | tf_op jit(solution)/shard_map/ppermute | solution.py:23
  168.3 37.1 %collective-permute-start.3 = (bf16[128,4096]{1,0:T(8,128)(2,1)}, bf16[128,4096]{1,0:T(8,128)(2,1)S(1)}, u32[]{:S(2)}, u32[]{:S(2)}) collective-permute-start(bf16[128,4096]{1,0:T(8,128)(2,1)} %convolution_convert_fusion.3), channel_id=1, source_target_pairs={{0,1},{1,2},{2,3},{3,0},{4,5},{5,6},{6,7},{7,4},{8,9},{9,10},{10,1... | collective-permute-start | bytes 3145736 | tf_op jit(solution)/shard_map/ppermute | solution.py:23

commit v4 on v1

--- a/solution.py
+++ b/solution.py
@@ -30,29 +30,38 @@
     r1 = shift_up(keys_values, "ctx")
     r2 = shift_up(r1, "ctx")
     r3 = shift_up(r2[:, rows - tail:], "ctx")
-    window = jnp.concatenate([r3, r2, r1, keys_values], axis=1)
+    sources = [r3, r2, r1, keys_values]
+    offsets = [-DOC_MOST, -2 * rows, -rows, 0]
     padded_docs = jnp.concatenate([jnp.full((DOC_MOST,), -1, jnp.int32), doc_index])
-    span = DOC_MOST + CHUNK
     scale = HD ** (-0.5)
 
     def chunk_part(c):
         start = c * CHUNK
         q = lax.dynamic_slice_in_dim(queries, start, CHUNK, 0).reshape(CHUNK, heads, HD)
-        kv = lax.dynamic_slice_in_dim(window, start, span, 1)
-        k = kv[0].reshape(span, heads, HD)
-        v = kv[1].reshape(span, heads, HD)
         q_docs = lax.dynamic_slice_in_dim(doc_index, first_row + start, CHUNK)
-        k_docs = lax.dynamic_slice_in_dim(padded_docs, first_row + start, span)
         q_place = start + jnp.arange(CHUNK, dtype=jnp.int32)
-        k_place = start - DOC_MOST + jnp.arange(span, dtype=jnp.int32)
-        allowed = (k_docs[None, :] == q_docs[:, None]) & (k_place[None, :] <= q_place[:, None])
-        raw = jnp.einsum("qhd,khd->hqk", q, k, preferred_element_type=jnp.float32) * scale
-        scores = jnp.where(allowed[None], raw, jnp.float32(-1e30))
-        top = jnp.max(scores, axis=2, keepdims=True)
-        weights = jnp.exp(scores - top)
-        total = jnp.sum(weights, axis=2)
-        probs = weights.astype(jnp.bfloat16)
-        summed = jnp.einsum("hqk,khd->qhd", probs, v, preferred_element_type=jnp.float32)
+        score_list = []
+        for kv, off in zip(sources, offsets):
+            n = kv.shape[1]
+            k = kv[0].reshape(n, heads, HD)
+            k_docs = lax.dynamic_slice_in_dim(padded_docs, first_row + DOC_MOST + off, n)
+            k_place = off + jnp.arange(n, dtype=jnp.int32)
+            allowed = (k_docs[None, :] == q_docs[:, None]) & (k_place[None, :] <= q_place[:, None])
+            raw = jnp.einsum("qhd,khd->hqk", q, k, preferred_element_type=jnp.float32) * scale
+            score_list.append(jnp.where(allowed[None], raw, jnp.float32(-1e30)))
+        top = score_list[0].max(axis=2, keepdims=True)
+        for s in score_list[1:]:
+            top = jnp.maximum(top, s.max(axis=2, keepdims=True))
+        total = None
+        summed = None
+        for kv, s in zip(sources, score_list):
+            n = kv.shape[1]
+            weights = jnp.exp(s - top)
+            t = jnp.sum(weights, axis=2)
+            probs = weights.astype(jnp.bfloat16)
+            pv = jnp.einsum("hqk,khd->qhd", probs, kv[1].reshape(n, heads, HD), preferred_element_type=jnp.float32)
+            total = t if total is None else total + t
+            summed = pv if summed is None else summed + pv
         attended = (summed / jnp.transpose(total)[:, :, None]).astype(jnp.bfloat16)
         attended = attended.reshape(CHUNK, heads * HD)
         return jnp.dot(attended, w_out, preferred_element_type=jnp.float32).astype(jnp.bfloat16)

time: 146 us -> 142 us (0.973)
  waiting for transfers between devices: 91.5 us -> 65.6 us
  matrix products: 17.6 us -> 31.5 us
  local copies, waits for them, and re-layouts: 13 us -> 19.8 us
    ppermute x3, waiting for transfers between devices: 56 us -> 30.5 us  [shift_up(): return lax.ppermute(x, axis, [(i, i + 1) for i in range(peers - 1)])]
    dot_general x4 -> x16, matrix products: 3.93 us -> 12 us  [chunk_part(): jnp.einsum('hqk,khd->qhd', probs, kv[1].reshape(n, heads, HD), preferred_...]
    dot_general x4 -> x16, matrix products: 7.17 us -> 13.1 us  [chunk_part(): jnp.einsum('qhd,khd->hqk', q, k, preferred_element_type=jnp.float32) * scale]
    unnamed x29 -> x73, local copies, waits for them, and re-layouts: 3.92 us -> 9.13 us
    concatenate x1 -> x0, other arithmetic: 3.63 us -> none  [per_device(): window = jnp.concatenate([r3, r2, r1, keys_values], axis=1)]
    reduce_sum x4 -> x6, other arithmetic: 4.05 us -> 6.65 us  [chunk_part(): t = jnp.sum(weights, axis=2)]
    slice x1 -> x6, local copies, waits for them, and re-layouts: 6.5 us -> 8.12 us  [the longest x5 6.82 us: chunk_part(): kv[1].reshape(n, heads, HD)]
  transfers between devices with their start and end apart: 6 -> 6, of which waited for: 6 -> 6; matrix products, arithmetic and copies ran while one was open for 11% -> 28% of each run, Pallas kernels for 0% -> 0%
where the time goes in v4:
time: 142 us; the launch traced here: 140 us
  waiting for transfers between devices  65.6 us (46%)
  matrix products  31.5 us (22%)
  local copies, waits for them, and re-layouts  19.8 us (14%)
  starting transfers between devices  12.3 us (9%)
  other arithmetic  9.52 us (7%)
    ppermute x3, waiting for transfers between devices, rotate(): return lax.ppermute(x, axis, [(i, (i + by) % peers) for i in range(peers)])  35 us
    ppermute x3, waiting for transfers between devices, shift_up(): return lax.ppermute(x, axis, [(i, i + 1) for i in range(peers - 1)])  30.5 us
    dot_general x16, matrix products, chunk_part(): jnp.einsum('qhd,khd->hqk', q, k, preferred_element_type=jnp.float32) * scale  13.1 us
    dot_general x16, matrix products, chunk_part(): jnp.einsum('hqk,khd->qhd', probs, kv[1].reshape(n, heads, HD), preferred_...  12 us
    unnamed x73, local copies, waits for them, and re-layouts  9.13 us
    slice x5, local copies, waits for them, and re-layouts, chunk_part(): kv[1].reshape(n, heads, HD)  6.82 us
    reduce_sum x6, other arithmetic, chunk_part(): t = jnp.sum(weights, axis=2)  6.65 us
    dot_general x4, matrix products, chunk_part(): jnp.dot(attended, w_out, preferred_element_type=jnp.float32)  6.46 us
  transfers between devices with their start and end apart: 6, of which 6 were waited for; matrix products, arithmetic and copies ran while one was open for 28% of the time, Pallas kernels for 0%

profile of v4, /device:TPU:98, one launch (start us, length us, event | category | flops | bytes accessed | tf_op | source)
XLA Modules:
  0.0 139.5 jit_solution(16830340005301698893)
XLA Ops:
  0.0 3.9 %copy.14 = bf16[2,512,1024]{1,2,0:T(8,128)(2,1)} copy(bf16[2,512,1024]{2,1,0:T(8,128)(2,1)} %param.5) | data formatting | bytes 4194304 | tf_op args[1]
  4.0 2.0 %collective-permute-start = (bf16[2,512,1024]{1,2,0:T(8,128)(2,1)}, bf16[2,512,1024]{1,2,0:T(8,128)(2,1)}, u32[]{:S(2)}, u32[]{:S(2)}) collective-permute-start(bf16[2,512,1024]{1,2,0:T(8,128)(2,1)} %copy.14), channel_id=1, source_target_pairs={{0,4},{4,8},{8,12},{12,16},{16,20},{20,24},{24,28},{28,32},{32,36}... | collective-permute-start | bytes 6291464 | tf_op jit(solution)/shard_map/ppermute | solution.py:14
  12.5 1.6 %fusion.12 = (f32[8,128]{1,0:T(8,128)S(1)}, f32[8,128,512]{2,1,0:T(8,128)S(1)}) fusion(pred[128,512]{1,0:T(8,128)(4,1)S(1)} %get-tuple-element.58, bf16[128,8,128]{0,2,1:T(8,128)(2,1)} %bitcast.130, bf16[512,8,128]{0,2,1:T(8,128)(2,1)S(1)} %bitcast.106), kind=kOutput, calls=%fused_computation.41 | convolution fusion | flops 135789568 | bytes 3477504 | tf_op jit(solution)/shard_map/qhd,khd->hqk/dot_general | solution.py:50
  14.1 1.8 %fusion.9 = (f32[8,128]{1,0:T(8,128)S(1)}, f32[8,128,512]{2,1,0:T(8,128)}) fusion(pred[128,512]{1,0:T(8,128)(4,1)S(1)} %get-tuple-element.57, bf16[128,8,128]{0,2,1:T(8,128)(2,1)S(1)} %bitcast.126, bf16[512,8,128]{0,2,1:T(8,128)(2,1)S(1)} %bitcast.107), kind=kOutput, calls=%fused_computation.38 | convolution fusion | flops 135789568 | bytes 3477504 | tf_op jit(solution)/shard_map/qhd,khd->hqk/dot_general | solution.py:50
  15.9 1.9 %fusion.3 = (f32[8,128]{1,0:T(8,128)S(1)}, f32[8,128,512]{2,1,0:T(8,128)}) fusion(pred[128,512]{1,0:T(8,128)(4,1)S(1)} %get-tuple-element.47, bf16[128,8,128]{0,2,1:T(8,128)(2,1)S(1)} %bitcast.134, bf16[512,8,128]{0,2,1:T(8,128)(2,1)S(1)} %bitcast.108), kind=kOutput, calls=%fused_computation.32 | convolution fusion | flops 135789568 | bytes 3477504 | tf_op jit(solution)/shard_map/qhd,khd->hqk/dot_general | solution.py:50
  17.8 13.9 %collective-permute-done = bf16[2,512,1024]{1,2,0:T(8,128)(2,1)} collective-permute-done((bf16[2,512,1024]{1,2,0:T(8,128)(2,1)}, bf16[2,512,1024]{1,2,0:T(8,128)(2,1)}, u32[]{:S(2)}, u32[]{:S(2)}) %collective-permute-start) | collective-permute-done | bytes 2097184 | tf_op jit(solution)/shard_map/ppermute | solution.py:14
  31.7 1.9 %collective-permute-start.1 = (bf16[2,512,1024]{1,2,0:T(8,128)(2,1)}, bf16[2,512,1024]{1,2,0:T(8,128)(2,1)}, u32[]{:S(2)}, u32[]{:S(2)}) collective-permute-start(bf16[2,512,1024]{1,2,0:T(8,128)(2,1)} %collective-permute-done), channel_id=1, source_target_pairs={{0,4},{4,8},{8,12},{12,16},{16,20},{20,24},{24,28},{28,32},{32,36}... | collective-permute-start | bytes 6291464 | tf_op jit(solution)/shard_map/ppermute | solution.py:14
  35.2 2.4 %copy.25 = bf16[1,512,1024]{1,2,0:T(8,128)(2,1)} copy(bf16[1,512,1024]{2,1,0:T(8,128)(2,1)} %slice.26) | data formatting | bytes 2097152 | tf_op jit(solution)/shard_map/slice | solution.py:62
  37.5 1.8 %copy.93 = bf16[128,1024]{0,1:T(8,128)(2,1)} copy(bf16[128,1024]{1,0:T(8,128)(2,1)} %get-tuple-element.23) | data formatting | bytes 524288
  40.2 1.6 %fusion.6 = (f32[8,128]{1,0:T(8,128)S(1)}, f32[8,128,512]{2,1,0:T(8,128)S(1)}) fusion(pred[128,512]{1,0:T(8,128)(4,1)} %get-tuple-element.48, bf16[128,8,128]{0,2,1:T(8,128)(2,1)} %bitcast.138, bf16[512,8,128]{0,2,1:T(8,128)(2,1)S(1)} %bitcast.109), kind=kOutput, calls=%fused_computation.35 | convolution fusion | flops 135789568 | bytes 3477504 | tf_op jit(solution)/shard_map/qhd,khd->hqk/dot_general | solution.py:50
  41.8 1.7 %fusion.178 = (bf16[1,512,1024]{1,2,0:T(8,128)(2,1)S(1)}, bf16[1,512,1024]{1,2,0:T(8,128)(2,1)S(1)}) fusion(bf16[2,512,1024]{1,2,0:T(8,128)(2,1)} %collective-permute-done), kind=kLoop, calls=%fused_computation.242 | loop fusion | bytes 4194304 | tf_op jit(solution)/shard_map/slice | solution.py:62
  46.6 12.8 %collective-permute-done.1 = bf16[2,512,1024]{1,2,0:T(8,128)(2,1)} collective-permute-done((bf16[2,512,1024]{1,2,0:T(8,128)(2,1)}, bf16[2,512,1024]{1,2,0:T(8,128)(2,1)}, u32[]{:S(2)}, u32[]{:S(2)}) %collective-permute-start.1) | collective-permute-done | bytes 2097184 | tf_op jit(solution)/shard_map/ppermute | solution.py:14
  60.5 2.1 %collective-permute-start.2 = (bf16[2,128,1024]{1,2,0:T(8,128)(2,1)S(1)}, bf16[2,128,1024]{1,2,0:T(8,128)(2,1)S(1)}, u32[]{:S(2)}, u32[]{:S(2)}) collective-permute-start(bf16[2,128,1024]{1,2,0:T(8,128)(2,1)S(1)} %slice.27), channel_id=1, source_target_pairs={{0,4},{4,8},{8,12},{12,16},{16,20},{20,24},{24,28},{28,32},{32,36}... | collective-permute-start | bytes 1572872 | tf_op jit(solution)/shard_map/ppermute | solution.py:14
  62.6 1.7 %fusion.177 = (bf16[1,512,1024]{1,2,0:T(8,128)(2,1)S(1)}, bf16[1,512,1024]{1,2,0:T(8,128)(2,1)S(1)}) fusion(bf16[2,512,1024]{1,2,0:T(8,128)(2,1)} %collective-permute-done.1), kind=kLoop, calls=%fused_computation.241 | loop fusion | bytes 4194304 | tf_op jit(solution)/shard_map/slice | solution.py:62
  67.2 3.8 %collective-permute-done.2 = bf16[2,128,1024]{1,2,0:T(8,128)(2,1)S(1)} collective-permute-done((bf16[2,128,1024]{1,2,0:T(8,128)(2,1)S(1)}, bf16[2,128,1024]{1,2,0:T(8,128)(2,1)S(1)}, u32[]{:S(2)}, u32[]{:S(2)}) %collective-permute-start.2) | collective-permute-done | bytes 524320 | tf_op jit(solution)/shard_map/ppermute | solution.py:14
  77.9 1.6 %fusion.71 = f32[8,128,128]{1,2,0:T(8,128)} fusion(bf16[512,8,128]{0,2,1:T(8,128)(2,1)S(1)} %bitcast.143, f32[8,128,512]{2,1,0:T(8,128)S(1)} %get-tuple-element.80, f32[8,128]{1,0:T(8,128)S(1)} %maximum_maximum_fusion.2, pred[128,512]{1,0:T(8,128)(4,1)S(1)} %copy-done.18), kind=kOutput, calls=%fused_computation.102 | convolution fusion | flops 136314880 | bytes 3739648 | tf_op jit(solution)/shard_map/hqk,khd->qhd/dot_general | solution.py:62
  79.5 3.1 %fusion.13 = (f32[8,128]{1,0:T(8,128)S(1)}, f32[8,128]{1,0:T(8,128)S(1)}, f32[8,128]{1,0:T(8,128)S(1)}, f32[8,128]{1,0:T(8,128)S(1)}, f32[8,128]{1,0:T(8,128)S(1)}, /*index=5*/f32[8,128]{1,0:T(8,128)S(1)}) fusion(f32[8,128,512]{2,1,0:T(8,128)S(1)} %get-tuple-element.94, f32[8,128]{1,0:T(8,128)S(1)} %maximum_maximum_fusion.3, ...), kind=kLoop, calls=%fused_computation.42 | loop fusion | flops 12576768 | bytes 13008896 | tf_op jit(solution)/shard_map/reduce_sum | solution.py:60
  84.7 1.9 %collective-permute-start.3 = (bf16[128,4096]{1,0:T(8,128)(2,1)S(1)}, bf16[128,4096]{1,0:T(8,128)(2,1)S(1)}, u32[]{:S(2)}, u32[]{:S(2)}) collective-permute-start(bf16[128,4096]{1,0:T(8,128)(2,1)S(1)} %convolution_convert_fusion.3), channel_id=1, source_target_pairs={{0,1},{1,2},{2,3},{3,0},{4,5},{5,6},{6,7},{7,4},{8,9},{9,10},{10,1... | collective-permute-start | bytes 3145736 | tf_op jit(solution)/shard_map/ppermute | solution.py:19
  88.6 3.0 %collective-permute-start.4 = (bf16[128,4096]{1,0:T(8,128)(2,1)S(1)}, bf16[128,4096]{1,0:T(8,128)(2,1)S(1)}, u32[]{:S(2)}, u32[]{:S(2)}) collective-permute-start(bf16[128,4096]{1,0:T(8,128)(2,1)S(1)} %convolution_convert_fusion.2), channel_id=1, source_target_pairs={{0,2},{1,3},{2,0},{3,1},{4,6},{5,7},{6,4},{7,5},{8,10},{9,11},{10,... | collective-permute-start | bytes 3145736 | tf_op jit(solution)/shard_map/ppermute | solution.py:19
  93.1 3.2 %fusion.25 = (f32[8,128]{1,0:T(8,128)S(1)}, f32[8,128]{1,0:T(8,128)S(1)}, f32[8,128]{1,0:T(8,128)S(1)}, f32[8,128]{1,0:T(8,128)S(1)}, f32[8,128]{1,0:T(8,128)S(1)}, /*index=5*/f32[8,128]{1,0:T(8,128)S(1)}) fusion(f32[8,128,512]{2,1,0:T(8,128)S(1)} %get-tuple-element.78, f32[8,128]{1,0:T(8,128)S(1)} %maximum_maximum_fusion.1, ...), kind=kLoop, calls=%fused_computation.54 | loop fusion | flops 12576768 | bytes 13008896 | tf_op jit(solution)/shard_map/reduce_sum | solution.py:60
  101.9 9.3 %collective-permute-done.3 = bf16[128,4096]{1,0:T(8,128)(2,1)S(1)} collective-permute-done((bf16[128,4096]{1,0:T(8,128)(2,1)S(1)}, bf16[128,4096]{1,0:T(8,128)(2,1)S(1)}, u32[]{:S(2)}, u32[]{:S(2)}) %collective-permute-start.3) | collective-permute-done | bytes 1048608 | tf_op jit(solution)/shard_map/ppermute | solution.py:19
  111.1 23.8 %collective-permute-done.4 = bf16[128,4096]{1,0:T(8,128)(2,1)S(1)} collective-permute-done((bf16[128,4096]{1,0:T(8,128)(2,1)S(1)}, bf16[128,4096]{1,0:T(8,128)(2,1)S(1)}, u32[]{:S(2)}, u32[]{:S(2)}) %collective-permute-start.4) | collective-permute-done | bytes 1048608 | tf_op jit(solution)/shard_map/ppermute | solution.py:19
  134.9 2.0 %collective-permute-done.5 = bf16[128,4096]{1,0:T(8,128)(2,1)S(1)} collective-permute-done((bf16[128,4096]{1,0:T(8,128)(2,1)S(1)}, bf16[128,4096]{1,0:T(8,128)(2,1)S(1)}, u32[]{:S(2)}, u32[]{:S(2)}) %collective-permute-start.5) | collective-permute-done | bytes 1048608 | tf_op jit(solution)/shard_map/ppermute | solution.py:19
  136.9 2.6 %add_convert_fusion = bf16[128,4096]{1,0:T(8,128)(2,1)} fusion(bf16[128,4096]{1,0:T(8,128)(2,1)S(1)} %collective-permute-done.5, bf16[128,4096]{1,0:T(8,128)(2,1)S(1)} %collective-permute-done.4, bf16[128,4096]{1,0:T(8,128)(2,1)S(1)} %collective-permute-done.3, bf16[128,1024]{0,1:T(8,128)(2,1)S(1)} %bitcast.157, bf16[1024,4096]{1,0:T(8,128)(2,1)S(1)} %bitcast.105), kind=kOutput, calls=%fused_computation.5 | convolution fusion | flops 1078460416 | bytes 12845056 | tf_op jit(solution)/shard_map/dot_general | solution.py:67
  (131 shorter events, 33.4 us)
Async XLA Ops:
  4.0 3.5 %copy-start.7 = (bf16[512,1024]{1,0:T(8,128)(2,1)S(1)}, bf16[512,1024]{1,0:T(8,128)(2,1)}, u32[]{:S(2)}) copy-start(bf16[512,1024]{1,0:T(8,128)(2,1)} %param.4) | copy-start | bytes 3145732
  4.0 27.8 %collective-permute-start = (bf16[2,512,1024]{1,2,0:T(8,128)(2,1)}, bf16[2,512,1024]{1,2,0:T(8,128)(2,1)}, u32[]{:S(2)}, u32[]{:S(2)}) collective-permute-start(bf16[2,512,1024]{1,2,0:T(8,128)(2,1)} %copy.14), channel_id=1, source_target_pairs={{0,4},{4,8},{8,12},{12,16},{16,20},{20,24},{24,28},{28,32},{32,36}... | collective-permute-start | bytes 6291464 | tf_op jit(solution)/shard_map/ppermute | solution.py:14
  7.4 2.8 %copy-start.22 = (s32[16384]{0:T(1024)S(1)}, s32[16384]{0:T(1024)}, u32[]{:S(2)}) copy-start(s32[16384]{0:T(1024)} %param.7) | copy-start | bytes 196612
  10.1 2.3 %copy-start.26 = (s32[128]{0:T(128)}, s32[128]{0:T(128)S(1)}, u32[]{:S(2)}) copy-start(s32[128]{0:T(128)S(1)} %iota_add_fusion.3) | copy-start | bytes 1540
  10.1 2.3 %copy-start.27 = (s32[128]{0:T(128)}, s32[128]{0:T(128)S(1)}, u32[]{:S(2)}) copy-start(s32[128]{0:T(128)S(1)} %iota_add_fusion.4) | copy-start | bytes 1540
  10.2 2.3 %copy-start.28 = (s32[128]{0:T(128)}, s32[128]{0:T(128)S(1)}, u32[]{:S(2)}) copy-start(s32[128]{0:T(128)S(1)} %iota_add_fusion.5) | copy-start | bytes 1540
  10.2 2.3 %copy-start.29 = (s32[128]{0:T(128)}, s32[128]{0:T(128)S(1)}, u32[]{:S(2)}) copy-start(s32[128]{0:T(128)S(1)} %iota_add_fusion.2) | copy-start | bytes 1540
  10.8 3.2 %copy-start.23 = (s32[128]{0:T(128)}, s32[128]{0:T(128)S(1)}, u32[]{:S(2)}) copy-start(s32[128]{0:T(128)S(1)} %get-tuple-element.28) | copy-start | bytes 1540
  10.8 3.2 %copy-start.24 = (s32[128]{0:T(128)}, s32[128]{0:T(128)S(1)}, u32[]{:S(2)}) copy-start(s32[128]{0:T(128)S(1)} %get-tuple-element.30) | copy-start | bytes 1540
  12.4 3.5 %copy-start.16 = (pred[128,512]{1,0:T(8,128)(4,1)}, pred[128,512]{1,0:T(8,128)(4,1)S(1)}, u32[]{:S(2)}) copy-start(pred[128,512]{1,0:T(8,128)(4,1)S(1)} %get-tuple-element.47) | copy-start | bytes 196612
  15.9 18.2 %copy-start.6 = (bf16[2,512,1024]{2,1,0:T(8,128)(2,1)S(1)}, bf16[2,512,1024]{2,1,0:T(8,128)(2,1)}, u32[]{:S(2)}) copy-start(bf16[2,512,1024]{2,1,0:T(8,128)(2,1)} %param.5) | copy-start | bytes 6291460
  31.7 27.7 %collective-permute-start.1 = (bf16[2,512,1024]{1,2,0:T(8,128)(2,1)}, bf16[2,512,1024]{1,2,0:T(8,128)(2,1)}, u32[]{:S(2)}, u32[]{:S(2)}) collective-permute-start(bf16[2,512,1024]{1,2,0:T(8,128)(2,1)} %collective-permute-done), channel_id=1, source_target_pairs={{0,4},{4,8},{8,12},{12,16},{16,20},{20,24},{24,28},{28,32},{32,36}... | collective-permute-start | bytes 6291464 | tf_op jit(solution)/shard_map/ppermute | solution.py:14
  60.5 10.5 %collective-permute-start.2 = (bf16[2,128,1024]{1,2,0:T(8,128)(2,1)S(1)}, bf16[2,128,1024]{1,2,0:T(8,128)(2,1)S(1)}, u32[]{:S(2)}, u32[]{:S(2)}) collective-permute-start(bf16[2,128,1024]{1,2,0:T(8,128)(2,1)S(1)} %slice.27), channel_id=1, source_target_pairs={{0,4},{4,8},{8,12},{12,16},{16,20},{20,24},{24,28},{28,32},{32,36}... | collective-permute-start | bytes 1572872 | tf_op jit(solution)/shard_map/ppermute | solution.py:14
  75.1 2.0 %copy-start.8 = (bf16[1,512,1024]{1,2,0:T(8,128)(2,1)S(1)}, bf16[1,512,1024]{1,2,0:T(8,128)(2,1)}, u32[]{:S(2)}) copy-start(bf16[1,512,1024]{1,2,0:T(8,128)(2,1)} %copy.25) | copy-start | bytes 3145732
  77.9 5.5 %slice-start = ((s8[8388608]{0:T(1024)(128)(4,1)}), s8[4194304]{0:T(1024)(128)(4,1)S(1)}, s32[]{:S(2)}) async-start(s8[8388608]{0:T(1024)(128)(4,1)} %bitcast.104), calls=%async_computation | async-start | bytes 8388608
  79.5 3.9 %slice-start.1 = ((s8[8388608]{0:T(1024)(128)(4,1)}), s8[4194304]{0:T(1024)(128)(4,1)S(1)}, s32[]{:S(2)}) async-start(s8[8388608]{0:T(1024)(128)(4,1)} %bitcast.104), calls=%async_computation.1 | async-start | bytes 8388608
  83.4 3.2 %copy-start.30 = (f32[8,128,128]{1,2,0:T(8,128)S(1)}, f32[8,128,128]{1,2,0:T(8,128)}, u32[]{:S(2)}) copy-start(f32[8,128,128]{1,2,0:T(8,128)} %fusion.73) | copy-start | bytes 1572868
  83.4 3.2 %copy-start.31 = (f32[8,128,128]{1,2,0:T(8,128)S(1)}, f32[8,128,128]{1,2,0:T(8,128)}, u32[]{:S(2)}) copy-start(f32[8,128,128]{1,2,0:T(8,128)} %fusion.71) | copy-start | bytes 1572868
  84.7 26.4 %collective-permute-start.3 = (bf16[128,4096]{1,0:T(8,128)(2,1)S(1)}, bf16[128,4096]{1,0:T(8,128)(2,1)S(1)}, u32[]{:S(2)}, u32[]{:S(2)}) collective-permute-start(bf16[128,4096]{1,0:T(8,128)(2,1)S(1)} %convolution_convert_fusion.3), channel_id=1, source_target_pairs={{0,1},{1,2},{2,3},{3,0},{4,5},{5,6},{6,7},{7,4},{8,9},{9,10},{10,1... | collective-permute-start | bytes 3145736 | tf_op jit(solution)/shard_map/ppermute | solution.py:19
  88.6 3.7 %copy-start = (f32[8,128,512]{2,1,0:T(8,128)S(1)}, f32[8,128,512]{2,1,0:T(8,128)}, u32[]{:S(2)}) copy-start(f32[8,128,512]{2,1,0:T(8,128)} %get-tuple-element.72) | copy-start | bytes 6291460
  88.6 3.7 %copy-start.13 = (pred[128,512]{1,0:T(8,128)(4,1)S(1)}, pred[128,512]{1,0:T(8,128)(4,1)}, u32[]{:S(2)}) copy-start(pred[128,512]{1,0:T(8,128)(4,1)} %copy-done.12) | copy-start | bytes 196612
  88.6 46.3 %collective-permute-start.4 = (bf16[128,4096]{1,0:T(8,128)(2,1)S(1)}, bf16[128,4096]{1,0:T(8,128)(2,1)S(1)}, u32[]{:S(2)}, u32[]{:S(2)}) collective-permute-start(bf16[128,4096]{1,0:T(8,128)(2,1)S(1)} %convolution_convert_fusion.2), channel_id=1, source_target_pairs={{0,2},{1,3},{2,0},{3,1},{4,6},{5,7},{6,4},{7,5},{8,10},{9,11},{10,... | collective-permute-start | bytes 3145736 | tf_op jit(solution)/shard_map/ppermute | solution.py:19
  93.1 3.2 %copy-start.21 = (f32[8,128,128]{1,2,0:T(8,128)S(1)}, f32[8,128,128]{1,2,0:T(8,128)}, u32[]{:S(2)}) copy-start(f32[8,128,128]{1,2,0:T(8,128)} %fusion.139) | copy-start | bytes 1572868
  98.3 38.6 %collective-permute-start.5 = (bf16[128,4096]{1,0:T(8,128)(2,1)S(1)}, bf16[128,4096]{1,0:T(8,128)(2,1)S(1)}, u32[]{:S(2)}, u32[]{:S(2)}) collective-permute-start(bf16[128,4096]{1,0:T(8,128)(2,1)S(1)} %convolution_convert_fusion.1), channel_id=1, source_target_pairs={{0,3},{1,0},{2,1},{3,2},{4,7},{5,4},{6,5},{7,6},{8,11},{9,8},{10,9... | collective-permute-start | bytes 3145736 | tf_op jit(solution)/shard_map/ppermute | solution.py:19
  (16 other events, 20.8 us)

commit v5 on v4

--- a/solution.py
+++ b/solution.py
@@ -28,10 +28,11 @@
     first_row = me * rows
     tail = DOC_MOST - 2 * rows
     r1 = shift_up(keys_values, "ctx")
-    r2 = shift_up(r1, "ctx")
-    r3 = shift_up(r2[:, rows - tail:], "ctx")
-    sources = [r3, r2, r1, keys_values]
-    offsets = [-DOC_MOST, -2 * rows, -rows, 0]
+    r2_tail = shift_up(r1[:, rows - tail:], "ctx")
+    r3 = shift_up(r2_tail, "ctx")
+    r2_head = shift_up(r1[:, :rows - tail], "ctx")
+    sources = [r3, r2_head, r2_tail, r1, keys_values]
+    offsets = [-DOC_MOST, -2 * rows, -rows - tail, -rows, 0]
     padded_docs = jnp.concatenate([jnp.full((DOC_MOST,), -1, jnp.int32), doc_index])
     scale = HD ** (-0.5)
 

time: 142 us -> 146 us (1.028)
  waiting for transfers between devices: 65.6 us -> 77 us
  matrix products: 31.5 us -> 26 us
  local copies, waits for them, and re-layouts: 19.8 us -> 14.3 us
  starting transfers between devices: 12.3 us -> 16.2 us
    ppermute x3 -> x4, waiting for transfers between devices: 30.5 us -> 40.9 us  [shift_up(): return lax.ppermute(x, axis, [(i, i + 1) for i in range(peers - 1)])]
    ppermute x3 -> x4, starting transfers between devices: 6.05 us -> 10.2 us  [shift_up(): return lax.ppermute(x, axis, [(i, i + 1) for i in range(peers - 1)])]
    dot_general x16 -> x20, matrix products: 13.1 us -> 9.45 us  [chunk_part(): jnp.einsum('qhd,khd->hqk', q, k, preferred_element_type=jnp.float32) * scale]
    unnamed x73 -> x15, local copies, waits for them, and re-layouts: 9.13 us -> 5.94 us
    slice x5 -> x7, local copies, waits for them, and re-layouts: 6.82 us -> 4.09 us  [chunk_part(): kv[1].reshape(n, heads, HD)]
    dot_general x16 -> x20, matrix products: 12 us -> 10.1 us  [chunk_part(): jnp.einsum('hqk,khd->qhd', probs, kv[1].reshape(n, heads, HD), preferred_...]
    slice x1 -> x2, local copies, waits for them, and re-layouts: 1.08 us -> 2.64 us  [the longest x1 1.57 us: per_device(): r2_head = shift_up(r1[:, :rows - tail], 'ctx')]
    reduce_sum x6 -> x10, other arithmetic: 6.65 us -> 8.14 us  [chunk_part(): t = jnp.sum(weights, axis=2)]
  transfers between devices with their start and end apart: 6 -> 7, of which waited for: 6 -> 6; matrix products, arithmetic and copies ran while one was open for 28% -> 17% of each run, Pallas kernels for 0% -> 0%
where the time goes in v5:
time: 146 us; the launch traced here: 143 us
  waiting for transfers between devices  77 us (53%)
  matrix products  26 us (18%)
  starting transfers between devices  16.2 us (11%)
  local copies, waits for them, and re-layouts  14.3 us (10%)
  other arithmetic  9.17 us (6%)
    ppermute x4, waiting for transfers between devices, shift_up(): return lax.ppermute(x, axis, [(i, i + 1) for i in range(peers - 1)])  40.9 us
    ppermute x3, waiting for transfers between devices, rotate(): return lax.ppermute(x, axis, [(i, (i + by) % peers) for i in range(peers)])  36.1 us
    ppermute x4, starting transfers between devices, shift_up(): return lax.ppermute(x, axis, [(i, i + 1) for i in range(peers - 1)])  10.2 us
    dot_general x20, matrix products, chunk_part(): jnp.einsum('hqk,khd->qhd', probs, kv[1].reshape(n, heads, HD), preferred_...  10.1 us
    dot_general x20, matrix products, chunk_part(): jnp.einsum('qhd,khd->hqk', q, k, preferred_element_type=jnp.float32) * scale  9.45 us
    reduce_sum x10, other arithmetic, chunk_part(): t = jnp.sum(weights, axis=2)  8.14 us
    dot_general x4, matrix products, chunk_part(): jnp.dot(attended, w_out, preferred_element_type=jnp.float32)  6.47 us
    ppermute x3, starting transfers between devices, rotate(): return lax.ppermute(x, axis, [(i, (i + by) % peers) for i in range(peers)])  6.05 us
  transfers between devices with their start and end apart: 7, of which 6 were waited for; matrix products, arithmetic and copies ran while one was open for 17% of the time, Pallas kernels for 0%

profile of v5, /device:TPU:98, one launch (start us, length us, event | category | flops | bytes accessed | tf_op | source)
XLA Modules:
  0.0 143.4 jit_solution(6404104821235967320)
XLA Ops:
  0.0 4.1 %copy.19 = bf16[2,512,1024]{1,2,0:T(8,128)(2,1)} copy(bf16[2,512,1024]{2,1,0:T(8,128)(2,1)} %param.5) | data formatting | bytes 4194304 | tf_op args[1]
  4.1 1.9 %collective-permute-start = (bf16[2,512,1024]{1,2,0:T(8,128)(2,1)}, bf16[2,512,1024]{1,2,0:T(8,128)(2,1)}, u32[]{:S(2)}, u32[]{:S(2)}) collective-permute-start(bf16[2,512,1024]{1,2,0:T(8,128)(2,1)} %copy.19), channel_id=1, source_target_pairs={{0,4},{4,8},{8,12},{12,16},{16,20},{20,24},{24,28},{28,32},{32,36}... | collective-permute-start | bytes 6291464 | tf_op jit(solution)/shard_map/ppermute | solution.py:14
  6.5 1.3 slice.85
  9.0 1.3 copy.33
  14.2 17.5 %collective-permute-done = bf16[2,512,1024]{1,2,0:T(8,128)(2,1)} collective-permute-done((bf16[2,512,1024]{1,2,0:T(8,128)(2,1)}, bf16[2,512,1024]{1,2,0:T(8,128)(2,1)}, u32[]{:S(2)}, u32[]{:S(2)}) %collective-permute-start) | collective-permute-done | bytes 2097184 | tf_op jit(solution)/shard_map/ppermute | solution.py:14
  31.7 1.6 %slice.39 = bf16[2,384,1024]{1,2,0:T(8,128)(2,1)S(1)} slice(bf16[2,512,1024]{1,2,0:T(8,128)(2,1)} %collective-permute-done), slice={[0:2], [0:384], [0:1024]} | slice | bytes 3145728 | tf_op jit(solution)/shard_map/slice | solution.py:33
  33.3 1.9 %collective-permute-start.3 = (bf16[2,384,1024]{1,2,0:T(8,128)(2,1)S(1)}, bf16[2,384,1024]{1,2,0:T(8,128)(2,1)S(1)}, u32[]{:S(2)}, u32[]{:S(2)}) collective-permute-start(bf16[2,384,1024]{1,2,0:T(8,128)(2,1)S(1)} %slice.39), channel_id=1, source_target_pairs={{0,4},{4,8},{8,12},{12,16},{16,20},{20,24},{24,28},{28,32},{32,36}... | collective-permute-start | bytes 4718600 | tf_op jit(solution)/shard_map/ppermute | solution.py:14
  36.3 4.2 %collective-permute-start.1 = (bf16[2,128,1024]{1,2,0:T(8,128)(2,1)S(1)}, bf16[2,128,1024]{1,2,0:T(8,128)(2,1)S(1)}, u32[]{:S(2)}, u32[]{:S(2)}) collective-permute-start(bf16[2,128,1024]{1,2,0:T(8,128)(2,1)S(1)} %slice.36), channel_id=1, source_target_pairs={{0,4},{4,8},{8,12},{12,16},{16,20},{20,24},{24,28},{28,32},{32,36}... | collective-permute-start | bytes 1572872 | tf_op jit(solution)/shard_map/ppermute | solution.py:14
  40.5 1.7 %fusion.181 = (bf16[1,512,1024]{1,2,0:T(8,128)(2,1)S(1)}, bf16[1,512,1024]{1,2,0:T(8,128)(2,1)S(1)}) fusion(bf16[2,512,1024]{1,2,0:T(8,128)(2,1)} %collective-permute-done), kind=kLoop, calls=%fused_computation.255 | loop fusion | bytes 4194304 | tf_op jit(solution)/shard_map/slice | solution.py:63
  44.7 15.9 %collective-permute-done.1 = bf16[2,128,1024]{1,2,0:T(8,128)(2,1)S(1)} collective-permute-done((bf16[2,128,1024]{1,2,0:T(8,128)(2,1)S(1)}, bf16[2,128,1024]{1,2,0:T(8,128)(2,1)S(1)}, u32[]{:S(2)}, u32[]{:S(2)}) %collective-permute-start.1) | collective-permute-done | bytes 524320 | tf_op jit(solution)/shard_map/ppermute | solution.py:14
  61.0 2.1 %collective-permute-start.2 = (bf16[2,128,1024]{1,2,0:T(8,128)(2,1)S(1)}, bf16[2,128,1024]{1,2,0:T(8,128)(2,1)S(1)}, u32[]{:S(2)}, u32[]{:S(2)}) collective-permute-start(bf16[2,128,1024]{1,2,0:T(8,128)(2,1)S(1)} %collective-permute-done.1), channel_id=1, source_target_pairs={{0,4},{4,8},{8,12},{12,16},{16,20},{20,24},{24,28},{28,32},{32,36}... | collective-permute-start | bytes 1572872 | tf_op jit(solution)/shard_map/ppermute | solution.py:14
  64.0 7.5 %collective-permute-done.2 = bf16[2,128,1024]{1,2,0:T(8,128)(2,1)S(1)} collective-permute-done((bf16[2,128,1024]{1,2,0:T(8,128)(2,1)S(1)}, bf16[2,128,1024]{1,2,0:T(8,128)(2,1)S(1)}, u32[]{:S(2)}, u32[]{:S(2)}) %collective-permute-start.2) | collective-permute-done | bytes 524320 | tf_op jit(solution)/shard_map/ppermute | solution.py:14
  79.4 2.7 %fusion.9 = (f32[8,128]{1,0:T(8,128)S(1)}, f32[8,128]{1,0:T(8,128)S(1)}, f32[8,128]{1,0:T(8,128)S(1)}, f32[8,128]{1,0:T(8,128)S(1)}) fusion(f32[8,128,512]{2,1,0:T(8,128)S(1)} %get-tuple-element.98, f32[8,128]{1,0:T(8,128)S(1)} %maximum_maximum_fusion.3, pred[128,512]{1,0:T(8,128)(4,1)S(1)} %get-tuple-element.54, f32[8,128,512]{2,1,0:T(8,128)S(1)} %get-tuple-element.96, ...), kind=kLoop, calls=%fused_computation.30 | loop fusion | flops 8384512 | bytes 8675328 | tf_op jit(solution)/shard_map/reduce_sum | solution.py:61
  87.5 1.3 convolution_convert_fusion.3
  88.8 1.7 %collective-permute-start.4 = (bf16[128,4096]{1,0:T(8,128)(2,1)S(1)}, bf16[128,4096]{1,0:T(8,128)(2,1)S(1)}, u32[]{:S(2)}, u32[]{:S(2)}) collective-permute-start(bf16[128,4096]{1,0:T(8,128)(2,1)S(1)} %convolution_convert_fusion.3), channel_id=1, source_target_pairs={{0,1},{1,2},{2,3},{3,0},{4,5},{5,6},{6,7},{7,4},{8,9},{9,10},{10,1... | collective-permute-start | bytes 3145736 | tf_op jit(solution)/shard_map/ppermute | solution.py:19
  91.2 1.3 convolution_convert_fusion.2
  92.5 3.0 %collective-permute-start.5 = (bf16[128,4096]{1,0:T(8,128)(2,1)S(1)}, bf16[128,4096]{1,0:T(8,128)(2,1)S(1)}, u32[]{:S(2)}, u32[]{:S(2)}) collective-permute-start(bf16[128,4096]{1,0:T(8,128)(2,1)S(1)} %convolution_convert_fusion.2), channel_id=1, source_target_pairs={{0,2},{1,3},{2,0},{3,1},{4,6},{5,7},{6,4},{7,5},{8,10},{9,11},{10,... | collective-permute-start | bytes 3145736 | tf_op jit(solution)/shard_map/ppermute | solution.py:19
  97.3 2.6 %fusion.17 = (f32[8,128]{1,0:T(8,128)S(1)}, f32[8,128]{1,0:T(8,128)S(1)}, f32[8,128]{1,0:T(8,128)S(1)}, f32[8,128]{1,0:T(8,128)S(1)}) fusion(f32[8,128,512]{2,1,0:T(8,128)S(1)} %get-tuple-element.78, f32[8,128]{1,0:T(8,128)S(1)} %maximum_maximum_fusion.1, pred[128,512]{1,0:T(8,128)(4,1)S(1)} %get-tuple-element.52, f32[8,128,512]{2,1,0:T(8,128)S(1)} %get-tuple-element.76, ...), kind=kLoop, calls=%fused_computation.38 | loop fusion | flops 8384512 | bytes 8675328 | tf_op jit(solution)/shard_map/reduce_sum | solution.py:61
  100.2 1.3 convolution_convert_fusion.1
  101.5 1.4 collective-permute-start.6
  104.7 10.4 %collective-permute-done.4 = bf16[128,4096]{1,0:T(8,128)(2,1)S(1)} collective-permute-done((bf16[128,4096]{1,0:T(8,128)(2,1)S(1)}, bf16[128,4096]{1,0:T(8,128)(2,1)S(1)}, u32[]{:S(2)}, u32[]{:S(2)}) %collective-permute-start.4) | collective-permute-done | bytes 1048608 | tf_op jit(solution)/shard_map/ppermute | solution.py:19
  115.0 23.8 %collective-permute-done.5 = bf16[128,4096]{1,0:T(8,128)(2,1)S(1)} collective-permute-done((bf16[128,4096]{1,0:T(8,128)(2,1)S(1)}, bf16[128,4096]{1,0:T(8,128)(2,1)S(1)}, u32[]{:S(2)}, u32[]{:S(2)}) %collective-permute-start.5) | collective-permute-done | bytes 1048608 | tf_op jit(solution)/shard_map/ppermute | solution.py:19
  138.8 1.9 %collective-permute-done.6 = bf16[128,4096]{1,0:T(8,128)(2,1)S(1)} collective-permute-done((bf16[128,4096]{1,0:T(8,128)(2,1)S(1)}, bf16[128,4096]{1,0:T(8,128)(2,1)S(1)}, u32[]{:S(2)}, u32[]{:S(2)}) %collective-permute-start.6) | collective-permute-done | bytes 1048608 | tf_op jit(solution)/shard_map/ppermute | solution.py:19
  140.8 2.6 %add_convert_fusion = bf16[128,4096]{1,0:T(8,128)(2,1)} fusion(bf16[128,4096]{1,0:T(8,128)(2,1)S(1)} %collective-permute-done.6, bf16[128,4096]{1,0:T(8,128)(2,1)S(1)} %collective-permute-done.5, bf16[128,4096]{1,0:T(8,128)(2,1)S(1)} %collective-permute-done.4, bf16[128,1024]{0,1:T(8,128)(2,1)S(1)} %bitcast.175, bf16[1024,4096]{1,0:T(8,128)(2,1)S(1)} %bitcast.119), kind=kOutput, calls=%fused_computation.5 | convolution fusion | flops 1078460416 | bytes 12845056 | tf_op jit(solution)/shard_map/dot_general | solution.py:68
  (93 shorter events, 27.8 us)
Async XLA Ops:
  0.0 6.2 %copy-start.2 = (s32[16384]{0:T(1024)S(1)}, s32[16384]{0:T(1024)}, u32[]{:S(2)}) copy-start(s32[16384]{0:T(1024)} %param.7) | copy-start | bytes 196612
  0.0 6.3 %copy-start = (bf16[512,1024]{1,0:T(8,128)(2,1)S(1)}, bf16[512,1024]{1,0:T(8,128)(2,1)}, u32[]{:S(2)}) copy-start(bf16[512,1024]{1,0:T(8,128)(2,1)} %param.4) | copy-start | bytes 3145732
  4.1 27.7 %collective-permute-start = (bf16[2,512,1024]{1,2,0:T(8,128)(2,1)}, bf16[2,512,1024]{1,2,0:T(8,128)(2,1)}, u32[]{:S(2)}, u32[]{:S(2)}) collective-permute-start(bf16[2,512,1024]{1,2,0:T(8,128)(2,1)} %copy.19), channel_id=1, source_target_pairs={{0,4},{4,8},{8,12},{12,16},{16,20},{20,24},{24,28},{28,32},{32,36}... | collective-permute-start | bytes 6291464 | tf_op jit(solution)/shard_map/ppermute | solution.py:14
  7.7 1.2 slice-start.2
  33.3 39.5 %collective-permute-start.3 = (bf16[2,384,1024]{1,2,0:T(8,128)(2,1)S(1)}, bf16[2,384,1024]{1,2,0:T(8,128)(2,1)S(1)}, u32[]{:S(2)}, u32[]{:S(2)}) collective-permute-start(bf16[2,384,1024]{1,2,0:T(8,128)(2,1)S(1)} %slice.39), channel_id=1, source_target_pairs={{0,4},{4,8},{8,12},{12,16},{16,20},{20,24},{24,28},{28,32},{32,36}... | collective-permute-start | bytes 4718600 | tf_op jit(solution)/shard_map/ppermute | solution.py:14
  36.3 24.3 %collective-permute-start.1 = (bf16[2,128,1024]{1,2,0:T(8,128)(2,1)S(1)}, bf16[2,128,1024]{1,2,0:T(8,128)(2,1)S(1)}, u32[]{:S(2)}, u32[]{:S(2)}) collective-permute-start(bf16[2,128,1024]{1,2,0:T(8,128)(2,1)S(1)} %slice.36), channel_id=1, source_target_pairs={{0,4},{4,8},{8,12},{12,16},{16,20},{20,24},{24,28},{28,32},{32,36}... | collective-permute-start | bytes 1572872 | tf_op jit(solution)/shard_map/ppermute | solution.py:14
  61.0 10.5 %collective-permute-start.2 = (bf16[2,128,1024]{1,2,0:T(8,128)(2,1)S(1)}, bf16[2,128,1024]{1,2,0:T(8,128)(2,1)S(1)}, u32[]{:S(2)}, u32[]{:S(2)}) collective-permute-start(bf16[2,128,1024]{1,2,0:T(8,128)(2,1)S(1)} %collective-permute-done.1), channel_id=1, source_target_pairs={{0,4},{4,8},{8,12},{12,16},{16,20},{20,24},{24,28},{28,32},{32,36}... | collective-permute-start | bytes 1572872 | tf_op jit(solution)/shard_map/ppermute | solution.py:14
  79.4 2.7 %copy-start.1 = (bf16[1,512,1024]{1,2,0:T(8,128)(2,1)S(1)}, bf16[1,512,1024]{1,2,0:T(8,128)(2,1)}, u32[]{:S(2)}) copy-start(bf16[1,512,1024]{1,2,0:T(8,128)(2,1)} %copy.33) | copy-start | bytes 3145732
  83.6 2.8 %slice-start = ((s8[8388608]{0:T(1024)(128)(4,1)}), s8[4194304]{0:T(1024)(128)(4,1)S(1)}, s32[]{:S(2)}) async-start(s8[8388608]{0:T(1024)(128)(4,1)} %bitcast.118), calls=%async_computation | async-start | bytes 8388608
  85.2 2.3 %slice-start.1 = ((s8[8388608]{0:T(1024)(128)(4,1)}), s8[4194304]{0:T(1024)(128)(4,1)S(1)}, s32[]{:S(2)}) async-start(s8[8388608]{0:T(1024)(128)(4,1)} %bitcast.118), calls=%async_computation.1 | async-start | bytes 8388608
  88.8 26.2 %collective-permute-start.4 = (bf16[128,4096]{1,0:T(8,128)(2,1)S(1)}, bf16[128,4096]{1,0:T(8,128)(2,1)S(1)}, u32[]{:S(2)}, u32[]{:S(2)}) collective-permute-start(bf16[128,4096]{1,0:T(8,128)(2,1)S(1)} %convolution_convert_fusion.3), channel_id=1, source_target_pairs={{0,1},{1,2},{2,3},{3,0},{4,5},{5,6},{6,7},{7,4},{8,9},{9,10},{10,1... | collective-permute-start | bytes 3145736 | tf_op jit(solution)/shard_map/ppermute | solution.py:19
  92.5 46.4 %collective-permute-start.5 = (bf16[128,4096]{1,0:T(8,128)(2,1)S(1)}, bf16[128,4096]{1,0:T(8,128)(2,1)S(1)}, u32[]{:S(2)}, u32[]{:S(2)}) collective-permute-start(bf16[128,4096]{1,0:T(8,128)(2,1)S(1)} %convolution_convert_fusion.2), channel_id=1, source_target_pairs={{0,2},{1,3},{2,0},{3,1},{4,6},{5,7},{6,4},{7,5},{8,10},{9,11},{10,... | collective-permute-start | bytes 3145736 | tf_op jit(solution)/shard_map/ppermute | solution.py:19
  101.5 39.3 %collective-permute-start.6 = (bf16[128,4096]{1,0:T(8,128)(2,1)S(1)}, bf16[128,4096]{1,0:T(8,128)(2,1)S(1)}, u32[]{:S(2)}, u32[]{:S(2)}) collective-permute-start(bf16[128,4096]{1,0:T(8,128)(2,1)S(1)} %convolution_convert_fusion.1), channel_id=1, source_target_pairs={{0,3},{1,0},{2,1},{3,2},{4,7},{5,4},{6,5},{7,6},{8,11},{9,8},{10,9... | collective-permute-start | bytes 3145736 | tf_op jit(solution)/shard_map/ppermute | solution.py:19

commit v6 on v4

--- a/solution.py
+++ b/solution.py
@@ -40,28 +40,39 @@
         q = lax.dynamic_slice_in_dim(queries, start, CHUNK, 0).reshape(CHUNK, heads, HD)
         q_docs = lax.dynamic_slice_in_dim(doc_index, first_row + start, CHUNK)
         q_place = start + jnp.arange(CHUNK, dtype=jnp.int32)
-        score_list = []
-        for kv, off in zip(sources, offsets):
+        def scores(kv, off):
             n = kv.shape[1]
             k = kv[0].reshape(n, heads, HD)
             k_docs = lax.dynamic_slice_in_dim(padded_docs, first_row + DOC_MOST + off, n)
             k_place = off + jnp.arange(n, dtype=jnp.int32)
             allowed = (k_docs[None, :] == q_docs[:, None]) & (k_place[None, :] <= q_place[:, None])
             raw = jnp.einsum("qhd,khd->hqk", q, k, preferred_element_type=jnp.float32) * scale
-            score_list.append(jnp.where(allowed[None], raw, jnp.float32(-1e30)))
-        top = score_list[0].max(axis=2, keepdims=True)
-        for s in score_list[1:]:
-            top = jnp.maximum(top, s.max(axis=2, keepdims=True))
-        total = None
-        summed = None
-        for kv, s in zip(sources, score_list):
-            n = kv.shape[1]
-            weights = jnp.exp(s - top)
-            t = jnp.sum(weights, axis=2)
-            probs = weights.astype(jnp.bfloat16)
-            pv = jnp.einsum("hqk,khd->qhd", probs, kv[1].reshape(n, heads, HD), preferred_element_type=jnp.float32)
-            total = t if total is None else total + t
-            summed = pv if summed is None else summed + pv
+            return jnp.where(allowed[None], raw, jnp.float32(-1e30))
+
+        def stage(pairs, top):
+            score_list = [scores(kv, off) for kv, off in pairs]
+            for s in score_list:
+                top = jnp.maximum(top, s.max(axis=2, keepdims=True))
+            total = None
+            summed = None
+            for (kv, _), s in zip(pairs, score_list):
+                n = kv.shape[1]
+                weights = jnp.exp(s - top)
+                t = jnp.sum(weights, axis=2)
+                probs = weights.astype(jnp.bfloat16)
+                pv = jnp.einsum("hqk,khd->qhd", probs, kv[1].reshape(n, heads, HD), preferred_element_type=jnp.float32)
+                total = t if total is None else total + t
+                summed = pv if summed is None else summed + pv
+            return top, total, summed
+
+        near = list(zip(sources[2:], offsets[2:]))
+        far = list(zip(sources[:2], offsets[:2]))
+        floor = jnp.full((heads, CHUNK, 1), -1e30, jnp.float32)
+        top_a, total_a, summed_a = stage(near, floor)
+        top, total_b, summed_b = stage(far, top_a)
+        alpha = jnp.exp(top_a - top)
+        total = alpha[:, :, 0] * total_a + total_b
+        summed = jnp.transpose(alpha, (1, 0, 2)) * summed_a + summed_b
         attended = (summed / jnp.transpose(total)[:, :, None]).astype(jnp.bfloat16)
         attended = attended.reshape(CHUNK, heads * HD)
         return jnp.dot(attended, w_out, preferred_element_type=jnp.float32).astype(jnp.bfloat16)

time: 142 us -> 142 us (level)
  matrix products: 31.5 us -> 29.6 us
    dot_general x32, matrix products: 25 us -> 23 us  [the longest x16 13.2 us: scores(): jnp.einsum('qhd,khd->hqk', q, k, preferred_element_type=jnp.float32) * scale]
    reduce_sum x6 -> x8, other arithmetic: 6.65 us -> 7.95 us  [stage(): t = jnp.sum(weights, axis=2)]
    unnamed x73 -> x69, local copies, waits for them, and re-layouts: 9.13 us -> 10.3 us
  transfers between devices with their start and end apart: 6 -> 6, of which waited for: 6 -> 6; matrix products, arithmetic and copies ran while one was open for 28% -> 31% of each run, Pallas kernels for 0% -> 0%
where the time goes in v6:
time: 142 us; the launch traced here: 139 us
  waiting for transfers between devices  64.4 us (45%)
  matrix products  29.6 us (21%)
  local copies, waits for them, and re-layouts  21 us (15%)
  starting transfers between devices  12.6 us (9%)
  other arithmetic  10.8 us (8%)
    ppermute x3, waiting for transfers between devices, rotate(): return lax.ppermute(x, axis, [(i, (i + by) % peers) for i in range(peers)])  34 us
    ppermute x3, waiting for transfers between devices, shift_up(): return lax.ppermute(x, axis, [(i, i + 1) for i in range(peers - 1)])  30.4 us
    dot_general x16, matrix products, scores(): jnp.einsum('qhd,khd->hqk', q, k, preferred_element_type=jnp.float32) * scale  13.2 us
    unnamed x69, local copies, waits for them, and re-layouts  10.3 us
    dot_general x16, matrix products, stage(): jnp.einsum('hqk,khd->qhd', probs, kv[1].reshape(n, heads, HD), preferred_...  9.81 us
    reduce_sum x8, other arithmetic, stage(): t = jnp.sum(weights, axis=2)  7.95 us
    slice x5, local copies, waits for them, and re-layouts, stage(): kv[1].reshape(n, heads, HD)  6.82 us
    dot_general x4, matrix products, chunk_part(): jnp.dot(attended, w_out, preferred_element_type=jnp.float32)  6.59 us
  transfers between devices with their start and end apart: 6, of which 6 were waited for; matrix products, arithmetic and copies ran while one was open for 31% of the time, Pallas kernels for 0%

profile of v6, /device:TPU:98, one launch (start us, length us, event | category | flops | bytes accessed | tf_op | source)
XLA Modules:
  0.0 139.3 jit_solution(1152032484529587511)
XLA Ops:
  0.0 3.9 %copy.14 = bf16[2,512,1024]{1,2,0:T(8,128)(2,1)} copy(bf16[2,512,1024]{2,1,0:T(8,128)(2,1)} %param.5) | data formatting | bytes 4194304 | tf_op args[1]
  4.0 2.0 %collective-permute-start = (bf16[2,512,1024]{1,2,0:T(8,128)(2,1)}, bf16[2,512,1024]{1,2,0:T(8,128)(2,1)}, u32[]{:S(2)}, u32[]{:S(2)}) collective-permute-start(bf16[2,512,1024]{1,2,0:T(8,128)(2,1)} %copy.14), channel_id=1, source_target_pairs={{0,4},{4,8},{8,12},{12,16},{16,20},{20,24},{24,28},{28,32},{32,36}... | collective-permute-start | bytes 6291464 | tf_op jit(solution)/shard_map/ppermute | solution.py:14
  14.1 1.9 %fusion.2 = (f32[8,128]{1,0:T(8,128)S(1)}, f32[8,128,512]{2,1,0:T(8,128)}) fusion(pred[128,512]{1,0:T(8,128)(4,1)S(1)} %get-tuple-element.51, bf16[128,8,128]{0,2,1:T(8,128)(2,1)S(1)} %bitcast.302, bf16[512,8,128]{0,2,1:T(8,128)(2,1)S(1)} %bitcast.275), kind=kOutput, calls=%fused_computation.31 | convolution fusion | flops 135789568 | bytes 3477504 | tf_op jit(solution)/shard_map/qhd,khd->hqk/dot_general | solution.py:49
  16.0 1.8 %fusion.5 = (f32[8,128]{1,0:T(8,128)S(1)}, f32[8,128,512]{2,1,0:T(8,128)}) fusion(pred[128,512]{1,0:T(8,128)(4,1)S(1)} %get-tuple-element.52, bf16[128,8,128]{0,2,1:T(8,128)(2,1)S(1)} %bitcast.294, bf16[512,8,128]{0,2,1:T(8,128)(2,1)S(1)} %bitcast.276), kind=kOutput, calls=%fused_computation.34 | convolution fusion | flops 135789568 | bytes 3477504 | tf_op jit(solution)/shard_map/qhd,khd->hqk/dot_general | solution.py:49
  17.8 13.9 %collective-permute-done = bf16[2,512,1024]{1,2,0:T(8,128)(2,1)} collective-permute-done((bf16[2,512,1024]{1,2,0:T(8,128)(2,1)}, bf16[2,512,1024]{1,2,0:T(8,128)(2,1)}, u32[]{:S(2)}, u32[]{:S(2)}) %collective-permute-start) | collective-permute-done | bytes 2097184 | tf_op jit(solution)/shard_map/ppermute | solution.py:14
  31.7 1.9 %collective-permute-start.1 = (bf16[2,512,1024]{1,2,0:T(8,128)(2,1)}, bf16[2,512,1024]{1,2,0:T(8,128)(2,1)}, u32[]{:S(2)}, u32[]{:S(2)}) collective-permute-start(bf16[2,512,1024]{1,2,0:T(8,128)(2,1)} %collective-permute-done), channel_id=1, source_target_pairs={{0,4},{4,8},{8,12},{12,16},{16,20},{20,24},{24,28},{28,32},{32,36}... | collective-permute-start | bytes 6291464 | tf_op jit(solution)/shard_map/ppermute | solution.py:14
  35.2 2.4 %copy.24 = bf16[1,512,1024]{1,2,0:T(8,128)(2,1)} copy(bf16[1,512,1024]{2,1,0:T(8,128)(2,1)} %slice.24) | data formatting | bytes 2097152 | tf_op jit(solution)/shard_map/slice | solution.py:63
  37.5 1.8 %copy.94 = bf16[128,1024]{0,1:T(8,128)(2,1)} copy(bf16[128,1024]{1,0:T(8,128)(2,1)} %get-tuple-element.26) | data formatting | bytes 524288
  41.7 1.7 %fusion.198 = (bf16[1,512,1024]{1,2,0:T(8,128)(2,1)S(1)}, bf16[1,512,1024]{1,2,0:T(8,128)(2,1)S(1)}) fusion(bf16[2,512,1024]{1,2,0:T(8,128)(2,1)} %collective-permute-done), kind=kLoop, calls=%fused_computation.290 | loop fusion | bytes 4194304 | tf_op jit(solution)/shard_map/slice | solution.py:63
  46.7 12.7 %collective-permute-done.1 = bf16[2,512,1024]{1,2,0:T(8,128)(2,1)} collective-permute-done((bf16[2,512,1024]{1,2,0:T(8,128)(2,1)}, bf16[2,512,1024]{1,2,0:T(8,128)(2,1)}, u32[]{:S(2)}, u32[]{:S(2)}) %collective-permute-start.1) | collective-permute-done | bytes 2097184 | tf_op jit(solution)/shard_map/ppermute | solution.py:14
  60.5 2.1 %collective-permute-start.2 = (bf16[2,128,1024]{1,2,0:T(8,128)(2,1)S(1)}, bf16[2,128,1024]{1,2,0:T(8,128)(2,1)S(1)}, u32[]{:S(2)}, u32[]{:S(2)}) collective-permute-start(bf16[2,128,1024]{1,2,0:T(8,128)(2,1)S(1)} %slice.29), channel_id=1, source_target_pairs={{0,4},{4,8},{8,12},{12,16},{16,20},{20,24},{24,28},{28,32},{32,36}... | collective-permute-start | bytes 1572872 | tf_op jit(solution)/shard_map/ppermute | solution.py:14
  62.6 1.7 %fusion.197 = (bf16[1,512,1024]{1,2,0:T(8,128)(2,1)S(1)}, bf16[1,512,1024]{1,2,0:T(8,128)(2,1)S(1)}) fusion(bf16[2,512,1024]{1,2,0:T(8,128)(2,1)} %collective-permute-done.1), kind=kLoop, calls=%fused_computation.289 | loop fusion | bytes 4194304 | tf_op jit(solution)/shard_map/slice | solution.py:63
  67.2 3.7 %collective-permute-done.2 = bf16[2,128,1024]{1,2,0:T(8,128)(2,1)S(1)} collective-permute-done((bf16[2,128,1024]{1,2,0:T(8,128)(2,1)S(1)}, bf16[2,128,1024]{1,2,0:T(8,128)(2,1)S(1)}, u32[]{:S(2)}, u32[]{:S(2)}) %collective-permute-start.2) | collective-permute-done | bytes 524320 | tf_op jit(solution)/shard_map/ppermute | solution.py:14
  75.4 1.9 %fusion.15 = (f32[8,128]{1,0:T(8,128)S(1)}, f32[8,128]{1,0:T(8,128)S(1)}, f32[8,128]{1,0:T(8,128)S(1)}) fusion(f32[8,128,512]{2,1,0:T(8,128)S(1)} %copy-done.1, f32[8,128]{1,0:T(8,128)S(1)} %get-tuple-element.14, pred[128,512]{1,0:T(8,128)(4,1)S(1)} %copy-done.21, f32[8,128,512]{2,1,0:T(8,128)S(1)} %get-tuple-element.98, pred[128,512]{1,0:T(8,128)(4,1)S(1)} %copy-done.19, ...), kind=kLoop, calls=%fused_computation.44 | loop fusion | flops 6288384 | bytes 6508544 | tf_op jit(solution)/shard_map/reduce_sum | solution.py:61
  80.9 1.9 %collective-permute-start.3 = (bf16[128,4096]{1,0:T(8,128)(2,1)S(1)}, bf16[128,4096]{1,0:T(8,128)(2,1)S(1)}, u32[]{:S(2)}, u32[]{:S(2)}) collective-permute-start(bf16[128,4096]{1,0:T(8,128)(2,1)S(1)} %convolution_convert_fusion.3), channel_id=1, source_target_pairs={{0,1},{1,2},{2,3},{3,0},{4,5},{5,6},{6,7},{7,4},{8,9},{9,10},{10,1... | collective-permute-start | bytes 3145736 | tf_op jit(solution)/shard_map/ppermute | solution.py:19
  83.5 1.9 %fusion.21 = (f32[8,128]{1,0:T(8,128)S(1)}, f32[8,128]{1,0:T(8,128)S(1)}, f32[8,128]{1,0:T(8,128)S(1)}) fusion(f32[8,128,512]{2,1,0:T(8,128)S(1)} %copy-done, f32[8,128]{1,0:T(8,128)S(1)} %get-tuple-element.16, pred[128,512]{1,0:T(8,128)(4,1)S(1)} %copy-done.17, f32[8,128,512]{2,1,0:T(8,128)S(1)} %get-tuple-element.90, pred[128,512]{1,0:T(8,128)(4,1)S(1)} %copy-done.15, ...), kind=kLoop, calls=%fused_computation.50 | loop fusion | flops 6288384 | bytes 6508544 | tf_op jit(solution)/shard_map/reduce_sum | solution.py:61
  88.2 3.0 %collective-permute-start.4 = (bf16[128,4096]{1,0:T(8,128)(2,1)S(1)}, bf16[128,4096]{1,0:T(8,128)(2,1)S(1)}, u32[]{:S(2)}, u32[]{:S(2)}) collective-permute-start(bf16[128,4096]{1,0:T(8,128)(2,1)S(1)} %convolution_convert_fusion.2), channel_id=1, source_target_pairs={{0,2},{1,3},{2,0},{3,1},{4,6},{5,7},{6,4},{7,5},{8,10},{9,11},{10,... | collective-permute-start | bytes 3145736 | tf_op jit(solution)/shard_map/ppermute | solution.py:19
  92.0 1.9 %fusion.27 = (f32[8,128]{1,0:T(8,128)S(1)}, f32[8,128]{1,0:T(8,128)S(1)}, f32[8,128]{1,0:T(8,128)S(1)}) fusion(f32[8,128,512]{2,1,0:T(8,128)S(1)} %get-tuple-element.80, f32[8,128]{1,0:T(8,128)S(1)} %get-tuple-element.18, pred[128,512]{1,0:T(8,128)(4,1)S(1)} %copy-done.13, f32[8,128,512]{2,1,0:T(8,128)S(1)} %get-tuple-element.82, ...), kind=kLoop, calls=%fused_computation.56 | loop fusion | flops 6288384 | bytes 6508544 | tf_op jit(solution)/shard_map/reduce_sum | solution.py:61
  96.6 1.7 %collective-permute-start.5 = (bf16[128,4096]{1,0:T(8,128)(2,1)S(1)}, bf16[128,4096]{1,0:T(8,128)(2,1)S(1)}, u32[]{:S(2)}, u32[]{:S(2)}) collective-permute-start(bf16[128,4096]{1,0:T(8,128)(2,1)S(1)} %convolution_convert_fusion.1), channel_id=1, source_target_pairs={{0,3},{1,0},{2,1},{3,2},{4,7},{5,4},{6,5},{7,6},{8,11},{9,8},{10,9... | collective-permute-start | bytes 3145736 | tf_op jit(solution)/shard_map/ppermute | solution.py:19
  98.3 1.9 %fusion.33 = (f32[8,128]{1,0:T(8,128)S(1)}, f32[8,128]{1,0:T(8,128)S(1)}, f32[8,128]{1,0:T(8,128)S(1)}) fusion(f32[8,128,512]{2,1,0:T(8,128)S(1)} %get-tuple-element.72, f32[8,128]{1,0:T(8,128)S(1)} %get-tuple-element.20, pred[128,512]{1,0:T(8,128)(4,1)S(1)} %copy-done.10, f32[8,128,512]{2,1,0:T(8,128)S(1)} %get-tuple-element.74, ...), kind=kLoop, calls=%fused_computation.62 | loop fusion | flops 6288384 | bytes 6508544 | tf_op jit(solution)/shard_map/reduce_sum | solution.py:61
  102.5 4.8 %collective-permute-done.3 = bf16[128,4096]{1,0:T(8,128)(2,1)S(1)} collective-permute-done((bf16[128,4096]{1,0:T(8,128)(2,1)S(1)}, bf16[128,4096]{1,0:T(8,128)(2,1)S(1)}, u32[]{:S(2)}, u32[]{:S(2)}) %collective-permute-start.3) | collective-permute-done | bytes 1048608 | tf_op jit(solution)/shard_map/ppermute | solution.py:19
  107.3 23.8 %collective-permute-done.4 = bf16[128,4096]{1,0:T(8,128)(2,1)S(1)} collective-permute-done((bf16[128,4096]{1,0:T(8,128)(2,1)S(1)}, bf16[128,4096]{1,0:T(8,128)(2,1)S(1)}, u32[]{:S(2)}, u32[]{:S(2)}) %collective-permute-start.4) | collective-permute-done | bytes 1048608 | tf_op jit(solution)/shard_map/ppermute | solution.py:19
  131.1 5.4 %collective-permute-done.5 = bf16[128,4096]{1,0:T(8,128)(2,1)S(1)} collective-permute-done((bf16[128,4096]{1,0:T(8,128)(2,1)S(1)}, bf16[128,4096]{1,0:T(8,128)(2,1)S(1)}, u32[]{:S(2)}, u32[]{:S(2)}) %collective-permute-start.5) | collective-permute-done | bytes 1048608 | tf_op jit(solution)/shard_map/ppermute | solution.py:19
  136.5 2.7 %add_convert_fusion = bf16[128,4096]{1,0:T(8,128)(2,1)} fusion(bf16[128,4096]{1,0:T(8,128)(2,1)S(1)} %collective-permute-done.5, bf16[128,4096]{1,0:T(8,128)(2,1)S(1)} %collective-permute-done.4, bf16[128,4096]{1,0:T(8,128)(2,1)S(1)} %collective-permute-done.3, bf16[128,1024]{0,1:T(8,128)(2,1)S(1)} %bitcast.325, bf16[1024,4096]{1,0:T(8,128)(2,1)S(1)} %bitcast.273), kind=kOutput, calls=%fused_computation.5 | convolution fusion | flops 1078460416 | bytes 12845056 | tf_op jit(solution)/shard_map/dot_general | solution.py:78
  (133 shorter events, 35.9 us)
Async XLA Ops:
  4.0 3.5 %copy-start.7 = (bf16[512,1024]{1,0:T(8,128)(2,1)S(1)}, bf16[512,1024]{1,0:T(8,128)(2,1)}, u32[]{:S(2)}) copy-start(bf16[512,1024]{1,0:T(8,128)(2,1)} %param.4) | copy-start | bytes 3145732
  4.0 27.8 %collective-permute-start = (bf16[2,512,1024]{1,2,0:T(8,128)(2,1)}, bf16[2,512,1024]{1,2,0:T(8,128)(2,1)}, u32[]{:S(2)}, u32[]{:S(2)}) collective-permute-start(bf16[2,512,1024]{1,2,0:T(8,128)(2,1)} %copy.14), channel_id=1, source_target_pairs={{0,4},{4,8},{8,12},{12,16},{16,20},{20,24},{24,28},{28,32},{32,36}... | collective-permute-start | bytes 6291464 | tf_op jit(solution)/shard_map/ppermute | solution.py:14
  7.4 2.9 %copy-start.22 = (s32[16384]{0:T(1024)S(1)}, s32[16384]{0:T(1024)}, u32[]{:S(2)}) copy-start(s32[16384]{0:T(1024)} %param.7) | copy-start | bytes 196612
  10.2 2.2 %copy-start.26 = (s32[128]{0:T(128)}, s32[128]{0:T(128)S(1)}, u32[]{:S(2)}) copy-start(s32[128]{0:T(128)S(1)} %iota_add_fusion.3) | copy-start | bytes 1540
  10.2 2.2 %copy-start.27 = (s32[128]{0:T(128)}, s32[128]{0:T(128)S(1)}, u32[]{:S(2)}) copy-start(s32[128]{0:T(128)S(1)} %iota_add_fusion.4) | copy-start | bytes 1540
  10.2 2.2 %copy-start.28 = (s32[128]{0:T(128)}, s32[128]{0:T(128)S(1)}, u32[]{:S(2)}) copy-start(s32[128]{0:T(128)S(1)} %iota_add_fusion.6) | copy-start | bytes 1540
  10.2 2.2 %copy-start.29 = (s32[128]{0:T(128)}, s32[128]{0:T(128)S(1)}, u32[]{:S(2)}) copy-start(s32[128]{0:T(128)S(1)} %iota_add_fusion.2) | copy-start | bytes 1540
  10.9 3.2 %copy-start.23 = (s32[128]{0:T(128)}, s32[128]{0:T(128)S(1)}, u32[]{:S(2)}) copy-start(s32[128]{0:T(128)S(1)} %get-tuple-element.33) | copy-start | bytes 1540
  10.9 3.2 %copy-start.24 = (s32[128]{0:T(128)}, s32[128]{0:T(128)S(1)}, u32[]{:S(2)}) copy-start(s32[128]{0:T(128)S(1)} %get-tuple-element.34) | copy-start | bytes 1540
  11.0 3.1 %copy-start.3 = (bf16[128,1024]{0,1:T(8,128)(2,1)S(1)}, bf16[128,1024]{0,1:T(8,128)(2,1)}, u32[]{:S(2)}) copy-start(bf16[128,1024]{0,1:T(8,128)(2,1)} %copy.92) | copy-start | bytes 786436
  12.4 3.6 %copy-start.16 = (pred[128,512]{1,0:T(8,128)(4,1)}, pred[128,512]{1,0:T(8,128)(4,1)S(1)}, u32[]{:S(2)}) copy-start(pred[128,512]{1,0:T(8,128)(4,1)S(1)} %get-tuple-element.52) | copy-start | bytes 196612
  16.0 18.2 %copy-start.6 = (bf16[2,512,1024]{2,1,0:T(8,128)(2,1)S(1)}, bf16[2,512,1024]{2,1,0:T(8,128)(2,1)}, u32[]{:S(2)}) copy-start(bf16[2,512,1024]{2,1,0:T(8,128)(2,1)} %param.5) | copy-start | bytes 6291460
  31.7 27.7 %collective-permute-start.1 = (bf16[2,512,1024]{1,2,0:T(8,128)(2,1)}, bf16[2,512,1024]{1,2,0:T(8,128)(2,1)}, u32[]{:S(2)}, u32[]{:S(2)}) collective-permute-start(bf16[2,512,1024]{1,2,0:T(8,128)(2,1)} %collective-permute-done), channel_id=1, source_target_pairs={{0,4},{4,8},{8,12},{12,16},{16,20},{20,24},{24,28},{28,32},{32,36}... | collective-permute-start | bytes 6291464 | tf_op jit(solution)/shard_map/ppermute | solution.py:14
  60.5 10.5 %collective-permute-start.2 = (bf16[2,128,1024]{1,2,0:T(8,128)(2,1)S(1)}, bf16[2,128,1024]{1,2,0:T(8,128)(2,1)S(1)}, u32[]{:S(2)}, u32[]{:S(2)}) collective-permute-start(bf16[2,128,1024]{1,2,0:T(8,128)(2,1)S(1)} %slice.29), channel_id=1, source_target_pairs={{0,4},{4,8},{8,12},{12,16},{16,20},{20,24},{24,28},{28,32},{32,36}... | collective-permute-start | bytes 1572872 | tf_op jit(solution)/shard_map/ppermute | solution.py:14
  72.8 1.9 %copy-start.21 = (pred[128,512]{1,0:T(8,128)(4,1)S(1)}, pred[128,512]{1,0:T(8,128)(4,1)}, u32[]{:S(2)}) copy-start(pred[128,512]{1,0:T(8,128)(4,1)} %copy-done.20) | copy-start | bytes 196612
  75.4 3.5 %slice-start = ((s8[8388608]{0:T(1024)(128)(4,1)}), s8[4194304]{0:T(1024)(128)(4,1)S(1)}, s32[]{:S(2)}) async-start(s8[8388608]{0:T(1024)(128)(4,1)} %bitcast.272), calls=%async_computation | async-start | bytes 8388608
  77.3 2.3 %slice-start.1 = ((s8[8388608]{0:T(1024)(128)(4,1)}), s8[4194304]{0:T(1024)(128)(4,1)S(1)}, s32[]{:S(2)}) async-start(s8[8388608]{0:T(1024)(128)(4,1)} %bitcast.272), calls=%async_computation.1 | async-start | bytes 8388608
  79.6 3.2 %copy-start = (f32[8,128,512]{2,1,0:T(8,128)S(1)}, f32[8,128,512]{2,1,0:T(8,128)}, u32[]{:S(2)}) copy-start(f32[8,128,512]{2,1,0:T(8,128)} %get-tuple-element.88) | copy-start | bytes 6291460
  79.6 3.2 %copy-start.17 = (pred[128,512]{1,0:T(8,128)(4,1)S(1)}, pred[128,512]{1,0:T(8,128)(4,1)}, u32[]{:S(2)}) copy-start(pred[128,512]{1,0:T(8,128)(4,1)} %copy-done.16) | copy-start | bytes 196612
  80.9 26.5 %collective-permute-start.3 = (bf16[128,4096]{1,0:T(8,128)(2,1)S(1)}, bf16[128,4096]{1,0:T(8,128)(2,1)S(1)}, u32[]{:S(2)}, u32[]{:S(2)}) collective-permute-start(bf16[128,4096]{1,0:T(8,128)(2,1)S(1)} %convolution_convert_fusion.3), channel_id=1, source_target_pairs={{0,1},{1,2},{2,3},{3,0},{4,5},{5,6},{6,7},{7,4},{8,9},{9,10},{10,1... | collective-permute-start | bytes 3145736 | tf_op jit(solution)/shard_map/ppermute | solution.py:19
  86.9 4.3 %copy-start.13 = (pred[128,512]{1,0:T(8,128)(4,1)S(1)}, pred[128,512]{1,0:T(8,128)(4,1)}, u32[]{:S(2)}) copy-start(pred[128,512]{1,0:T(8,128)(4,1)} %get-tuple-element.61) | copy-start | bytes 196612
  88.2 42.9 %collective-permute-start.4 = (bf16[128,4096]{1,0:T(8,128)(2,1)S(1)}, bf16[128,4096]{1,0:T(8,128)(2,1)S(1)}, u32[]{:S(2)}, u32[]{:S(2)}) collective-permute-start(bf16[128,4096]{1,0:T(8,128)(2,1)S(1)} %convolution_convert_fusion.2), channel_id=1, source_target_pairs={{0,2},{1,3},{2,0},{3,1},{4,6},{5,7},{6,4},{7,5},{8,10},{9,11},{10,... | collective-permute-start | bytes 3145736 | tf_op jit(solution)/shard_map/ppermute | solution.py:19
  95.3 3.0 %copy-start.10 = (pred[128,512]{1,0:T(8,128)(4,1)S(1)}, pred[128,512]{1,0:T(8,128)(4,1)}, u32[]{:S(2)}) copy-start(pred[128,512]{1,0:T(8,128)(4,1)} %copy-done.9) | copy-start | bytes 196612
  96.6 39.9 %collective-permute-start.5 = (bf16[128,4096]{1,0:T(8,128)(2,1)S(1)}, bf16[128,4096]{1,0:T(8,128)(2,1)S(1)}, u32[]{:S(2)}, u32[]{:S(2)}) collective-permute-start(bf16[128,4096]{1,0:T(8,128)(2,1)S(1)} %convolution_convert_fusion.1), channel_id=1, source_target_pairs={{0,3},{1,0},{2,1},{3,2},{4,7},{5,4},{6,5},{7,6},{8,11},{9,8},{10,9... | collective-permute-start | bytes 3145736 | tf_op jit(solution)/shard_map/ppermute | solution.py:19
  (14 other events, 17.4 us)

commit v7 on v6

--- a/solution.py
+++ b/solution.py
@@ -77,14 +77,25 @@
         attended = attended.reshape(CHUNK, heads * HD)
         return jnp.dot(attended, w_out, preferred_element_type=jnp.float32).astype(jnp.bfloat16)
 
-    total_out = None
-    for step in range(groups):
-        by = (step + 1) % groups
-        part = chunk_part((h + by) % groups)
-        if by:
-            part = rotate(part, "head", by)
-        part = part.astype(jnp.float32)
-        total_out = part if total_out is None else total_out + part
+    assert groups == 4
+    cols = w_out.shape[1] // 2
+    far = chunk_part((h + 2) % groups)
+    via_left = rotate(far[:, :cols], "head", groups - 1)
+    via_right = rotate(far[:, cols:], "head", 1)
+    nxt = chunk_part((h + 1) % groups)
+    nxt = jnp.concatenate(
+        [nxt[:, :cols], (nxt[:, cols:].astype(jnp.float32) + via_right.astype(jnp.float32)).astype(jnp.bfloat16)],
+        axis=1,
+    )
+    from_left = rotate(nxt, "head", 1)
+    prv = chunk_part((h + groups - 1) % groups)
+    prv = jnp.concatenate(
+        [(prv[:, :cols].astype(jnp.float32) + via_left.astype(jnp.float32)).astype(jnp.bfloat16), prv[:, cols:]],
+        axis=1,
+    )
+    from_right = rotate(prv, "head", groups - 1)
+    own = chunk_part(h)
+    total_out = own.astype(jnp.float32) + from_left.astype(jnp.float32) + from_right.astype(jnp.float32)
     return total_out.astype(jnp.bfloat16)
 
 

time: 142 us -> 132 us (0.930); the launches traced: 139 us -> 131 us
  waiting for transfers between devices: 64.4 us -> 57.1 us
  matrix products: 29.6 us -> 27 us
  other arithmetic: 10.8 us -> 13.1 us
    ppermute x3 -> x4, waiting for transfers between devices: 34 us -> 24.2 us  [rotate(): return lax.ppermute(x, axis, [(i, (i + by) % peers) for i in range(peers)])]
    ppermute x3, waiting for transfers between devices: 30.4 us -> 32.8 us  [shift_up(): return lax.ppermute(x, axis, [(i, i + 1) for i in range(peers - 1)])]
    convert_element_type x0 -> x3, other arithmetic: none -> 1.59 us  [the longest x1 1.34 us: per_device(): return total_out.astype(jnp.bfloat16)]
    dot_general x4, matrix products: 6.59 us -> 5.14 us  [chunk_part(): jnp.dot(attended, w_out, preferred_element_type=jnp.float32)]
    unnamed x69 -> x71, local copies, waits for them, and re-layouts: 10.3 us -> 9.07 us
    ppermute x3 -> x4, starting transfers between devices: 6.53 us -> 6.67 us  [rotate(): return lax.ppermute(x, axis, [(i, (i + by) % peers) for i in range(peers)])]
  transfers between devices with their start and end apart: 6 -> 7, of which waited for: 6 -> 7; matrix products, arithmetic and copies ran while one was open for 31% -> 29% of each run, Pallas kernels for 0% -> 0%
where the time goes in v7:
time: 132 us; the launch traced here: 131 us
  waiting for transfers between devices  57.1 us (43%)
  matrix products  27 us (20%)
  local copies, waits for them, and re-layouts  20 us (15%)
  other arithmetic  13.1 us (10%)
  starting transfers between devices  12.9 us (10%)
    ppermute x3, waiting for transfers between devices, shift_up(): return lax.ppermute(x, axis, [(i, i + 1) for i in range(peers - 1)])  32.8 us
    ppermute x4, waiting for transfers between devices, rotate(): return lax.ppermute(x, axis, [(i, (i + by) % peers) for i in range(peers)])  24.2 us
    dot_general x16, matrix products, scores(): jnp.einsum('qhd,khd->hqk', q, k, preferred_element_type=jnp.float32) * scale  12.2 us
    dot_general x16, matrix products, stage(): jnp.einsum('hqk,khd->qhd', probs, kv[1].reshape(n, heads, HD), preferred_...  9.73 us
    unnamed x71, local copies, waits for them, and re-layouts  9.07 us
    reduce_sum x8, other arithmetic, stage(): t = jnp.sum(weights, axis=2)  8.43 us
    slice x5, local copies, waits for them, and re-layouts, stage(): kv[1].reshape(n, heads, HD)  6.82 us
    ppermute x4, starting transfers between devices, rotate(): return lax.ppermute(x, axis, [(i, (i + by) % peers) for i in range(peers)])  6.67 us
  transfers between devices with their start and end apart: 7, of which 7 were waited for; matrix products, arithmetic and copies ran while one was open for 29% of the time, Pallas kernels for 0%

profile of v7, /device:TPU:98, one launch (start us, length us, event | category | flops | bytes accessed | tf_op | source)
XLA Modules:
  0.0 130.8 jit_solution(6970453010177193324)
XLA Ops:
  0.0 3.9 %copy.14 = bf16[2,512,1024]{1,2,0:T(8,128)(2,1)} copy(bf16[2,512,1024]{2,1,0:T(8,128)(2,1)} %param.5) | data formatting | bytes 4194304 | tf_op args[1]
  4.0 2.0 %collective-permute-start = (bf16[2,512,1024]{1,2,0:T(8,128)(2,1)}, bf16[2,512,1024]{1,2,0:T(8,128)(2,1)}, u32[]{:S(2)}, u32[]{:S(2)}) collective-permute-start(bf16[2,512,1024]{1,2,0:T(8,128)(2,1)} %copy.14), channel_id=1, source_target_pairs={{0,4},{4,8},{8,12},{12,16},{16,20},{20,24},{24,28},{28,32},{32,36}... | collective-permute-start | bytes 6291464 | tf_op jit(solution)/shard_map/ppermute | solution.py:14
  9.6 1.4 %fusion.150 = (pred[128,512]{1,0:T(8,128)(4,1)S(1)}, pred[128,512]{1,0:T(8,128)(4,1)S(1)}, pred[128,512]{1,0:T(8,128)(4,1)}, pred[128,512]{1,0:T(8,128)(4,1)}, p...) fusion(s32[512]{0:T(512)S(1)} %get-tuple-element.39, ...), kind=kLoop, calls=%fused_computation.187 | loop fusion | flops 2359296 | bytes 800768 | tf_op jit(solution)/shard_map/and | solution.py:48
  11.0 1.9 %fusion.5 = (f32[8,128]{1,0:T(8,128)S(1)}, f32[8,128,512]{2,1,0:T(8,128)}) fusion(pred[128,512]{1,0:T(8,128)(4,1)S(1)} %get-tuple-element.53, bf16[128,8,128]{0,2,1:T(8,128)(2,1)S(1)} %bitcast.302, bf16[512,8,128]{0,2,1:T(8,128)(2,1)S(1)} %bitcast.274), kind=kOutput, calls=%fused_computation.34 | convolution fusion | flops 135789568 | bytes 3477504 | tf_op jit(solution)/shard_map/qhd,khd->hqk/dot_general | solution.py:49
  13.0 1.8 %fusion.8 = (f32[8,128]{1,0:T(8,128)S(1)}, f32[8,128,512]{2,1,0:T(8,128)}) fusion(pred[128,512]{1,0:T(8,128)(4,1)S(1)} %get-tuple-element.54, bf16[128,8,128]{0,2,1:T(8,128)(2,1)S(1)} %bitcast.298, bf16[512,8,128]{0,2,1:T(8,128)(2,1)S(1)} %bitcast.275), kind=kOutput, calls=%fused_computation.37 | convolution fusion | flops 135789568 | bytes 3477504 | tf_op jit(solution)/shard_map/qhd,khd->hqk/dot_general | solution.py:49
  15.4 16.3 %collective-permute-done = bf16[2,512,1024]{1,2,0:T(8,128)(2,1)} collective-permute-done((bf16[2,512,1024]{1,2,0:T(8,128)(2,1)}, bf16[2,512,1024]{1,2,0:T(8,128)(2,1)}, u32[]{:S(2)}, u32[]{:S(2)}) %collective-permute-start) | collective-permute-done | bytes 2097184 | tf_op jit(solution)/shard_map/ppermute | solution.py:14
  31.7 1.9 %collective-permute-start.1 = (bf16[2,512,1024]{1,2,0:T(8,128)(2,1)}, bf16[2,512,1024]{1,2,0:T(8,128)(2,1)}, u32[]{:S(2)}, u32[]{:S(2)}) collective-permute-start(bf16[2,512,1024]{1,2,0:T(8,128)(2,1)} %collective-permute-done), channel_id=1, source_target_pairs={{0,4},{4,8},{8,12},{12,16},{16,20},{20,24},{24,28},{28,32},{32,36}... | collective-permute-start | bytes 6291464 | tf_op jit(solution)/shard_map/ppermute | solution.py:14
  35.2 2.4 %copy.24 = bf16[1,512,1024]{1,2,0:T(8,128)(2,1)} copy(bf16[1,512,1024]{2,1,0:T(8,128)(2,1)} %slice.36) | data formatting | bytes 2097152 | tf_op jit(solution)/shard_map/slice | solution.py:63
  37.5 1.8 %copy.95 = bf16[128,1024]{0,1:T(8,128)(2,1)} copy(bf16[128,1024]{1,0:T(8,128)(2,1)} %get-tuple-element.28) | data formatting | bytes 524288
  40.2 1.6 %fusion.11 = (f32[8,128]{1,0:T(8,128)S(1)}, f32[8,128,512]{2,1,0:T(8,128)S(1)}) fusion(pred[128,512]{1,0:T(8,128)(4,1)} %get-tuple-element.63, bf16[128,8,128]{0,2,1:T(8,128)(2,1)} %bitcast.306, bf16[512,8,128]{0,2,1:T(8,128)(2,1)S(1)} %bitcast.277), kind=kOutput, calls=%fused_computation.40 | convolution fusion | flops 135789568 | bytes 3477504 | tf_op jit(solution)/shard_map/qhd,khd->hqk/dot_general | solution.py:49
  41.8 1.7 %fusion.198 = (bf16[1,512,1024]{1,2,0:T(8,128)(2,1)S(1)}, bf16[1,512,1024]{1,2,0:T(8,128)(2,1)S(1)}) fusion(bf16[2,512,1024]{1,2,0:T(8,128)(2,1)} %collective-permute-done), kind=kLoop, calls=%fused_computation.294 | loop fusion | bytes 4194304 | tf_op jit(solution)/shard_map/slice | solution.py:63
  46.6 12.8 %collective-permute-done.1 = bf16[2,512,1024]{1,2,0:T(8,128)(2,1)} collective-permute-done((bf16[2,512,1024]{1,2,0:T(8,128)(2,1)}, bf16[2,512,1024]{1,2,0:T(8,128)(2,1)}, u32[]{:S(2)}, u32[]{:S(2)}) %collective-permute-start.1) | collective-permute-done | bytes 2097184 | tf_op jit(solution)/shard_map/ppermute | solution.py:14
  60.5 2.2 %collective-permute-start.2 = (bf16[2,128,1024]{1,2,0:T(8,128)(2,1)S(1)}, bf16[2,128,1024]{1,2,0:T(8,128)(2,1)S(1)}, u32[]{:S(2)}, u32[]{:S(2)}) collective-permute-start(bf16[2,128,1024]{1,2,0:T(8,128)(2,1)S(1)} %slice.86), channel_id=1, source_target_pairs={{0,4},{4,8},{8,12},{12,16},{16,20},{20,24},{24,28},{28,32},{32,36}... | collective-permute-start | bytes 1572872 | tf_op jit(solution)/shard_map/ppermute | solution.py:14
  62.7 1.7 %fusion.197 = (bf16[1,512,1024]{1,2,0:T(8,128)(2,1)S(1)}, bf16[1,512,1024]{1,2,0:T(8,128)(2,1)S(1)}) fusion(bf16[2,512,1024]{1,2,0:T(8,128)(2,1)} %collective-permute-done.1), kind=kLoop, calls=%fused_computation.293 | loop fusion | bytes 4194304 | tf_op jit(solution)/shard_map/slice | solution.py:63
  67.4 3.7 %collective-permute-done.2 = bf16[2,128,1024]{1,2,0:T(8,128)(2,1)S(1)} collective-permute-done((bf16[2,128,1024]{1,2,0:T(8,128)(2,1)S(1)}, bf16[2,128,1024]{1,2,0:T(8,128)(2,1)S(1)}, u32[]{:S(2)}, u32[]{:S(2)}) %collective-permute-start.2) | collective-permute-done | bytes 524320 | tf_op jit(solution)/shard_map/ppermute | solution.py:14
  75.8 2.1 %fusion.21 = (f32[8,128]{1,0:T(8,128)S(1)}, f32[8,128]{1,0:T(8,128)S(1)}, f32[8,128]{1,0:T(8,128)S(1)}) fusion(f32[8,128,512]{2,1,0:T(8,128)S(1)} %copy-done.1, f32[8,128]{1,0:T(8,128)S(1)} %get-tuple-element.14, pred[128,512]{1,0:T(8,128)(4,1)S(1)} %copy-done.22, f32[8,128,512]{2,1,0:T(8,128)S(1)} %get-tuple-element.100, ...), kind=kLoop, calls=%fused_computation.50 | loop fusion | flops 6288384 | bytes 6508544 | tf_op jit(solution)/shard_map/reduce_sum | solution.py:61
  81.4 1.9 %fusion.27 = (f32[8,128]{1,0:T(8,128)S(1)}, f32[8,128]{1,0:T(8,128)S(1)}, f32[8,128]{1,0:T(8,128)S(1)}) fusion(f32[8,128,512]{2,1,0:T(8,128)S(1)} %copy-done, f32[8,128]{1,0:T(8,128)S(1)} %get-tuple-element.18, pred[128,512]{1,0:T(8,128)(4,1)S(1)} %copy-done.18, f32[8,128,512]{2,1,0:T(8,128)S(1)} %get-tuple-element.76, pred[128,512]{1,0:T(8,128)(4,1)S(1)} %copy-done.16, ...), kind=kLoop, calls=%fused_computation.56 | loop fusion | flops 6288384 | bytes 6508544 | tf_op jit(solution)/shard_map/reduce_sum | solution.py:61
  86.2 1.6 %collective-permute-start.3 = (bf16[128,2048]{1,0:T(8,128)(2,1)S(1)}, bf16[128,2048]{1,0:T(8,128)(2,1)S(1)}, u32[]{:S(2)}, u32[]{:S(2)}) collective-permute-start(bf16[128,2048]{1,0:T(8,128)(2,1)S(1)} %get-tuple-element.29), channel_id=1, source_target_pairs={{0,1},{1,2},{2,3},{3,0},{4,5},{5,6},{6,7},{7,4},{8,9},{9,10},{10,1... | collective-permute-start | bytes 1572872 | tf_op jit(solution)/shard_map/ppermute | solution.py:19
  88.9 1.8 %collective-permute-start.5 = (bf16[128,2048]{1,0:T(8,128)(2,1)S(1)}, bf16[128,2048]{1,0:T(8,128)(2,1)S(1)}, u32[]{:S(2)}, u32[]{:S(2)}) collective-permute-start(bf16[128,2048]{1,0:T(8,128)(2,1)S(1)} %get-tuple-element.30), channel_id=1, source_target_pairs={{0,3},{1,0},{2,1},{3,2},{4,7},{5,4},{6,5},{7,6},{8,11},{9,8},{10,9... | collective-permute-start | bytes 1572872 | tf_op jit(solution)/shard_map/ppermute | solution.py:19
  91.5 2.2 %fusion.33 = (f32[8,128]{1,0:T(8,128)S(1)}, f32[8,128]{1,0:T(8,128)S(1)}, f32[8,128]{1,0:T(8,128)S(1)}) fusion(f32[8,128,512]{2,1,0:T(8,128)S(1)} %get-tuple-element.82, f32[8,128]{1,0:T(8,128)S(1)} %get-tuple-element.20, pred[128,512]{1,0:T(8,128)(4,1)S(1)} %copy-done.14, f32[8,128,512]{2,1,0:T(8,128)S(1)} %get-tuple-element.84, ...), kind=kLoop, calls=%fused_computation.62 | loop fusion | flops 6288384 | bytes 6508544 | tf_op jit(solution)/shard_map/reduce_sum | solution.py:61
  97.6 1.9 %fusion.15 = (f32[8,128]{1,0:T(8,128)S(1)}, f32[8,128]{1,0:T(8,128)S(1)}, f32[8,128]{1,0:T(8,128)S(1)}) fusion(f32[8,128,512]{2,1,0:T(8,128)S(1)} %get-tuple-element.90, f32[8,128]{1,0:T(8,128)S(1)} %get-tuple-element.16, pred[128,512]{1,0:T(8,128)(4,1)S(1)} %copy-done.11, f32[8,128,512]{2,1,0:T(8,128)S(1)} %get-tuple-element.92, ...), kind=kLoop, calls=%fused_computation.44 | loop fusion | flops 6288384 | bytes 6508544 | tf_op jit(solution)/shard_map/reduce_sum | solution.py:61
  99.5 1.7 %collective-permute-done.3 = bf16[128,2048]{1,0:T(8,128)(2,1)S(1)} collective-permute-done((bf16[128,2048]{1,0:T(8,128)(2,1)S(1)}, bf16[128,2048]{1,0:T(8,128)(2,1)S(1)}, u32[]{:S(2)}, u32[]{:S(2)}) %collective-permute-start.3) | collective-permute-done | bytes 524320 | tf_op jit(solution)/shard_map/ppermute | solution.py:19
  103.3 2.7 %collective-permute-start.6 = (bf16[128,4096]{1,0:T(8,128)(2,1)S(1)}, bf16[128,4096]{1,0:T(8,128)(2,1)S(1)}, u32[]{:S(2)}, u32[]{:S(2)}) collective-permute-start(bf16[128,4096]{1,0:T(8,128)(2,1)S(1)} %pad_maximum_fusion.1), channel_id=1, source_target_pairs={{0,3},{1,0},{2,1},{3,2},{4,7},{5,4},{6,5},{7,6},{8,11},{9,8},{10,9... | collective-permute-start | bytes 3145736 | tf_op jit(solution)/shard_map/ppermute | solution.py:19
  108.1 20.6 %collective-permute-done.4 = bf16[128,4096]{1,0:T(8,128)(2,1)S(1)} collective-permute-done((bf16[128,4096]{1,0:T(8,128)(2,1)S(1)}, bf16[128,4096]{1,0:T(8,128)(2,1)S(1)}, u32[]{:S(2)}, u32[]{:S(2)}) %collective-permute-start.4) | collective-permute-done | bytes 1048608 | tf_op jit(solution)/shard_map/ppermute | solution.py:19
  (145 shorter events, 36.2 us)
Async XLA Ops:
  4.0 3.4 %copy-start.8 = (bf16[512,1024]{1,0:T(8,128)(2,1)S(1)}, bf16[512,1024]{1,0:T(8,128)(2,1)}, u32[]{:S(2)}) copy-start(bf16[512,1024]{1,0:T(8,128)(2,1)} %param.4) | copy-start | bytes 3145732
  4.0 27.8 %collective-permute-start = (bf16[2,512,1024]{1,2,0:T(8,128)(2,1)}, bf16[2,512,1024]{1,2,0:T(8,128)(2,1)}, u32[]{:S(2)}, u32[]{:S(2)}) collective-permute-start(bf16[2,512,1024]{1,2,0:T(8,128)(2,1)} %copy.14), channel_id=1, source_target_pairs={{0,4},{4,8},{8,12},{12,16},{16,20},{20,24},{24,28},{28,32},{32,36}... | collective-permute-start | bytes 6291464 | tf_op jit(solution)/shard_map/ppermute | solution.py:14
  8.4 4.5 %copy-start.4 = (bf16[128,1024]{0,1:T(8,128)(2,1)}, bf16[128,1024]{0,1:T(8,128)(2,1)S(1)}, u32[]{:S(2)}) copy-start(bf16[128,1024]{0,1:T(8,128)(2,1)S(1)} %copy.93) | copy-start | bytes 786436
  8.6 4.4 %copy-start.2 = (bf16[128,1024]{0,1:T(8,128)(2,1)}, bf16[128,1024]{0,1:T(8,128)(2,1)S(1)}, u32[]{:S(2)}) copy-start(bf16[128,1024]{0,1:T(8,128)(2,1)S(1)} %copy.94) | copy-start | bytes 786436
  8.8 4.1 %copy-start.27 = (s32[128]{0:T(128)}, s32[128]{0:T(128)S(1)}, u32[]{:S(2)}) copy-start(s32[128]{0:T(128)S(1)} %iota_add_fusion.2) | copy-start | bytes 1540
  8.8 4.1 %copy-start.28 = (s32[128]{0:T(128)}, s32[128]{0:T(128)S(1)}, u32[]{:S(2)}) copy-start(s32[128]{0:T(128)S(1)} %iota_add_fusion.3) | copy-start | bytes 1540
  8.8 4.1 %copy-start.29 = (s32[128]{0:T(128)}, s32[128]{0:T(128)S(1)}, u32[]{:S(2)}) copy-start(s32[128]{0:T(128)S(1)} %iota_add_fusion.4) | copy-start | bytes 1540
  8.8 4.1 %copy-start.30 = (s32[128]{0:T(128)}, s32[128]{0:T(128)S(1)}, u32[]{:S(2)}) copy-start(s32[128]{0:T(128)S(1)} %iota_add_fusion.6) | copy-start | bytes 1540
  9.5 3.4 %copy-start.24 = (s32[128]{0:T(128)}, s32[128]{0:T(128)S(1)}, u32[]{:S(2)}) copy-start(s32[128]{0:T(128)S(1)} %get-tuple-element.35) | copy-start | bytes 1540
  9.5 3.4 %copy-start.25 = (s32[128]{0:T(128)}, s32[128]{0:T(128)S(1)}, u32[]{:S(2)}) copy-start(s32[128]{0:T(128)S(1)} %get-tuple-element.36) | copy-start | bytes 1540
  11.0 3.8 %copy-start.17 = (pred[128,512]{1,0:T(8,128)(4,1)}, pred[128,512]{1,0:T(8,128)(4,1)S(1)}, u32[]{:S(2)}) copy-start(pred[128,512]{1,0:T(8,128)(4,1)S(1)} %get-tuple-element.54) | copy-start | bytes 196612
  11.0 3.8 %copy-start.21 = (pred[128,512]{1,0:T(8,128)(4,1)}, pred[128,512]{1,0:T(8,128)(4,1)S(1)}, u32[]{:S(2)}) copy-start(pred[128,512]{1,0:T(8,128)(4,1)S(1)} %get-tuple-element.53) | copy-start | bytes 196612
  11.0 3.8 %copy-start.10 = (pred[128,512]{1,0:T(8,128)(4,1)}, pred[128,512]{1,0:T(8,128)(4,1)S(1)}, u32[]{:S(2)}) copy-start(pred[128,512]{1,0:T(8,128)(4,1)S(1)} %get-tuple-element.64) | copy-start | bytes 196612
  14.8 19.3 %copy-start.7 = (bf16[2,512,1024]{2,1,0:T(8,128)(2,1)S(1)}, bf16[2,512,1024]{2,1,0:T(8,128)(2,1)}, u32[]{:S(2)}) copy-start(bf16[2,512,1024]{2,1,0:T(8,128)(2,1)} %param.5) | copy-start | bytes 6291460
  31.7 27.7 %collective-permute-start.1 = (bf16[2,512,1024]{1,2,0:T(8,128)(2,1)}, bf16[2,512,1024]{1,2,0:T(8,128)(2,1)}, u32[]{:S(2)}, u32[]{:S(2)}) collective-permute-start(bf16[2,512,1024]{1,2,0:T(8,128)(2,1)} %collective-permute-done), channel_id=1, source_target_pairs={{0,4},{4,8},{8,12},{12,16},{16,20},{20,24},{24,28},{28,32},{32,36}... | collective-permute-start | bytes 6291464 | tf_op jit(solution)/shard_map/ppermute | solution.py:14
  60.5 3.9 %copy-start.19 = (pred[128,512]{1,0:T(8,128)(4,1)S(1)}, pred[128,512]{1,0:T(8,128)(4,1)}, u32[]{:S(2)}) copy-start(pred[128,512]{1,0:T(8,128)(4,1)} %get-tuple-element.62) | copy-start | bytes 196612
  60.5 10.6 %collective-permute-start.2 = (bf16[2,128,1024]{1,2,0:T(8,128)(2,1)S(1)}, bf16[2,128,1024]{1,2,0:T(8,128)(2,1)S(1)}, u32[]{:S(2)}, u32[]{:S(2)}) collective-permute-start(bf16[2,128,1024]{1,2,0:T(8,128)(2,1)S(1)} %slice.86), channel_id=1, source_target_pairs={{0,4},{4,8},{8,12},{12,16},{16,20},{20,24},{24,28},{28,32},{32,36}... | collective-permute-start | bytes 1572872 | tf_op jit(solution)/shard_map/ppermute | solution.py:14
  75.8 3.7 %slice-start = ((s8[8388608]{0:T(1024)(128)(4,1)}), s8[4194304]{0:T(1024)(128)(4,1)S(1)}, s32[]{:S(2)}) async-start(s8[8388608]{0:T(1024)(128)(4,1)} %bitcast.272), calls=%async_computation | async-start | bytes 8388608
  77.9 2.2 %slice-start.1 = ((s8[8388608]{0:T(1024)(128)(4,1)}), s8[4194304]{0:T(1024)(128)(4,1)S(1)}, s32[]{:S(2)}) async-start(s8[8388608]{0:T(1024)(128)(4,1)} %bitcast.272), calls=%async_computation.1 | async-start | bytes 8388608
  86.2 15.0 %collective-permute-start.3 = (bf16[128,2048]{1,0:T(8,128)(2,1)S(1)}, bf16[128,2048]{1,0:T(8,128)(2,1)S(1)}, u32[]{:S(2)}, u32[]{:S(2)}) collective-permute-start(bf16[128,2048]{1,0:T(8,128)(2,1)S(1)} %get-tuple-element.29), channel_id=1, source_target_pairs={{0,1},{1,2},{2,3},{3,0},{4,5},{5,6},{6,7},{7,4},{8,9},{9,10},{10,1... | collective-permute-start | bytes 1572872 | tf_op jit(solution)/shard_map/ppermute | solution.py:19
  88.2 2.6 %copy-start.14 = (pred[128,512]{1,0:T(8,128)(4,1)S(1)}, pred[128,512]{1,0:T(8,128)(4,1)}, u32[]{:S(2)}) copy-start(pred[128,512]{1,0:T(8,128)(4,1)} %get-tuple-element.63) | copy-start | bytes 196612
  88.9 14.2 %collective-permute-start.5 = (bf16[128,2048]{1,0:T(8,128)(2,1)S(1)}, bf16[128,2048]{1,0:T(8,128)(2,1)S(1)}, u32[]{:S(2)}, u32[]{:S(2)}) collective-permute-start(bf16[128,2048]{1,0:T(8,128)(2,1)S(1)} %get-tuple-element.30), channel_id=1, source_target_pairs={{0,3},{1,0},{2,1},{3,2},{4,7},{5,4},{6,5},{7,6},{8,11},{9,8},{10,9... | collective-permute-start | bytes 1572872 | tf_op jit(solution)/shard_map/ppermute | solution.py:19
  101.4 27.3 %collective-permute-start.4 = (bf16[128,4096]{1,0:T(8,128)(2,1)S(1)}, bf16[128,4096]{1,0:T(8,128)(2,1)S(1)}, u32[]{:S(2)}, u32[]{:S(2)}) collective-permute-start(bf16[128,4096]{1,0:T(8,128)(2,1)S(1)} %pad_maximum_fusion), channel_id=1, source_target_pairs={{0,1},{1,2},{2,3},{3,0},{4,5},{5,6},{6,7},{7,4},{8,9},{9,10},{10,1... | collective-permute-start | bytes 3145736 | tf_op jit(solution)/shard_map/ppermute | solution.py:19
  103.3 26.1 %collective-permute-start.6 = (bf16[128,4096]{1,0:T(8,128)(2,1)S(1)}, bf16[128,4096]{1,0:T(8,128)(2,1)S(1)}, u32[]{:S(2)}, u32[]{:S(2)}) collective-permute-start(bf16[128,4096]{1,0:T(8,128)(2,1)S(1)} %pad_maximum_fusion.1), channel_id=1, source_target_pairs={{0,3},{1,0},{2,1},{3,2},{4,7},{5,4},{6,5},{7,6},{8,11},{9,8},{10,9... | collective-permute-start | bytes 3145736 | tf_op jit(solution)/shard_map/ppermute | solution.py:19
  (16 other events, 23.2 us)

commit v8 on v7

--- a/solution.py
+++ b/solution.py
@@ -65,14 +65,14 @@
                 summed = pv if summed is None else summed + pv
             return top, total, summed
 
-        near = list(zip(sources[2:], offsets[2:]))
-        far = list(zip(sources[:2], offsets[:2]))
         floor = jnp.full((heads, CHUNK, 1), -1e30, jnp.float32)
-        top_a, total_a, summed_a = stage(near, floor)
-        top, total_b, summed_b = stage(far, top_a)
-        alpha = jnp.exp(top_a - top)
-        total = alpha[:, :, 0] * total_a + total_b
-        summed = jnp.transpose(alpha, (1, 0, 2)) * summed_a + summed_b
+        top, total, summed = stage(list(zip(sources[2:], offsets[2:])), floor)
+        for kv, off in zip(sources[1::-1], offsets[1::-1]):
+            new_top, new_total, new_summed = stage([(kv, off)], top)
+            alpha = jnp.exp(top - new_top)
+            total = alpha[:, :, 0] * total + new_total
+            summed = jnp.transpose(alpha, (1, 0, 2)) * summed + new_summed
+            top = new_top
         attended = (summed / jnp.transpose(total)[:, :, None]).astype(jnp.bfloat16)
         attended = attended.reshape(CHUNK, heads * HD)
         return jnp.dot(attended, w_out, preferred_element_type=jnp.float32).astype(jnp.bfloat16)

time: 132 us -> 132 us (level)
    reduce_sum x8 -> x12, other arithmetic: 8.43 us -> 7.61 us  [stage(): t = jnp.sum(weights, axis=2)]
    unnamed x71 -> x69, local copies, waits for them, and re-layouts: 9.07 us -> 9.47 us
    slice x5 -> x4, local copies, waits for them, and re-layouts: 6.82 us -> 6.79 us  [stage(): kv[1].reshape(n, heads, HD)]
  transfers between devices with their start and end apart: 7 -> 7, of which waited for: 7 -> 7; matrix products, arithmetic and copies ran while one was open for 29% -> 28% of each run, Pallas kernels for 0% -> 0%
where the time goes in v8:
time: 132 us; the launch traced here: 131 us
  waiting for transfers between devices  57.2 us (43%)
  matrix products  27.3 us (21%)
  local copies, waits for them, and re-layouts  19.7 us (15%)
  other arithmetic  13.1 us (10%)
  starting transfers between devices  12.9 us (10%)
    ppermute x3, waiting for transfers between devices, shift_up(): return lax.ppermute(x, axis, [(i, i + 1) for i in range(peers - 1)])  32.7 us
    ppermute x4, waiting for transfers between devices, rotate(): return lax.ppermute(x, axis, [(i, (i + by) % peers) for i in range(peers)])  24.5 us
    dot_general x16, matrix products, scores(): jnp.einsum('qhd,khd->hqk', q, k, preferred_element_type=jnp.float32) * scale  12.2 us
    dot_general x16, matrix products, stage(): jnp.einsum('hqk,khd->qhd', probs, kv[1].reshape(n, heads, HD), preferred_...  9.96 us
    unnamed x69, local copies, waits for them, and re-layouts  9.47 us
    reduce_sum x12, other arithmetic, stage(): t = jnp.sum(weights, axis=2)  7.61 us
    slice x4, local copies, waits for them, and re-layouts, stage(): kv[1].reshape(n, heads, HD)  6.79 us
    ppermute x4, starting transfers between devices, rotate(): return lax.ppermute(x, axis, [(i, (i + by) % peers) for i in range(peers)])  6.73 us
  transfers between devices with their start and end apart: 7, of which 7 were waited for; matrix products, arithmetic and copies ran while one was open for 28% of the time, Pallas kernels for 0%

profile of v8, /device:TPU:98, one launch (start us, length us, event | category | flops | bytes accessed | tf_op | source)
XLA Modules:
  0.0 131.0 jit_solution(2773596771509458035)
XLA Ops:
  0.0 4.0 %copy.14 = bf16[2,512,1024]{1,2,0:T(8,128)(2,1)} copy(bf16[2,512,1024]{2,1,0:T(8,128)(2,1)} %param.5) | data formatting | bytes 4194304 | tf_op args[1]
  4.0 2.0 %collective-permute-start = (bf16[2,512,1024]{1,2,0:T(8,128)(2,1)}, bf16[2,512,1024]{1,2,0:T(8,128)(2,1)}, u32[]{:S(2)}, u32[]{:S(2)}) collective-permute-start(bf16[2,512,1024]{1,2,0:T(8,128)(2,1)} %copy.14), channel_id=1, source_target_pairs={{0,4},{4,8},{8,12},{12,16},{16,20},{20,24},{24,28},{28,32},{32,36}... | collective-permute-start | bytes 6291464 | tf_op jit(solution)/shard_map/ppermute | solution.py:14
  6.1 1.3 slice.85
  10.1 1.5 %fusion.150 = (pred[128,512]{1,0:T(8,128)(4,1)S(1)}, pred[128,512]{1,0:T(8,128)(4,1)S(1)}, pred[128,512]{1,0:T(8,128)(4,1)}, pred[128,512]{1,0:T(8,128)(4,1)}, p...) fusion(s32[512]{0:T(512)S(1)} %get-tuple-element.47, ...), kind=kLoop, calls=%fused_computation.191 | loop fusion | flops 2359296 | bytes 800768 | tf_op jit(solution)/shard_map/and | solution.py:48
  11.6 1.9 %fusion.5 = (f32[8,128]{1,0:T(8,128)S(1)}, f32[8,128,512]{2,1,0:T(8,128)}) fusion(pred[128,512]{1,0:T(8,128)(4,1)S(1)} %get-tuple-element.61, bf16[128,8,128]{0,2,1:T(8,128)(2,1)S(1)} %bitcast.382, bf16[512,8,128]{0,2,1:T(8,128)(2,1)S(1)} %bitcast.354), kind=kOutput, calls=%fused_computation.34 | convolution fusion | flops 135789568 | bytes 3477504 | tf_op jit(solution)/shard_map/qhd,khd->hqk/dot_general | solution.py:49
  13.5 1.8 %fusion.8 = (f32[8,128]{1,0:T(8,128)S(1)}, f32[8,128,512]{2,1,0:T(8,128)}) fusion(pred[128,512]{1,0:T(8,128)(4,1)S(1)} %get-tuple-element.62, bf16[128,8,128]{0,2,1:T(8,128)(2,1)S(1)} %bitcast.378, bf16[512,8,128]{0,2,1:T(8,128)(2,1)S(1)} %bitcast.355), kind=kOutput, calls=%fused_computation.37 | convolution fusion | flops 135789568 | bytes 3477504 | tf_op jit(solution)/shard_map/qhd,khd->hqk/dot_general | solution.py:49
  15.4 16.3 %collective-permute-done = bf16[2,512,1024]{1,2,0:T(8,128)(2,1)} collective-permute-done((bf16[2,512,1024]{1,2,0:T(8,128)(2,1)}, bf16[2,512,1024]{1,2,0:T(8,128)(2,1)}, u32[]{:S(2)}, u32[]{:S(2)}) %collective-permute-start) | collective-permute-done | bytes 2097184 | tf_op jit(solution)/shard_map/ppermute | solution.py:14
  31.8 1.9 %collective-permute-start.1 = (bf16[2,512,1024]{1,2,0:T(8,128)(2,1)}, bf16[2,512,1024]{1,2,0:T(8,128)(2,1)}, u32[]{:S(2)}, u32[]{:S(2)}) collective-permute-start(bf16[2,512,1024]{1,2,0:T(8,128)(2,1)} %collective-permute-done), channel_id=1, source_target_pairs={{0,4},{4,8},{8,12},{12,16},{16,20},{20,24},{24,28},{28,32},{32,36}... | collective-permute-start | bytes 6291464 | tf_op jit(solution)/shard_map/ppermute | solution.py:14
  35.3 2.4 %copy.24 = bf16[1,512,1024]{1,2,0:T(8,128)(2,1)} copy(bf16[1,512,1024]{2,1,0:T(8,128)(2,1)} %slice.36) | data formatting | bytes 2097152 | tf_op jit(solution)/shard_map/slice | solution.py:63
  37.7 1.8 %copy.95 = bf16[128,1024]{0,1:T(8,128)(2,1)} copy(bf16[128,1024]{1,0:T(8,128)(2,1)} %get-tuple-element.36) | data formatting | bytes 524288
  40.3 1.6 %fusion.11 = (f32[8,128]{1,0:T(8,128)S(1)}, f32[8,128,512]{2,1,0:T(8,128)S(1)}) fusion(pred[128,512]{1,0:T(8,128)(4,1)} %get-tuple-element.71, bf16[128,8,128]{0,2,1:T(8,128)(2,1)} %bitcast.386, bf16[512,8,128]{0,2,1:T(8,128)(2,1)S(1)} %bitcast.357), kind=kOutput, calls=%fused_computation.40 | convolution fusion | flops 135789568 | bytes 3477504 | tf_op jit(solution)/shard_map/qhd,khd->hqk/dot_general | solution.py:49
  41.9 1.7 %fusion.214 = (bf16[1,512,1024]{1,2,0:T(8,128)(2,1)S(1)}, bf16[1,512,1024]{1,2,0:T(8,128)(2,1)S(1)}) fusion(bf16[2,512,1024]{1,2,0:T(8,128)(2,1)} %collective-permute-done), kind=kLoop, calls=%fused_computation.318 | loop fusion | bytes 4194304 | tf_op jit(solution)/shard_map/slice | solution.py:63
  46.8 12.6 %collective-permute-done.1 = bf16[2,512,1024]{1,2,0:T(8,128)(2,1)} collective-permute-done((bf16[2,512,1024]{1,2,0:T(8,128)(2,1)}, bf16[2,512,1024]{1,2,0:T(8,128)(2,1)}, u32[]{:S(2)}, u32[]{:S(2)}) %collective-permute-start.1) | collective-permute-done | bytes 2097184 | tf_op jit(solution)/shard_map/ppermute | solution.py:14
  60.5 2.2 %collective-permute-start.2 = (bf16[2,128,1024]{1,2,0:T(8,128)(2,1)S(1)}, bf16[2,128,1024]{1,2,0:T(8,128)(2,1)S(1)}, u32[]{:S(2)}, u32[]{:S(2)}) collective-permute-start(bf16[2,128,1024]{1,2,0:T(8,128)(2,1)S(1)} %slice.87), channel_id=1, source_target_pairs={{0,4},{4,8},{8,12},{12,16},{16,20},{20,24},{24,28},{28,32},{32,36}... | collective-permute-start | bytes 1572872 | tf_op jit(solution)/shard_map/ppermute | solution.py:14
  62.7 1.7 %fusion.213 = (bf16[1,512,1024]{1,2,0:T(8,128)(2,1)S(1)}, bf16[1,512,1024]{1,2,0:T(8,128)(2,1)S(1)}) fusion(bf16[2,512,1024]{1,2,0:T(8,128)(2,1)} %collective-permute-done.1), kind=kLoop, calls=%fused_computation.317 | loop fusion | bytes 4194304 | tf_op jit(solution)/shard_map/slice | solution.py:63
  67.4 3.8 %collective-permute-done.2 = bf16[2,128,1024]{1,2,0:T(8,128)(2,1)S(1)} collective-permute-done((bf16[2,128,1024]{1,2,0:T(8,128)(2,1)S(1)}, bf16[2,128,1024]{1,2,0:T(8,128)(2,1)S(1)}, u32[]{:S(2)}, u32[]{:S(2)}) %collective-permute-start.2) | collective-permute-done | bytes 524320 | tf_op jit(solution)/shard_map/ppermute | solution.py:14
  81.8 1.3 convolution_convert_fusion.2
  86.8 1.6 %collective-permute-start.3 = (bf16[128,2048]{1,0:T(8,128)(2,1)S(1)}, bf16[128,2048]{1,0:T(8,128)(2,1)S(1)}, u32[]{:S(2)}, u32[]{:S(2)}) collective-permute-start(bf16[128,2048]{1,0:T(8,128)(2,1)S(1)} %get-tuple-element.37), channel_id=1, source_target_pairs={{0,1},{1,2},{2,3},{3,0},{4,5},{5,6},{6,7},{7,4},{8,9},{9,10},{10,1... | collective-permute-start | bytes 1572872 | tf_op jit(solution)/shard_map/ppermute | solution.py:19
  89.2 1.7 %collective-permute-start.5 = (bf16[128,2048]{1,0:T(8,128)(2,1)S(1)}, bf16[128,2048]{1,0:T(8,128)(2,1)S(1)}, u32[]{:S(2)}, u32[]{:S(2)}) collective-permute-start(bf16[128,2048]{1,0:T(8,128)(2,1)S(1)} %get-tuple-element.38), channel_id=1, source_target_pairs={{0,3},{1,0},{2,1},{3,2},{4,7},{5,4},{6,5},{7,6},{8,11},{9,8},{10,9... | collective-permute-start | bytes 1572872 | tf_op jit(solution)/shard_map/ppermute | solution.py:19
  95.0 1.3 convolution_convert_fusion
  99.3 2.6 %collective-permute-done.3 = bf16[128,2048]{1,0:T(8,128)(2,1)S(1)} collective-permute-done((bf16[128,2048]{1,0:T(8,128)(2,1)S(1)}, bf16[128,2048]{1,0:T(8,128)(2,1)S(1)}, u32[]{:S(2)}, u32[]{:S(2)}) %collective-permute-start.3) | collective-permute-done | bytes 524320 | tf_op jit(solution)/shard_map/ppermute | solution.py:19
  103.6 2.9 %collective-permute-start.6 = (bf16[128,4096]{1,0:T(8,128)(2,1)S(1)}, bf16[128,4096]{1,0:T(8,128)(2,1)S(1)}, u32[]{:S(2)}, u32[]{:S(2)}) collective-permute-start(bf16[128,4096]{1,0:T(8,128)(2,1)S(1)} %pad_maximum_fusion.1), channel_id=1, source_target_pairs={{0,3},{1,0},{2,1},{3,2},{4,7},{5,4},{6,5},{7,6},{8,11},{9,8},{10,9... | collective-permute-start | bytes 3145736 | tf_op jit(solution)/shard_map/ppermute | solution.py:19
  108.5 20.8 %collective-permute-done.4 = bf16[128,4096]{1,0:T(8,128)(2,1)S(1)} collective-permute-done((bf16[128,4096]{1,0:T(8,128)(2,1)S(1)}, bf16[128,4096]{1,0:T(8,128)(2,1)S(1)}, u32[]{:S(2)}, u32[]{:S(2)}) %collective-permute-start.4) | collective-permute-done | bytes 1048608 | tf_op jit(solution)/shard_map/ppermute | solution.py:19
  129.7 1.3 %add_convert_fusion = bf16[128,4096]{1,0:T(8,128)(2,1)} fusion(bf16[128,4096]{1,0:T(8,128)(2,1)S(1)} %collective-permute-done.6, f32[128,4096]{1,0:T(8,128)S(1)} %fusion, bf16[128,4096]{1,0:T(8,128)(2,1)S(1)} %collective-permute-done.4), kind=kLoop, calls=%fused_computation.5 | loop fusion | flops 2621440 | bytes 5242880 | tf_op jit(solution)/shard_map/convert_element_type | solution.py:99
  (147 shorter events, 38.2 us)
Async XLA Ops:
  4.0 3.4 %copy-start.8 = (bf16[512,1024]{1,0:T(8,128)(2,1)S(1)}, bf16[512,1024]{1,0:T(8,128)(2,1)}, u32[]{:S(2)}) copy-start(bf16[512,1024]{1,0:T(8,128)(2,1)} %param.4) | copy-start | bytes 3145732
  4.0 27.8 %collective-permute-start = (bf16[2,512,1024]{1,2,0:T(8,128)(2,1)}, bf16[2,512,1024]{1,2,0:T(8,128)(2,1)}, u32[]{:S(2)}, u32[]{:S(2)}) collective-permute-start(bf16[2,512,1024]{1,2,0:T(8,128)(2,1)} %copy.14), channel_id=1, source_target_pairs={{0,4},{4,8},{8,12},{12,16},{16,20},{20,24},{24,28},{28,32},{32,36}... | collective-permute-start | bytes 6291464 | tf_op jit(solution)/shard_map/ppermute | solution.py:14
  7.4 2.0 %copy-start.22 = (s32[16384]{0:T(1024)S(1)}, s32[16384]{0:T(1024)}, u32[]{:S(2)}) copy-start(s32[16384]{0:T(1024)} %param.7) | copy-start | bytes 196612
  8.4 5.1 %copy-start.4 = (bf16[128,1024]{0,1:T(8,128)(2,1)}, bf16[128,1024]{0,1:T(8,128)(2,1)S(1)}, u32[]{:S(2)}) copy-start(bf16[128,1024]{0,1:T(8,128)(2,1)S(1)} %copy.93) | copy-start | bytes 786436
  8.6 5.0 %copy-start.2 = (bf16[128,1024]{0,1:T(8,128)(2,1)}, bf16[128,1024]{0,1:T(8,128)(2,1)S(1)}, u32[]{:S(2)}) copy-start(bf16[128,1024]{0,1:T(8,128)(2,1)S(1)} %copy.94) | copy-start | bytes 786436
  8.8 4.7 %copy-start.27 = (s32[128]{0:T(128)}, s32[128]{0:T(128)S(1)}, u32[]{:S(2)}) copy-start(s32[128]{0:T(128)S(1)} %get-tuple-element.109) | copy-start | bytes 1540
  8.8 4.7 %copy-start.28 = (s32[128]{0:T(128)}, s32[128]{0:T(128)S(1)}, u32[]{:S(2)}) copy-start(s32[128]{0:T(128)S(1)} %get-tuple-element.110) | copy-start | bytes 1540
  9.3 4.2 %copy-start.29 = (s32[128]{0:T(128)}, s32[128]{0:T(128)S(1)}, u32[]{:S(2)}) copy-start(s32[128]{0:T(128)S(1)} %get-tuple-element.111) | copy-start | bytes 1540
  10.0 3.5 %copy-start.23 = (s32[128]{0:T(128)}, s32[128]{0:T(128)S(1)}, u32[]{:S(2)}) copy-start(s32[128]{0:T(128)S(1)} %get-tuple-element.43) | copy-start | bytes 1540
  10.0 3.5 %copy-start.24 = (s32[128]{0:T(128)}, s32[128]{0:T(128)S(1)}, u32[]{:S(2)}) copy-start(s32[128]{0:T(128)S(1)} %get-tuple-element.44) | copy-start | bytes 1540
  10.0 3.5 %copy-start.26 = (s32[128]{0:T(128)}, s32[128]{0:T(128)S(1)}, u32[]{:S(2)}) copy-start(s32[128]{0:T(128)S(1)} %get-tuple-element.113) | copy-start | bytes 1540
  11.6 3.8 %copy-start.14 = (pred[128,512]{1,0:T(8,128)(4,1)}, pred[128,512]{1,0:T(8,128)(4,1)S(1)}, u32[]{:S(2)}) copy-start(pred[128,512]{1,0:T(8,128)(4,1)S(1)} %get-tuple-element.62) | copy-start | bytes 196612
  11.6 3.8 %copy-start.16 = (pred[128,512]{1,0:T(8,128)(4,1)}, pred[128,512]{1,0:T(8,128)(4,1)S(1)}, u32[]{:S(2)}) copy-start(pred[128,512]{1,0:T(8,128)(4,1)S(1)} %get-tuple-element.61) | copy-start | bytes 196612
  15.4 18.9 %copy-start.7 = (bf16[2,512,1024]{2,1,0:T(8,128)(2,1)S(1)}, bf16[2,512,1024]{2,1,0:T(8,128)(2,1)}, u32[]{:S(2)}) copy-start(bf16[2,512,1024]{2,1,0:T(8,128)(2,1)} %param.5) | copy-start | bytes 6291460
  31.8 27.7 %collective-permute-start.1 = (bf16[2,512,1024]{1,2,0:T(8,128)(2,1)}, bf16[2,512,1024]{1,2,0:T(8,128)(2,1)}, u32[]{:S(2)}, u32[]{:S(2)}) collective-permute-start(bf16[2,512,1024]{1,2,0:T(8,128)(2,1)} %collective-permute-done), channel_id=1, source_target_pairs={{0,4},{4,8},{8,12},{12,16},{16,20},{20,24},{24,28},{28,32},{32,36}... | collective-permute-start | bytes 6291464 | tf_op jit(solution)/shard_map/ppermute | solution.py:14
  60.5 3.9 %copy-start.21 = (pred[128,512]{1,0:T(8,128)(4,1)S(1)}, pred[128,512]{1,0:T(8,128)(4,1)}, u32[]{:S(2)}) copy-start(pred[128,512]{1,0:T(8,128)(4,1)} %get-tuple-element.70) | copy-start | bytes 196612
  60.5 10.6 %collective-permute-start.2 = (bf16[2,128,1024]{1,2,0:T(8,128)(2,1)S(1)}, bf16[2,128,1024]{1,2,0:T(8,128)(2,1)S(1)}, u32[]{:S(2)}, u32[]{:S(2)}) collective-permute-start(bf16[2,128,1024]{1,2,0:T(8,128)(2,1)S(1)} %slice.87), channel_id=1, source_target_pairs={{0,4},{4,8},{8,12},{12,16},{16,20},{20,24},{24,28},{28,32},{32,36}... | collective-permute-start | bytes 1572872 | tf_op jit(solution)/shard_map/ppermute | solution.py:14
  77.7 3.4 %slice-start = ((s8[8388608]{0:T(1024)(128)(4,1)}), s8[4194304]{0:T(1024)(128)(4,1)S(1)}, s32[]{:S(2)}) async-start(s8[8388608]{0:T(1024)(128)(4,1)} %bitcast.352), calls=%async_computation | async-start | bytes 8388608
  79.5 2.3 %slice-start.1 = ((s8[8388608]{0:T(1024)(128)(4,1)}), s8[4194304]{0:T(1024)(128)(4,1)S(1)}, s32[]{:S(2)}) async-start(s8[8388608]{0:T(1024)(128)(4,1)} %bitcast.352), calls=%async_computation.1 | async-start | bytes 8388608
  86.8 4.1 %copy-start.11 = (pred[128,512]{1,0:T(8,128)(4,1)S(1)}, pred[128,512]{1,0:T(8,128)(4,1)}, u32[]{:S(2)}) copy-start(pred[128,512]{1,0:T(8,128)(4,1)} %get-tuple-element.71) | copy-start | bytes 196612
  86.8 15.0 %collective-permute-start.3 = (bf16[128,2048]{1,0:T(8,128)(2,1)S(1)}, bf16[128,2048]{1,0:T(8,128)(2,1)S(1)}, u32[]{:S(2)}, u32[]{:S(2)}) collective-permute-start(bf16[128,2048]{1,0:T(8,128)(2,1)S(1)} %get-tuple-element.37), channel_id=1, source_target_pairs={{0,1},{1,2},{2,3},{3,0},{4,5},{5,6},{6,7},{7,4},{8,9},{9,10},{10,1... | collective-permute-start | bytes 1572872 | tf_op jit(solution)/shard_map/ppermute | solution.py:19
  89.2 14.2 %collective-permute-start.5 = (bf16[128,2048]{1,0:T(8,128)(2,1)S(1)}, bf16[128,2048]{1,0:T(8,128)(2,1)S(1)}, u32[]{:S(2)}, u32[]{:S(2)}) collective-permute-start(bf16[128,2048]{1,0:T(8,128)(2,1)S(1)} %get-tuple-element.38), channel_id=1, source_target_pairs={{0,3},{1,0},{2,1},{3,2},{4,7},{5,4},{6,5},{7,6},{8,11},{9,8},{10,9... | collective-permute-start | bytes 1572872 | tf_op jit(solution)/shard_map/ppermute | solution.py:19
  102.1 27.2 %collective-permute-start.4 = (bf16[128,4096]{1,0:T(8,128)(2,1)S(1)}, bf16[128,4096]{1,0:T(8,128)(2,1)S(1)}, u32[]{:S(2)}, u32[]{:S(2)}) collective-permute-start(bf16[128,4096]{1,0:T(8,128)(2,1)S(1)} %pad_maximum_fusion), channel_id=1, source_target_pairs={{0,1},{1,2},{2,3},{3,0},{4,5},{5,6},{6,7},{7,4},{8,9},{9,10},{10,1... | collective-permute-start | bytes 3145736 | tf_op jit(solution)/shard_map/ppermute | solution.py:19
  103.6 26.0 %collective-permute-start.6 = (bf16[128,4096]{1,0:T(8,128)(2,1)S(1)}, bf16[128,4096]{1,0:T(8,128)(2,1)S(1)}, u32[]{:S(2)}, u32[]{:S(2)}) collective-permute-start(bf16[128,4096]{1,0:T(8,128)(2,1)S(1)} %pad_maximum_fusion.1), channel_id=1, source_target_pairs={{0,3},{1,0},{2,1},{3,2},{4,7},{5,4},{6,5},{7,6},{8,11},{9,8},{10,9... | collective-permute-start | bytes 3145736 | tf_op jit(solution)/shard_map/ppermute | solution.py:19
  (15 other events, 19.1 us)

commit v9 on v7

--- a/solution.py
+++ b/solution.py
@@ -83,17 +83,17 @@
     via_left = rotate(far[:, :cols], "head", groups - 1)
     via_right = rotate(far[:, cols:], "head", 1)
     nxt = chunk_part((h + 1) % groups)
-    nxt = jnp.concatenate(
-        [nxt[:, :cols], (nxt[:, cols:].astype(jnp.float32) + via_right.astype(jnp.float32)).astype(jnp.bfloat16)],
-        axis=1,
+    left_of_next = rotate(nxt[:, :cols], "head", 1)
+    right_of_next = rotate(
+        (nxt[:, cols:].astype(jnp.float32) + via_right.astype(jnp.float32)).astype(jnp.bfloat16), "head", 1
     )
-    from_left = rotate(nxt, "head", 1)
     prv = chunk_part((h + groups - 1) % groups)
-    prv = jnp.concatenate(
-        [(prv[:, :cols].astype(jnp.float32) + via_left.astype(jnp.float32)).astype(jnp.bfloat16), prv[:, cols:]],
-        axis=1,
+    right_of_prev = rotate(prv[:, cols:], "head", groups - 1)
+    left_of_prev = rotate(
+        (prv[:, :cols].astype(jnp.float32) + via_left.astype(jnp.float32)).astype(jnp.bfloat16), "head", groups - 1
     )
-    from_right = rotate(prv, "head", groups - 1)
+    from_left = jnp.concatenate([left_of_next, right_of_next], axis=1)
+    from_right = jnp.concatenate([left_of_prev, right_of_prev], axis=1)
     own = chunk_part(h)
     total_out = own.astype(jnp.float32) + from_left.astype(jnp.float32) + from_right.astype(jnp.float32)
     return total_out.astype(jnp.bfloat16)

time: 132 us -> 142 us (1.076)
  waiting for transfers between devices: 57.1 us -> 64.2 us
  starting transfers between devices: 12.9 us -> 14.8 us
  other arithmetic: 13.1 us -> 11.5 us
  matrix products: 27 us -> 28.5 us
    ppermute x4 -> x6, waiting for transfers between devices: 24.2 us -> 32.7 us  [rotate(): return lax.ppermute(x, axis, [(i, (i + by) % peers) for i in range(peers)])]
    ppermute x4 -> x6, starting transfers between devices: 6.67 us -> 8.71 us  [rotate(): return lax.ppermute(x, axis, [(i, (i + by) % peers) for i in range(peers)])]
  transfers between devices with their start and end apart: 7 -> 9, of which waited for: 7 -> 5; matrix products, arithmetic and copies ran while one was open for 29% -> 27% of each run, Pallas kernels for 0% -> 0%
where the time goes in v9:
time: 142 us; the launch traced here: 141 us
  waiting for transfers between devices  64.2 us (45%)
  matrix products  28.5 us (20%)
  local copies, waits for them, and re-layouts  21.2 us (15%)
  starting transfers between devices  14.8 us (10%)
  other arithmetic  11.5 us (8%)
    ppermute x6, waiting for transfers between devices, rotate(): return lax.ppermute(x, axis, [(i, (i + by) % peers) for i in range(peers)])  32.7 us
    ppermute x3, waiting for transfers between devices, shift_up(): return lax.ppermute(x, axis, [(i, i + 1) for i in range(peers - 1)])  31.5 us
    dot_general x16, matrix products, scores(): jnp.einsum('qhd,khd->hqk', q, k, preferred_element_type=jnp.float32) * scale  12.2 us
    unnamed x71, local copies, waits for them, and re-layouts  10.4 us
    dot_general x16, matrix products, stage(): jnp.einsum('hqk,khd->qhd', probs, kv[1].reshape(n, heads, HD), preferred_...  9.79 us
    ppermute x6, starting transfers between devices, rotate(): return lax.ppermute(x, axis, [(i, (i + by) % peers) for i in range(peers)])  8.71 us
    reduce_sum x8, other arithmetic, stage(): t = jnp.sum(weights, axis=2)  8.43 us
    slice x5, local copies, waits for them, and re-layouts, stage(): kv[1].reshape(n, heads, HD)  6.78 us
  transfers between devices with their start and end apart: 9, of which 5 were waited for; matrix products, arithmetic and copies ran while one was open for 27% of the time, Pallas kernels for 0%

profile of v9, /device:TPU:98, one launch (start us, length us, event | category | flops | bytes accessed | tf_op | source)
XLA Modules:
  0.0 141.1 jit_solution(13911975398045439806)
XLA Ops:
  0.0 3.9 %copy.14 = bf16[2,512,1024]{1,2,0:T(8,128)(2,1)} copy(bf16[2,512,1024]{2,1,0:T(8,128)(2,1)} %param.5) | data formatting | bytes 4194304 | tf_op args[1]
  4.0 2.0 %collective-permute-start = (bf16[2,512,1024]{1,2,0:T(8,128)(2,1)}, bf16[2,512,1024]{1,2,0:T(8,128)(2,1)}, u32[]{:S(2)}, u32[]{:S(2)}) collective-permute-start(bf16[2,512,1024]{1,2,0:T(8,128)(2,1)} %copy.14), channel_id=1, source_target_pairs={{0,4},{4,8},{8,12},{12,16},{16,20},{20,24},{24,28},{28,32},{32,36}... | collective-permute-start | bytes 6291464 | tf_op jit(solution)/shard_map/ppermute | solution.py:14
  10.9 1.4 %fusion.152 = (pred[128,512]{1,0:T(8,128)(4,1)S(1)}, pred[128,512]{1,0:T(8,128)(4,1)}, pred[128,512]{1,0:T(8,128)(4,1)}, pred[128,512]{1,0:T(8,128)(4,1)}, pred[...) fusion(s32[512]{0:T(512)S(1)} %get-tuple-element.39, ...), kind=kLoop, calls=%fused_computation.187 | loop fusion | flops 2359296 | bytes 800768 | tf_op jit(solution)/shard_map/and | solution.py:48
  13.1 1.9 %fusion.11 = (f32[8,128]{1,0:T(8,128)S(1)}, f32[8,128,512]{2,1,0:T(8,128)}) fusion(pred[128,512]{1,0:T(8,128)(4,1)S(1)} %get-tuple-element.53, bf16[128,8,128]{0,2,1:T(8,128)(2,1)S(1)} %bitcast.302, bf16[512,8,128]{0,2,1:T(8,128)(2,1)S(1)} %bitcast.275), kind=kOutput, calls=%fused_computation.40 | convolution fusion | flops 135789568 | bytes 3477504 | tf_op jit(solution)/shard_map/qhd,khd->hqk/dot_general | solution.py:49
  14.9 1.8 %fusion.8 = (f32[8,128]{1,0:T(8,128)S(1)}, f32[8,128,512]{2,1,0:T(8,128)}) fusion(pred[128,512]{1,0:T(8,128)(4,1)S(1)} %get-tuple-element.63, bf16[128,8,128]{0,2,1:T(8,128)(2,1)S(1)} %bitcast.298, bf16[512,8,128]{0,2,1:T(8,128)(2,1)S(1)} %bitcast.276), kind=kOutput, calls=%fused_computation.37 | convolution fusion | flops 135789568 | bytes 3477504 | tf_op jit(solution)/shard_map/qhd,khd->hqk/dot_general | solution.py:49
  16.8 15.0 %collective-permute-done = bf16[2,512,1024]{1,2,0:T(8,128)(2,1)} collective-permute-done((bf16[2,512,1024]{1,2,0:T(8,128)(2,1)}, bf16[2,512,1024]{1,2,0:T(8,128)(2,1)}, u32[]{:S(2)}, u32[]{:S(2)}) %collective-permute-start) | collective-permute-done | bytes 2097184 | tf_op jit(solution)/shard_map/ppermute | solution.py:14
  31.7 1.9 %collective-permute-start.1 = (bf16[2,512,1024]{1,2,0:T(8,128)(2,1)}, bf16[2,512,1024]{1,2,0:T(8,128)(2,1)}, u32[]{:S(2)}, u32[]{:S(2)}) collective-permute-start(bf16[2,512,1024]{1,2,0:T(8,128)(2,1)} %collective-permute-done), channel_id=1, source_target_pairs={{0,4},{4,8},{8,12},{12,16},{16,20},{20,24},{24,28},{28,32},{32,36}... | collective-permute-start | bytes 6291464 | tf_op jit(solution)/shard_map/ppermute | solution.py:14
  35.2 2.4 %copy.24 = bf16[1,512,1024]{1,2,0:T(8,128)(2,1)} copy(bf16[1,512,1024]{2,1,0:T(8,128)(2,1)} %slice.36) | data formatting | bytes 2097152 | tf_op jit(solution)/shard_map/slice | solution.py:63
  37.5 1.8 %copy.93 = bf16[128,1024]{0,1:T(8,128)(2,1)} copy(bf16[128,1024]{1,0:T(8,128)(2,1)} %get-tuple-element.29) | data formatting | bytes 524288
  40.2 1.6 %fusion.5 = (f32[8,128]{1,0:T(8,128)S(1)}, f32[8,128,512]{2,1,0:T(8,128)S(1)}) fusion(pred[128,512]{1,0:T(8,128)(4,1)} %get-tuple-element.54, bf16[128,8,128]{0,2,1:T(8,128)(2,1)} %bitcast.306, bf16[512,8,128]{0,2,1:T(8,128)(2,1)S(1)} %bitcast.277), kind=kOutput, calls=%fused_computation.34 | convolution fusion | flops 135789568 | bytes 3477504 | tf_op jit(solution)/shard_map/qhd,khd->hqk/dot_general | solution.py:49
  41.7 1.7 %fusion.198 = (bf16[1,512,1024]{1,2,0:T(8,128)(2,1)S(1)}, bf16[1,512,1024]{1,2,0:T(8,128)(2,1)S(1)}) fusion(bf16[2,512,1024]{1,2,0:T(8,128)(2,1)} %collective-permute-done), kind=kLoop, calls=%fused_computation.292 | loop fusion | bytes 4194304 | tf_op jit(solution)/shard_map/slice | solution.py:63
  46.6 12.8 %collective-permute-done.1 = bf16[2,512,1024]{1,2,0:T(8,128)(2,1)} collective-permute-done((bf16[2,512,1024]{1,2,0:T(8,128)(2,1)}, bf16[2,512,1024]{1,2,0:T(8,128)(2,1)}, u32[]{:S(2)}, u32[]{:S(2)}) %collective-permute-start.1) | collective-permute-done | bytes 2097184 | tf_op jit(solution)/shard_map/ppermute | solution.py:14
  60.5 2.1 %collective-permute-start.2 = (bf16[2,128,1024]{1,2,0:T(8,128)(2,1)S(1)}, bf16[2,128,1024]{1,2,0:T(8,128)(2,1)S(1)}, u32[]{:S(2)}, u32[]{:S(2)}) collective-permute-start(bf16[2,128,1024]{1,2,0:T(8,128)(2,1)S(1)} %slice.86), channel_id=1, source_target_pairs={{0,4},{4,8},{8,12},{12,16},{16,20},{20,24},{24,28},{28,32},{32,36}... | collective-permute-start | bytes 1572872 | tf_op jit(solution)/shard_map/ppermute | solution.py:14
  62.6 1.7 %fusion.197 = (bf16[1,512,1024]{1,2,0:T(8,128)(2,1)S(1)}, bf16[1,512,1024]{1,2,0:T(8,128)(2,1)S(1)}) fusion(bf16[2,512,1024]{1,2,0:T(8,128)(2,1)} %collective-permute-done.1), kind=kLoop, calls=%fused_computation.291 | loop fusion | bytes 4194304 | tf_op jit(solution)/shard_map/slice | solution.py:63
  67.2 3.8 %collective-permute-done.2 = bf16[2,128,1024]{1,2,0:T(8,128)(2,1)S(1)} collective-permute-done((bf16[2,128,1024]{1,2,0:T(8,128)(2,1)S(1)}, bf16[2,128,1024]{1,2,0:T(8,128)(2,1)S(1)}, u32[]{:S(2)}, u32[]{:S(2)}) %collective-permute-start.2) | collective-permute-done | bytes 524320 | tf_op jit(solution)/shard_map/ppermute | solution.py:14
  75.9 2.1 %fusion.33 = (f32[8,128]{1,0:T(8,128)S(1)}, f32[8,128]{1,0:T(8,128)S(1)}, f32[8,128]{1,0:T(8,128)S(1)}) fusion(f32[8,128,512]{2,1,0:T(8,128)S(1)} %copy-done.1, f32[8,128]{1,0:T(8,128)S(1)} %get-tuple-element.14, pred[128,512]{1,0:T(8,128)(4,1)S(1)} %copy-done.22, f32[8,128,512]{2,1,0:T(8,128)S(1)} %get-tuple-element.100, ...), kind=kLoop, calls=%fused_computation.62 | loop fusion | flops 6288384 | bytes 6508544 | tf_op jit(solution)/shard_map/reduce_sum | solution.py:61
  81.6 1.9 %fusion.27 = (f32[8,128]{1,0:T(8,128)S(1)}, f32[8,128]{1,0:T(8,128)S(1)}, f32[8,128]{1,0:T(8,128)S(1)}) fusion(f32[8,128,512]{2,1,0:T(8,128)S(1)} %copy-done, f32[8,128]{1,0:T(8,128)S(1)} %get-tuple-element.18, pred[128,512]{1,0:T(8,128)(4,1)S(1)} %copy-done.18, f32[8,128,512]{2,1,0:T(8,128)S(1)} %get-tuple-element.76, pred[128,512]{1,0:T(8,128)(4,1)S(1)} %copy-done.16, ...), kind=kLoop, calls=%fused_computation.56 | loop fusion | flops 6288384 | bytes 6508544 | tf_op jit(solution)/shard_map/reduce_sum | solution.py:61
  86.3 3.1 %collective-permute-start.6 = (bf16[128,2048]{1,0:T(8,128)(2,1)S(1)}, bf16[128,2048]{1,0:T(8,128)(2,1)S(1)}, u32[]{:S(2)}, u32[]{:S(2)}) collective-permute-start(bf16[128,2048]{1,0:T(8,128)(2,1)S(1)} %get-tuple-element.25), channel_id=1, source_target_pairs={{0,3},{1,0},{2,1},{3,2},{4,7},{5,4},{6,5},{7,6},{8,11},{9,8},{10,9... | collective-permute-start | bytes 1572872 | tf_op jit(solution)/shard_map/ppermute | solution.py:19
  91.0 2.1 %fusion.21 = (f32[8,128]{1,0:T(8,128)S(1)}, f32[8,128]{1,0:T(8,128)S(1)}, f32[8,128]{1,0:T(8,128)S(1)}) fusion(f32[8,128,512]{2,1,0:T(8,128)S(1)} %get-tuple-element.90, f32[8,128]{1,0:T(8,128)S(1)} %get-tuple-element.16, pred[128,512]{1,0:T(8,128)(4,1)S(1)} %copy-done.14, f32[8,128,512]{2,1,0:T(8,128)S(1)} %get-tuple-element.92, ...), kind=kLoop, calls=%fused_computation.50 | loop fusion | flops 6288384 | bytes 6508544 | tf_op jit(solution)/shard_map/reduce_sum | solution.py:61
  98.5 1.9 %fusion.15 = (f32[8,128]{1,0:T(8,128)S(1)}, f32[8,128]{1,0:T(8,128)S(1)}, f32[8,128]{1,0:T(8,128)S(1)}) fusion(f32[8,128,512]{2,1,0:T(8,128)S(1)} %get-tuple-element.82, f32[8,128]{1,0:T(8,128)S(1)} %get-tuple-element.20, pred[128,512]{1,0:T(8,128)(4,1)S(1)} %copy-done.11, f32[8,128,512]{2,1,0:T(8,128)S(1)} %get-tuple-element.84, ...), kind=kLoop, calls=%fused_computation.44 | loop fusion | flops 6288384 | bytes 6508544 | tf_op jit(solution)/shard_map/reduce_sum | solution.py:61
  101.4 3.2 %collective-permute-start.7 = (bf16[128,2048]{1,0:T(8,128)(2,1)S(1)}, bf16[128,2048]{1,0:T(8,128)(2,1)S(1)}, u32[]{:S(2)}, u32[]{:S(2)}) collective-permute-start(bf16[128,2048]{1,0:T(8,128)(2,1)S(1)} %add_convert_fusion.1), channel_id=1, source_target_pairs={{0,3},{1,0},{2,1},{3,2},{4,7},{5,4},{6,5},{7,6},{8,11},{9,8},{10,9... | collective-permute-start | bytes 1572872 | tf_op jit(solution)/shard_map/ppermute | solution.py:19
  104.6 18.3 %collective-permute-done.4 = bf16[128,2048]{1,0:T(8,128)(2,1)S(1)} collective-permute-done((bf16[128,2048]{1,0:T(8,128)(2,1)S(1)}, bf16[128,2048]{1,0:T(8,128)(2,1)S(1)}, u32[]{:S(2)}, u32[]{:S(2)}) %collective-permute-start.4) | collective-permute-done | bytes 524320 | tf_op jit(solution)/shard_map/ppermute | solution.py:19
  124.0 14.4 %collective-permute-done.5 = bf16[128,2048]{1,0:T(8,128)(2,1)S(1)} collective-permute-done((bf16[128,2048]{1,0:T(8,128)(2,1)S(1)}, bf16[128,2048]{1,0:T(8,128)(2,1)S(1)}, u32[]{:S(2)}, u32[]{:S(2)}) %collective-permute-start.5) | collective-permute-done | bytes 524320 | tf_op jit(solution)/shard_map/ppermute | solution.py:19
  138.4 2.6 %add_convert_fusion = bf16[128,4096]{1,0:T(8,128)(2,1)} fusion(bf16[128,2048]{1,0:T(8,128)(2,1)S(1)} %collective-permute-done.5, bf16[128,2048]{1,0:T(8,128)(2,1)S(1)} %collective-permute-done.3, bf16[128,2048]{1,0:T(8,128)(2,1)S(1)} %collective-permute-done.8, bf16[128,2048]{1,0:T(8,128)(2,1)S(1)} %collective-permute-done.7, ...), kind=kOutput, calls=%fused_computation.5 | convolution fusion | flops 1080557568 | bytes 11796480 | tf_op jit(solution)/shard_map/dot_general | solution.py:78
  (146 shorter events, 34.8 us)
Async XLA Ops:
  4.0 3.4 %copy-start.8 = (bf16[512,1024]{1,0:T(8,128)(2,1)S(1)}, bf16[512,1024]{1,0:T(8,128)(2,1)}, u32[]{:S(2)}) copy-start(bf16[512,1024]{1,0:T(8,128)(2,1)} %param.4) | copy-start | bytes 3145732
  4.0 27.8 %collective-permute-start = (bf16[2,512,1024]{1,2,0:T(8,128)(2,1)}, bf16[2,512,1024]{1,2,0:T(8,128)(2,1)}, u32[]{:S(2)}, u32[]{:S(2)}) collective-permute-start(bf16[2,512,1024]{1,2,0:T(8,128)(2,1)} %copy.14), channel_id=1, source_target_pairs={{0,4},{4,8},{8,12},{12,16},{16,20},{20,24},{24,28},{28,32},{32,36}... | collective-permute-start | bytes 6291464 | tf_op jit(solution)/shard_map/ppermute | solution.py:14
  7.4 2.8 %copy-start.23 = (s32[16384]{0:T(1024)S(1)}, s32[16384]{0:T(1024)}, u32[]{:S(2)}) copy-start(s32[16384]{0:T(1024)} %param.7) | copy-start | bytes 196612
  10.1 2.9 %copy-start.27 = (s32[128]{0:T(128)}, s32[128]{0:T(128)S(1)}, u32[]{:S(2)}) copy-start(s32[128]{0:T(128)S(1)} %iota_add_fusion.2) | copy-start | bytes 1540
  10.1 2.9 %copy-start.28 = (s32[128]{0:T(128)}, s32[128]{0:T(128)S(1)}, u32[]{:S(2)}) copy-start(s32[128]{0:T(128)S(1)} %iota_add_fusion.3) | copy-start | bytes 1540
  10.1 2.8 %copy-start.29 = (s32[128]{0:T(128)}, s32[128]{0:T(128)S(1)}, u32[]{:S(2)}) copy-start(s32[128]{0:T(128)S(1)} %iota_add_fusion.4) | copy-start | bytes 1540
  10.1 2.8 %copy-start.30 = (s32[128]{0:T(128)}, s32[128]{0:T(128)S(1)}, u32[]{:S(2)}) copy-start(s32[128]{0:T(128)S(1)} %iota_add_fusion.6) | copy-start | bytes 1540
  10.8 2.2 %copy-start.25 = (s32[128]{0:T(128)}, s32[128]{0:T(128)S(1)}, u32[]{:S(2)}) copy-start(s32[128]{0:T(128)S(1)} %get-tuple-element.36) | copy-start | bytes 1540
  10.8 2.2 %copy-start.26 = (s32[128]{0:T(128)}, s32[128]{0:T(128)S(1)}, u32[]{:S(2)}) copy-start(s32[128]{0:T(128)S(1)} %get-tuple-element.37) | copy-start | bytes 1540
  10.9 2.2 %copy-start.4 = (bf16[128,1024]{0,1:T(8,128)(2,1)S(1)}, bf16[128,1024]{0,1:T(8,128)(2,1)}, u32[]{:S(2)}) copy-start(bf16[128,1024]{0,1:T(8,128)(2,1)} %copy.95) | copy-start | bytes 786436
  12.3 2.6 %copy-start.17 = (pred[128,512]{1,0:T(8,128)(4,1)}, pred[128,512]{1,0:T(8,128)(4,1)S(1)}, u32[]{:S(2)}) copy-start(pred[128,512]{1,0:T(8,128)(4,1)S(1)} %get-tuple-element.63) | copy-start | bytes 196612
  13.0 1.9 %copy-start.2 = (bf16[128,1024]{0,1:T(8,128)(2,1)S(1)}, bf16[128,1024]{0,1:T(8,128)(2,1)}, u32[]{:S(2)}) copy-start(bf16[128,1024]{0,1:T(8,128)(2,1)} %copy.94) | copy-start | bytes 786436
  14.9 19.2 %copy-start.7 = (bf16[2,512,1024]{2,1,0:T(8,128)(2,1)S(1)}, bf16[2,512,1024]{2,1,0:T(8,128)(2,1)}, u32[]{:S(2)}) copy-start(bf16[2,512,1024]{2,1,0:T(8,128)(2,1)} %param.5) | copy-start | bytes 6291460
  31.7 27.7 %collective-permute-start.1 = (bf16[2,512,1024]{1,2,0:T(8,128)(2,1)}, bf16[2,512,1024]{1,2,0:T(8,128)(2,1)}, u32[]{:S(2)}, u32[]{:S(2)}) collective-permute-start(bf16[2,512,1024]{1,2,0:T(8,128)(2,1)} %collective-permute-done), channel_id=1, source_target_pairs={{0,4},{4,8},{8,12},{12,16},{16,20},{20,24},{24,28},{28,32},{32,36}... | collective-permute-start | bytes 6291464 | tf_op jit(solution)/shard_map/ppermute | solution.py:14
  60.5 10.5 %collective-permute-start.2 = (bf16[2,128,1024]{1,2,0:T(8,128)(2,1)S(1)}, bf16[2,128,1024]{1,2,0:T(8,128)(2,1)S(1)}, u32[]{:S(2)}, u32[]{:S(2)}) collective-permute-start(bf16[2,128,1024]{1,2,0:T(8,128)(2,1)S(1)} %slice.86), channel_id=1, source_target_pairs={{0,4},{4,8},{8,12},{12,16},{16,20},{20,24},{24,28},{28,32},{32,36}... | collective-permute-start | bytes 1572872 | tf_op jit(solution)/shard_map/ppermute | solution.py:14
  75.9 3.7 %slice-start = ((s8[8388608]{0:T(1024)(128)(4,1)}), s8[4194304]{0:T(1024)(128)(4,1)S(1)}, s32[]{:S(2)}) async-start(s8[8388608]{0:T(1024)(128)(4,1)} %bitcast.272), calls=%async_computation | async-start | bytes 8388608
  78.1 2.2 %slice-start.1 = ((s8[8388608]{0:T(1024)(128)(4,1)}), s8[4194304]{0:T(1024)(128)(4,1)S(1)}, s32[]{:S(2)}) async-start(s8[8388608]{0:T(1024)(128)(4,1)} %bitcast.272), calls=%async_computation.1 | async-start | bytes 8388608
  86.2 4.1 %copy-start.14 = (pred[128,512]{1,0:T(8,128)(4,1)S(1)}, pred[128,512]{1,0:T(8,128)(4,1)}, u32[]{:S(2)}) copy-start(pred[128,512]{1,0:T(8,128)(4,1)} %get-tuple-element.54) | copy-start | bytes 196612
  86.3 14.9 %collective-permute-start.6 = (bf16[128,2048]{1,0:T(8,128)(2,1)S(1)}, bf16[128,2048]{1,0:T(8,128)(2,1)S(1)}, u32[]{:S(2)}, u32[]{:S(2)}) collective-permute-start(bf16[128,2048]{1,0:T(8,128)(2,1)S(1)} %get-tuple-element.25), channel_id=1, source_target_pairs={{0,3},{1,0},{2,1},{3,2},{4,7},{5,4},{6,5},{7,6},{8,11},{9,8},{10,9... | collective-permute-start | bytes 1572872 | tf_op jit(solution)/shard_map/ppermute | solution.py:19
  89.5 34.5 %collective-permute-start.8 = (bf16[128,2048]{1,0:T(8,128)(2,1)S(1)}, bf16[128,2048]{1,0:T(8,128)(2,1)S(1)}, u32[]{:S(2)}, u32[]{:S(2)}) collective-permute-start(bf16[128,2048]{1,0:T(8,128)(2,1)S(1)} %slice.97), channel_id=1, source_target_pairs={{0,3},{1,0},{2,1},{3,2},{4,7},{5,4},{6,5},{7,6},{8,11},{9,8},{10,9... | collective-permute-start | bytes 1572872 | tf_op jit(solution)/shard_map/ppermute | solution.py:19
  96.0 28.0 %collective-permute-start.3 = (bf16[128,2048]{1,0:T(8,128)(2,1)S(1)}, bf16[128,2048]{1,0:T(8,128)(2,1)S(1)}, u32[]{:S(2)}, u32[]{:S(2)}) collective-permute-start(bf16[128,2048]{1,0:T(8,128)(2,1)S(1)} %slice.92), channel_id=1, source_target_pairs={{0,1},{1,2},{2,3},{3,0},{4,5},{5,6},{6,7},{7,4},{8,9},{9,10},{10,1... | collective-permute-start | bytes 1572872 | tf_op jit(solution)/shard_map/ppermute | solution.py:19
  97.4 25.6 %collective-permute-start.4 = (bf16[128,2048]{1,0:T(8,128)(2,1)S(1)}, bf16[128,2048]{1,0:T(8,128)(2,1)S(1)}, u32[]{:S(2)}, u32[]{:S(2)}) collective-permute-start(bf16[128,2048]{1,0:T(8,128)(2,1)S(1)} %get-tuple-element.26), channel_id=1, source_target_pairs={{0,1},{1,2},{2,3},{3,0},{4,5},{5,6},{6,7},{7,4},{8,9},{9,10},{10,1... | collective-permute-start | bytes 1572872 | tf_op jit(solution)/shard_map/ppermute | solution.py:19
  101.4 22.7 %collective-permute-start.7 = (bf16[128,2048]{1,0:T(8,128)(2,1)S(1)}, bf16[128,2048]{1,0:T(8,128)(2,1)S(1)}, u32[]{:S(2)}, u32[]{:S(2)}) collective-permute-start(bf16[128,2048]{1,0:T(8,128)(2,1)S(1)} %add_convert_fusion.1), channel_id=1, source_target_pairs={{0,3},{1,0},{2,1},{3,2},{4,7},{5,4},{6,5},{7,6},{8,11},{9,8},{10,9... | collective-permute-start | bytes 1572872 | tf_op jit(solution)/shard_map/ppermute | solution.py:19
  123.1 15.3 %collective-permute-start.5 = (bf16[128,2048]{1,0:T(8,128)(2,1)S(1)}, bf16[128,2048]{1,0:T(8,128)(2,1)S(1)}, u32[]{:S(2)}, u32[]{:S(2)}) collective-permute-start(bf16[128,2048]{1,0:T(8,128)(2,1)S(1)} %add_convert_fusion.2), channel_id=1, source_target_pairs={{0,1},{1,2},{2,3},{3,0},{4,5},{5,6},{6,7},{7,4},{8,9},{9,10},{10,1... | collective-permute-start | bytes 1572872 | tf_op jit(solution)/shard_map/ppermute | solution.py:19
  (18 other events, 22.0 us)

commit v10 on v7

--- a/solution.py
+++ b/solution.py
@@ -27,10 +27,11 @@
     h = lax.axis_index("head")
     first_row = me * rows
     tail = DOC_MOST - 2 * rows
-    r1 = shift_up(keys_values, "ctx")
-    r2 = shift_up(r1, "ctx")
-    r3 = shift_up(r2[:, rows - tail:], "ctx")
-    sources = [r3, r2, r1, keys_values]
+    keys, values = keys_values[0], keys_values[1]
+    r1 = (shift_up(keys, "ctx"), shift_up(values, "ctx"))
+    r2 = tuple(shift_up(x, "ctx") for x in r1)
+    r3 = tuple(shift_up(x[rows - tail:], "ctx") for x in r2)
+    sources = [r3, r2, r1, (keys, values)]
     offsets = [-DOC_MOST, -2 * rows, -rows, 0]
     padded_docs = jnp.concatenate([jnp.full((DOC_MOST,), -1, jnp.int32), doc_index])
     scale = HD ** (-0.5)
@@ -41,7 +42,7 @@
         q_docs = lax.dynamic_slice_in_dim(doc_index, first_row + start, CHUNK)
         q_place = start + jnp.arange(CHUNK, dtype=jnp.int32)
         def scores(kv, off):
-            n = kv.shape[1]
+            n = kv[0].shape[0]
             k = kv[0].reshape(n, heads, HD)
             k_docs = lax.dynamic_slice_in_dim(padded_docs, first_row + DOC_MOST + off, n)
             k_place = off + jnp.arange(n, dtype=jnp.int32)
@@ -56,7 +57,7 @@
             total = None
             summed = None
             for (kv, _), s in zip(pairs, score_list):
-                n = kv.shape[1]
+                n = kv[0].shape[0]
                 weights = jnp.exp(s - top)
                 t = jnp.sum(weights, axis=2)
                 probs = weights.astype(jnp.bfloat16)

time: 132 us -> 149 us (1.13)
  the two profiles are of different devices: /device:TPU:98 before, /device:TPU:1 now
where the time goes in v10:
time: 149 us; the launch traced here: 148 us
  matrix products  50.3 us (34%)
  waiting for transfers between devices  28.3 us (19%)
  starting transfers between devices  27 us (18%)
  local copies, waits for them, and re-layouts  26.2 us (18%)
  other arithmetic  15.4 us (10%)
    dot_general x16, matrix products, scores(): jnp.einsum('qhd,khd->hqk', q, k, preferred_element_type=jnp.float32) * scale  35.4 us
    ppermute x4, waiting for transfers between devices, rotate(): return lax.ppermute(x, axis, [(i, (i + by) % peers) for i in range(peers)])  23.9 us
    ppermute x6, starting transfers between devices, shift_up(): return lax.ppermute(x, axis, [(i, i + 1) for i in range(peers - 1)])  21 us
    unnamed x137, local copies, waits for them, and re-layouts  11.3 us
    dot_general x16, matrix products, stage(): jnp.einsum('hqk,khd->qhd', probs, kv[1].reshape(n, heads, HD), preferred_...  9.73 us
    reduce_sum x8, other arithmetic, stage(): t = jnp.sum(weights, axis=2)  8.23 us
    ppermute x4, starting transfers between devices, rotate(): return lax.ppermute(x, axis, [(i, (i + by) % peers) for i in range(peers)])  6.03 us
    ppermute x3, local copies, waits for them, and re-layouts, shift_up(): return lax.ppermute(x, axis, [(i, i + 1) for i in range(peers - 1)])  5.7 us
  transfers between devices with their start and end apart: 10, of which 3 were waited for; matrix products, arithmetic and copies ran while one was open for 43% of the time, Pallas kernels for 0%

profile of v10, /device:TPU:1, one launch (start us, length us, event | category | flops | bytes accessed | tf_op | source)
XLA Modules:
  0.0 148.5 jit_solution(3417564465727623884)
XLA Ops:
  0.0 3.0 %slice_bitcast_fusion = (bf16[512,1024]{1,0:T(8,128)(2,1)}, bf16[1,512,1024]{2,1,0:T(8,128)(2,1)S(1)}, bf16[1,512,1024]{2,1,0:T(8,128)(2,1)S(1)}) fusion(bf16[2,512,1024]{2,1,0:T(8,128)(2,1)} %param.5), kind=kLoop, calls=%fused_computation.293 | loop fusion | bytes 5242880 | tf_op jit(solution)/shard_map/squeeze | solution.py:30
  3.5 4.9 %collective-permute-start = (bf16[512,1024]{0,1:T(8,128)(2,1)S(1)}, bf16[512,1024]{0,1:T(8,128)(2,1)S(1)}, u32[]{:S(2)}, u32[]{:S(2)}) collective-permute-start(bf16[512,1024]{0,1:T(8,128)(2,1)S(1)} %bitcast.277), channel_id=1, source_target_pairs={{0,4},{4,8},{8,12},{12,16},{16,20},{20,24},{24,28},{28,32},{32,36}... | collective-permute-start | bytes 3145736 | tf_op jit(solution)/shard_map/ppermute | solution.py:14
  18.6 2.5 %fusion.11 = (f32[8,128]{1,0:T(8,128)}, f32[8,128,512]{2,1,0:T(8,128)}) fusion(pred[128,512]{1,0:T(8,128)(4,1)S(1)} %get-tuple-element.60, bf16[128,8,128]{0,2,1:T(8,128)(2,1)S(1)} %bitcast.294, bf16[512,8,128]{0,2,1:T(8,128)(2,1)S(1)} %bitcast.278), kind=kOutput, calls=%fused_computation.40 | convolution fusion | flops 135789568 | bytes 3477504 | tf_op jit(solution)/shard_map/qhd,khd->hqk/dot_general | solution.py:50
  27.4 3.4 %fusion.8 = (f32[8,128]{1,0:T(8,128)}, f32[8,128,512]{2,1,0:T(8,128)}) fusion(pred[128,512]{1,0:T(8,128)(4,1)} %get-tuple-element.51, bf16[128,8,128]{0,2,1:T(8,128)(2,1)S(1)} %bitcast.306, bf16[512,8,128]{0,2,1:T(8,128)(2,1)S(1)} %bitcast.279), kind=kOutput, calls=%fused_computation.37 | convolution fusion | flops 135789568 | bytes 3477504 | tf_op jit(solution)/shard_map/qhd,khd->hqk/dot_general | solution.py:50
  30.8 2.5 %fusion.2 = (f32[8,128]{1,0:T(8,128)}, f32[8,128,512]{2,1,0:T(8,128)}) fusion(pred[128,512]{1,0:T(8,128)(4,1)S(1)} %copy-done.28, bf16[128,8,128]{0,2,1:T(8,128)(2,1)S(1)} %bitcast.302, bf16[512,8,128]{0,2,1:T(8,128)(2,1)S(1)} %bitcast.280), kind=kOutput, calls=%fused_computation.31 | convolution fusion | flops 135789568 | bytes 3477504 | tf_op jit(solution)/shard_map/qhd,khd->hqk/dot_general | solution.py:50
  33.2 2.5 %fusion.5 = (f32[8,128]{1,0:T(8,128)}, f32[8,128,512]{2,1,0:T(8,128)}) fusion(pred[128,512]{1,0:T(8,128)(4,1)S(1)} %copy-done.26, bf16[128,8,128]{0,2,1:T(8,128)(2,1)S(1)} %bitcast.298, bf16[512,8,128]{0,2,1:T(8,128)(2,1)S(1)} %bitcast.281), kind=kOutput, calls=%fused_computation.34 | convolution fusion | flops 135789568 | bytes 3477504 | tf_op jit(solution)/shard_map/qhd,khd->hqk/dot_general | solution.py:50
  35.7 3.9 %collective-permute-start.1 = (bf16[512,1024]{0,1:T(8,128)(2,1)S(1)}, bf16[512,1024]{0,1:T(8,128)(2,1)S(1)}, u32[]{:S(2)}, u32[]{:S(2)}) collective-permute-start(bf16[512,1024]{0,1:T(8,128)(2,1)S(1)} %collective-permute-done), channel_id=1, source_target_pairs={{0,4},{4,8},{8,12},{12,16},{16,20},{20,24},{24,28},{28,32},{32,36}... | collective-permute-start | bytes 3145736 | tf_op jit(solution)/shard_map/ppermute | solution.py:14
  41.6 2.5 %fusion.10 = (f32[8,128]{1,0:T(8,128)}, f32[8,128,512]{2,1,0:T(8,128)}) fusion(pred[128,512]{1,0:T(8,128)(4,1)S(1)} %copy-done.36, bf16[128,8,128]{0,2,1:T(8,128)(2,1)S(1)} %bitcast.295, bf16[512,8,128]{0,2,1:T(8,128)(2,1)S(1)} %bitcast.286), kind=kOutput, calls=%fused_computation.39 | convolution fusion | flops 135789568 | bytes 3477504 | tf_op jit(solution)/shard_map/qhd,khd->hqk/dot_general | solution.py:50
  46.3 2.4 %fusion.7 = (f32[8,128]{1,0:T(8,128)}, f32[8,128,512]{2,1,0:T(8,128)}) fusion(pred[128,512]{1,0:T(8,128)(4,1)S(1)} %copy-done.32, bf16[128,8,128]{0,2,1:T(8,128)(2,1)S(1)} %bitcast.307, bf16[512,8,128]{0,2,1:T(8,128)(2,1)S(1)} %bitcast.287), kind=kOutput, calls=%fused_computation.36 | convolution fusion | flops 135789568 | bytes 3477504 | tf_op jit(solution)/shard_map/qhd,khd->hqk/dot_general | solution.py:50
  48.8 2.5 %fusion.1 = (f32[8,128]{1,0:T(8,128)}, f32[8,128,512]{2,1,0:T(8,128)}) fusion(pred[128,512]{1,0:T(8,128)(4,1)S(1)} %get-tuple-element.55, bf16[128,8,128]{0,2,1:T(8,128)(2,1)S(1)} %bitcast.303, bf16[512,8,128]{0,2,1:T(8,128)(2,1)S(1)} %bitcast.288), kind=kOutput, calls=%fused_computation.30 | convolution fusion | flops 135789568 | bytes 3477504 | tf_op jit(solution)/shard_map/qhd,khd->hqk/dot_general | solution.py:50
  51.3 2.5 %fusion.4 = (f32[8,128]{1,0:T(8,128)}, f32[8,128,512]{2,1,0:T(8,128)}) fusion(pred[128,512]{1,0:T(8,128)(4,1)S(1)} %copy-done.24, bf16[128,8,128]{0,2,1:T(8,128)(2,1)S(1)} %bitcast.300, bf16[512,8,128]{0,2,1:T(8,128)(2,1)S(1)} %bitcast.289), kind=kOutput, calls=%fused_computation.33 | convolution fusion | flops 135789568 | bytes 3477504 | tf_op jit(solution)/shard_map/qhd,khd->hqk/dot_general | solution.py:50
  54.5 3.8 %collective-permute-start.2 = (bf16[128,1024]{0,1:T(8,128)(2,1)}, bf16[128,1024]{0,1:T(8,128)(2,1)}, u32[]{:S(2)}, u32[]{:S(2)}) collective-permute-start(bf16[128,1024]{0,1:T(8,128)(2,1)} %slice.40), channel_id=1, source_target_pairs={{0,4},{4,8},{8,12},{12,16},{16,20},{20,24},{24,28},{28,32},{32,36}... | collective-permute-start | bytes 786440 | tf_op jit(solution)/shard_map/ppermute | solution.py:14
  58.3 4.4 %collective-permute-done.4 = bf16[512,1024]{1,0:T(8,128)(2,1)} collective-permute-done((bf16[512,1024]{1,0:T(8,128)(2,1)}, bf16[512,1024]{1,0:T(8,128)(2,1)}, u32[]{:S(2)}, u32[]{:S(2)}) %collective-permute-start.4) | collective-permute-done | bytes 1048608 | tf_op jit(solution)/shard_map/ppermute | solution.py:14
  64.3 4.6 %collective-permute-start.5 = (bf16[128,1024]{1,0:T(8,128)(2,1)}, bf16[128,1024]{1,0:T(8,128)(2,1)}, u32[]{:S(2)}, u32[]{:S(2)}) collective-permute-start(bf16[128,1024]{1,0:T(8,128)(2,1)} %slice.41), channel_id=1, source_target_pairs={{0,4},{4,8},{8,12},{12,16},{16,20},{20,24},{24,28},{28,32},{32,36}... | collective-permute-start | bytes 786440 | tf_op jit(solution)/shard_map/ppermute | solution.py:14
  68.9 2.5 %fusion.12 = (f32[8,128]{1,0:T(8,128)}, f32[8,128,512]{2,1,0:T(8,128)}) fusion(pred[128,512]{1,0:T(8,128)(4,1)S(1)} %copy-done.34, bf16[128,8,128]{0,2,1:T(8,128)(2,1)S(1)} %bitcast.296, bf16[512,8,128]{0,2,1:T(8,128)(2,1)S(1)} %bitcast.282), kind=kOutput, calls=%fused_computation.41 | convolution fusion | flops 135789568 | bytes 3477504 | tf_op jit(solution)/shard_map/qhd,khd->hqk/dot_general | solution.py:50
  71.4 2.5 %fusion.9 = (f32[8,128]{1,0:T(8,128)}, f32[8,128,512]{2,1,0:T(8,128)}) fusion(pred[128,512]{1,0:T(8,128)(4,1)S(1)} %copy-done.30, bf16[128,8,128]{0,2,1:T(8,128)(2,1)S(1)} %bitcast.308, bf16[512,8,128]{0,2,1:T(8,128)(2,1)S(1)} %bitcast.283), kind=kOutput, calls=%fused_computation.38 | convolution fusion | flops 135789568 | bytes 3477504 | tf_op jit(solution)/shard_map/qhd,khd->hqk/dot_general | solution.py:50
  75.1 2.3 %copy.27 = bf16[512,1024]{0,1:T(8,128)(2,1)} copy(bf16[512,1024]{1,0:T(8,128)(2,1)} %collective-permute-done.4) | data formatting | bytes 2097152 | tf_op jit(solution)/shard_map/ppermute | solution.py:14
  77.4 3.4 %fusion.6 = (f32[8,128]{1,0:T(8,128)}, f32[8,128,512]{2,1,0:T(8,128)}) fusion(pred[128,512]{1,0:T(8,128)(4,1)} %get-tuple-element.59, bf16[128,8,128]{0,2,1:T(8,128)(2,1)} %bitcast.299, bf16[512,8,128]{0,2,1:T(8,128)(2,1)S(1)} %bitcast.285), kind=kOutput, calls=%fused_computation.35 | convolution fusion | flops 135789568 | bytes 3477504 | tf_op jit(solution)/shard_map/qhd,khd->hqk/dot_general | solution.py:50
  94.7 2.7 %fusion.27 = (f32[8,128]{1,0:T(8,128)S(1)}, f32[8,128]{1,0:T(8,128)S(1)}, f32[8,128]{1,0:T(8,128)S(1)}, f32[8,128]{1,0:T(8,128)S(1)}) fusion(f32[8,128,512]{2,1,0:T(8,128)S(1)} %copy-done.5, f32[8,128]{1,0:T(8,128)S(1)} %get-tuple-element.18, pred[128,512]{1,0:T(8,128)(4,1)S(1)} %copy-done.38, f32[8,128,512]{2,1,0:T(8,128)S(1)} %copy-done.6, ...), kind=kLoop, calls=%fused_computation.56 | loop fusion | flops 8384512 | bytes 8675328 | tf_op jit(solution)/shard_map/reduce_sum | solution.py:62
  103.9 2.8 %collective-permute-start.8 = (bf16[128,2048]{1,0:T(8,128)(2,1)S(1)}, bf16[128,2048]{1,0:T(8,128)(2,1)S(1)}, u32[]{:S(2)}, u32[]{:S(2)}) collective-permute-start(bf16[128,2048]{1,0:T(8,128)(2,1)S(1)} %get-tuple-element.29), channel_id=1, source_target_pairs={{0,3},{1,0},{2,1},{3,2},{4,7},{5,4},{6,5},{7,6},{8,11},{9,8},{10,9... | collective-permute-start | bytes 1572872 | tf_op jit(solution)/shard_map/ppermute | solution.py:19
  111.4 2.4 %fusion.15 = (f32[8,128]{1,0:T(8,128)S(1)}, f32[8,128]{1,0:T(8,128)S(1)}, f32[8,128]{1,0:T(8,128)S(1)}, f32[8,128]{1,0:T(8,128)S(1)}) fusion(f32[8,128,512]{2,1,0:T(8,128)S(1)} %copy-done, f32[8,128]{1,0:T(8,128)S(1)} %get-tuple-element.16, pred[128,512]{1,0:T(8,128)(4,1)S(1)} %copy-done.29, f32[8,128,512]{2,1,0:T(8,128)S(1)} %copy-done.1, ...), kind=kLoop, calls=%fused_computation.44 | loop fusion | flops 8384512 | bytes 8675328 | tf_op jit(solution)/shard_map/reduce_sum | solution.py:62
  117.7 3.1 %collective-permute-start.9 = (bf16[128,4096]{1,0:T(8,128)(2,1)S(1)}, bf16[128,4096]{1,0:T(8,128)(2,1)S(1)}, u32[]{:S(2)}, u32[]{:S(2)}) collective-permute-start(bf16[128,4096]{1,0:T(8,128)(2,1)S(1)} %pad_maximum_fusion.1), channel_id=1, source_target_pairs={{0,3},{1,0},{2,1},{3,2},{4,7},{5,4},{6,5},{7,6},{8,11},{9,8},{10,9... | collective-permute-start | bytes 3145736 | tf_op jit(solution)/shard_map/ppermute | solution.py:19
  123.2 20.5 %collective-permute-done.9 = bf16[128,4096]{1,0:T(8,128)(2,1)S(1)} collective-permute-done((bf16[128,4096]{1,0:T(8,128)(2,1)S(1)}, bf16[128,4096]{1,0:T(8,128)(2,1)S(1)}, u32[]{:S(2)}, u32[]{:S(2)}) %collective-permute-start.9) | collective-permute-done | bytes 1048608 | tf_op jit(solution)/shard_map/ppermute | solution.py:19
  143.6 3.5 %collective-permute-done.7 = bf16[128,4096]{1,0:T(8,128)(2,1)S(1)} collective-permute-done((bf16[128,4096]{1,0:T(8,128)(2,1)S(1)}, bf16[128,4096]{1,0:T(8,128)(2,1)S(1)}, u32[]{:S(2)}, u32[]{:S(2)}) %collective-permute-start.7) | collective-permute-done | bytes 1048608 | tf_op jit(solution)/shard_map/ppermute | solution.py:19
  (217 shorter events, 56.5 us)
Async XLA Ops:
  3.0 12.5 %copy-start.41 = (s32[16384]{0:T(1024)S(1)}, s32[16384]{0:T(1024)}, u32[]{:S(2)}) copy-start(s32[16384]{0:T(1024)} %param.7) | copy-start | bytes 196612
  3.5 32.2 %collective-permute-start = (bf16[512,1024]{0,1:T(8,128)(2,1)S(1)}, bf16[512,1024]{0,1:T(8,128)(2,1)S(1)}, u32[]{:S(2)}, u32[]{:S(2)}) collective-permute-start(bf16[512,1024]{0,1:T(8,128)(2,1)S(1)} %bitcast.277), channel_id=1, source_target_pairs={{0,4},{4,8},{8,12},{12,16},{16,20},{20,24},{24,28},{28,32},{32,36}... | collective-permute-start | bytes 3145736 | tf_op jit(solution)/shard_map/ppermute | solution.py:14
  8.5 31.2 %collective-permute-start.3 = (bf16[512,1024]{1,0:T(8,128)(2,1)}, bf16[512,1024]{1,0:T(8,128)(2,1)}, u32[]{:S(2)}, u32[]{:S(2)}) collective-permute-start(bf16[512,1024]{1,0:T(8,128)(2,1)} %get-tuple-element.21), channel_id=1, source_target_pairs={{0,4},{4,8},{8,12},{12,16},{16,20},{20,24},{24,28},{28,32},{32,36}... | collective-permute-start | bytes 3145736 | tf_op jit(solution)/shard_map/ppermute | solution.py:14
  10.4 10.6 %copy-start.59 = (s32[128]{0:T(128)}, s32[128]{0:T(128)S(1)}, u32[]{:S(2)}) copy-start(s32[128]{0:T(128)S(1)} %iota_add_fusion.4) | copy-start | bytes 1540
  10.5 10.5 %copy-start.60 = (s32[128]{0:T(128)}, s32[128]{0:T(128)S(1)}, u32[]{:S(2)}) copy-start(s32[128]{0:T(128)S(1)} %iota_add_fusion.3) | copy-start | bytes 1540
  15.7 5.3 %copy-start.61 = (s32[128]{0:T(128)S(1)}, s32[128]{0:T(128)}, u32[]{:S(2)}) copy-start(s32[128]{0:T(128)} %iota_add_fusion.2) | copy-start | bytes 1540
  15.7 5.3 %copy-start.62 = (s32[128]{0:T(128)S(1)}, s32[128]{0:T(128)}, u32[]{:S(2)}) copy-start(s32[128]{0:T(128)} %iota_add_fusion.6) | copy-start | bytes 1540
  15.7 5.3 %copy-start.63 = (s32[128]{0:T(128)S(1)}, s32[128]{0:T(128)}, u32[]{:S(2)}) copy-start(s32[128]{0:T(128)} %iota_add_fusion.5) | copy-start | bytes 1540
  24.9 5.9 %copy-start.17 = (bf16[128,1024]{0,1:T(8,128)(2,1)}, bf16[128,1024]{0,1:T(8,128)(2,1)S(1)}, u32[]{:S(2)}) copy-start(bf16[128,1024]{0,1:T(8,128)(2,1)S(1)} %copy.97) | copy-start | bytes 786436
  26.1 7.1 %copy-start.14 = (bf16[128,1024]{0,1:T(8,128)(2,1)}, bf16[128,1024]{0,1:T(8,128)(2,1)S(1)}, u32[]{:S(2)}) copy-start(bf16[128,1024]{0,1:T(8,128)(2,1)S(1)} %copy.94) | copy-start | bytes 786436
  27.4 5.8 %copy-start.11 = (bf16[128,1024]{0,1:T(8,128)(2,1)}, bf16[128,1024]{0,1:T(8,128)(2,1)S(1)}, u32[]{:S(2)}) copy-start(bf16[128,1024]{0,1:T(8,128)(2,1)S(1)} %copy.96) | copy-start | bytes 786436
  33.2 8.4 %copy-start.36 = (pred[128,512]{1,0:T(8,128)(4,1)S(1)}, pred[128,512]{1,0:T(8,128)(4,1)}, u32[]{:S(2)}) copy-start(pred[128,512]{1,0:T(8,128)(4,1)} %get-tuple-element.54) | copy-start | bytes 196612
  35.7 18.1 %collective-permute-start.1 = (bf16[512,1024]{0,1:T(8,128)(2,1)S(1)}, bf16[512,1024]{0,1:T(8,128)(2,1)S(1)}, u32[]{:S(2)}, u32[]{:S(2)}) collective-permute-start(bf16[512,1024]{0,1:T(8,128)(2,1)S(1)} %collective-permute-done), channel_id=1, source_target_pairs={{0,4},{4,8},{8,12},{12,16},{16,20},{20,24},{24,28},{28,32},{32,36}... | collective-permute-start | bytes 3145736 | tf_op jit(solution)/shard_map/ppermute | solution.py:14
  39.6 23.1 %collective-permute-start.4 = (bf16[512,1024]{1,0:T(8,128)(2,1)}, bf16[512,1024]{1,0:T(8,128)(2,1)}, u32[]{:S(2)}, u32[]{:S(2)}) collective-permute-start(bf16[512,1024]{1,0:T(8,128)(2,1)} %collective-permute-done.3), channel_id=1, source_target_pairs={{0,4},{4,8},{8,12},{12,16},{16,20},{20,24},{24,28},{28,32},{32,36}... | collective-permute-start | bytes 3145736 | tf_op jit(solution)/shard_map/ppermute | solution.py:14
  51.3 17.6 %copy-start.34 = (pred[128,512]{1,0:T(8,128)(4,1)S(1)}, pred[128,512]{1,0:T(8,128)(4,1)}, u32[]{:S(2)}) copy-start(pred[128,512]{1,0:T(8,128)(4,1)} %get-tuple-element.57) | copy-start | bytes 196612
  54.5 16.9 %copy-start.30 = (pred[128,512]{1,0:T(8,128)(4,1)S(1)}, pred[128,512]{1,0:T(8,128)(4,1)}, u32[]{:S(2)}) copy-start(pred[128,512]{1,0:T(8,128)(4,1)} %get-tuple-element.58) | copy-start | bytes 196612
  54.5 26.3 %collective-permute-start.2 = (bf16[128,1024]{0,1:T(8,128)(2,1)}, bf16[128,1024]{0,1:T(8,128)(2,1)}, u32[]{:S(2)}, u32[]{:S(2)}) collective-permute-start(bf16[128,1024]{0,1:T(8,128)(2,1)} %slice.40), channel_id=1, source_target_pairs={{0,4},{4,8},{8,12},{12,16},{16,20},{20,24},{24,28},{28,32},{32,36}... | collective-permute-start | bytes 786440 | tf_op jit(solution)/shard_map/ppermute | solution.py:14
  64.3 18.4 %collective-permute-start.5 = (bf16[128,1024]{1,0:T(8,128)(2,1)}, bf16[128,1024]{1,0:T(8,128)(2,1)}, u32[]{:S(2)}, u32[]{:S(2)}) collective-permute-start(bf16[128,1024]{1,0:T(8,128)(2,1)} %slice.41), channel_id=1, source_target_pairs={{0,4},{4,8},{8,12},{12,16},{16,20},{20,24},{24,28},{28,32},{32,36}... | collective-permute-start | bytes 786440 | tf_op jit(solution)/shard_map/ppermute | solution.py:14
  77.4 4.8 %copy-start.53 = (f32[8,128]{1,0:T(8,128)S(1)}, f32[8,128]{1,0:T(8,128)}, u32[]{:S(2)}) copy-start(f32[8,128]{1,0:T(8,128)} %get-tuple-element.78) | copy-start | bytes 12292
  77.4 4.8 %copy-start.58 = (f32[8,128]{1,0:T(8,128)S(1)}, f32[8,128]{1,0:T(8,128)}, u32[]{:S(2)}) copy-start(f32[8,128]{1,0:T(8,128)} %get-tuple-element.80) | copy-start | bytes 12292
  103.9 13.6 %collective-permute-start.8 = (bf16[128,2048]{1,0:T(8,128)(2,1)S(1)}, bf16[128,2048]{1,0:T(8,128)(2,1)S(1)}, u32[]{:S(2)}, u32[]{:S(2)}) collective-permute-start(bf16[128,2048]{1,0:T(8,128)(2,1)S(1)} %get-tuple-element.29), channel_id=1, source_target_pairs={{0,3},{1,0},{2,1},{3,2},{4,7},{5,4},{6,5},{7,6},{8,11},{9,8},{10,9... | collective-permute-start | bytes 1572872 | tf_op jit(solution)/shard_map/ppermute | solution.py:19
  106.7 14.2 %collective-permute-start.6 = (bf16[128,2048]{1,0:T(8,128)(2,1)S(1)}, bf16[128,2048]{1,0:T(8,128)(2,1)S(1)}, u32[]{:S(2)}, u32[]{:S(2)}) collective-permute-start(bf16[128,2048]{1,0:T(8,128)(2,1)S(1)} %get-tuple-element.28), channel_id=1, source_target_pairs={{0,1},{1,2},{2,3},{3,0},{4,5},{5,6},{6,7},{7,4},{8,9},{9,10},{10,1... | collective-permute-start | bytes 1572872 | tf_op jit(solution)/shard_map/ppermute | solution.py:19
  117.7 26.0 %collective-permute-start.9 = (bf16[128,4096]{1,0:T(8,128)(2,1)S(1)}, bf16[128,4096]{1,0:T(8,128)(2,1)S(1)}, u32[]{:S(2)}, u32[]{:S(2)}) collective-permute-start(bf16[128,4096]{1,0:T(8,128)(2,1)S(1)} %pad_maximum_fusion.1), channel_id=1, source_target_pairs={{0,3},{1,0},{2,1},{3,2},{4,7},{5,4},{6,5},{7,6},{8,11},{9,8},{10,9... | collective-permute-start | bytes 3145736 | tf_op jit(solution)/shard_map/ppermute | solution.py:19
  121.1 26.1 %collective-permute-start.7 = (bf16[128,4096]{1,0:T(8,128)(2,1)S(1)}, bf16[128,4096]{1,0:T(8,128)(2,1)S(1)}, u32[]{:S(2)}, u32[]{:S(2)}) collective-permute-start(bf16[128,4096]{1,0:T(8,128)(2,1)S(1)} %pad_maximum_fusion), channel_id=1, source_target_pairs={{0,1},{1,2},{2,3},{3,0},{4,5},{5,6},{6,7},{7,4},{8,9},{9,10},{10,1... | collective-permute-start | bytes 3145736 | tf_op jit(solution)/shard_map/ppermute | solution.py:19
  (52 other events, 135.3 us)

commit v11 on v8

--- a/solution.py
+++ b/solution.py
@@ -29,17 +29,17 @@
     tail = DOC_MOST - 2 * rows
     r1 = shift_up(keys_values, "ctx")
     r2 = shift_up(r1, "ctx")
-    r3 = shift_up(r2[:, rows - tail:], "ctx")
-    sources = [r3, r2, r1, keys_values]
+    sources = [None, r2, r1, keys_values]
     offsets = [-DOC_MOST, -2 * rows, -rows, 0]
     padded_docs = jnp.concatenate([jnp.full((DOC_MOST,), -1, jnp.int32), doc_index])
     scale = HD ** (-0.5)
 
-    def chunk_part(c):
+    def chunk_state(c, upto):
         start = c * CHUNK
         q = lax.dynamic_slice_in_dim(queries, start, CHUNK, 0).reshape(CHUNK, heads, HD)
         q_docs = lax.dynamic_slice_in_dim(doc_index, first_row + start, CHUNK)
         q_place = start + jnp.arange(CHUNK, dtype=jnp.int32)
+
         def scores(kv, off):
             n = kv.shape[1]
             k = kv[0].reshape(n, heads, HD)
@@ -65,21 +65,36 @@
                 summed = pv if summed is None else summed + pv
             return top, total, summed
 
-        floor = jnp.full((heads, CHUNK, 1), -1e30, jnp.float32)
-        top, total, summed = stage(list(zip(sources[2:], offsets[2:])), floor)
-        for kv, off in zip(sources[1::-1], offsets[1::-1]):
+        def fold(state, kv, off):
+            top, total, summed = state
             new_top, new_total, new_summed = stage([(kv, off)], top)
             alpha = jnp.exp(top - new_top)
             total = alpha[:, :, 0] * total + new_total
             summed = jnp.transpose(alpha, (1, 0, 2)) * summed + new_summed
-            top = new_top
+            return new_top, total, summed
+
+        floor = jnp.full((heads, CHUNK, 1), -1e30, jnp.float32)
+        state = stage(list(zip(sources[2:], offsets[2:])), floor)
+        for kv, off in upto:
+            state = fold(state, kv, off)
+        return state, fold
+
+    def finish(state):
+        top, total, summed = state
         attended = (summed / jnp.transpose(total)[:, :, None]).astype(jnp.bfloat16)
         attended = attended.reshape(CHUNK, heads * HD)
         return jnp.dot(attended, w_out, preferred_element_type=jnp.float32).astype(jnp.bfloat16)
 
+    def chunk_part(c):
+        state, fold = chunk_state(c, [(r2, offsets[1])])
+        return finish(fold(state, r3, offsets[0]))
+
     assert groups == 4
     cols = w_out.shape[1] // 2
-    far = chunk_part((h + 2) % groups)
+    far_state, fold = chunk_state((h + 2) % groups, [(r2, offsets[1])])
+    relay, far_state = lax.optimization_barrier((r2[:, rows - tail:], far_state))
+    r3 = shift_up(relay, "ctx")
+    far = finish(fold(far_state, r3, offsets[0]))
     via_left = rotate(far[:, :cols], "head", groups - 1)
     via_right = rotate(far[:, cols:], "head", 1)
     nxt = chunk_part((h + 1) % groups)

time: 132 us -> 154 us (1.17)
  matrix products: 27.3 us -> 44.6 us
  other arithmetic: 13.1 us -> 20 us
  waiting for transfers between devices: 57.2 us -> 54.2 us
    dot_general x16, matrix products: 12.2 us -> 21.1 us  [scores(): jnp.einsum('qhd,khd->hqk', q, k, preferred_element_type=jnp.float32) * scale]
    dot_general x16, matrix products: 9.96 us -> 14.6 us  [stage(): jnp.einsum('hqk,khd->qhd', probs, kv[1].reshape(n, heads, HD), preferred_...]
    ppermute x3, waiting for transfers between devices: 32.7 us -> 28.5 us  [shift_up(): return lax.ppermute(x, axis, [(i, i + 1) for i in range(peers - 1)])]
    dot_general x4, matrix products: 5.14 us -> 8.92 us  [finish(): jnp.dot(attended, w_out, preferred_element_type=jnp.float32)]
    mul x8, other arithmetic: 0.08 us -> 3.65 us  [fold(): summed = jnp.transpose(alpha, (1, 0, 2)) * summed + new_summed]
    unnamed x69 -> x149, local copies, waits for them, and re-layouts: 9.47 us -> 11.6 us
    reduce_sum x12 -> x11, other arithmetic: 7.61 us -> 9.44 us  [stage(): t = jnp.sum(weights, axis=2)]
    max x4 -> x5, other arithmetic: 0.03 us -> 1.79 us  [stage(): top = jnp.maximum(top, s.max(axis=2, keepdims=True))]
  transfers between devices with their start and end apart: 7 -> 7, of which waited for: 7 -> 6; matrix products, arithmetic and copies ran while one was open for 28% -> 27% of each run, Pallas kernels for 0% -> 0%
where the time goes in v11:
time: 154 us
  waiting for transfers between devices  54.2 us (35%)
  matrix products  44.6 us (29%)
  local copies, waits for them, and re-layouts  20.8 us (14%)
  other arithmetic  20 us (13%)
  starting transfers between devices  12.7 us (8%)
    ppermute x3, waiting for transfers between devices, shift_up(): return lax.ppermute(x, axis, [(i, i + 1) for i in range(peers - 1)])  28.5 us
    ppermute x4, waiting for transfers between devices, rotate(): return lax.ppermute(x, axis, [(i, (i + by) % peers) for i in range(peers)])  25.8 us
    dot_general x16, matrix products, scores(): jnp.einsum('qhd,khd->hqk', q, k, preferred_element_type=jnp.float32) * scale  21.1 us
    dot_general x16, matrix products, stage(): jnp.einsum('hqk,khd->qhd', probs, kv[1].reshape(n, heads, HD), preferred_...  14.6 us
    unnamed x149, local copies, waits for them, and re-layouts  11.6 us
    reduce_sum x11, other arithmetic, stage(): t = jnp.sum(weights, axis=2)  9.44 us
    dot_general x4, matrix products, finish(): jnp.dot(attended, w_out, preferred_element_type=jnp.float32)  8.92 us
    ppermute x4, starting transfers between devices, rotate(): return lax.ppermute(x, axis, [(i, (i + by) % peers) for i in range(peers)])  6.67 us
  transfers between devices with their start and end apart: 7, of which 6 were waited for; matrix products, arithmetic and copies ran while one was open for 27% of the time, Pallas kernels for 0%

profile of v11, /device:TPU:98, one launch (start us, length us, event | category | flops | bytes accessed | tf_op | source)
XLA Modules:
  0.0 153.5 jit_solution(9513624319469874146)
XLA Ops:
  0.0 4.0 %copy.21 = bf16[2,512,1024]{1,2,0:T(8,128)(2,1)} copy(bf16[2,512,1024]{2,1,0:T(8,128)(2,1)} %param.5) | data formatting | bytes 4194304 | tf_op args[1]
  4.0 2.0 %collective-permute-start = (bf16[2,512,1024]{1,2,0:T(8,128)(2,1)}, bf16[2,512,1024]{1,2,0:T(8,128)(2,1)}, u32[]{:S(2)}, u32[]{:S(2)}) collective-permute-start(bf16[2,512,1024]{1,2,0:T(8,128)(2,1)} %copy.21), channel_id=1, source_target_pairs={{0,4},{4,8},{8,12},{12,16},{16,20},{20,24},{24,28},{28,32},{32,36}... | collective-permute-start | bytes 6291464 | tf_op jit(solution)/shard_map/ppermute | solution.py:14
  9.9 2.7 %fusion.208 = (bf16[1,512,1024]{1,2,0:T(8,128)(2,1)}, bf16[1,512,1024]{1,2,0:T(8,128)(2,1)S(1)}) fusion(bf16[2,512,1024]{1,2,0:T(8,128)(2,1)} %copy.21), kind=kLoop, calls=%fused_computation.311 | loop fusion | bytes 4194304 | tf_op jit(solution)/shard_map/slice | solution.py:63
  12.6 1.9 %fusion.5 = (f32[8,128]{1,0:T(8,128)S(1)}, f32[8,128,512]{2,1,0:T(8,128)}) fusion(pred[128,512]{1,0:T(8,128)(4,1)S(1)} %get-tuple-element.72, bf16[128,8,128]{0,2,1:T(8,128)(2,1)S(1)} %bitcast.359, bf16[512,8,128]{0,2,1:T(8,128)(2,1)S(1)} %bitcast.339), kind=kOutput, calls=%fused_computation.34 | convolution fusion | flops 135789568 | bytes 3477504 | tf_op jit(solution)/shard_map/qhd,khd->hqk/dot_general | solution.py:49
  14.5 2.5 %fusion.11 = (f32[8,128]{1,0:T(8,128)}, f32[8,128,512]{2,1,0:T(8,128)}) fusion(pred[128,512]{1,0:T(8,128)(4,1)S(1)} %get-tuple-element.81, bf16[128,8,128]{0,2,1:T(8,128)(2,1)S(1)} %bitcast.363, bf16[512,8,128]{0,2,1:T(8,128)(2,1)S(1)} %bitcast.340), kind=kOutput, calls=%fused_computation.40 | convolution fusion | flops 135789568 | bytes 3477504 | tf_op jit(solution)/shard_map/qhd,khd->hqk/dot_general | solution.py:49
  18.2 13.6 %collective-permute-done = bf16[2,512,1024]{1,2,0:T(8,128)(2,1)} collective-permute-done((bf16[2,512,1024]{1,2,0:T(8,128)(2,1)}, bf16[2,512,1024]{1,2,0:T(8,128)(2,1)}, u32[]{:S(2)}, u32[]{:S(2)}) %collective-permute-start) | collective-permute-done | bytes 2097184 | tf_op jit(solution)/shard_map/ppermute | solution.py:14
  31.8 1.9 %collective-permute-start.1 = (bf16[2,512,1024]{1,2,0:T(8,128)(2,1)}, bf16[2,512,1024]{1,2,0:T(8,128)(2,1)}, u32[]{:S(2)}, u32[]{:S(2)}) collective-permute-start(bf16[2,512,1024]{1,2,0:T(8,128)(2,1)} %collective-permute-done), channel_id=1, source_target_pairs={{0,4},{4,8},{8,12},{12,16},{16,20},{20,24},{24,28},{28,32},{32,36}... | collective-permute-start | bytes 6291464 | tf_op jit(solution)/shard_map/ppermute | solution.py:14
  34.3 1.8 %copy.110 = bf16[128,1024]{0,1:T(8,128)(2,1)} copy(bf16[128,1024]{1,0:T(8,128)(2,1)} %get-tuple-element.41) | data formatting | bytes 524288
  36.9 2.9 %fusion.8 = (f32[8,128]{1,0:T(8,128)S(1)}, f32[8,128,512]{2,1,0:T(8,128)}) fusion(pred[128,512]{1,0:T(8,128)(4,1)} %get-tuple-element.71, bf16[128,8,128]{0,2,1:T(8,128)(2,1)} %bitcast.367, bf16[512,8,128]{0,2,1:T(8,128)(2,1)S(1)} %bitcast.342), kind=kOutput, calls=%fused_computation.37 | convolution fusion | flops 135789568 | bytes 3477504 | tf_op jit(solution)/shard_map/qhd,khd->hqk/dot_general | solution.py:49
  43.3 2.0 %fusion.1 = (f32[8,128]{1,0:T(8,128)S(1)}, f32[8,128,512]{2,1,0:T(8,128)}) fusion(pred[128,512]{1,0:T(8,128)(4,1)S(1)} %get-tuple-element.76, bf16[128,8,128]{0,2,1:T(8,128)(2,1)S(1)} %bitcast.356, bf16[512,8,128]{0,2,1:T(8,128)(2,1)S(1)} %bitcast.345), kind=kOutput, calls=%fused_computation.30 | convolution fusion | flops 135789568 | bytes 3477504 | tf_op jit(solution)/shard_map/qhd,khd->hqk/dot_general | solution.py:49
  45.4 1.9 %fusion.7 = (f32[8,128]{1,0:T(8,128)S(1)}, f32[8,128,512]{2,1,0:T(8,128)}) fusion(pred[128,512]{1,0:T(8,128)(4,1)S(1)} %copy-done.21, bf16[128,8,128]{0,2,1:T(8,128)(2,1)S(1)} %bitcast.368, bf16[512,8,128]{0,2,1:T(8,128)(2,1)S(1)} %bitcast.346), kind=kOutput, calls=%fused_computation.36 | convolution fusion | flops 135789568 | bytes 3477504 | tf_op jit(solution)/shard_map/qhd,khd->hqk/dot_general | solution.py:49
  47.3 12.2 %collective-permute-done.1 = bf16[2,512,1024]{1,2,0:T(8,128)(2,1)} collective-permute-done((bf16[2,512,1024]{1,2,0:T(8,128)(2,1)}, bf16[2,512,1024]{1,2,0:T(8,128)(2,1)}, u32[]{:S(2)}, u32[]{:S(2)}) %collective-permute-start.1) | collective-permute-done | bytes 2097184 | tf_op jit(solution)/shard_map/ppermute | solution.py:14
  64.1 1.9 %fusion.16 = (f32[8,128]{1,0:T(8,128)S(1)}, f32[8,128]{1,0:T(8,128)S(1)}, f32[8,128]{1,0:T(8,128)S(1)}) fusion(f32[8,128,512]{2,1,0:T(8,128)S(1)} %copy-done.8, f32[8,128]{1,0:T(8,128)S(1)} %get-tuple-element.34, pred[128,512]{1,0:T(8,128)(4,1)S(1)} %copy-done.30, f32[8,128,512]{2,1,0:T(8,128)S(1)} %get-tuple-element.92, pred[128,512]{1,0:T(8,128)(4,1)S(1)} %copy-done.28, ...), kind=kLoop, calls=%fused_computation.45 | loop fusion | flops 6288384 | bytes 6508544 | tf_op jit(solution)/shard_map/reduce_sum | solution.py:61
  68.8 2.1 %collective-permute-start.2 = (bf16[2,128,1024]{1,2,0:T(8,128)(2,1)S(1)}, bf16[2,128,1024]{1,2,0:T(8,128)(2,1)S(1)}, u32[]{:S(2)}, u32[]{:S(2)}) collective-permute-start(bf16[2,128,1024]{1,2,0:T(8,128)(2,1)S(1)} %slice.87), channel_id=1, source_target_pairs={{0,4},{4,8},{8,12},{12,16},{16,20},{20,24},{24,28},{28,32},{32,36}... | collective-permute-start | bytes 1572872 | tf_op jit(solution)/shard_map/ppermute | solution.py:14
  70.9 1.9 %fusion.12 = (f32[8,128]{1,0:T(8,128)S(1)}, f32[8,128,512]{2,1,0:T(8,128)}) fusion(pred[128,512]{1,0:T(8,128)(4,1)S(1)} %copy-done.35, bf16[128,8,128]{0,2,1:T(8,128)(2,1)S(1)} %bitcast.365, bf16[512,8,128]{0,2,1:T(8,128)(2,1)S(1)} %bitcast.336), kind=kOutput, calls=%fused_computation.41 | convolution fusion | flops 135789568 | bytes 3477504 | tf_op jit(solution)/shard_map/qhd,khd->hqk/dot_general | solution.py:49
  72.8 1.8 %fusion.3 = (f32[8,128]{1,0:T(8,128)S(1)}, f32[8,128,512]{2,1,0:T(8,128)}) fusion(pred[128,512]{1,0:T(8,128)(4,1)S(1)} %copy-done.31, bf16[128,8,128]{0,2,1:T(8,128)(2,1)S(1)} %bitcast.357, bf16[512,8,128]{0,2,1:T(8,128)(2,1)S(1)} %bitcast.337), kind=kOutput, calls=%fused_computation.32 | convolution fusion | flops 135789568 | bytes 3477504 | tf_op jit(solution)/shard_map/qhd,khd->hqk/dot_general | solution.py:49
  74.6 1.9 %fusion.9 = (f32[8,128]{1,0:T(8,128)S(1)}, f32[8,128,512]{2,1,0:T(8,128)}) fusion(pred[128,512]{1,0:T(8,128)(4,1)S(1)} %copy-done.33, bf16[128,8,128]{0,2,1:T(8,128)(2,1)S(1)} %bitcast.369, bf16[512,8,128]{0,2,1:T(8,128)(2,1)S(1)} %bitcast.338), kind=kOutput, calls=%fused_computation.38 | convolution fusion | flops 135789568 | bytes 3477504 | tf_op jit(solution)/shard_map/qhd,khd->hqk/dot_general | solution.py:49
  76.5 2.8 %collective-permute-done.2 = bf16[2,128,1024]{1,2,0:T(8,128)(2,1)S(1)} collective-permute-done((bf16[2,128,1024]{1,2,0:T(8,128)(2,1)S(1)}, bf16[2,128,1024]{1,2,0:T(8,128)(2,1)S(1)}, u32[]{:S(2)}, u32[]{:S(2)}) %collective-permute-start.2) | collective-permute-done | bytes 524320 | tf_op jit(solution)/shard_map/ppermute | solution.py:14
  93.9 2.8 %fusion.52 = f32[128,8,128]{0,2,1:T(8,128)S(1)} fusion(f32[8,128,128]{1,2,0:T(8,128)} %fusion.66, bf16[512,8,128]{0,2,1:T(8,128)(2,1)} %bitcast.381, f32[8,128,512]{2,1,0:T(8,128)} %copy-done.4, f32[8,128]{1,0:T(8,128)} %copy-done.42, pred[128,512]{1,0:T(8,128)(4,1)} %get-tuple-element.75, f32[128,8]{0,1:T(8,128)} %fusion.166), kind=kOutput, calls=%fused_computation.97 | convolution fusion | flops 136577024 | bytes 4268032 | tf_op jit(solution)/shard_map/hqk,khd->qhd/dot_general | solution.py:63
  98.9 5.1 %convolution_convert_fusion = bf16[128,4096]{1,0:T(8,128)(2,1)S(1)} fusion(bf16[128,1024]{0,1:T(8,128)(2,1)S(1)} %bitcast.384, bf16[1024,4096]{1,0:T(8,128)(2,1)} %param.6), kind=kOutput, calls=%fused_computation | convolution fusion | flops 1074266112 | bytes 9699328 | tf_op jit(solution)/shard_map/dot_general | solution.py:86
  105.6 3.1 %collective-permute-start.5 = (bf16[128,2048]{1,0:T(8,128)(2,1)S(1)}, bf16[128,2048]{1,0:T(8,128)(2,1)S(1)}, u32[]{:S(2)}, u32[]{:S(2)}) collective-permute-start(bf16[128,2048]{1,0:T(8,128)(2,1)S(1)} %get-tuple-element.46), channel_id=1, source_target_pairs={{0,3},{1,0},{2,1},{3,2},{4,7},{5,4},{6,5},{7,6},{8,11},{9,8},{10,9... | collective-permute-start | bytes 1572872 | tf_op jit(solution)/shard_map/ppermute | solution.py:19
  120.8 3.2 %collective-permute-start.6 = (bf16[128,4096]{1,0:T(8,128)(2,1)S(1)}, bf16[128,4096]{1,0:T(8,128)(2,1)S(1)}, u32[]{:S(2)}, u32[]{:S(2)}) collective-permute-start(bf16[128,4096]{1,0:T(8,128)(2,1)S(1)} %pad_maximum_fusion.1), channel_id=1, source_target_pairs={{0,3},{1,0},{2,1},{3,2},{4,7},{5,4},{6,5},{7,6},{8,11},{9,8},{10,9... | collective-permute-start | bytes 3145736 | tf_op jit(solution)/shard_map/ppermute | solution.py:19
  127.5 20.1 %collective-permute-done.6 = bf16[128,4096]{1,0:T(8,128)(2,1)S(1)} collective-permute-done((bf16[128,4096]{1,0:T(8,128)(2,1)S(1)}, bf16[128,4096]{1,0:T(8,128)(2,1)S(1)}, u32[]{:S(2)}, u32[]{:S(2)}) %collective-permute-start.6) | collective-permute-done | bytes 1048608 | tf_op jit(solution)/shard_map/ppermute | solution.py:19
  147.5 4.6 %collective-permute-done.4 = bf16[128,4096]{1,0:T(8,128)(2,1)S(1)} collective-permute-done((bf16[128,4096]{1,0:T(8,128)(2,1)S(1)}, bf16[128,4096]{1,0:T(8,128)(2,1)S(1)}, u32[]{:S(2)}, u32[]{:S(2)}) %collective-permute-start.4) | collective-permute-done | bytes 1048608 | tf_op jit(solution)/shard_map/ppermute | solution.py:19
  (232 shorter events, 51.6 us)
Async XLA Ops:
  0.0 6.2 %copy-start.14 = (bf16[512,1024]{1,0:T(8,128)(2,1)S(1)}, bf16[512,1024]{1,0:T(8,128)(2,1)}, u32[]{:S(2)}) copy-start(bf16[512,1024]{1,0:T(8,128)(2,1)} %param.4) | copy-start | bytes 3145732
  4.0 27.8 %collective-permute-start = (bf16[2,512,1024]{1,2,0:T(8,128)(2,1)}, bf16[2,512,1024]{1,2,0:T(8,128)(2,1)}, u32[]{:S(2)}, u32[]{:S(2)}) collective-permute-start(bf16[2,512,1024]{1,2,0:T(8,128)(2,1)} %copy.21), channel_id=1, source_target_pairs={{0,4},{4,8},{8,12},{12,16},{16,20},{20,24},{24,28},{28,32},{32,36}... | collective-permute-start | bytes 6291464 | tf_op jit(solution)/shard_map/ppermute | solution.py:14
  7.0 5.6 %copy-start.68 = (s32[128]{0:T(128)}, s32[128]{0:T(128)S(1)}, u32[]{:S(2)}) copy-start(s32[128]{0:T(128)S(1)} %iota_add_fusion.2) | copy-start | bytes 1540
  7.2 5.4 %copy-start.9 = (bf16[128,1024]{0,1:T(8,128)(2,1)}, bf16[128,1024]{0,1:T(8,128)(2,1)S(1)}, u32[]{:S(2)}) copy-start(bf16[128,1024]{0,1:T(8,128)(2,1)S(1)} %copy.109) | copy-start | bytes 786436
  7.4 7.1 %copy-start.11 = (bf16[128,1024]{0,1:T(8,128)(2,1)}, bf16[128,1024]{0,1:T(8,128)(2,1)S(1)}, u32[]{:S(2)}) copy-start(bf16[128,1024]{0,1:T(8,128)(2,1)S(1)} %copy.111) | copy-start | bytes 786436
  7.6 5.0 %copy-start.69 = (s32[128]{0:T(128)}, s32[128]{0:T(128)S(1)}, u32[]{:S(2)}) copy-start(s32[128]{0:T(128)S(1)} %iota_add_fusion.6) | copy-start | bytes 1540
  31.8 27.7 %collective-permute-start.1 = (bf16[2,512,1024]{1,2,0:T(8,128)(2,1)}, bf16[2,512,1024]{1,2,0:T(8,128)(2,1)}, u32[]{:S(2)}, u32[]{:S(2)}) collective-permute-start(bf16[2,512,1024]{1,2,0:T(8,128)(2,1)} %collective-permute-done), channel_id=1, source_target_pairs={{0,4},{4,8},{8,12},{12,16},{16,20},{20,24},{24,28},{28,32},{32,36}... | collective-permute-start | bytes 6291464 | tf_op jit(solution)/shard_map/ppermute | solution.py:14
  41.5 24.5 %copy-start.19 = (bf16[1,512,1024]{1,2,0:T(8,128)(2,1)}, bf16[1,512,1024]{1,2,0:T(8,128)(2,1)S(1)}, u32[]{:S(2)}) copy-start(bf16[1,512,1024]{1,2,0:T(8,128)(2,1)S(1)} %get-tuple-element.37) | copy-start | bytes 3145732
  43.3 48.2 %copy-start.4 = (f32[8,128,512]{2,1,0:T(8,128)}, f32[8,128,512]{2,1,0:T(8,128)S(1)}, u32[]{:S(2)}) copy-start(f32[8,128,512]{2,1,0:T(8,128)S(1)} %get-tuple-element.102) | copy-start | bytes 6291460
  47.3 13.9 %copy-start.27 = (pred[128,512]{1,0:T(8,128)(4,1)S(1)}, pred[128,512]{1,0:T(8,128)(4,1)}, u32[]{:S(2)}) copy-start(pred[128,512]{1,0:T(8,128)(4,1)} %get-tuple-element.79) | copy-start | bytes 196612
  61.2 5.8 %copy-start.15 = (bf16[1,512,1024]{1,2,0:T(8,128)(2,1)}, bf16[1,512,1024]{1,2,0:T(8,128)(2,1)S(1)}, u32[]{:S(2)}) copy-start(bf16[1,512,1024]{1,2,0:T(8,128)(2,1)S(1)} %get-tuple-element.35) | copy-start | bytes 3145732
  67.6 5.1 %copy-start.31 = (pred[128,512]{1,0:T(8,128)(4,1)S(1)}, pred[128,512]{1,0:T(8,128)(4,1)}, u32[]{:S(2)}) copy-start(pred[128,512]{1,0:T(8,128)(4,1)} %get-tuple-element.77) | copy-start | bytes 196612
  68.8 10.5 %collective-permute-start.2 = (bf16[2,128,1024]{1,2,0:T(8,128)(2,1)S(1)}, bf16[2,128,1024]{1,2,0:T(8,128)(2,1)S(1)}, u32[]{:S(2)}, u32[]{:S(2)}) collective-permute-start(bf16[2,128,1024]{1,2,0:T(8,128)(2,1)S(1)} %slice.87), channel_id=1, source_target_pairs={{0,4},{4,8},{8,12},{12,16},{16,20},{20,24},{24,28},{28,32},{32,36}... | collective-permute-start | bytes 1572872 | tf_op jit(solution)/shard_map/ppermute | solution.py:14
  74.6 5.0 %copy-start.55 = (f32[8,128]{1,0:T(8,128)S(1)}, f32[8,128]{1,0:T(8,128)}, u32[]{:S(2)}) copy-start(f32[8,128]{1,0:T(8,128)} %get-tuple-element.99) | copy-start | bytes 12292
  80.2 11.3 %copy-start.42 = (f32[8,128]{1,0:T(8,128)}, f32[8,128]{1,0:T(8,128)S(1)}, u32[]{:S(2)}) copy-start(f32[8,128]{1,0:T(8,128)S(1)} %get-tuple-element.30) | copy-start | bytes 12292
  83.9 6.0 %copy-start.3 = (f32[8,128,512]{2,1,0:T(8,128)S(1)}, f32[8,128,512]{2,1,0:T(8,128)}, u32[]{:S(2)}) copy-start(f32[8,128,512]{2,1,0:T(8,128)} %get-tuple-element.100) | copy-start | bytes 6291460
  83.9 6.0 %copy-start.26 = (pred[128,512]{1,0:T(8,128)(4,1)S(1)}, pred[128,512]{1,0:T(8,128)(4,1)}, u32[]{:S(2)}) copy-start(pred[128,512]{1,0:T(8,128)(4,1)} %copy-done.25) | copy-start | bytes 196612
  86.3 5.2 %copy-start.46 = (f32[8,128]{1,0:T(8,128)}, f32[8,128]{1,0:T(8,128)S(1)}, u32[]{:S(2)}) copy-start(f32[8,128]{1,0:T(8,128)S(1)} %get-tuple-element.111) | copy-start | bytes 12292
  98.1 5.9 %slice-start = ((s8[8388608]{0:T(1024)(128)(4,1)}), s8[4194304]{0:T(1024)(128)(4,1)S(1)}, s32[]{:S(2)}) async-start(s8[8388608]{0:T(1024)(128)(4,1)} %bitcast.333), calls=%async_computation | async-start | bytes 8388608
  98.9 5.3 %slice-start.1 = ((s8[8388608]{0:T(1024)(128)(4,1)}), s8[4194304]{0:T(1024)(128)(4,1)S(1)}, s32[]{:S(2)}) async-start(s8[8388608]{0:T(1024)(128)(4,1)} %bitcast.333), calls=%async_computation.1 | async-start | bytes 8388608
  105.6 14.9 %collective-permute-start.5 = (bf16[128,2048]{1,0:T(8,128)(2,1)S(1)}, bf16[128,2048]{1,0:T(8,128)(2,1)S(1)}, u32[]{:S(2)}, u32[]{:S(2)}) collective-permute-start(bf16[128,2048]{1,0:T(8,128)(2,1)S(1)} %get-tuple-element.46), channel_id=1, source_target_pairs={{0,3},{1,0},{2,1},{3,2},{4,7},{5,4},{6,5},{7,6},{8,11},{9,8},{10,9... | collective-permute-start | bytes 1572872 | tf_op jit(solution)/shard_map/ppermute | solution.py:19
  109.5 15.6 %collective-permute-start.3 = (bf16[128,2048]{1,0:T(8,128)(2,1)S(1)}, bf16[128,2048]{1,0:T(8,128)(2,1)S(1)}, u32[]{:S(2)}, u32[]{:S(2)}) collective-permute-start(bf16[128,2048]{1,0:T(8,128)(2,1)S(1)} %get-tuple-element.45), channel_id=1, source_target_pairs={{0,1},{1,2},{2,3},{3,0},{4,5},{5,6},{6,7},{7,4},{8,9},{9,10},{10,1... | collective-permute-start | bytes 1572872 | tf_op jit(solution)/shard_map/ppermute | solution.py:19
  120.8 26.7 %collective-permute-start.6 = (bf16[128,4096]{1,0:T(8,128)(2,1)S(1)}, bf16[128,4096]{1,0:T(8,128)(2,1)S(1)}, u32[]{:S(2)}, u32[]{:S(2)}) collective-permute-start(bf16[128,4096]{1,0:T(8,128)(2,1)S(1)} %pad_maximum_fusion.1), channel_id=1, source_target_pairs={{0,3},{1,0},{2,1},{3,2},{4,7},{5,4},{6,5},{7,6},{8,11},{9,8},{10,9... | collective-permute-start | bytes 3145736 | tf_op jit(solution)/shard_map/ppermute | solution.py:19
  125.3 26.9 %collective-permute-start.4 = (bf16[128,4096]{1,0:T(8,128)(2,1)S(1)}, bf16[128,4096]{1,0:T(8,128)(2,1)S(1)}, u32[]{:S(2)}, u32[]{:S(2)}) collective-permute-start(bf16[128,4096]{1,0:T(8,128)(2,1)S(1)} %pad_maximum_fusion), channel_id=1, source_target_pairs={{0,1},{1,2},{2,3},{3,0},{4,5},{5,6},{6,7},{7,4},{8,9},{9,10},{10,1... | collective-permute-start | bytes 3145736 | tf_op jit(solution)/shard_map/ppermute | solution.py:19
  (55 other events, 123.9 us)

commit v12 on v7

--- a/solution.py
+++ b/solution.py
@@ -1,6 +1,7 @@
 import jax
 import jax.numpy as jnp
 from jax import lax
+from jax.experimental.layout import Layout, with_layout_constraint
 from jax.sharding import PartitionSpec as P
 
 HD = 128
@@ -27,9 +28,13 @@
     h = lax.axis_index("head")
     first_row = me * rows
     tail = DOC_MOST - 2 * rows
-    r1 = shift_up(keys_values, "ctx")
-    r2 = shift_up(r1, "ctx")
-    r3 = shift_up(r2[:, rows - tail:], "ctx")
+    def relay(x):
+        x = with_layout_constraint(x, Layout(major_to_minor=(0, 1, 2)))
+        return with_layout_constraint(shift_up(x, "ctx"), Layout(major_to_minor=(0, 1, 2)))
+
+    r1 = relay(keys_values)
+    r2 = relay(r1)
+    r3 = relay(r2[:, rows - tail:])
     sources = [r3, r2, r1, keys_values]
     offsets = [-DOC_MOST, -2 * rows, -rows, 0]
     padded_docs = jnp.concatenate([jnp.full((DOC_MOST,), -1, jnp.int32), doc_index])

time: 132 us -> 143 us (1.083)
  waiting for transfers between devices: 57.1 us -> 34 us
  matrix products: 27 us -> 46.3 us
  local copies, waits for them, and re-layouts: 20 us -> 31.1 us
  starting transfers between devices: 12.9 us -> 15 us
    ppermute x3, waiting for transfers between devices: 32.8 us -> 12.4 us  [shift_up(): return lax.ppermute(x, axis, [(i, i + 1) for i in range(peers - 1)])]
    dot_general x16, matrix products: 12.2 us -> 31.3 us  [scores(): jnp.einsum('qhd,khd->hqk', q, k, preferred_element_type=jnp.float32) * scale]
    another operation x0 -> x3, local copies, waits for them, and re-layouts: none -> 4.82 us  [stage(): kv[1].reshape(n, heads, HD)]
    ppermute x4, waiting for transfers between devices: 24.2 us -> 21.6 us  [rotate(): return lax.ppermute(x, axis, [(i, (i + by) % peers) for i in range(peers)])]
    ppermute x3, starting transfers between devices: 6.18 us -> 8.24 us  [shift_up(): return lax.ppermute(x, axis, [(i, i + 1) for i in range(peers - 1)])]
    slice x5 -> x4, local copies, waits for them, and re-layouts: 6.82 us -> 8.83 us  [stage(): kv[1].reshape(n, heads, HD)]
    unnamed x71 -> x126, local copies, waits for them, and re-layouts: 9.07 us -> 11 us
    slice x1, local copies, waits for them, and re-layouts: 1.29 us -> 2.77 us  [scores(): k = kv[0].reshape(n, heads, HD)]
  transfers between devices with their start and end apart: 7 -> 7, of which waited for: 7 -> 4; matrix products, arithmetic and copies ran while one was open for 29% -> 44% of each run, Pallas kernels for 0% -> 0%
where the time goes in v12:
time: 143 us; the launch traced here: 142 us
  matrix products  46.3 us (32%)
  waiting for transfers between devices  34 us (24%)
  local copies, waits for them, and re-layouts  31.1 us (22%)
  starting transfers between devices  15 us (10%)
  other arithmetic  14.2 us (10%)
    dot_general x16, matrix products, scores(): jnp.einsum('qhd,khd->hqk', q, k, preferred_element_type=jnp.float32) * scale  31.3 us
    ppermute x4, waiting for transfers between devices, rotate(): return lax.ppermute(x, axis, [(i, (i + by) % peers) for i in range(peers)])  21.6 us
    ppermute x3, waiting for transfers between devices, shift_up(): return lax.ppermute(x, axis, [(i, i + 1) for i in range(peers - 1)])  12.4 us
    unnamed x126, local copies, waits for them, and re-layouts  11 us
    dot_general x16, matrix products, stage(): jnp.einsum('hqk,khd->qhd', probs, kv[1].reshape(n, heads, HD), preferred_...  9.81 us
    slice x4, local copies, waits for them, and re-layouts, stage(): kv[1].reshape(n, heads, HD)  8.83 us
    ppermute x3, starting transfers between devices, shift_up(): return lax.ppermute(x, axis, [(i, i + 1) for i in range(peers - 1)])  8.24 us
    reduce_sum x8, other arithmetic, stage(): t = jnp.sum(weights, axis=2)  8.14 us
  transfers between devices with their start and end apart: 7, of which 4 were waited for; matrix products, arithmetic and copies ran while one was open for 44% of the time, Pallas kernels for 0%

profile of v12, /device:TPU:98, one launch (start us, length us, event | category | flops | bytes accessed | tf_op | source)
XLA Modules:
  0.0 141.6 jit_solution(14923142382277366577)
XLA Ops:
  2.0 2.8 %fusion.219 = (bf16[1,512,1024]{2,1,0:T(8,128)(2,1)S(1)}, bf16[1,512,1024]{2,1,0:T(8,128)(2,1)}) fusion(bf16[2,512,1024]{2,1,0:T(8,128)(2,1)} %param.5), kind=kLoop, calls=%fused_computation.318 | loop fusion | bytes 4194304 | tf_op jit(solution)/shard_map/slice | solution.py:50
  9.1 2.5 %fusion.5 = (f32[8,128]{1,0:T(8,128)}, f32[8,128,512]{2,1,0:T(8,128)}) fusion(pred[128,512]{1,0:T(8,128)(4,1)S(1)} %get-tuple-element.55, bf16[128,8,128]{0,2,1:T(8,128)(2,1)S(1)} %bitcast.295, bf16[512,8,128]{0,2,1:T(8,128)(2,1)S(1)} %bitcast.271), kind=kOutput, calls=%fused_computation.34 | convolution fusion | flops 135789568 | bytes 3477504 | tf_op jit(solution)/shard_map/qhd,khd->hqk/dot_general | solution.py:54
  11.6 2.5 %fusion.8 = (f32[8,128]{1,0:T(8,128)}, f32[8,128,512]{2,1,0:T(8,128)}) fusion(pred[128,512]{1,0:T(8,128)(4,1)S(1)} %get-tuple-element.56, bf16[128,8,128]{0,2,1:T(8,128)(2,1)S(1)} %bitcast.291, bf16[512,8,128]{0,2,1:T(8,128)(2,1)S(1)} %bitcast.272), kind=kOutput, calls=%fused_computation.37 | convolution fusion | flops 135789568 | bytes 3477504 | tf_op jit(solution)/shard_map/qhd,khd->hqk/dot_general | solution.py:54
  15.3 12.4 %collective-permute-done = bf16[2,512,1024]{2,1,0:T(8,128)(2,1)} collective-permute-done((bf16[2,512,1024]{2,1,0:T(8,128)(2,1)}, bf16[2,512,1024]{2,1,0:T(8,128)(2,1)}, u32[]{:S(2)}, u32[]{:S(2)}) %collective-permute-start) | collective-permute-done | bytes 2097184 | tf_op jit(solution)/shard_map/ppermute | solution.py:15
  27.7 1.9 %collective-permute-start.1 = (bf16[2,512,1024]{2,1,0:T(8,128)(2,1)}, bf16[2,512,1024]{2,1,0:T(8,128)(2,1)}, u32[]{:S(2)}, u32[]{:S(2)}) collective-permute-start(bf16[2,512,1024]{2,1,0:T(8,128)(2,1)} %collective-permute-done), channel_id=1, source_target_pairs={{0,4},{4,8},{8,12},{12,16},{16,20},{20,24},{24,28},{28,32},{32,36}... | collective-permute-start | bytes 6291464 | tf_op jit(solution)/shard_map/ppermute | solution.py:15
  30.1 2.3 %copy.45 = bf16[1,512,1024]{1,2,0:T(8,128)(2,1)} copy(bf16[1,512,1024]{2,1,0:T(8,128)(2,1)} %get-tuple-element.26) | data formatting | bytes 2097152 | tf_op jit(solution)/shard_map/slice | solution.py:68
  35.7 3.4 %fusion.11 = (f32[8,128]{1,0:T(8,128)}, f32[8,128,512]{2,1,0:T(8,128)}) fusion(pred[128,512]{1,0:T(8,128)(4,1)} %get-tuple-element.65, bf16[128,8,128]{0,2,1:T(8,128)(2,1)} %bitcast.299, bf16[512,8,128]{0,2,1:T(8,128)(2,1)S(1)} %bitcast.274), kind=kOutput, calls=%fused_computation.40 | convolution fusion | flops 135789568 | bytes 3477504 | tf_op jit(solution)/shard_map/qhd,khd->hqk/dot_general | solution.py:54
  39.1 2.7 %fusion.218 = (bf16[1,512,1024]{2,1,0:T(8,128)(2,1)}, bf16[64,8,8,128]{3,1,2,0:T(8,128)(2,1)S(1)}) fusion(bf16[2,512,1024]{2,1,0:T(8,128)(2,1)} %collective-permute-done), kind=kLoop, calls=%fused_computation.317 | loop fusion | bytes 4194304 | tf_op jit(solution)/shard_map/slice | solution.py:68
  42.1 2.3 %copy.112 = bf16[1,512,1024]{1,2,0:T(8,128)(2,1)} copy(bf16[1,512,1024]{2,1,0:T(8,128)(2,1)} %get-tuple-element.23) | data formatting | bytes 2097152 | tf_op jit(solution)/shard_map/reshape;squeeze | solution.py:68
  44.4 3.5 %fusion.4 = (f32[8,128]{1,0:T(8,128)}, f32[8,128,512]{2,1,0:T(8,128)}) fusion(pred[128,512]{1,0:T(8,128)(4,1)} %get-tuple-element.57, bf16[128,8,128]{0,2,1:T(8,128)(2,1)} %bitcast.296, bf16[512,8,128]{2,1,0:T(8,128)(2,1)S(1)} %bitcast.279), kind=kOutput, calls=%fused_computation.33 | convolution fusion | flops 135789568 | bytes 3477504 | tf_op jit(solution)/shard_map/qhd,khd->hqk/dot_general | solution.py:54
  48.0 2.5 %fusion.7 = (f32[8,128]{1,0:T(8,128)}, f32[8,128,512]{2,1,0:T(8,128)}) fusion(pred[128,512]{1,0:T(8,128)(4,1)S(1)} %copy-done.34, bf16[128,8,128]{0,2,1:T(8,128)(2,1)S(1)} %bitcast.292, bf16[512,8,128]{2,1,0:T(8,128)(2,1)S(1)} %bitcast.280), kind=kOutput, calls=%fused_computation.36 | convolution fusion | flops 135789568 | bytes 3477504 | tf_op jit(solution)/shard_map/qhd,khd->hqk/dot_general | solution.py:54
  50.5 2.5 %fusion.1 = (f32[8,128]{1,0:T(8,128)}, f32[8,128,512]{2,1,0:T(8,128)}) fusion(pred[128,512]{1,0:T(8,128)(4,1)S(1)} %get-tuple-element.60, bf16[128,8,128]{0,2,1:T(8,128)(2,1)S(1)} %bitcast.288, bf16[512,8,128]{2,1,0:T(8,128)(2,1)S(1)} %bitcast.281), kind=kOutput, calls=%fused_computation.30 | convolution fusion | flops 135789568 | bytes 3477504 | tf_op jit(solution)/shard_map/qhd,khd->hqk/dot_general | solution.py:54
  53.0 2.5 %fusion.10 = (f32[8,128]{1,0:T(8,128)}, f32[8,128,512]{2,1,0:T(8,128)}) fusion(pred[128,512]{1,0:T(8,128)(4,1)S(1)} %copy-done.29, bf16[128,8,128]{0,2,1:T(8,128)(2,1)S(1)} %bitcast.300, bf16[512,8,128]{2,1,0:T(8,128)(2,1)S(1)} %bitcast.282), kind=kOutput, calls=%fused_computation.39 | convolution fusion | flops 135789568 | bytes 3477504 | tf_op jit(solution)/shard_map/qhd,khd->hqk/dot_general | solution.py:54
  55.6 2.7 %fusion.217 = (bf16[1,512,1024]{2,1,0:T(8,128)(2,1)}, bf16[64,8,8,128]{3,1,2,0:T(8,128)(2,1)S(1)}) fusion(bf16[2,512,1024]{2,1,0:T(8,128)(2,1)} %collective-permute-done.1), kind=kLoop, calls=%fused_computation.316 | loop fusion | bytes 4194304 | tf_op jit(solution)/shard_map/slice | solution.py:68
  60.4 4.4 %collective-permute-start.2 = (bf16[2,128,1024]{2,1,0:T(8,128)(2,1)}, bf16[2,128,1024]{2,1,0:T(8,128)(2,1)}, u32[]{:S(2)}, u32[]{:S(2)}) collective-permute-start(bf16[2,128,1024]{2,1,0:T(8,128)(2,1)} %slice.85), channel_id=1, source_target_pairs={{0,4},{4,8},{8,12},{12,16},{16,20},{20,24},{24,28},{28,32},{32,36}... | collective-permute-start | bytes 1572872 | tf_op jit(solution)/shard_map/ppermute | solution.py:15
  64.9 2.3 %copy.114 = bf16[1,512,1024]{1,2,0:T(8,128)(2,1)} copy(bf16[1,512,1024]{2,1,0:T(8,128)(2,1)} %get-tuple-element.21) | data formatting | bytes 2097152 | tf_op jit(solution)/shard_map/reshape;squeeze | solution.py:68
  67.2 2.9 %fusion.6 = (f32[8,128]{1,0:T(8,128)S(1)}, f32[8,128,512]{2,1,0:T(8,128)}) fusion(pred[128,512]{1,0:T(8,128)(4,1)} %get-tuple-element.64, bf16[128,8,128]{0,2,1:T(8,128)(2,1)} %bitcast.297, bf16[512,8,128]{2,1,0:T(8,128)(2,1)S(1)} %bitcast.275), kind=kOutput, calls=%fused_computation.35 | convolution fusion | flops 135789568 | bytes 3477504 | tf_op jit(solution)/shard_map/qhd,khd->hqk/dot_general | solution.py:54
  70.1 1.9 %fusion.9 = (f32[8,128]{1,0:T(8,128)S(1)}, f32[8,128,512]{2,1,0:T(8,128)}) fusion(pred[128,512]{1,0:T(8,128)(4,1)S(1)} %copy-done.32, bf16[128,8,128]{0,2,1:T(8,128)(2,1)S(1)} %bitcast.293, bf16[512,8,128]{2,1,0:T(8,128)(2,1)S(1)} %bitcast.276), kind=kOutput, calls=%fused_computation.38 | convolution fusion | flops 135789568 | bytes 3477504 | tf_op jit(solution)/shard_map/qhd,khd->hqk/dot_general | solution.py:54
  72.0 2.0 %fusion.3 = (f32[8,128]{1,0:T(8,128)S(1)}, f32[8,128,512]{2,1,0:T(8,128)}) fusion(pred[128,512]{1,0:T(8,128)(4,1)S(1)} %get-tuple-element.61, bf16[128,8,128]{0,2,1:T(8,128)(2,1)S(1)} %bitcast.289, bf16[512,8,128]{2,1,0:T(8,128)(2,1)S(1)} %bitcast.277), kind=kOutput, calls=%fused_computation.32 | convolution fusion | flops 135789568 | bytes 3477504 | tf_op jit(solution)/shard_map/qhd,khd->hqk/dot_general | solution.py:54
  74.0 1.9 %fusion.12 = (f32[8,128]{1,0:T(8,128)S(1)}, f32[8,128,512]{2,1,0:T(8,128)}) fusion(pred[128,512]{1,0:T(8,128)(4,1)S(1)} %copy-done.27, bf16[128,8,128]{0,2,1:T(8,128)(2,1)S(1)} %bitcast.301, bf16[512,8,128]{2,1,0:T(8,128)(2,1)S(1)} %bitcast.278), kind=kOutput, calls=%fused_computation.41 | convolution fusion | flops 135789568 | bytes 3477504 | tf_op jit(solution)/shard_map/qhd,khd->hqk/dot_general | solution.py:54
  91.7 2.1 %fusion.27 = (f32[8,128]{1,0:T(8,128)S(1)}, f32[8,128]{1,0:T(8,128)S(1)}, f32[8,128]{1,0:T(8,128)S(1)}) fusion(f32[8,128,512]{2,1,0:T(8,128)S(1)} %copy-done.4, f32[8,128]{1,0:T(8,128)S(1)} %get-tuple-element.18, pred[128,512]{1,0:T(8,128)(4,1)S(1)} %copy-done.37, f32[8,128,512]{2,1,0:T(8,128)S(1)} %copy-done.7, pred[128,512]{1,0:T(8,128)(4,1)S(1)} %copy-done.35, ...), kind=kLoop, calls=%fused_computation.56 | loop fusion | flops 6288384 | bytes 6508544 | tf_op jit(solution)/shard_map/reduce_sum | solution.py:66
  99.5 2.0 %collective-permute-start.5 = (bf16[128,2048]{1,0:T(8,128)(2,1)S(1)}, bf16[128,2048]{1,0:T(8,128)(2,1)S(1)}, u32[]{:S(2)}, u32[]{:S(2)}) collective-permute-start(bf16[128,2048]{1,0:T(8,128)(2,1)S(1)} %get-tuple-element.32), channel_id=1, source_target_pairs={{0,3},{1,0},{2,1},{3,2},{4,7},{5,4},{6,5},{7,6},{8,11},{9,8},{10,9... | collective-permute-start | bytes 1572872 | tf_op jit(solution)/shard_map/ppermute | solution.py:20
  114.0 2.9 %collective-permute-start.6 = (bf16[128,4096]{1,0:T(8,128)(2,1)S(1)}, bf16[128,4096]{1,0:T(8,128)(2,1)S(1)}, u32[]{:S(2)}, u32[]{:S(2)}) collective-permute-start(bf16[128,4096]{1,0:T(8,128)(2,1)S(1)} %pad_maximum_fusion.1), channel_id=1, source_target_pairs={{0,3},{1,0},{2,1},{3,2},{4,7},{5,4},{6,5},{7,6},{8,11},{9,8},{10,9... | collective-permute-start | bytes 3145736 | tf_op jit(solution)/shard_map/ppermute | solution.py:20
  119.0 20.9 %collective-permute-done.4 = bf16[128,4096]{1,0:T(8,128)(2,1)S(1)} collective-permute-done((bf16[128,4096]{1,0:T(8,128)(2,1)S(1)}, bf16[128,4096]{1,0:T(8,128)(2,1)S(1)}, u32[]{:S(2)}, u32[]{:S(2)}) %collective-permute-start.4) | collective-permute-done | bytes 1048608 | tf_op jit(solution)/shard_map/ppermute | solution.py:20
  (202 shorter events, 50.6 us)
Async XLA Ops:
  0.0 27.7 %collective-permute-start = (bf16[2,512,1024]{2,1,0:T(8,128)(2,1)}, bf16[2,512,1024]{2,1,0:T(8,128)(2,1)}, u32[]{:S(2)}, u32[]{:S(2)}) collective-permute-start(bf16[2,512,1024]{2,1,0:T(8,128)(2,1)} %param.5), channel_id=1, source_target_pairs={{0,4},{4,8},{8,12},{12,16},{16,20},{20,24},{24,28},{28,32},{32,36}... | collective-permute-start | bytes 6291464 | tf_op jit(solution)/shard_map/ppermute | solution.py:15
  5.9 5.7 %copy-start.15 = (bf16[128,1024]{0,1:T(8,128)(2,1)}, bf16[128,1024]{0,1:T(8,128)(2,1)S(1)}, u32[]{:S(2)}) copy-start(bf16[128,1024]{0,1:T(8,128)(2,1)S(1)} %copy.117) | copy-start | bytes 786436
  6.6 5.0 %copy-start.11 = (bf16[128,1024]{0,1:T(8,128)(2,1)}, bf16[128,1024]{0,1:T(8,128)(2,1)S(1)}, u32[]{:S(2)}) copy-start(bf16[128,1024]{0,1:T(8,128)(2,1)S(1)} %copy.118) | copy-start | bytes 786436
  6.8 4.7 %copy-start.53 = (s32[128]{0:T(128)}, s32[128]{0:T(128)S(1)}, u32[]{:S(2)}) copy-start(s32[128]{0:T(128)S(1)} %iota_add_fusion.2) | copy-start | bytes 1540
  6.9 4.7 %copy-start.54 = (s32[128]{0:T(128)}, s32[128]{0:T(128)S(1)}, u32[]{:S(2)}) copy-start(s32[128]{0:T(128)S(1)} %iota_add_fusion.3) | copy-start | bytes 1540
  6.9 4.7 %copy-start.55 = (s32[128]{0:T(128)}, s32[128]{0:T(128)S(1)}, u32[]{:S(2)}) copy-start(s32[128]{0:T(128)S(1)} %iota_add_fusion.4) | copy-start | bytes 1540
  6.9 4.6 %copy-start.56 = (s32[128]{0:T(128)}, s32[128]{0:T(128)S(1)}, u32[]{:S(2)}) copy-start(s32[128]{0:T(128)S(1)} %iota_add_fusion.6) | copy-start | bytes 1540
  9.1 5.0 %copy-start.36 = (pred[128,512]{1,0:T(8,128)(4,1)}, pred[128,512]{1,0:T(8,128)(4,1)S(1)}, u32[]{:S(2)}) copy-start(pred[128,512]{1,0:T(8,128)(4,1)S(1)} %get-tuple-element.56) | copy-start | bytes 196612
  9.1 5.0 %copy-start.40 = (pred[128,512]{1,0:T(8,128)(4,1)}, pred[128,512]{1,0:T(8,128)(4,1)S(1)}, u32[]{:S(2)}) copy-start(pred[128,512]{1,0:T(8,128)(4,1)S(1)} %get-tuple-element.55) | copy-start | bytes 196612
  9.1 5.0 %copy-start.25 = (pred[128,512]{1,0:T(8,128)(4,1)}, pred[128,512]{1,0:T(8,128)(4,1)S(1)}, u32[]{:S(2)}) copy-start(pred[128,512]{1,0:T(8,128)(4,1)S(1)} %get-tuple-element.66) | copy-start | bytes 196612
  27.7 27.9 %collective-permute-start.1 = (bf16[2,512,1024]{2,1,0:T(8,128)(2,1)}, bf16[2,512,1024]{2,1,0:T(8,128)(2,1)}, u32[]{:S(2)}, u32[]{:S(2)}) collective-permute-start(bf16[2,512,1024]{2,1,0:T(8,128)(2,1)} %collective-permute-done), channel_id=1, source_target_pairs={{0,4},{4,8},{8,12},{12,16},{16,20},{20,24},{24,28},{28,32},{32,36}... | collective-permute-start | bytes 6291464 | tf_op jit(solution)/shard_map/ppermute | solution.py:15
  44.4 3.6 %copy-start.12 = (bf16[128,1024]{0,1:T(8,128)(2,1)S(1)}, bf16[128,1024]{0,1:T(8,128)(2,1)}, u32[]{:S(2)}) copy-start(bf16[128,1024]{0,1:T(8,128)(2,1)} %copy-done.11) | copy-start | bytes 786436
  44.4 3.6 %copy-start.34 = (pred[128,512]{1,0:T(8,128)(4,1)S(1)}, pred[128,512]{1,0:T(8,128)(4,1)}, u32[]{:S(2)}) copy-start(pred[128,512]{1,0:T(8,128)(4,1)} %get-tuple-element.58) | copy-start | bytes 196612
  60.4 15.5 %collective-permute-start.2 = (bf16[2,128,1024]{2,1,0:T(8,128)(2,1)}, bf16[2,128,1024]{2,1,0:T(8,128)(2,1)}, u32[]{:S(2)}, u32[]{:S(2)}) collective-permute-start(bf16[2,128,1024]{2,1,0:T(8,128)(2,1)} %slice.85), channel_id=1, source_target_pairs={{0,4},{4,8},{8,12},{12,16},{16,20},{20,24},{24,28},{28,32},{32,36}... | collective-permute-start | bytes 1572872 | tf_op jit(solution)/shard_map/ppermute | solution.py:15
  67.2 2.9 %copy-start.13 = (bf16[128,1024]{0,1:T(8,128)(2,1)S(1)}, bf16[128,1024]{0,1:T(8,128)(2,1)}, u32[]{:S(2)}) copy-start(bf16[128,1024]{0,1:T(8,128)(2,1)} %copy-done.11) | copy-start | bytes 786436
  67.2 2.9 %copy-start.32 = (pred[128,512]{1,0:T(8,128)(4,1)S(1)}, pred[128,512]{1,0:T(8,128)(4,1)}, u32[]{:S(2)}) copy-start(pred[128,512]{1,0:T(8,128)(4,1)} %get-tuple-element.63) | copy-start | bytes 196612
  77.0 3.3 %copy-start.14 = (bf16[128,1024]{0,1:T(8,128)(2,1)S(1)}, bf16[128,1024]{0,1:T(8,128)(2,1)}, u32[]{:S(2)}) copy-start(bf16[128,1024]{0,1:T(8,128)(2,1)} %copy-done.11) | copy-start | bytes 786436
  85.2 3.5 %slice-start = ((s8[8388608]{0:T(1024)(128)(4,1)}), s8[4194304]{0:T(1024)(128)(4,1)S(1)}, s32[]{:S(2)}) async-start(s8[8388608]{0:T(1024)(128)(4,1)} %bitcast.269), calls=%async_computation | async-start | bytes 8388608
  96.8 16.2 %collective-permute-start.3 = (bf16[128,2048]{1,0:T(8,128)(2,1)S(1)}, bf16[128,2048]{1,0:T(8,128)(2,1)S(1)}, u32[]{:S(2)}, u32[]{:S(2)}) collective-permute-start(bf16[128,2048]{1,0:T(8,128)(2,1)S(1)} %get-tuple-element.31), channel_id=1, source_target_pairs={{0,1},{1,2},{2,3},{3,0},{4,5},{5,6},{6,7},{7,4},{8,9},{9,10},{10,1... | collective-permute-start | bytes 1572872 | tf_op jit(solution)/shard_map/ppermute | solution.py:20
  98.7 3.6 %copy-start.28 = (pred[128,512]{1,0:T(8,128)(4,1)S(1)}, pred[128,512]{1,0:T(8,128)(4,1)}, u32[]{:S(2)}) copy-start(pred[128,512]{1,0:T(8,128)(4,1)} %get-tuple-element.62) | copy-start | bytes 196612
  98.7 3.6 %copy-start.30 = (pred[128,512]{1,0:T(8,128)(4,1)S(1)}, pred[128,512]{1,0:T(8,128)(4,1)}, u32[]{:S(2)}) copy-start(pred[128,512]{1,0:T(8,128)(4,1)} %get-tuple-element.59) | copy-start | bytes 196612
  99.5 14.3 %collective-permute-start.5 = (bf16[128,2048]{1,0:T(8,128)(2,1)S(1)}, bf16[128,2048]{1,0:T(8,128)(2,1)S(1)}, u32[]{:S(2)}, u32[]{:S(2)}) collective-permute-start(bf16[128,2048]{1,0:T(8,128)(2,1)S(1)} %get-tuple-element.32), channel_id=1, source_target_pairs={{0,3},{1,0},{2,1},{3,2},{4,7},{5,4},{6,5},{7,6},{8,11},{9,8},{10,9... | collective-permute-start | bytes 1572872 | tf_op jit(solution)/shard_map/ppermute | solution.py:20
  113.2 26.7 %collective-permute-start.4 = (bf16[128,4096]{1,0:T(8,128)(2,1)S(1)}, bf16[128,4096]{1,0:T(8,128)(2,1)S(1)}, u32[]{:S(2)}, u32[]{:S(2)}) collective-permute-start(bf16[128,4096]{1,0:T(8,128)(2,1)S(1)} %pad_maximum_fusion), channel_id=1, source_target_pairs={{0,1},{1,2},{2,3},{3,0},{4,5},{5,6},{6,7},{7,4},{8,9},{9,10},{10,1... | collective-permute-start | bytes 3145736 | tf_op jit(solution)/shard_map/ppermute | solution.py:20
  114.0 26.2 %collective-permute-start.6 = (bf16[128,4096]{1,0:T(8,128)(2,1)S(1)}, bf16[128,4096]{1,0:T(8,128)(2,1)S(1)}, u32[]{:S(2)}, u32[]{:S(2)}) collective-permute-start(bf16[128,4096]{1,0:T(8,128)(2,1)S(1)} %pad_maximum_fusion.1), channel_id=1, source_target_pairs={{0,3},{1,0},{2,1},{3,2},{4,7},{5,4},{6,5},{7,6},{8,11},{9,8},{10,9... | collective-permute-start | bytes 3145736 | tf_op jit(solution)/shard_map/ppermute | solution.py:20
  (42 other events, 81.7 us)

commit v13 on v7

--- a/solution.py
+++ b/solution.py
@@ -29,7 +29,10 @@
     tail = DOC_MOST - 2 * rows
     r1 = shift_up(keys_values, "ctx")
     r2 = shift_up(r1, "ctx")
-    r3 = shift_up(r2[:, rows - tail:], "ctx")
+    peers = lax.axis_size("ctx")
+    tail_even = lax.ppermute(r1[:, rows - tail:], "ctx", [(i, i + 2) for i in range(0, peers - 2, 2)])
+    tail_odd = lax.ppermute(r2[:, rows - tail:], "ctx", [(i, i + 1) for i in range(0, peers - 1, 2)])
+    r3 = jnp.where(me % 2 == 0, tail_even, tail_odd)
     sources = [r3, r2, r1, keys_values]
     offsets = [-DOC_MOST, -2 * rows, -rows, 0]
     padded_docs = jnp.concatenate([jnp.full((DOC_MOST,), -1, jnp.int32), doc_index])

time: 132 us -> 131 us (level)
  waiting for transfers between devices: 57.1 us -> 48.9 us
  starting transfers between devices: 12.9 us -> 17.5 us
  local copies, waits for them, and re-layouts: 20 us -> 22.2 us
    ppermute x0 -> x2, starting transfers between devices: none -> 6.39 us  [the longest x1 4.27 us: per_device(): lax.ppermute(r1[:, rows - tail:], 'ctx', [(i, i + 2) for i in range(0, pe...]
    ppermute x3 -> x2, waiting for transfers between devices: 32.8 us -> 28.1 us  [shift_up(): return lax.ppermute(x, axis, [(i, i + 1) for i in range(peers - 1)])]
    ppermute x4, waiting for transfers between devices: 24.2 us -> 20.8 us  [rotate(): return lax.ppermute(x, axis, [(i, (i + by) % peers) for i in range(peers)])]
    ppermute x3 -> x2, starting transfers between devices: 6.18 us -> 3.95 us  [shift_up(): return lax.ppermute(x, axis, [(i, i + 1) for i in range(peers - 1)])]
    unnamed x71 -> x69, local copies, waits for them, and re-layouts: 9.07 us -> 9.03 us
  transfers between devices with their start and end apart: 7 -> 8, of which waited for: 7 -> 6; matrix products, arithmetic and copies ran while one was open for 29% -> 32% of each run, Pallas kernels for 0% -> 0%
where the time goes in v13:
time: 131 us; the launch traced here: 130 us
  waiting for transfers between devices  48.9 us (37%)
  matrix products  27.1 us (21%)
  local copies, waits for them, and re-layouts  22.2 us (17%)
  starting transfers between devices  17.5 us (13%)
  other arithmetic  13.1 us (10%)
    ppermute x2, waiting for transfers between devices, shift_up(): return lax.ppermute(x, axis, [(i, i + 1) for i in range(peers - 1)])  28.1 us
    ppermute x4, waiting for transfers between devices, rotate(): return lax.ppermute(x, axis, [(i, (i + by) % peers) for i in range(peers)])  20.8 us
    dot_general x16, matrix products, scores(): jnp.einsum('qhd,khd->hqk', q, k, preferred_element_type=jnp.float32) * scale  12.2 us
    dot_general x16, matrix products, stage(): jnp.einsum('hqk,khd->qhd', probs, kv[1].reshape(n, heads, HD), preferred_...  9.78 us
    unnamed x69, local copies, waits for them, and re-layouts  9.03 us
    reduce_sum x8, other arithmetic, stage(): t = jnp.sum(weights, axis=2)  8.44 us
    slice x5, local copies, waits for them, and re-layouts, stage(): kv[1].reshape(n, heads, HD)  8 us
    ppermute x4, starting transfers between devices, rotate(): return lax.ppermute(x, axis, [(i, (i + by) % peers) for i in range(peers)])  7.13 us
  transfers between devices with their start and end apart: 8, of which 6 were waited for; matrix products, arithmetic and copies ran while one was open for 32% of the time, Pallas kernels for 0%

profile of v13, /device:TPU:98, one launch (start us, length us, event | category | flops | bytes accessed | tf_op | source)
XLA Modules:
  0.0 129.7 jit_solution(7942524401471691004)
XLA Ops:
  0.0 3.9 %copy.14 = bf16[2,512,1024]{1,2,0:T(8,128)(2,1)} copy(bf16[2,512,1024]{2,1,0:T(8,128)(2,1)} %param.5) | data formatting | bytes 4194304 | tf_op args[1]
  4.0 2.0 %collective-permute-start = (bf16[2,512,1024]{1,2,0:T(8,128)(2,1)}, bf16[2,512,1024]{1,2,0:T(8,128)(2,1)}, u32[]{:S(2)}, u32[]{:S(2)}) collective-permute-start(bf16[2,512,1024]{1,2,0:T(8,128)(2,1)} %copy.14), channel_id=1, source_target_pairs={{0,4},{4,8},{8,12},{12,16},{16,20},{20,24},{24,28},{28,32},{32,36}... | collective-permute-start | bytes 6291464 | tf_op jit(solution)/shard_map/ppermute | solution.py:14
  9.6 1.4 %fusion.146 = (pred[128,512]{1,0:T(8,128)(4,1)S(1)}, pred[128,512]{1,0:T(8,128)(4,1)S(1)}, pred[128,512]{1,0:T(8,128)(4,1)}, pred[128,512]{1,0:T(8,128)(4,1)}, p...) fusion(s32[512]{0:T(512)S(1)} %get-tuple-element.39, ...), kind=kLoop, calls=%fused_computation.188 | loop fusion | flops 2359296 | bytes 800768 | tf_op jit(solution)/shard_map/and | solution.py:51
  11.0 1.9 %fusion.5 = (f32[8,128]{1,0:T(8,128)S(1)}, f32[8,128,512]{2,1,0:T(8,128)}) fusion(pred[128,512]{1,0:T(8,128)(4,1)S(1)} %get-tuple-element.53, bf16[128,8,128]{0,2,1:T(8,128)(2,1)S(1)} %bitcast.314, bf16[512,8,128]{0,2,1:T(8,128)(2,1)S(1)} %bitcast.290), kind=kOutput, calls=%fused_computation.34 | convolution fusion | flops 135789568 | bytes 3477504 | tf_op jit(solution)/shard_map/qhd,khd->hqk/dot_general | solution.py:52
  13.0 1.8 %fusion.8 = (f32[8,128]{1,0:T(8,128)S(1)}, f32[8,128,512]{2,1,0:T(8,128)}) fusion(pred[128,512]{1,0:T(8,128)(4,1)S(1)} %get-tuple-element.54, bf16[128,8,128]{0,2,1:T(8,128)(2,1)S(1)} %bitcast.318, bf16[512,8,128]{0,2,1:T(8,128)(2,1)S(1)} %bitcast.291), kind=kOutput, calls=%fused_computation.37 | convolution fusion | flops 135789568 | bytes 3477504 | tf_op jit(solution)/shard_map/qhd,khd->hqk/dot_general | solution.py:52
  15.4 16.3 %collective-permute-done = bf16[2,512,1024]{1,2,0:T(8,128)(2,1)} collective-permute-done((bf16[2,512,1024]{1,2,0:T(8,128)(2,1)}, bf16[2,512,1024]{1,2,0:T(8,128)(2,1)}, u32[]{:S(2)}, u32[]{:S(2)}) %collective-permute-start) | collective-permute-done | bytes 2097184 | tf_op jit(solution)/shard_map/ppermute | solution.py:14
  31.7 1.9 %collective-permute-start.2 = (bf16[2,512,1024]{1,2,0:T(8,128)(2,1)}, bf16[2,512,1024]{1,2,0:T(8,128)(2,1)}, u32[]{:S(2)}, u32[]{:S(2)}) collective-permute-start(bf16[2,512,1024]{1,2,0:T(8,128)(2,1)} %collective-permute-done), channel_id=1, source_target_pairs={{0,4},{4,8},{8,12},{12,16},{16,20},{20,24},{24,28},{28,32},{32,36}... | collective-permute-start | bytes 6291464 | tf_op jit(solution)/shard_map/ppermute | solution.py:14
  34.1 2.3 %slice.39 = bf16[1,512,1024]{2,1,0:T(8,128)(2,1)} slice(bf16[2,512,1024]{2,1,0:T(8,128)(2,1)} %param.5), slice={[1:2], [0:512], [0:1024]} | slice | bytes 2097152 | tf_op jit(solution)/shard_map/slice | solution.py:66
  36.4 2.4 %copy.24 = bf16[1,512,1024]{1,2,0:T(8,128)(2,1)} copy(bf16[1,512,1024]{2,1,0:T(8,128)(2,1)} %slice.39) | data formatting | bytes 2097152 | tf_op jit(solution)/shard_map/slice | solution.py:66
  38.8 1.8 %copy.95 = bf16[128,1024]{0,1:T(8,128)(2,1)} copy(bf16[128,1024]{1,0:T(8,128)(2,1)} %get-tuple-element.28) | data formatting | bytes 524288
  41.4 1.6 %fusion.11 = (f32[8,128]{1,0:T(8,128)S(1)}, f32[8,128,512]{2,1,0:T(8,128)S(1)}) fusion(pred[128,512]{1,0:T(8,128)(4,1)} %get-tuple-element.63, bf16[128,8,128]{0,2,1:T(8,128)(2,1)} %bitcast.322, bf16[512,8,128]{0,2,1:T(8,128)(2,1)S(1)} %bitcast.293), kind=kOutput, calls=%fused_computation.40 | convolution fusion | flops 135789568 | bytes 3477504 | tf_op jit(solution)/shard_map/qhd,khd->hqk/dot_general | solution.py:52
  44.1 4.3 %collective-permute-start.1 = (bf16[2,128,1024]{1,2,0:T(8,128)(2,1)S(1)}, bf16[2,128,1024]{1,2,0:T(8,128)(2,1)S(1)}, u32[]{:S(2)}, u32[]{:S(2)}) collective-permute-start(bf16[2,128,1024]{1,2,0:T(8,128)(2,1)S(1)} %slice.90), channel_id=1, source_target_pairs={{0,8},{8,16},{16,24},{24,32},{32,40},{40,48},{48,56},{56,64},{64,7... | collective-permute-start | bytes 1572872 | tf_op jit(solution)/shard_map/ppermute | solution.py:33
  48.3 1.7 %fusion.194 = (bf16[1,512,1024]{1,2,0:T(8,128)(2,1)S(1)}, bf16[1,512,1024]{1,2,0:T(8,128)(2,1)S(1)}) fusion(bf16[2,512,1024]{1,2,0:T(8,128)(2,1)} %collective-permute-done), kind=kLoop, calls=%fused_computation.295 | loop fusion | bytes 4194304 | tf_op jit(solution)/shard_map/slice | solution.py:66
  53.2 11.8 %collective-permute-done.2 = bf16[2,512,1024]{1,2,0:T(8,128)(2,1)} collective-permute-done((bf16[2,512,1024]{1,2,0:T(8,128)(2,1)}, bf16[2,512,1024]{1,2,0:T(8,128)(2,1)}, u32[]{:S(2)}, u32[]{:S(2)}) %collective-permute-start.2) | collective-permute-done | bytes 2097184 | tf_op jit(solution)/shard_map/ppermute | solution.py:14
  66.1 2.1 %collective-permute-start.3 = (bf16[2,128,1024]{1,2,0:T(8,128)(2,1)S(1)}, bf16[2,128,1024]{1,2,0:T(8,128)(2,1)S(1)}, u32[]{:S(2)}, u32[]{:S(2)}) collective-permute-start(bf16[2,128,1024]{1,2,0:T(8,128)(2,1)S(1)} %slice.91), channel_id=1, source_target_pairs={{0,4},{8,12},{16,20},{24,28},{32,36},{40,44},{48,52},{56,60},{64,6... | collective-permute-start | bytes 1572872 | tf_op jit(solution)/shard_map/ppermute | solution.py:34
  68.2 1.7 %fusion.193 = (bf16[1,512,1024]{1,2,0:T(8,128)(2,1)S(1)}, bf16[1,512,1024]{1,2,0:T(8,128)(2,1)S(1)}) fusion(bf16[2,512,1024]{1,2,0:T(8,128)(2,1)} %collective-permute-done.2), kind=kLoop, calls=%fused_computation.294 | loop fusion | bytes 4194304 | tf_op jit(solution)/shard_map/slice | solution.py:66
  77.6 2.1 %fusion.21 = (f32[8,128]{1,0:T(8,128)S(1)}, f32[8,128]{1,0:T(8,128)S(1)}, f32[8,128]{1,0:T(8,128)S(1)}) fusion(f32[8,128,512]{2,1,0:T(8,128)S(1)} %copy-done.1, f32[8,128]{1,0:T(8,128)S(1)} %get-tuple-element.14, pred[128,512]{1,0:T(8,128)(4,1)S(1)} %copy-done.21, f32[8,128,512]{2,1,0:T(8,128)S(1)} %get-tuple-element.100, ...), kind=kLoop, calls=%fused_computation.50 | loop fusion | flops 6288384 | bytes 6508544 | tf_op jit(solution)/shard_map/reduce_sum | solution.py:64
  83.3 1.9 %fusion.27 = (f32[8,128]{1,0:T(8,128)S(1)}, f32[8,128]{1,0:T(8,128)S(1)}, f32[8,128]{1,0:T(8,128)S(1)}) fusion(f32[8,128,512]{2,1,0:T(8,128)S(1)} %copy-done, f32[8,128]{1,0:T(8,128)S(1)} %get-tuple-element.18, pred[128,512]{1,0:T(8,128)(4,1)S(1)} %copy-done.17, f32[8,128,512]{2,1,0:T(8,128)S(1)} %get-tuple-element.76, pred[128,512]{1,0:T(8,128)(4,1)S(1)} %copy-done.15, ...), kind=kLoop, calls=%fused_computation.56 | loop fusion | flops 6288384 | bytes 6508544 | tf_op jit(solution)/shard_map/reduce_sum | solution.py:64
  88.1 1.6 %collective-permute-start.4 = (bf16[128,2048]{1,0:T(8,128)(2,1)S(1)}, bf16[128,2048]{1,0:T(8,128)(2,1)S(1)}, u32[]{:S(2)}, u32[]{:S(2)}) collective-permute-start(bf16[128,2048]{1,0:T(8,128)(2,1)S(1)} %get-tuple-element.29), channel_id=1, source_target_pairs={{0,1},{1,2},{2,3},{3,0},{4,5},{5,6},{6,7},{7,4},{8,9},{9,10},{10,1... | collective-permute-start | bytes 1572872 | tf_op jit(solution)/shard_map/ppermute | solution.py:19
  90.8 1.8 %collective-permute-start.6 = (bf16[128,2048]{1,0:T(8,128)(2,1)S(1)}, bf16[128,2048]{1,0:T(8,128)(2,1)S(1)}, u32[]{:S(2)}, u32[]{:S(2)}) collective-permute-start(bf16[128,2048]{1,0:T(8,128)(2,1)S(1)} %get-tuple-element.30), channel_id=1, source_target_pairs={{0,3},{1,0},{2,1},{3,2},{4,7},{5,4},{6,5},{7,6},{8,11},{9,8},{10,9... | collective-permute-start | bytes 1572872 | tf_op jit(solution)/shard_map/ppermute | solution.py:19
  93.4 2.2 %fusion.33 = (f32[8,128]{1,0:T(8,128)S(1)}, f32[8,128]{1,0:T(8,128)S(1)}, f32[8,128]{1,0:T(8,128)S(1)}) fusion(f32[8,128,512]{2,1,0:T(8,128)S(1)} %get-tuple-element.82, f32[8,128]{1,0:T(8,128)S(1)} %get-tuple-element.20, pred[128,512]{1,0:T(8,128)(4,1)S(1)} %copy-done.13, f32[8,128,512]{2,1,0:T(8,128)S(1)} %get-tuple-element.84, ...), kind=kLoop, calls=%fused_computation.62 | loop fusion | flops 6288384 | bytes 6508544 | tf_op jit(solution)/shard_map/reduce_sum | solution.py:64
  99.5 1.9 %fusion.15 = (f32[8,128]{1,0:T(8,128)S(1)}, f32[8,128]{1,0:T(8,128)S(1)}, f32[8,128]{1,0:T(8,128)S(1)}) fusion(f32[8,128,512]{2,1,0:T(8,128)S(1)} %get-tuple-element.90, f32[8,128]{1,0:T(8,128)S(1)} %get-tuple-element.16, pred[128,512]{1,0:T(8,128)(4,1)S(1)} %copy-done.10, f32[8,128,512]{2,1,0:T(8,128)S(1)} %get-tuple-element.92, ...), kind=kLoop, calls=%fused_computation.44 | loop fusion | flops 6288384 | bytes 6508544 | tf_op jit(solution)/shard_map/reduce_sum | solution.py:64
  104.0 3.3 %collective-permute-start.7 = (bf16[128,4096]{1,0:T(8,128)(2,1)S(1)}, bf16[128,4096]{1,0:T(8,128)(2,1)S(1)}, u32[]{:S(2)}, u32[]{:S(2)}) collective-permute-start(bf16[128,4096]{1,0:T(8,128)(2,1)S(1)} %pad_maximum_fusion.1), channel_id=1, source_target_pairs={{0,3},{1,0},{2,1},{3,2},{4,7},{5,4},{6,5},{7,6},{8,11},{9,8},{10,9... | collective-permute-start | bytes 3145736 | tf_op jit(solution)/shard_map/ppermute | solution.py:19
  109.4 18.3 %collective-permute-done.5 = bf16[128,4096]{1,0:T(8,128)(2,1)S(1)} collective-permute-done((bf16[128,4096]{1,0:T(8,128)(2,1)S(1)}, bf16[128,4096]{1,0:T(8,128)(2,1)S(1)}, u32[]{:S(2)}, u32[]{:S(2)}) %collective-permute-start.5) | collective-permute-done | bytes 1048608 | tf_op jit(solution)/shard_map/ppermute | solution.py:19
  (147 shorter events, 36.8 us)
Async XLA Ops:
  4.0 3.4 %copy-start.7 = (bf16[512,1024]{1,0:T(8,128)(2,1)S(1)}, bf16[512,1024]{1,0:T(8,128)(2,1)}, u32[]{:S(2)}) copy-start(bf16[512,1024]{1,0:T(8,128)(2,1)} %param.4) | copy-start | bytes 3145732
  4.0 27.8 %collective-permute-start = (bf16[2,512,1024]{1,2,0:T(8,128)(2,1)}, bf16[2,512,1024]{1,2,0:T(8,128)(2,1)}, u32[]{:S(2)}, u32[]{:S(2)}) collective-permute-start(bf16[2,512,1024]{1,2,0:T(8,128)(2,1)} %copy.14), channel_id=1, source_target_pairs={{0,4},{4,8},{8,12},{12,16},{16,20},{20,24},{24,28},{28,32},{32,36}... | collective-permute-start | bytes 6291464 | tf_op jit(solution)/shard_map/ppermute | solution.py:14
  8.4 4.5 %copy-start.2 = (bf16[128,1024]{0,1:T(8,128)(2,1)}, bf16[128,1024]{0,1:T(8,128)(2,1)S(1)}, u32[]{:S(2)}) copy-start(bf16[128,1024]{0,1:T(8,128)(2,1)S(1)} %copy.93) | copy-start | bytes 786436
  8.6 4.4 %copy-start.4 = (bf16[128,1024]{0,1:T(8,128)(2,1)}, bf16[128,1024]{0,1:T(8,128)(2,1)S(1)}, u32[]{:S(2)}) copy-start(bf16[128,1024]{0,1:T(8,128)(2,1)S(1)} %copy.94) | copy-start | bytes 786436
  8.8 4.1 %copy-start.26 = (s32[128]{0:T(128)}, s32[128]{0:T(128)S(1)}, u32[]{:S(2)}) copy-start(s32[128]{0:T(128)S(1)} %iota_add_fusion.2) | copy-start | bytes 1540
  8.8 4.1 %copy-start.27 = (s32[128]{0:T(128)}, s32[128]{0:T(128)S(1)}, u32[]{:S(2)}) copy-start(s32[128]{0:T(128)S(1)} %iota_add_fusion.3) | copy-start | bytes 1540
  8.8 4.1 %copy-start.28 = (s32[128]{0:T(128)}, s32[128]{0:T(128)S(1)}, u32[]{:S(2)}) copy-start(s32[128]{0:T(128)S(1)} %iota_add_fusion.4) | copy-start | bytes 1540
  8.8 4.1 %copy-start.29 = (s32[128]{0:T(128)}, s32[128]{0:T(128)S(1)}, u32[]{:S(2)}) copy-start(s32[128]{0:T(128)S(1)} %iota_add_fusion.6) | copy-start | bytes 1540
  9.5 3.4 %copy-start.23 = (s32[128]{0:T(128)}, s32[128]{0:T(128)S(1)}, u32[]{:S(2)}) copy-start(s32[128]{0:T(128)S(1)} %get-tuple-element.35) | copy-start | bytes 1540
  9.5 3.4 %copy-start.24 = (s32[128]{0:T(128)}, s32[128]{0:T(128)S(1)}, u32[]{:S(2)}) copy-start(s32[128]{0:T(128)S(1)} %get-tuple-element.36) | copy-start | bytes 1540
  11.0 3.8 %copy-start.16 = (pred[128,512]{1,0:T(8,128)(4,1)}, pred[128,512]{1,0:T(8,128)(4,1)S(1)}, u32[]{:S(2)}) copy-start(pred[128,512]{1,0:T(8,128)(4,1)S(1)} %get-tuple-element.54) | copy-start | bytes 196612
  11.0 3.8 %copy-start.20 = (pred[128,512]{1,0:T(8,128)(4,1)}, pred[128,512]{1,0:T(8,128)(4,1)S(1)}, u32[]{:S(2)}) copy-start(pred[128,512]{1,0:T(8,128)(4,1)S(1)} %get-tuple-element.53) | copy-start | bytes 196612
  11.0 3.8 %copy-start.9 = (pred[128,512]{1,0:T(8,128)(4,1)}, pred[128,512]{1,0:T(8,128)(4,1)S(1)}, u32[]{:S(2)}) copy-start(pred[128,512]{1,0:T(8,128)(4,1)S(1)} %get-tuple-element.64) | copy-start | bytes 196612
  31.7 33.3 %collective-permute-start.2 = (bf16[2,512,1024]{1,2,0:T(8,128)(2,1)}, bf16[2,512,1024]{1,2,0:T(8,128)(2,1)}, u32[]{:S(2)}, u32[]{:S(2)}) collective-permute-start(bf16[2,512,1024]{1,2,0:T(8,128)(2,1)} %collective-permute-done), channel_id=1, source_target_pairs={{0,4},{4,8},{8,12},{12,16},{16,20},{20,24},{24,28},{28,32},{32,36}... | collective-permute-start | bytes 6291464 | tf_op jit(solution)/shard_map/ppermute | solution.py:14
  44.0 6.0 %copy-start.3 = (bf16[128,1024]{0,1:T(8,128)(2,1)S(1)}, bf16[128,1024]{0,1:T(8,128)(2,1)}, u32[]{:S(2)}) copy-start(bf16[128,1024]{0,1:T(8,128)(2,1)} %copy-done.2) | copy-start | bytes 786436
  44.1 6.0 %copy-start.19 = (pred[128,512]{1,0:T(8,128)(4,1)S(1)}, pred[128,512]{1,0:T(8,128)(4,1)}, u32[]{:S(2)}) copy-start(pred[128,512]{1,0:T(8,128)(4,1)} %get-tuple-element.55) | copy-start | bytes 196612
  44.1 28.8 %collective-permute-start.1 = (bf16[2,128,1024]{1,2,0:T(8,128)(2,1)S(1)}, bf16[2,128,1024]{1,2,0:T(8,128)(2,1)S(1)}, u32[]{:S(2)}, u32[]{:S(2)}) collective-permute-start(bf16[2,128,1024]{1,2,0:T(8,128)(2,1)S(1)} %slice.90), channel_id=1, source_target_pairs={{0,8},{8,16},{16,24},{24,32},{32,40},{40,48},{48,56},{56,64},{64,7... | collective-permute-start | bytes 1572872 | tf_op jit(solution)/shard_map/ppermute | solution.py:33
  66.1 3.8 %copy-start.18 = (pred[128,512]{1,0:T(8,128)(4,1)S(1)}, pred[128,512]{1,0:T(8,128)(4,1)}, u32[]{:S(2)}) copy-start(pred[128,512]{1,0:T(8,128)(4,1)} %get-tuple-element.62) | copy-start | bytes 196612
  66.1 6.8 %collective-permute-start.3 = (bf16[2,128,1024]{1,2,0:T(8,128)(2,1)S(1)}, bf16[2,128,1024]{1,2,0:T(8,128)(2,1)S(1)}, u32[]{:S(2)}, u32[]{:S(2)}) collective-permute-start(bf16[2,128,1024]{1,2,0:T(8,128)(2,1)S(1)} %slice.91), channel_id=1, source_target_pairs={{0,4},{8,12},{16,20},{24,28},{32,36},{40,44},{48,52},{56,60},{64,6... | collective-permute-start | bytes 1572872 | tf_op jit(solution)/shard_map/ppermute | solution.py:34
  77.6 3.7 %slice-start = ((s8[8388608]{0:T(1024)(128)(4,1)}), s8[4194304]{0:T(1024)(128)(4,1)S(1)}, s32[]{:S(2)}) async-start(s8[8388608]{0:T(1024)(128)(4,1)} %bitcast.288), calls=%async_computation | async-start | bytes 8388608
  88.1 14.5 %collective-permute-start.4 = (bf16[128,2048]{1,0:T(8,128)(2,1)S(1)}, bf16[128,2048]{1,0:T(8,128)(2,1)S(1)}, u32[]{:S(2)}, u32[]{:S(2)}) collective-permute-start(bf16[128,2048]{1,0:T(8,128)(2,1)S(1)} %get-tuple-element.29), channel_id=1, source_target_pairs={{0,1},{1,2},{2,3},{3,0},{4,5},{5,6},{6,7},{7,4},{8,9},{9,10},{10,1... | collective-permute-start | bytes 1572872 | tf_op jit(solution)/shard_map/ppermute | solution.py:19
  90.8 13.0 %collective-permute-start.6 = (bf16[128,2048]{1,0:T(8,128)(2,1)S(1)}, bf16[128,2048]{1,0:T(8,128)(2,1)S(1)}, u32[]{:S(2)}, u32[]{:S(2)}) collective-permute-start(bf16[128,2048]{1,0:T(8,128)(2,1)S(1)} %get-tuple-element.30), channel_id=1, source_target_pairs={{0,3},{1,0},{2,1},{3,2},{4,7},{5,4},{6,5},{7,6},{8,11},{9,8},{10,9... | collective-permute-start | bytes 1572872 | tf_op jit(solution)/shard_map/ppermute | solution.py:19
  102.9 24.9 %collective-permute-start.5 = (bf16[128,4096]{1,0:T(8,128)(2,1)S(1)}, bf16[128,4096]{1,0:T(8,128)(2,1)S(1)}, u32[]{:S(2)}, u32[]{:S(2)}) collective-permute-start(bf16[128,4096]{1,0:T(8,128)(2,1)S(1)} %pad_maximum_fusion), channel_id=1, source_target_pairs={{0,1},{1,2},{2,3},{3,0},{4,5},{5,6},{6,7},{7,4},{8,9},{9,10},{10,1... | collective-permute-start | bytes 3145736 | tf_op jit(solution)/shard_map/ppermute | solution.py:19
  104.0 24.3 %collective-permute-start.7 = (bf16[128,4096]{1,0:T(8,128)(2,1)S(1)}, bf16[128,4096]{1,0:T(8,128)(2,1)S(1)}, u32[]{:S(2)}, u32[]{:S(2)}) collective-permute-start(bf16[128,4096]{1,0:T(8,128)(2,1)S(1)} %pad_maximum_fusion.1), channel_id=1, source_target_pairs={{0,3},{1,0},{2,1},{3,2},{4,7},{5,4},{6,5},{7,6},{8,11},{9,8},{10,9... | collective-permute-start | bytes 3145736 | tf_op jit(solution)/shard_map/ppermute | solution.py:19
  (16 other events, 24.4 us)

commit v14 on v8

--- a/solution.py
+++ b/solution.py
@@ -29,7 +29,10 @@
     tail = DOC_MOST - 2 * rows
     r1 = shift_up(keys_values, "ctx")
     r2 = shift_up(r1, "ctx")
-    r3 = shift_up(r2[:, rows - tail:], "ctx")
+    peers = lax.axis_size("ctx")
+    tail_even = lax.ppermute(r1[:, rows - tail:], "ctx", [(i, i + 2) for i in range(0, peers - 2, 2)])
+    tail_odd = lax.ppermute(r2[:, rows - tail:], "ctx", [(i, i + 1) for i in range(0, peers - 1, 2)])
+    r3 = jnp.where(me % 2 == 0, tail_even, tail_odd)
     sources = [r3, r2, r1, keys_values]
     offsets = [-DOC_MOST, -2 * rows, -rows, 0]
     padded_docs = jnp.concatenate([jnp.full((DOC_MOST,), -1, jnp.int32), doc_index])

time: 132 us -> 131 us (level)
  waiting for transfers between devices: 57.2 us -> 49.2 us
  starting transfers between devices: 12.9 us -> 17.1 us
  local copies, waits for them, and re-layouts: 19.7 us -> 21.9 us
    ppermute x0 -> x2, starting transfers between devices: none -> 6.4 us  [the longest x1 4.28 us: per_device(): lax.ppermute(r1[:, rows - tail:], 'ctx', [(i, i + 2) for i in range(0, pe...]
    ppermute x3 -> x2, waiting for transfers between devices: 32.7 us -> 28 us  [shift_up(): return lax.ppermute(x, axis, [(i, i + 1) for i in range(peers - 1)])]
    ppermute x4, waiting for transfers between devices: 24.5 us -> 21.2 us  [rotate(): return lax.ppermute(x, axis, [(i, (i + by) % peers) for i in range(peers)])]
    ppermute x3 -> x2, starting transfers between devices: 6.18 us -> 3.95 us  [shift_up(): return lax.ppermute(x, axis, [(i, i + 1) for i in range(peers - 1)])]
    unnamed x69 -> x67, local copies, waits for them, and re-layouts: 9.47 us -> 9.44 us
  transfers between devices with their start and end apart: 7 -> 8, of which waited for: 7 -> 5; matrix products, arithmetic and copies ran while one was open for 28% -> 31% of each run, Pallas kernels for 0% -> 0%
where the time goes in v14:
time: 131 us; the launch traced here: 130 us
  waiting for transfers between devices  49.2 us (38%)
  matrix products  27.3 us (21%)
  local copies, waits for them, and re-layouts  21.9 us (17%)
  starting transfers between devices  17.1 us (13%)
  other arithmetic  13.3 us (10%)
    ppermute x2, waiting for transfers between devices, shift_up(): return lax.ppermute(x, axis, [(i, i + 1) for i in range(peers - 1)])  28 us
    ppermute x4, waiting for transfers between devices, rotate(): return lax.ppermute(x, axis, [(i, (i + by) % peers) for i in range(peers)])  21.2 us
    dot_general x16, matrix products, scores(): jnp.einsum('qhd,khd->hqk', q, k, preferred_element_type=jnp.float32) * scale  12.2 us
    dot_general x16, matrix products, stage(): jnp.einsum('hqk,khd->qhd', probs, kv[1].reshape(n, heads, HD), preferred_...  10 us
    unnamed x67, local copies, waits for them, and re-layouts  9.44 us
    slice x4, local copies, waits for them, and re-layouts, stage(): kv[1].reshape(n, heads, HD)  7.97 us
    reduce_sum x12, other arithmetic, stage(): t = jnp.sum(weights, axis=2)  7.62 us
    ppermute x4, starting transfers between devices, rotate(): return lax.ppermute(x, axis, [(i, (i + by) % peers) for i in range(peers)])  6.76 us
  transfers between devices with their start and end apart: 8, of which 5 were waited for; matrix products, arithmetic and copies ran while one was open for 31% of the time, Pallas kernels for 0%

profile of v14, /device:TPU:98, one launch (start us, length us, event | category | flops | bytes accessed | tf_op | source)
XLA Modules:
  0.0 129.7 jit_solution(18305908956202081813)
XLA Ops:
  0.0 4.0 %copy.14 = bf16[2,512,1024]{1,2,0:T(8,128)(2,1)} copy(bf16[2,512,1024]{2,1,0:T(8,128)(2,1)} %param.5) | data formatting | bytes 4194304 | tf_op args[1]
  4.0 2.0 %collective-permute-start = (bf16[2,512,1024]{1,2,0:T(8,128)(2,1)}, bf16[2,512,1024]{1,2,0:T(8,128)(2,1)}, u32[]{:S(2)}, u32[]{:S(2)}) collective-permute-start(bf16[2,512,1024]{1,2,0:T(8,128)(2,1)} %copy.14), channel_id=1, source_target_pairs={{0,4},{4,8},{8,12},{12,16},{16,20},{20,24},{24,28},{28,32},{32,36}... | collective-permute-start | bytes 6291464 | tf_op jit(solution)/shard_map/ppermute | solution.py:14
  6.1 1.3 slice.89
  10.1 1.5 %fusion.150 = (pred[128,512]{1,0:T(8,128)(4,1)S(1)}, pred[128,512]{1,0:T(8,128)(4,1)S(1)}, pred[128,512]{1,0:T(8,128)(4,1)}, pred[128,512]{1,0:T(8,128)(4,1)}, p...) fusion(s32[512]{0:T(512)S(1)} %get-tuple-element.47, ...), kind=kLoop, calls=%fused_computation.192 | loop fusion | flops 2359296 | bytes 800768 | tf_op jit(solution)/shard_map/and | solution.py:51
  11.6 1.9 %fusion.5 = (f32[8,128]{1,0:T(8,128)S(1)}, f32[8,128,512]{2,1,0:T(8,128)}) fusion(pred[128,512]{1,0:T(8,128)(4,1)S(1)} %get-tuple-element.61, bf16[128,8,128]{0,2,1:T(8,128)(2,1)S(1)} %bitcast.382, bf16[512,8,128]{0,2,1:T(8,128)(2,1)S(1)} %bitcast.354), kind=kOutput, calls=%fused_computation.34 | convolution fusion | flops 135789568 | bytes 3477504 | tf_op jit(solution)/shard_map/qhd,khd->hqk/dot_general | solution.py:52
  13.6 1.8 %fusion.8 = (f32[8,128]{1,0:T(8,128)S(1)}, f32[8,128,512]{2,1,0:T(8,128)}) fusion(pred[128,512]{1,0:T(8,128)(4,1)S(1)} %get-tuple-element.62, bf16[128,8,128]{0,2,1:T(8,128)(2,1)S(1)} %bitcast.378, bf16[512,8,128]{0,2,1:T(8,128)(2,1)S(1)} %bitcast.355), kind=kOutput, calls=%fused_computation.37 | convolution fusion | flops 135789568 | bytes 3477504 | tf_op jit(solution)/shard_map/qhd,khd->hqk/dot_general | solution.py:52
  15.4 16.3 %collective-permute-done = bf16[2,512,1024]{1,2,0:T(8,128)(2,1)} collective-permute-done((bf16[2,512,1024]{1,2,0:T(8,128)(2,1)}, bf16[2,512,1024]{1,2,0:T(8,128)(2,1)}, u32[]{:S(2)}, u32[]{:S(2)}) %collective-permute-start) | collective-permute-done | bytes 2097184 | tf_op jit(solution)/shard_map/ppermute | solution.py:14
  31.8 1.9 %collective-permute-start.1 = (bf16[2,512,1024]{1,2,0:T(8,128)(2,1)}, bf16[2,512,1024]{1,2,0:T(8,128)(2,1)}, u32[]{:S(2)}, u32[]{:S(2)}) collective-permute-start(bf16[2,512,1024]{1,2,0:T(8,128)(2,1)} %collective-permute-done), channel_id=1, source_target_pairs={{0,4},{4,8},{8,12},{12,16},{16,20},{20,24},{24,28},{28,32},{32,36}... | collective-permute-start | bytes 6291464 | tf_op jit(solution)/shard_map/ppermute | solution.py:14
  34.3 2.3 %slice.39 = bf16[1,512,1024]{2,1,0:T(8,128)(2,1)} slice(bf16[2,512,1024]{2,1,0:T(8,128)(2,1)} %param.5), slice={[1:2], [0:512], [0:1024]} | slice | bytes 2097152 | tf_op jit(solution)/shard_map/slice | solution.py:66
  36.6 2.4 %copy.24 = bf16[1,512,1024]{1,2,0:T(8,128)(2,1)} copy(bf16[1,512,1024]{2,1,0:T(8,128)(2,1)} %slice.39) | data formatting | bytes 2097152 | tf_op jit(solution)/shard_map/slice | solution.py:66
  38.9 1.8 %copy.95 = bf16[128,1024]{0,1:T(8,128)(2,1)} copy(bf16[128,1024]{1,0:T(8,128)(2,1)} %get-tuple-element.36) | data formatting | bytes 524288
  41.5 1.6 %fusion.11 = (f32[8,128]{1,0:T(8,128)S(1)}, f32[8,128,512]{2,1,0:T(8,128)S(1)}) fusion(pred[128,512]{1,0:T(8,128)(4,1)} %get-tuple-element.71, bf16[128,8,128]{0,2,1:T(8,128)(2,1)} %bitcast.386, bf16[512,8,128]{0,2,1:T(8,128)(2,1)S(1)} %bitcast.357), kind=kOutput, calls=%fused_computation.40 | convolution fusion | flops 135789568 | bytes 3477504 | tf_op jit(solution)/shard_map/qhd,khd->hqk/dot_general | solution.py:52
  44.2 4.3 %collective-permute-start.2 = (bf16[2,128,1024]{1,2,0:T(8,128)(2,1)S(1)}, bf16[2,128,1024]{1,2,0:T(8,128)(2,1)S(1)}, u32[]{:S(2)}, u32[]{:S(2)}) collective-permute-start(bf16[2,128,1024]{1,2,0:T(8,128)(2,1)S(1)} %slice.91), channel_id=1, source_target_pairs={{0,8},{8,16},{16,24},{24,32},{32,40},{40,48},{48,56},{56,64},{64,7... | collective-permute-start | bytes 1572872 | tf_op jit(solution)/shard_map/ppermute | solution.py:33
  48.5 1.7 %fusion.214 = (bf16[1,512,1024]{1,2,0:T(8,128)(2,1)S(1)}, bf16[1,512,1024]{1,2,0:T(8,128)(2,1)S(1)}) fusion(bf16[2,512,1024]{1,2,0:T(8,128)(2,1)} %collective-permute-done), kind=kLoop, calls=%fused_computation.319 | loop fusion | bytes 4194304 | tf_op jit(solution)/shard_map/slice | solution.py:66
  53.4 11.7 %collective-permute-done.1 = bf16[2,512,1024]{1,2,0:T(8,128)(2,1)} collective-permute-done((bf16[2,512,1024]{1,2,0:T(8,128)(2,1)}, bf16[2,512,1024]{1,2,0:T(8,128)(2,1)}, u32[]{:S(2)}, u32[]{:S(2)}) %collective-permute-start.1) | collective-permute-done | bytes 2097184 | tf_op jit(solution)/shard_map/ppermute | solution.py:14
  66.1 2.1 %collective-permute-start.3 = (bf16[2,128,1024]{1,2,0:T(8,128)(2,1)S(1)}, bf16[2,128,1024]{1,2,0:T(8,128)(2,1)S(1)}, u32[]{:S(2)}, u32[]{:S(2)}) collective-permute-start(bf16[2,128,1024]{1,2,0:T(8,128)(2,1)S(1)} %slice.92), channel_id=1, source_target_pairs={{0,4},{8,12},{16,20},{24,28},{32,36},{40,44},{48,52},{56,60},{64,6... | collective-permute-start | bytes 1572872 | tf_op jit(solution)/shard_map/ppermute | solution.py:34
  68.2 1.7 %fusion.213 = (bf16[1,512,1024]{1,2,0:T(8,128)(2,1)S(1)}, bf16[1,512,1024]{1,2,0:T(8,128)(2,1)S(1)}) fusion(bf16[2,512,1024]{1,2,0:T(8,128)(2,1)} %collective-permute-done.1), kind=kLoop, calls=%fused_computation.318 | loop fusion | bytes 4194304 | tf_op jit(solution)/shard_map/slice | solution.py:66
  87.3 1.3 convolution_convert_fusion.1
  88.7 1.6 %collective-permute-start.4 = (bf16[128,2048]{1,0:T(8,128)(2,1)S(1)}, bf16[128,2048]{1,0:T(8,128)(2,1)S(1)}, u32[]{:S(2)}, u32[]{:S(2)}) collective-permute-start(bf16[128,2048]{1,0:T(8,128)(2,1)S(1)} %get-tuple-element.37), channel_id=1, source_target_pairs={{0,1},{1,2},{2,3},{3,0},{4,5},{5,6},{6,7},{7,4},{8,9},{9,10},{10,1... | collective-permute-start | bytes 1572872 | tf_op jit(solution)/shard_map/ppermute | solution.py:19
  91.1 1.7 %collective-permute-start.6 = (bf16[128,2048]{1,0:T(8,128)(2,1)S(1)}, bf16[128,2048]{1,0:T(8,128)(2,1)S(1)}, u32[]{:S(2)}, u32[]{:S(2)}) collective-permute-start(bf16[128,2048]{1,0:T(8,128)(2,1)S(1)} %get-tuple-element.38), channel_id=1, source_target_pairs={{0,3},{1,0},{2,1},{3,2},{4,7},{5,4},{6,5},{7,6},{8,11},{9,8},{10,9... | collective-permute-start | bytes 1572872 | tf_op jit(solution)/shard_map/ppermute | solution.py:19
  101.1 2.1 %collective-permute-done.4 = bf16[128,2048]{1,0:T(8,128)(2,1)S(1)} collective-permute-done((bf16[128,2048]{1,0:T(8,128)(2,1)S(1)}, bf16[128,2048]{1,0:T(8,128)(2,1)S(1)}, u32[]{:S(2)}, u32[]{:S(2)}) %collective-permute-start.4) | collective-permute-done | bytes 524320 | tf_op jit(solution)/shard_map/ppermute | solution.py:19
  104.3 3.0 %collective-permute-start.7 = (bf16[128,4096]{1,0:T(8,128)(2,1)S(1)}, bf16[128,4096]{1,0:T(8,128)(2,1)S(1)}, u32[]{:S(2)}, u32[]{:S(2)}) collective-permute-start(bf16[128,4096]{1,0:T(8,128)(2,1)S(1)} %pad_maximum_fusion.1), channel_id=1, source_target_pairs={{0,3},{1,0},{2,1},{3,2},{4,7},{5,4},{6,5},{7,6},{8,11},{9,8},{10,9... | collective-permute-start | bytes 3145736 | tf_op jit(solution)/shard_map/ppermute | solution.py:19
  109.3 18.9 %collective-permute-done.5 = bf16[128,4096]{1,0:T(8,128)(2,1)S(1)} collective-permute-done((bf16[128,4096]{1,0:T(8,128)(2,1)S(1)}, bf16[128,4096]{1,0:T(8,128)(2,1)S(1)}, u32[]{:S(2)}, u32[]{:S(2)}) %collective-permute-start.5) | collective-permute-done | bytes 1048608 | tf_op jit(solution)/shard_map/ppermute | solution.py:19
  128.3 1.4 %add_convert_fusion = bf16[128,4096]{1,0:T(8,128)(2,1)} fusion(bf16[128,4096]{1,0:T(8,128)(2,1)S(1)} %collective-permute-done.7, f32[128,4096]{1,0:T(8,128)S(1)} %fusion, bf16[128,4096]{1,0:T(8,128)(2,1)S(1)} %collective-permute-done.5), kind=kLoop, calls=%fused_computation.5 | loop fusion | flops 2621440 | bytes 5242880 | tf_op jit(solution)/shard_map/convert_element_type | solution.py:102
  (149 shorter events, 38.6 us)
Async XLA Ops:
  4.0 3.4 %copy-start.7 = (bf16[512,1024]{1,0:T(8,128)(2,1)S(1)}, bf16[512,1024]{1,0:T(8,128)(2,1)}, u32[]{:S(2)}) copy-start(bf16[512,1024]{1,0:T(8,128)(2,1)} %param.4) | copy-start | bytes 3145732
  4.0 27.8 %collective-permute-start = (bf16[2,512,1024]{1,2,0:T(8,128)(2,1)}, bf16[2,512,1024]{1,2,0:T(8,128)(2,1)}, u32[]{:S(2)}, u32[]{:S(2)}) collective-permute-start(bf16[2,512,1024]{1,2,0:T(8,128)(2,1)} %copy.14), channel_id=1, source_target_pairs={{0,4},{4,8},{8,12},{12,16},{16,20},{20,24},{24,28},{28,32},{32,36}... | collective-permute-start | bytes 6291464 | tf_op jit(solution)/shard_map/ppermute | solution.py:14
  8.4 5.1 %copy-start.4 = (bf16[128,1024]{0,1:T(8,128)(2,1)}, bf16[128,1024]{0,1:T(8,128)(2,1)S(1)}, u32[]{:S(2)}) copy-start(bf16[128,1024]{0,1:T(8,128)(2,1)S(1)} %copy.93) | copy-start | bytes 786436
  8.6 5.0 %copy-start.2 = (bf16[128,1024]{0,1:T(8,128)(2,1)}, bf16[128,1024]{0,1:T(8,128)(2,1)S(1)}, u32[]{:S(2)}) copy-start(bf16[128,1024]{0,1:T(8,128)(2,1)S(1)} %copy.94) | copy-start | bytes 786436
  8.8 4.7 %copy-start.26 = (s32[128]{0:T(128)}, s32[128]{0:T(128)S(1)}, u32[]{:S(2)}) copy-start(s32[128]{0:T(128)S(1)} %get-tuple-element.109) | copy-start | bytes 1540
  8.8 4.7 %copy-start.27 = (s32[128]{0:T(128)}, s32[128]{0:T(128)S(1)}, u32[]{:S(2)}) copy-start(s32[128]{0:T(128)S(1)} %get-tuple-element.110) | copy-start | bytes 1540
  9.3 4.2 %copy-start.28 = (s32[128]{0:T(128)}, s32[128]{0:T(128)S(1)}, u32[]{:S(2)}) copy-start(s32[128]{0:T(128)S(1)} %get-tuple-element.111) | copy-start | bytes 1540
  10.0 3.5 %copy-start.22 = (s32[128]{0:T(128)}, s32[128]{0:T(128)S(1)}, u32[]{:S(2)}) copy-start(s32[128]{0:T(128)S(1)} %get-tuple-element.43) | copy-start | bytes 1540
  10.0 3.5 %copy-start.23 = (s32[128]{0:T(128)}, s32[128]{0:T(128)S(1)}, u32[]{:S(2)}) copy-start(s32[128]{0:T(128)S(1)} %get-tuple-element.44) | copy-start | bytes 1540
  10.0 3.5 %copy-start.25 = (s32[128]{0:T(128)}, s32[128]{0:T(128)S(1)}, u32[]{:S(2)}) copy-start(s32[128]{0:T(128)S(1)} %get-tuple-element.113) | copy-start | bytes 1540
  11.6 3.8 %copy-start.13 = (pred[128,512]{1,0:T(8,128)(4,1)}, pred[128,512]{1,0:T(8,128)(4,1)S(1)}, u32[]{:S(2)}) copy-start(pred[128,512]{1,0:T(8,128)(4,1)S(1)} %get-tuple-element.62) | copy-start | bytes 196612
  11.6 3.8 %copy-start.15 = (pred[128,512]{1,0:T(8,128)(4,1)}, pred[128,512]{1,0:T(8,128)(4,1)S(1)}, u32[]{:S(2)}) copy-start(pred[128,512]{1,0:T(8,128)(4,1)S(1)} %get-tuple-element.61) | copy-start | bytes 196612
  31.8 33.3 %collective-permute-start.1 = (bf16[2,512,1024]{1,2,0:T(8,128)(2,1)}, bf16[2,512,1024]{1,2,0:T(8,128)(2,1)}, u32[]{:S(2)}, u32[]{:S(2)}) collective-permute-start(bf16[2,512,1024]{1,2,0:T(8,128)(2,1)} %collective-permute-done), channel_id=1, source_target_pairs={{0,4},{4,8},{8,12},{12,16},{16,20},{20,24},{24,28},{28,32},{32,36}... | collective-permute-start | bytes 6291464 | tf_op jit(solution)/shard_map/ppermute | solution.py:14
  44.2 6.0 %copy-start.5 = (bf16[128,1024]{0,1:T(8,128)(2,1)S(1)}, bf16[128,1024]{0,1:T(8,128)(2,1)}, u32[]{:S(2)}) copy-start(bf16[128,1024]{0,1:T(8,128)(2,1)} %copy-done.4) | copy-start | bytes 786436
  44.2 6.0 %copy-start.12 = (pred[128,512]{1,0:T(8,128)(4,1)S(1)}, pred[128,512]{1,0:T(8,128)(4,1)}, u32[]{:S(2)}) copy-start(pred[128,512]{1,0:T(8,128)(4,1)} %get-tuple-element.63) | copy-start | bytes 196612
  44.2 28.7 %collective-permute-start.2 = (bf16[2,128,1024]{1,2,0:T(8,128)(2,1)S(1)}, bf16[2,128,1024]{1,2,0:T(8,128)(2,1)S(1)}, u32[]{:S(2)}, u32[]{:S(2)}) collective-permute-start(bf16[2,128,1024]{1,2,0:T(8,128)(2,1)S(1)} %slice.91), channel_id=1, source_target_pairs={{0,8},{8,16},{16,24},{24,32},{32,40},{40,48},{48,56},{56,64},{64,7... | collective-permute-start | bytes 1572872 | tf_op jit(solution)/shard_map/ppermute | solution.py:33
  66.1 3.8 %copy-start.20 = (pred[128,512]{1,0:T(8,128)(4,1)S(1)}, pred[128,512]{1,0:T(8,128)(4,1)}, u32[]{:S(2)}) copy-start(pred[128,512]{1,0:T(8,128)(4,1)} %get-tuple-element.70) | copy-start | bytes 196612
  66.1 6.8 %collective-permute-start.3 = (bf16[2,128,1024]{1,2,0:T(8,128)(2,1)S(1)}, bf16[2,128,1024]{1,2,0:T(8,128)(2,1)S(1)}, u32[]{:S(2)}, u32[]{:S(2)}) collective-permute-start(bf16[2,128,1024]{1,2,0:T(8,128)(2,1)S(1)} %slice.92), channel_id=1, source_target_pairs={{0,4},{8,12},{16,20},{24,28},{32,36},{40,44},{48,52},{56,60},{64,6... | collective-permute-start | bytes 1572872 | tf_op jit(solution)/shard_map/ppermute | solution.py:34
  79.5 3.4 %slice-start = ((s8[8388608]{0:T(1024)(128)(4,1)}), s8[4194304]{0:T(1024)(128)(4,1)S(1)}, s32[]{:S(2)}) async-start(s8[8388608]{0:T(1024)(128)(4,1)} %bitcast.352), calls=%async_computation | async-start | bytes 8388608
  88.7 4.1 %copy-start.10 = (pred[128,512]{1,0:T(8,128)(4,1)S(1)}, pred[128,512]{1,0:T(8,128)(4,1)}, u32[]{:S(2)}) copy-start(pred[128,512]{1,0:T(8,128)(4,1)} %get-tuple-element.71) | copy-start | bytes 196612
  88.7 14.5 %collective-permute-start.4 = (bf16[128,2048]{1,0:T(8,128)(2,1)S(1)}, bf16[128,2048]{1,0:T(8,128)(2,1)S(1)}, u32[]{:S(2)}, u32[]{:S(2)}) collective-permute-start(bf16[128,2048]{1,0:T(8,128)(2,1)S(1)} %get-tuple-element.37), channel_id=1, source_target_pairs={{0,1},{1,2},{2,3},{3,0},{4,5},{5,6},{6,7},{7,4},{8,9},{9,10},{10,1... | collective-permute-start | bytes 1572872 | tf_op jit(solution)/shard_map/ppermute | solution.py:19
  91.1 13.0 %collective-permute-start.6 = (bf16[128,2048]{1,0:T(8,128)(2,1)S(1)}, bf16[128,2048]{1,0:T(8,128)(2,1)S(1)}, u32[]{:S(2)}, u32[]{:S(2)}) collective-permute-start(bf16[128,2048]{1,0:T(8,128)(2,1)S(1)} %get-tuple-element.38), channel_id=1, source_target_pairs={{0,3},{1,0},{2,1},{3,2},{4,7},{5,4},{6,5},{7,6},{8,11},{9,8},{10,9... | collective-permute-start | bytes 1572872 | tf_op jit(solution)/shard_map/ppermute | solution.py:19
  103.4 24.8 %collective-permute-start.5 = (bf16[128,4096]{1,0:T(8,128)(2,1)S(1)}, bf16[128,4096]{1,0:T(8,128)(2,1)S(1)}, u32[]{:S(2)}, u32[]{:S(2)}) collective-permute-start(bf16[128,4096]{1,0:T(8,128)(2,1)S(1)} %pad_maximum_fusion), channel_id=1, source_target_pairs={{0,1},{1,2},{2,3},{3,0},{4,5},{5,6},{6,7},{7,4},{8,9},{9,10},{10,1... | collective-permute-start | bytes 3145736 | tf_op jit(solution)/shard_map/ppermute | solution.py:19
  104.3 24.0 %collective-permute-start.7 = (bf16[128,4096]{1,0:T(8,128)(2,1)S(1)}, bf16[128,4096]{1,0:T(8,128)(2,1)S(1)}, u32[]{:S(2)}, u32[]{:S(2)}) collective-permute-start(bf16[128,4096]{1,0:T(8,128)(2,1)S(1)} %pad_maximum_fusion.1), channel_id=1, source_target_pairs={{0,3},{1,0},{2,1},{3,2},{4,7},{5,4},{6,5},{7,6},{8,11},{9,8},{10,9... | collective-permute-start | bytes 3145736 | tf_op jit(solution)/shard_map/ppermute | solution.py:19
  (15 other events, 19.8 us)

commit v15 on v14

--- a/solution.py
+++ b/solution.py
@@ -38,7 +38,7 @@
     padded_docs = jnp.concatenate([jnp.full((DOC_MOST,), -1, jnp.int32), doc_index])
     scale = HD ** (-0.5)
 
-    def chunk_part(c):
+    def chunk_part(c, split=()):
         start = c * CHUNK
         q = lax.dynamic_slice_in_dim(queries, start, CHUNK, 0).reshape(CHUNK, heads, HD)
         q_docs = lax.dynamic_slice_in_dim(doc_index, first_row + start, CHUNK)
@@ -78,13 +78,17 @@
             top = new_top
         attended = (summed / jnp.transpose(total)[:, :, None]).astype(jnp.bfloat16)
         attended = attended.reshape(CHUNK, heads * HD)
+        if split:
+            return tuple(
+                jnp.dot(attended, w, preferred_element_type=jnp.float32).astype(jnp.bfloat16) for w in split
+            )
         return jnp.dot(attended, w_out, preferred_element_type=jnp.float32).astype(jnp.bfloat16)
 
     assert groups == 4
     cols = w_out.shape[1] // 2
-    far = chunk_part((h + 2) % groups)
-    via_left = rotate(far[:, :cols], "head", groups - 1)
-    via_right = rotate(far[:, cols:], "head", 1)
+    far_left, far_right = chunk_part((h + 2) % groups, (w_out[:, :cols], w_out[:, cols:]))
+    via_left = rotate(far_left, "head", groups - 1)
+    via_right = rotate(far_right, "head", 1)
     nxt = chunk_part((h + 1) % groups)
     nxt = jnp.concatenate(
         [nxt[:, :cols], (nxt[:, cols:].astype(jnp.float32) + via_right.astype(jnp.float32)).astype(jnp.bfloat16)],

time: 131 us -> 131 us (level)
    dot_general x0 -> x2, matrix products: none -> 1.48 us  [chunk_part(): jnp.dot(attended, w, preferred_element_type=jnp.float32)]
    dot_general x4 -> x3, matrix products: 5.12 us -> 3.86 us  [chunk_part(): jnp.dot(attended, w_out, preferred_element_type=jnp.float32)]
where the time goes in v15:
time: 131 us; the launch traced here: 130 us
  waiting for transfers between devices  49.3 us (38%)
  matrix products  27.3 us (21%)
  local copies, waits for them, and re-layouts  22.1 us (17%)
  starting transfers between devices  17.1 us (13%)
  other arithmetic  13.5 us (10%)
    ppermute x2, waiting for transfers between devices, shift_up(): return lax.ppermute(x, axis, [(i, i + 1) for i in range(peers - 1)])  28 us
    ppermute x4, waiting for transfers between devices, rotate(): return lax.ppermute(x, axis, [(i, (i + by) % peers) for i in range(peers)])  21.3 us
    dot_general x16, matrix products, scores(): jnp.einsum('qhd,khd->hqk', q, k, preferred_element_type=jnp.float32) * scale  12.2 us
    dot_general x16, matrix products, stage(): jnp.einsum('hqk,khd->qhd', probs, kv[1].reshape(n, heads, HD), preferred_...  9.78 us
    unnamed x67, local copies, waits for them, and re-layouts  9.75 us
    slice x4, local copies, waits for them, and re-layouts, stage(): kv[1].reshape(n, heads, HD)  7.97 us
    reduce_sum x12, other arithmetic, stage(): t = jnp.sum(weights, axis=2)  7.84 us
    ppermute x4, starting transfers between devices, rotate(): return lax.ppermute(x, axis, [(i, (i + by) % peers) for i in range(peers)])  6.75 us
  transfers between devices with their start and end apart: 8, of which 5 were waited for; matrix products, arithmetic and copies ran while one was open for 31% of the time, Pallas kernels for 0%

profile of v15, /device:TPU:98, one launch (start us, length us, event | category | flops | bytes accessed | tf_op | source)
XLA Modules:
  0.0 130.1 jit_solution(14046272998199554596)
XLA Ops:
  0.0 4.0 %copy.14 = bf16[2,512,1024]{1,2,0:T(8,128)(2,1)} copy(bf16[2,512,1024]{2,1,0:T(8,128)(2,1)} %param.5) | data formatting | bytes 4194304 | tf_op args[1]
  4.0 2.0 %collective-permute-start = (bf16[2,512,1024]{1,2,0:T(8,128)(2,1)}, bf16[2,512,1024]{1,2,0:T(8,128)(2,1)}, u32[]{:S(2)}, u32[]{:S(2)}) collective-permute-start(bf16[2,512,1024]{1,2,0:T(8,128)(2,1)} %copy.14), channel_id=1, source_target_pairs={{0,4},{4,8},{8,12},{12,16},{16,20},{20,24},{24,28},{28,32},{32,36}... | collective-permute-start | bytes 6291464 | tf_op jit(solution)/shard_map/ppermute | solution.py:14
  6.1 1.3 slice.89
  10.1 1.5 %fusion.160 = (pred[128,512]{1,0:T(8,128)(4,1)S(1)}, pred[128,512]{1,0:T(8,128)(4,1)S(1)}, pred[128,512]{1,0:T(8,128)(4,1)}, pred[128,512]{1,0:T(8,128)(4,1)}, p...) fusion(s32[512]{0:T(512)S(1)} %get-tuple-element.45, ...), kind=kLoop, calls=%fused_computation.197 | loop fusion | flops 2359296 | bytes 800768 | tf_op jit(solution)/shard_map/and | solution.py:51
  11.6 1.8 %fusion.15 = (f32[8,128]{1,0:T(8,128)S(1)}, f32[8,128,512]{2,1,0:T(8,128)}) fusion(pred[128,512]{1,0:T(8,128)(4,1)S(1)} %get-tuple-element.59, bf16[128,8,128]{0,2,1:T(8,128)(2,1)S(1)} %bitcast.382, bf16[512,8,128]{0,2,1:T(8,128)(2,1)S(1)} %bitcast.354), kind=kOutput, calls=%fused_computation.39 | convolution fusion | flops 135789568 | bytes 3477504 | tf_op jit(solution)/shard_map/qhd,khd->hqk/dot_general | solution.py:52
  13.5 1.9 %fusion.18 = (f32[8,128]{1,0:T(8,128)S(1)}, f32[8,128,512]{2,1,0:T(8,128)}) fusion(pred[128,512]{1,0:T(8,128)(4,1)S(1)} %get-tuple-element.60, bf16[128,8,128]{0,2,1:T(8,128)(2,1)S(1)} %bitcast.378, bf16[512,8,128]{0,2,1:T(8,128)(2,1)S(1)} %bitcast.355), kind=kOutput, calls=%fused_computation.42 | convolution fusion | flops 135789568 | bytes 3477504 | tf_op jit(solution)/shard_map/qhd,khd->hqk/dot_general | solution.py:52
  15.4 16.3 %collective-permute-done = bf16[2,512,1024]{1,2,0:T(8,128)(2,1)} collective-permute-done((bf16[2,512,1024]{1,2,0:T(8,128)(2,1)}, bf16[2,512,1024]{1,2,0:T(8,128)(2,1)}, u32[]{:S(2)}, u32[]{:S(2)}) %collective-permute-start) | collective-permute-done | bytes 2097184 | tf_op jit(solution)/shard_map/ppermute | solution.py:14
  31.8 1.9 %collective-permute-start.1 = (bf16[2,512,1024]{1,2,0:T(8,128)(2,1)}, bf16[2,512,1024]{1,2,0:T(8,128)(2,1)}, u32[]{:S(2)}, u32[]{:S(2)}) collective-permute-start(bf16[2,512,1024]{1,2,0:T(8,128)(2,1)} %collective-permute-done), channel_id=1, source_target_pairs={{0,4},{4,8},{8,12},{12,16},{16,20},{20,24},{24,28},{28,32},{32,36}... | collective-permute-start | bytes 6291464 | tf_op jit(solution)/shard_map/ppermute | solution.py:14
  34.3 2.3 %slice.39 = bf16[1,512,1024]{2,1,0:T(8,128)(2,1)} slice(bf16[2,512,1024]{2,1,0:T(8,128)(2,1)} %param.5), slice={[1:2], [0:512], [0:1024]} | slice | bytes 2097152 | tf_op jit(solution)/shard_map/slice | solution.py:66
  36.6 2.4 %copy.24 = bf16[1,512,1024]{1,2,0:T(8,128)(2,1)} copy(bf16[1,512,1024]{2,1,0:T(8,128)(2,1)} %slice.39) | data formatting | bytes 2097152 | tf_op jit(solution)/shard_map/slice | solution.py:66
  38.9 1.8 %copy.95 = bf16[128,1024]{0,1:T(8,128)(2,1)} copy(bf16[128,1024]{1,0:T(8,128)(2,1)} %get-tuple-element.36) | data formatting | bytes 524288
  41.5 1.6 %fusion.21 = (f32[8,128]{1,0:T(8,128)S(1)}, f32[8,128,512]{2,1,0:T(8,128)S(1)}) fusion(pred[128,512]{1,0:T(8,128)(4,1)} %get-tuple-element.69, bf16[128,8,128]{0,2,1:T(8,128)(2,1)} %bitcast.386, bf16[512,8,128]{0,2,1:T(8,128)(2,1)S(1)} %bitcast.357), kind=kOutput, calls=%fused_computation.45 | convolution fusion | flops 135789568 | bytes 3477504 | tf_op jit(solution)/shard_map/qhd,khd->hqk/dot_general | solution.py:52
  44.2 4.3 %collective-permute-start.2 = (bf16[2,128,1024]{1,2,0:T(8,128)(2,1)S(1)}, bf16[2,128,1024]{1,2,0:T(8,128)(2,1)S(1)}, u32[]{:S(2)}, u32[]{:S(2)}) collective-permute-start(bf16[2,128,1024]{1,2,0:T(8,128)(2,1)S(1)} %slice.91), channel_id=1, source_target_pairs={{0,8},{8,16},{16,24},{24,32},{32,40},{40,48},{48,56},{56,64},{64,7... | collective-permute-start | bytes 1572872 | tf_op jit(solution)/shard_map/ppermute | solution.py:33
  48.5 1.7 %fusion.224 = (bf16[1,512,1024]{1,2,0:T(8,128)(2,1)S(1)}, bf16[1,512,1024]{1,2,0:T(8,128)(2,1)S(1)}) fusion(bf16[2,512,1024]{1,2,0:T(8,128)(2,1)} %collective-permute-done), kind=kLoop, calls=%fused_computation.324 | loop fusion | bytes 4194304 | tf_op jit(solution)/shard_map/slice | solution.py:66
  53.4 11.7 %collective-permute-done.1 = bf16[2,512,1024]{1,2,0:T(8,128)(2,1)} collective-permute-done((bf16[2,512,1024]{1,2,0:T(8,128)(2,1)}, bf16[2,512,1024]{1,2,0:T(8,128)(2,1)}, u32[]{:S(2)}, u32[]{:S(2)}) %collective-permute-start.1) | collective-permute-done | bytes 2097184 | tf_op jit(solution)/shard_map/ppermute | solution.py:14
  66.1 2.1 %collective-permute-start.3 = (bf16[2,128,1024]{1,2,0:T(8,128)(2,1)S(1)}, bf16[2,128,1024]{1,2,0:T(8,128)(2,1)S(1)}, u32[]{:S(2)}, u32[]{:S(2)}) collective-permute-start(bf16[2,128,1024]{1,2,0:T(8,128)(2,1)S(1)} %slice.92), channel_id=1, source_target_pairs={{0,4},{8,12},{16,20},{24,28},{32,36},{40,44},{48,52},{56,60},{64,6... | collective-permute-start | bytes 1572872 | tf_op jit(solution)/shard_map/ppermute | solution.py:34
  68.2 1.7 %fusion.223 = (bf16[1,512,1024]{1,2,0:T(8,128)(2,1)S(1)}, bf16[1,512,1024]{1,2,0:T(8,128)(2,1)S(1)}) fusion(bf16[2,512,1024]{1,2,0:T(8,128)(2,1)} %collective-permute-done.1), kind=kLoop, calls=%fused_computation.323 | loop fusion | bytes 4194304 | tf_op jit(solution)/shard_map/slice | solution.py:66
  89.1 1.6 %collective-permute-start.4 = (bf16[128,2048]{1,0:T(8,128)(2,1)S(1)}, bf16[128,2048]{1,0:T(8,128)(2,1)S(1)}, u32[]{:S(2)}, u32[]{:S(2)}) collective-permute-start(bf16[128,2048]{1,0:T(8,128)(2,1)S(1)} %fusion.5), channel_id=1, source_target_pairs={{0,1},{1,2},{2,3},{3,0},{4,5},{5,6},{6,7},{7,4},{8,9},{9,10},{10,1... | collective-permute-start | bytes 1572872 | tf_op jit(solution)/shard_map/ppermute | solution.py:19
  91.5 1.7 %collective-permute-start.6 = (bf16[128,2048]{1,0:T(8,128)(2,1)S(1)}, bf16[128,2048]{1,0:T(8,128)(2,1)S(1)}, u32[]{:S(2)}, u32[]{:S(2)}) collective-permute-start(bf16[128,2048]{1,0:T(8,128)(2,1)S(1)} %fusion.8), channel_id=1, source_target_pairs={{0,3},{1,0},{2,1},{3,2},{4,7},{5,4},{6,5},{7,6},{8,11},{9,8},{10,9... | collective-permute-start | bytes 1572872 | tf_op jit(solution)/shard_map/ppermute | solution.py:19
  97.3 1.3 convolution_convert_fusion
  101.5 2.1 %collective-permute-done.4 = bf16[128,2048]{1,0:T(8,128)(2,1)S(1)} collective-permute-done((bf16[128,2048]{1,0:T(8,128)(2,1)S(1)}, bf16[128,2048]{1,0:T(8,128)(2,1)S(1)}, u32[]{:S(2)}, u32[]{:S(2)}) %collective-permute-start.4) | collective-permute-done | bytes 524320 | tf_op jit(solution)/shard_map/ppermute | solution.py:19
  104.7 3.0 %collective-permute-start.7 = (bf16[128,4096]{1,0:T(8,128)(2,1)S(1)}, bf16[128,4096]{1,0:T(8,128)(2,1)S(1)}, u32[]{:S(2)}, u32[]{:S(2)}) collective-permute-start(bf16[128,4096]{1,0:T(8,128)(2,1)S(1)} %pad_maximum_fusion.1), channel_id=1, source_target_pairs={{0,3},{1,0},{2,1},{3,2},{4,7},{5,4},{6,5},{7,6},{8,11},{9,8},{10,9... | collective-permute-start | bytes 3145736 | tf_op jit(solution)/shard_map/ppermute | solution.py:19
  109.7 18.9 %collective-permute-done.5 = bf16[128,4096]{1,0:T(8,128)(2,1)S(1)} collective-permute-done((bf16[128,4096]{1,0:T(8,128)(2,1)S(1)}, bf16[128,4096]{1,0:T(8,128)(2,1)S(1)}, u32[]{:S(2)}, u32[]{:S(2)}) %collective-permute-start.5) | collective-permute-done | bytes 1048608 | tf_op jit(solution)/shard_map/ppermute | solution.py:19
  128.7 1.4 %add_convert_fusion = bf16[128,4096]{1,0:T(8,128)(2,1)} fusion(bf16[128,4096]{1,0:T(8,128)(2,1)S(1)} %collective-permute-done.7, f32[128,4096]{1,0:T(8,128)S(1)} %fusion, bf16[128,4096]{1,0:T(8,128)(2,1)S(1)} %collective-permute-done.5), kind=kLoop, calls=%fused_computation.10 | loop fusion | flops 2621440 | bytes 5242880 | tf_op jit(solution)/shard_map/convert_element_type | solution.py:106
  (149 shorter events, 39.0 us)
Async XLA Ops:
  4.0 3.4 %copy-start.7 = (bf16[512,1024]{1,0:T(8,128)(2,1)S(1)}, bf16[512,1024]{1,0:T(8,128)(2,1)}, u32[]{:S(2)}) copy-start(bf16[512,1024]{1,0:T(8,128)(2,1)} %param.4) | copy-start | bytes 3145732
  4.0 27.8 %collective-permute-start = (bf16[2,512,1024]{1,2,0:T(8,128)(2,1)}, bf16[2,512,1024]{1,2,0:T(8,128)(2,1)}, u32[]{:S(2)}, u32[]{:S(2)}) collective-permute-start(bf16[2,512,1024]{1,2,0:T(8,128)(2,1)} %copy.14), channel_id=1, source_target_pairs={{0,4},{4,8},{8,12},{12,16},{16,20},{20,24},{24,28},{28,32},{32,36}... | collective-permute-start | bytes 6291464 | tf_op jit(solution)/shard_map/ppermute | solution.py:14
  8.4 5.1 %copy-start.4 = (bf16[128,1024]{0,1:T(8,128)(2,1)}, bf16[128,1024]{0,1:T(8,128)(2,1)S(1)}, u32[]{:S(2)}) copy-start(bf16[128,1024]{0,1:T(8,128)(2,1)S(1)} %copy.93) | copy-start | bytes 786436
  8.6 4.9 %copy-start.2 = (bf16[128,1024]{0,1:T(8,128)(2,1)}, bf16[128,1024]{0,1:T(8,128)(2,1)S(1)}, u32[]{:S(2)}) copy-start(bf16[128,1024]{0,1:T(8,128)(2,1)S(1)} %copy.94) | copy-start | bytes 786436
  8.8 4.7 %copy-start.26 = (s32[128]{0:T(128)}, s32[128]{0:T(128)S(1)}, u32[]{:S(2)}) copy-start(s32[128]{0:T(128)S(1)} %get-tuple-element.107) | copy-start | bytes 1540
  8.8 4.7 %copy-start.27 = (s32[128]{0:T(128)}, s32[128]{0:T(128)S(1)}, u32[]{:S(2)}) copy-start(s32[128]{0:T(128)S(1)} %get-tuple-element.108) | copy-start | bytes 1540
  9.3 4.1 %copy-start.28 = (s32[128]{0:T(128)}, s32[128]{0:T(128)S(1)}, u32[]{:S(2)}) copy-start(s32[128]{0:T(128)S(1)} %get-tuple-element.109) | copy-start | bytes 1540
  10.0 3.5 %copy-start.22 = (s32[128]{0:T(128)}, s32[128]{0:T(128)S(1)}, u32[]{:S(2)}) copy-start(s32[128]{0:T(128)S(1)} %get-tuple-element.41) | copy-start | bytes 1540
  10.0 3.5 %copy-start.23 = (s32[128]{0:T(128)}, s32[128]{0:T(128)S(1)}, u32[]{:S(2)}) copy-start(s32[128]{0:T(128)S(1)} %get-tuple-element.42) | copy-start | bytes 1540
  10.0 3.5 %copy-start.25 = (s32[128]{0:T(128)}, s32[128]{0:T(128)S(1)}, u32[]{:S(2)}) copy-start(s32[128]{0:T(128)S(1)} %get-tuple-element.111) | copy-start | bytes 1540
  11.6 3.8 %copy-start.12 = (pred[128,512]{1,0:T(8,128)(4,1)}, pred[128,512]{1,0:T(8,128)(4,1)S(1)}, u32[]{:S(2)}) copy-start(pred[128,512]{1,0:T(8,128)(4,1)S(1)} %get-tuple-element.59) | copy-start | bytes 196612
  11.6 3.8 %copy-start.15 = (pred[128,512]{1,0:T(8,128)(4,1)}, pred[128,512]{1,0:T(8,128)(4,1)S(1)}, u32[]{:S(2)}) copy-start(pred[128,512]{1,0:T(8,128)(4,1)S(1)} %get-tuple-element.60) | copy-start | bytes 196612
  31.8 33.3 %collective-permute-start.1 = (bf16[2,512,1024]{1,2,0:T(8,128)(2,1)}, bf16[2,512,1024]{1,2,0:T(8,128)(2,1)}, u32[]{:S(2)}, u32[]{:S(2)}) collective-permute-start(bf16[2,512,1024]{1,2,0:T(8,128)(2,1)} %collective-permute-done), channel_id=1, source_target_pairs={{0,4},{4,8},{8,12},{12,16},{16,20},{20,24},{24,28},{28,32},{32,36}... | collective-permute-start | bytes 6291464 | tf_op jit(solution)/shard_map/ppermute | solution.py:14
  44.2 6.0 %copy-start.5 = (bf16[128,1024]{0,1:T(8,128)(2,1)S(1)}, bf16[128,1024]{0,1:T(8,128)(2,1)}, u32[]{:S(2)}) copy-start(bf16[128,1024]{0,1:T(8,128)(2,1)} %copy-done.4) | copy-start | bytes 786436
  44.2 6.0 %copy-start.11 = (pred[128,512]{1,0:T(8,128)(4,1)S(1)}, pred[128,512]{1,0:T(8,128)(4,1)}, u32[]{:S(2)}) copy-start(pred[128,512]{1,0:T(8,128)(4,1)} %get-tuple-element.61) | copy-start | bytes 196612
  44.2 28.7 %collective-permute-start.2 = (bf16[2,128,1024]{1,2,0:T(8,128)(2,1)S(1)}, bf16[2,128,1024]{1,2,0:T(8,128)(2,1)S(1)}, u32[]{:S(2)}, u32[]{:S(2)}) collective-permute-start(bf16[2,128,1024]{1,2,0:T(8,128)(2,1)S(1)} %slice.91), channel_id=1, source_target_pairs={{0,8},{8,16},{16,24},{24,32},{32,40},{40,48},{48,56},{56,64},{64,7... | collective-permute-start | bytes 1572872 | tf_op jit(solution)/shard_map/ppermute | solution.py:33
  66.1 3.8 %copy-start.19 = (pred[128,512]{1,0:T(8,128)(4,1)S(1)}, pred[128,512]{1,0:T(8,128)(4,1)}, u32[]{:S(2)}) copy-start(pred[128,512]{1,0:T(8,128)(4,1)} %get-tuple-element.68) | copy-start | bytes 196612
  66.1 6.8 %collective-permute-start.3 = (bf16[2,128,1024]{1,2,0:T(8,128)(2,1)S(1)}, bf16[2,128,1024]{1,2,0:T(8,128)(2,1)S(1)}, u32[]{:S(2)}, u32[]{:S(2)}) collective-permute-start(bf16[2,128,1024]{1,2,0:T(8,128)(2,1)S(1)} %slice.92), channel_id=1, source_target_pairs={{0,4},{8,12},{16,20},{24,28},{32,36},{40,44},{48,52},{56,60},{64,6... | collective-permute-start | bytes 1572872 | tf_op jit(solution)/shard_map/ppermute | solution.py:34
  76.6 2.9 %slice-start = ((s8[8388608]{0:T(1024)(128)(4,1)}), s8[4194304]{0:T(1024)(128)(4,1)S(1)}, s32[]{:S(2)}) async-start(s8[8388608]{0:T(1024)(128)(4,1)} %bitcast.352), calls=%async_computation | async-start | bytes 8388608
  89.1 4.1 %copy-start.10 = (pred[128,512]{1,0:T(8,128)(4,1)S(1)}, pred[128,512]{1,0:T(8,128)(4,1)}, u32[]{:S(2)}) copy-start(pred[128,512]{1,0:T(8,128)(4,1)} %get-tuple-element.69) | copy-start | bytes 196612
  89.1 14.5 %collective-permute-start.4 = (bf16[128,2048]{1,0:T(8,128)(2,1)S(1)}, bf16[128,2048]{1,0:T(8,128)(2,1)S(1)}, u32[]{:S(2)}, u32[]{:S(2)}) collective-permute-start(bf16[128,2048]{1,0:T(8,128)(2,1)S(1)} %fusion.5), channel_id=1, source_target_pairs={{0,1},{1,2},{2,3},{3,0},{4,5},{5,6},{6,7},{7,4},{8,9},{9,10},{10,1... | collective-permute-start | bytes 1572872 | tf_op jit(solution)/shard_map/ppermute | solution.py:19
  91.5 13.0 %collective-permute-start.6 = (bf16[128,2048]{1,0:T(8,128)(2,1)S(1)}, bf16[128,2048]{1,0:T(8,128)(2,1)S(1)}, u32[]{:S(2)}, u32[]{:S(2)}) collective-permute-start(bf16[128,2048]{1,0:T(8,128)(2,1)S(1)} %fusion.8), channel_id=1, source_target_pairs={{0,3},{1,0},{2,1},{3,2},{4,7},{5,4},{6,5},{7,6},{8,11},{9,8},{10,9... | collective-permute-start | bytes 1572872 | tf_op jit(solution)/shard_map/ppermute | solution.py:19
  103.8 24.8 %collective-permute-start.5 = (bf16[128,4096]{1,0:T(8,128)(2,1)S(1)}, bf16[128,4096]{1,0:T(8,128)(2,1)S(1)}, u32[]{:S(2)}, u32[]{:S(2)}) collective-permute-start(bf16[128,4096]{1,0:T(8,128)(2,1)S(1)} %pad_maximum_fusion), channel_id=1, source_target_pairs={{0,1},{1,2},{2,3},{3,0},{4,5},{5,6},{6,7},{7,4},{8,9},{9,10},{10,1... | collective-permute-start | bytes 3145736 | tf_op jit(solution)/shard_map/ppermute | solution.py:19
  104.7 24.0 %collective-permute-start.7 = (bf16[128,4096]{1,0:T(8,128)(2,1)S(1)}, bf16[128,4096]{1,0:T(8,128)(2,1)S(1)}, u32[]{:S(2)}, u32[]{:S(2)}) collective-permute-start(bf16[128,4096]{1,0:T(8,128)(2,1)S(1)} %pad_maximum_fusion.1), channel_id=1, source_target_pairs={{0,3},{1,0},{2,1},{3,2},{4,7},{5,4},{6,5},{7,6},{8,11},{9,8},{10,9... | collective-permute-start | bytes 3145736 | tf_op jit(solution)/shard_map/ppermute | solution.py:19
  (15 other events, 19.9 us)

commit v16 on v11

--- a/solution.py
+++ b/solution.py
@@ -92,8 +92,11 @@
     assert groups == 4
     cols = w_out.shape[1] // 2
     far_state, fold = chunk_state((h + 2) % groups, [(r2, offsets[1])])
+    peers = lax.axis_size("ctx")
+    tail_even = lax.ppermute(r1[:, rows - tail:], "ctx", [(i, i + 2) for i in range(0, peers - 2, 2)])
     relay, far_state = lax.optimization_barrier((r2[:, rows - tail:], far_state))
-    r3 = shift_up(relay, "ctx")
+    tail_odd = lax.ppermute(relay, "ctx", [(i, i + 1) for i in range(0, peers - 1, 2)])
+    r3 = jnp.where(me % 2 == 0, tail_even, tail_odd)
     far = finish(fold(far_state, r3, offsets[0]))
     via_left = rotate(far[:, :cols], "head", groups - 1)
     via_right = rotate(far[:, cols:], "head", 1)

time: 154 us -> 154 us (level)
  waiting for transfers between devices: 54.2 us -> 48.8 us
  starting transfers between devices: 12.7 us -> 16.5 us
    ppermute x0 -> x2, starting transfers between devices: none -> 6.27 us  [the longest x1 4.28 us: per_device(): lax.ppermute(r1[:, rows - tail:], 'ctx', [(i, i + 2) for i in range(0, pe...]
    ppermute x4, waiting for transfers between devices: 25.8 us -> 22.7 us  [rotate(): return lax.ppermute(x, axis, [(i, (i + by) % peers) for i in range(peers)])]
    ppermute x3 -> x2, waiting for transfers between devices: 28.5 us -> 26.1 us  [shift_up(): return lax.ppermute(x, axis, [(i, i + 1) for i in range(peers - 1)])]
    ppermute x3 -> x2, starting transfers between devices: 6.05 us -> 3.95 us  [shift_up(): return lax.ppermute(x, axis, [(i, i + 1) for i in range(peers - 1)])]
  transfers between devices with their start and end apart: 7 -> 8, of which waited for: 6 -> 5; matrix products, arithmetic and copies ran while one was open for 27% -> 33% of each run, Pallas kernels for 0% -> 0%
where the time goes in v16:
time: 154 us; the launch traced here: 153 us
  waiting for transfers between devices  48.8 us (32%)
  matrix products  44.6 us (29%)
  local copies, waits for them, and re-layouts  22 us (14%)
  other arithmetic  20 us (13%)
  starting transfers between devices  16.5 us (11%)
    ppermute x2, waiting for transfers between devices, shift_up(): return lax.ppermute(x, axis, [(i, i + 1) for i in range(peers - 1)])  26.1 us
    ppermute x4, waiting for transfers between devices, rotate(): return lax.ppermute(x, axis, [(i, (i + by) % peers) for i in range(peers)])  22.7 us
    dot_general x16, matrix products, scores(): jnp.einsum('qhd,khd->hqk', q, k, preferred_element_type=jnp.float32) * scale  21.1 us
    dot_general x16, matrix products, stage(): jnp.einsum('hqk,khd->qhd', probs, kv[1].reshape(n, heads, HD), preferred_...  14.5 us
    unnamed x149, local copies, waits for them, and re-layouts  11.9 us
    reduce_sum x11, other arithmetic, stage(): t = jnp.sum(weights, axis=2)  9.46 us
    dot_general x4, matrix products, finish(): jnp.dot(attended, w_out, preferred_element_type=jnp.float32)  8.92 us
    ppermute x4, starting transfers between devices, rotate(): return lax.ppermute(x, axis, [(i, (i + by) % peers) for i in range(peers)])  6.25 us
  transfers between devices with their start and end apart: 8, of which 5 were waited for; matrix products, arithmetic and copies ran while one was open for 33% of the time, Pallas kernels for 0%

profile of v16, /device:TPU:98, one launch (start us, length us, event | category | flops | bytes accessed | tf_op | source)
XLA Modules:
  0.0 153.2 jit_solution(9914357780777313720)
XLA Ops:
  0.0 4.0 %copy.21 = bf16[2,512,1024]{1,2,0:T(8,128)(2,1)} copy(bf16[2,512,1024]{2,1,0:T(8,128)(2,1)} %param.5) | data formatting | bytes 4194304 | tf_op args[1]
  4.0 2.0 %collective-permute-start = (bf16[2,512,1024]{1,2,0:T(8,128)(2,1)}, bf16[2,512,1024]{1,2,0:T(8,128)(2,1)}, u32[]{:S(2)}, u32[]{:S(2)}) collective-permute-start(bf16[2,512,1024]{1,2,0:T(8,128)(2,1)} %copy.21), channel_id=1, source_target_pairs={{0,4},{4,8},{8,12},{12,16},{16,20},{20,24},{24,28},{28,32},{32,36}... | collective-permute-start | bytes 6291464 | tf_op jit(solution)/shard_map/ppermute | solution.py:14
  9.8 2.7 %fusion.208 = (bf16[1,512,1024]{1,2,0:T(8,128)(2,1)}, bf16[1,512,1024]{1,2,0:T(8,128)(2,1)S(1)}) fusion(bf16[2,512,1024]{1,2,0:T(8,128)(2,1)} %copy.21), kind=kLoop, calls=%fused_computation.312 | loop fusion | bytes 4194304 | tf_op jit(solution)/shard_map/slice | solution.py:63
  12.6 1.9 %fusion.5 = (f32[8,128]{1,0:T(8,128)S(1)}, f32[8,128,512]{2,1,0:T(8,128)}) fusion(pred[128,512]{1,0:T(8,128)(4,1)S(1)} %get-tuple-element.72, bf16[128,8,128]{0,2,1:T(8,128)(2,1)S(1)} %bitcast.359, bf16[512,8,128]{0,2,1:T(8,128)(2,1)S(1)} %bitcast.335), kind=kOutput, calls=%fused_computation.34 | convolution fusion | flops 135789568 | bytes 3477504 | tf_op jit(solution)/shard_map/qhd,khd->hqk/dot_general | solution.py:49
  14.5 2.5 %fusion.11 = (f32[8,128]{1,0:T(8,128)}, f32[8,128,512]{2,1,0:T(8,128)}) fusion(pred[128,512]{1,0:T(8,128)(4,1)S(1)} %get-tuple-element.81, bf16[128,8,128]{0,2,1:T(8,128)(2,1)S(1)} %bitcast.363, bf16[512,8,128]{0,2,1:T(8,128)(2,1)S(1)} %bitcast.336), kind=kOutput, calls=%fused_computation.40 | convolution fusion | flops 135789568 | bytes 3477504 | tf_op jit(solution)/shard_map/qhd,khd->hqk/dot_general | solution.py:49
  18.2 13.6 %collective-permute-done = bf16[2,512,1024]{1,2,0:T(8,128)(2,1)} collective-permute-done((bf16[2,512,1024]{1,2,0:T(8,128)(2,1)}, bf16[2,512,1024]{1,2,0:T(8,128)(2,1)}, u32[]{:S(2)}, u32[]{:S(2)}) %collective-permute-start) | collective-permute-done | bytes 2097184 | tf_op jit(solution)/shard_map/ppermute | solution.py:14
  31.8 1.9 %collective-permute-start.1 = (bf16[2,512,1024]{1,2,0:T(8,128)(2,1)}, bf16[2,512,1024]{1,2,0:T(8,128)(2,1)}, u32[]{:S(2)}, u32[]{:S(2)}) collective-permute-start(bf16[2,512,1024]{1,2,0:T(8,128)(2,1)} %collective-permute-done), channel_id=1, source_target_pairs={{0,4},{4,8},{8,12},{12,16},{16,20},{20,24},{24,28},{28,32},{32,36}... | collective-permute-start | bytes 6291464 | tf_op jit(solution)/shard_map/ppermute | solution.py:14
  34.3 1.8 %copy.110 = bf16[128,1024]{0,1:T(8,128)(2,1)} copy(bf16[128,1024]{1,0:T(8,128)(2,1)} %get-tuple-element.41) | data formatting | bytes 524288
  36.9 2.8 %fusion.8 = (f32[8,128]{1,0:T(8,128)S(1)}, f32[8,128,512]{2,1,0:T(8,128)}) fusion(pred[128,512]{1,0:T(8,128)(4,1)} %get-tuple-element.71, bf16[128,8,128]{0,2,1:T(8,128)(2,1)} %bitcast.367, bf16[512,8,128]{0,2,1:T(8,128)(2,1)S(1)} %bitcast.338), kind=kOutput, calls=%fused_computation.37 | convolution fusion | flops 135789568 | bytes 3477504 | tf_op jit(solution)/shard_map/qhd,khd->hqk/dot_general | solution.py:49
  40.9 4.3 %collective-permute-start.2 = (bf16[2,128,1024]{1,2,0:T(8,128)(2,1)S(1)}, bf16[2,128,1024]{1,2,0:T(8,128)(2,1)S(1)}, u32[]{:S(2)}, u32[]{:S(2)}) collective-permute-start(bf16[2,128,1024]{1,2,0:T(8,128)(2,1)S(1)} %slice.91), channel_id=1, source_target_pairs={{0,8},{8,16},{16,24},{24,32},{32,40},{40,48},{48,56},{56,64},{64,7... | collective-permute-start | bytes 1572872 | tf_op jit(solution)/shard_map/ppermute | solution.py:96
  48.7 2.0 %fusion.1 = (f32[8,128]{1,0:T(8,128)S(1)}, f32[8,128,512]{2,1,0:T(8,128)}) fusion(pred[128,512]{1,0:T(8,128)(4,1)S(1)} %get-tuple-element.76, bf16[128,8,128]{0,2,1:T(8,128)(2,1)S(1)} %bitcast.356, bf16[512,8,128]{0,2,1:T(8,128)(2,1)S(1)} %bitcast.345), kind=kOutput, calls=%fused_computation.30 | convolution fusion | flops 135789568 | bytes 3477504 | tf_op jit(solution)/shard_map/qhd,khd->hqk/dot_general | solution.py:49
  50.7 1.9 %fusion.7 = (f32[8,128]{1,0:T(8,128)S(1)}, f32[8,128,512]{2,1,0:T(8,128)}) fusion(pred[128,512]{1,0:T(8,128)(4,1)S(1)} %copy-done.21, bf16[128,8,128]{0,2,1:T(8,128)(2,1)S(1)} %bitcast.368, bf16[512,8,128]{0,2,1:T(8,128)(2,1)S(1)} %bitcast.346), kind=kOutput, calls=%fused_computation.36 | convolution fusion | flops 135789568 | bytes 3477504 | tf_op jit(solution)/shard_map/qhd,khd->hqk/dot_general | solution.py:49
  52.6 12.5 %collective-permute-done.1 = bf16[2,512,1024]{1,2,0:T(8,128)(2,1)} collective-permute-done((bf16[2,512,1024]{1,2,0:T(8,128)(2,1)}, bf16[2,512,1024]{1,2,0:T(8,128)(2,1)}, u32[]{:S(2)}, u32[]{:S(2)}) %collective-permute-start.1) | collective-permute-done | bytes 2097184 | tf_op jit(solution)/shard_map/ppermute | solution.py:14
  69.7 1.9 %fusion.16 = (f32[8,128]{1,0:T(8,128)S(1)}, f32[8,128]{1,0:T(8,128)S(1)}, f32[8,128]{1,0:T(8,128)S(1)}) fusion(f32[8,128,512]{2,1,0:T(8,128)S(1)} %copy-done.8, f32[8,128]{1,0:T(8,128)S(1)} %get-tuple-element.34, pred[128,512]{1,0:T(8,128)(4,1)S(1)} %copy-done.30, f32[8,128,512]{2,1,0:T(8,128)S(1)} %get-tuple-element.92, pred[128,512]{1,0:T(8,128)(4,1)S(1)} %copy-done.28, ...), kind=kLoop, calls=%fused_computation.45 | loop fusion | flops 6288384 | bytes 6508544 | tf_op jit(solution)/shard_map/reduce_sum | solution.py:61
  74.4 2.0 %collective-permute-start.3 = (bf16[2,128,1024]{1,2,0:T(8,128)(2,1)S(1)}, bf16[2,128,1024]{1,2,0:T(8,128)(2,1)S(1)}, u32[]{:S(2)}, u32[]{:S(2)}) collective-permute-start(bf16[2,128,1024]{1,2,0:T(8,128)(2,1)S(1)} %slice.92), channel_id=1, source_target_pairs={{0,4},{8,12},{16,20},{24,28},{32,36},{40,44},{48,52},{56,60},{64,6... | collective-permute-start | bytes 1572872 | tf_op jit(solution)/shard_map/ppermute | solution.py:98
  76.4 1.9 %fusion.12 = (f32[8,128]{1,0:T(8,128)S(1)}, f32[8,128,512]{2,1,0:T(8,128)}) fusion(pred[128,512]{1,0:T(8,128)(4,1)S(1)} %copy-done.35, bf16[128,8,128]{0,2,1:T(8,128)(2,1)S(1)} %bitcast.365, bf16[512,8,128]{0,2,1:T(8,128)(2,1)S(1)} %bitcast.340), kind=kOutput, calls=%fused_computation.41 | convolution fusion | flops 135789568 | bytes 3477504 | tf_op jit(solution)/shard_map/qhd,khd->hqk/dot_general | solution.py:49
  78.3 1.9 %fusion.3 = (f32[8,128]{1,0:T(8,128)S(1)}, f32[8,128,512]{2,1,0:T(8,128)}) fusion(pred[128,512]{1,0:T(8,128)(4,1)S(1)} %copy-done.31, bf16[128,8,128]{0,2,1:T(8,128)(2,1)S(1)} %bitcast.357, bf16[512,8,128]{0,2,1:T(8,128)(2,1)S(1)} %bitcast.341), kind=kOutput, calls=%fused_computation.32 | convolution fusion | flops 135789568 | bytes 3477504 | tf_op jit(solution)/shard_map/qhd,khd->hqk/dot_general | solution.py:49
  80.1 1.9 %fusion.9 = (f32[8,128]{1,0:T(8,128)S(1)}, f32[8,128,512]{2,1,0:T(8,128)}) fusion(pred[128,512]{1,0:T(8,128)(4,1)S(1)} %copy-done.33, bf16[128,8,128]{0,2,1:T(8,128)(2,1)S(1)} %bitcast.369, bf16[512,8,128]{0,2,1:T(8,128)(2,1)S(1)} %bitcast.342), kind=kOutput, calls=%fused_computation.38 | convolution fusion | flops 135789568 | bytes 3477504 | tf_op jit(solution)/shard_map/qhd,khd->hqk/dot_general | solution.py:49
  97.0 2.8 %fusion.52 = f32[128,8,128]{0,2,1:T(8,128)S(1)} fusion(f32[8,128,128]{1,2,0:T(8,128)} %fusion.66, bf16[512,8,128]{0,2,1:T(8,128)(2,1)} %bitcast.381, f32[8,128,512]{2,1,0:T(8,128)} %copy-done.4, f32[8,128]{1,0:T(8,128)} %copy-done.42, pred[128,512]{1,0:T(8,128)(4,1)} %get-tuple-element.75, f32[128,8]{0,1:T(8,128)} %fusion.166), kind=kOutput, calls=%fused_computation.97 | convolution fusion | flops 136577024 | bytes 4268032 | tf_op jit(solution)/shard_map/hqk,khd->qhd/dot_general | solution.py:63
  102.1 5.1 %convolution_convert_fusion = bf16[128,4096]{1,0:T(8,128)(2,1)S(1)} fusion(bf16[128,1024]{0,1:T(8,128)(2,1)S(1)} %bitcast.384, bf16[1024,4096]{1,0:T(8,128)(2,1)} %param.6), kind=kOutput, calls=%fused_computation | convolution fusion | flops 1074266112 | bytes 9699328 | tf_op jit(solution)/shard_map/dot_general | solution.py:86
  108.8 3.1 %collective-permute-start.6 = (bf16[128,2048]{1,0:T(8,128)(2,1)S(1)}, bf16[128,2048]{1,0:T(8,128)(2,1)S(1)}, u32[]{:S(2)}, u32[]{:S(2)}) collective-permute-start(bf16[128,2048]{1,0:T(8,128)(2,1)S(1)} %get-tuple-element.46), channel_id=1, source_target_pairs={{0,3},{1,0},{2,1},{3,2},{4,7},{5,4},{6,5},{7,6},{8,11},{9,8},{10,9... | collective-permute-start | bytes 1572872 | tf_op jit(solution)/shard_map/ppermute | solution.py:19
  124.0 2.8 %collective-permute-start.7 = (bf16[128,4096]{1,0:T(8,128)(2,1)S(1)}, bf16[128,4096]{1,0:T(8,128)(2,1)S(1)}, u32[]{:S(2)}, u32[]{:S(2)}) collective-permute-start(bf16[128,4096]{1,0:T(8,128)(2,1)S(1)} %pad_maximum_fusion.1), channel_id=1, source_target_pairs={{0,3},{1,0},{2,1},{3,2},{4,7},{5,4},{6,5},{7,6},{8,11},{9,8},{10,9... | collective-permute-start | bytes 3145736 | tf_op jit(solution)/shard_map/ppermute | solution.py:19
  129.4 18.8 %collective-permute-done.7 = bf16[128,4096]{1,0:T(8,128)(2,1)S(1)} collective-permute-done((bf16[128,4096]{1,0:T(8,128)(2,1)S(1)}, bf16[128,4096]{1,0:T(8,128)(2,1)S(1)}, u32[]{:S(2)}, u32[]{:S(2)}) %collective-permute-start.7) | collective-permute-done | bytes 1048608 | tf_op jit(solution)/shard_map/ppermute | solution.py:19
  148.2 3.7 %collective-permute-done.5 = bf16[128,4096]{1,0:T(8,128)(2,1)S(1)} collective-permute-done((bf16[128,4096]{1,0:T(8,128)(2,1)S(1)}, bf16[128,4096]{1,0:T(8,128)(2,1)S(1)}, u32[]{:S(2)}, u32[]{:S(2)}) %collective-permute-start.5) | collective-permute-done | bytes 1048608 | tf_op jit(solution)/shard_map/ppermute | solution.py:19
  (236 shorter events, 52.1 us)
Async XLA Ops:
  0.0 6.2 %copy-start.14 = (bf16[512,1024]{1,0:T(8,128)(2,1)S(1)}, bf16[512,1024]{1,0:T(8,128)(2,1)}, u32[]{:S(2)}) copy-start(bf16[512,1024]{1,0:T(8,128)(2,1)} %param.4) | copy-start | bytes 3145732
  4.0 27.8 %collective-permute-start = (bf16[2,512,1024]{1,2,0:T(8,128)(2,1)}, bf16[2,512,1024]{1,2,0:T(8,128)(2,1)}, u32[]{:S(2)}, u32[]{:S(2)}) collective-permute-start(bf16[2,512,1024]{1,2,0:T(8,128)(2,1)} %copy.21), channel_id=1, source_target_pairs={{0,4},{4,8},{8,12},{12,16},{16,20},{20,24},{24,28},{28,32},{32,36}... | collective-permute-start | bytes 6291464 | tf_op jit(solution)/shard_map/ppermute | solution.py:14
  7.0 5.5 %copy-start.68 = (s32[128]{0:T(128)}, s32[128]{0:T(128)S(1)}, u32[]{:S(2)}) copy-start(s32[128]{0:T(128)S(1)} %iota_add_fusion.2) | copy-start | bytes 1540
  7.2 5.3 %copy-start.9 = (bf16[128,1024]{0,1:T(8,128)(2,1)}, bf16[128,1024]{0,1:T(8,128)(2,1)S(1)}, u32[]{:S(2)}) copy-start(bf16[128,1024]{0,1:T(8,128)(2,1)S(1)} %copy.109) | copy-start | bytes 786436
  7.4 7.1 %copy-start.11 = (bf16[128,1024]{0,1:T(8,128)(2,1)}, bf16[128,1024]{0,1:T(8,128)(2,1)S(1)}, u32[]{:S(2)}) copy-start(bf16[128,1024]{0,1:T(8,128)(2,1)S(1)} %copy.111) | copy-start | bytes 786436
  31.8 33.3 %collective-permute-start.1 = (bf16[2,512,1024]{1,2,0:T(8,128)(2,1)}, bf16[2,512,1024]{1,2,0:T(8,128)(2,1)}, u32[]{:S(2)}, u32[]{:S(2)}) collective-permute-start(bf16[2,512,1024]{1,2,0:T(8,128)(2,1)} %collective-permute-done), channel_id=1, source_target_pairs={{0,4},{4,8},{8,12},{12,16},{16,20},{20,24},{24,28},{28,32},{32,36}... | collective-permute-start | bytes 6291464 | tf_op jit(solution)/shard_map/ppermute | solution.py:14
  40.8 6.0 %copy-start.10 = (bf16[128,1024]{0,1:T(8,128)(2,1)S(1)}, bf16[128,1024]{0,1:T(8,128)(2,1)}, u32[]{:S(2)}) copy-start(bf16[128,1024]{0,1:T(8,128)(2,1)} %copy-done.9) | copy-start | bytes 786436
  40.9 6.0 %copy-start.28 = (pred[128,512]{1,0:T(8,128)(4,1)S(1)}, pred[128,512]{1,0:T(8,128)(4,1)}, u32[]{:S(2)}) copy-start(pred[128,512]{1,0:T(8,128)(4,1)} %get-tuple-element.74) | copy-start | bytes 196612
  40.9 41.2 %collective-permute-start.2 = (bf16[2,128,1024]{1,2,0:T(8,128)(2,1)S(1)}, bf16[2,128,1024]{1,2,0:T(8,128)(2,1)S(1)}, u32[]{:S(2)}, u32[]{:S(2)}) collective-permute-start(bf16[2,128,1024]{1,2,0:T(8,128)(2,1)S(1)} %slice.91), channel_id=1, source_target_pairs={{0,8},{8,16},{16,24},{24,32},{32,40},{40,48},{48,56},{56,64},{64,7... | collective-permute-start | bytes 1572872 | tf_op jit(solution)/shard_map/ppermute | solution.py:96
  46.8 24.8 %copy-start.19 = (bf16[1,512,1024]{1,2,0:T(8,128)(2,1)}, bf16[1,512,1024]{1,2,0:T(8,128)(2,1)S(1)}, u32[]{:S(2)}) copy-start(bf16[1,512,1024]{1,2,0:T(8,128)(2,1)S(1)} %get-tuple-element.37) | copy-start | bytes 3145732
  48.6 46.0 %copy-start.4 = (f32[8,128,512]{2,1,0:T(8,128)}, f32[8,128,512]{2,1,0:T(8,128)S(1)}, u32[]{:S(2)}) copy-start(f32[8,128,512]{2,1,0:T(8,128)S(1)} %get-tuple-element.102) | copy-start | bytes 6291460
  52.6 14.2 %copy-start.27 = (pred[128,512]{1,0:T(8,128)(4,1)S(1)}, pred[128,512]{1,0:T(8,128)(4,1)}, u32[]{:S(2)}) copy-start(pred[128,512]{1,0:T(8,128)(4,1)} %get-tuple-element.79) | copy-start | bytes 196612
  66.8 5.7 %copy-start.15 = (bf16[1,512,1024]{1,2,0:T(8,128)(2,1)}, bf16[1,512,1024]{1,2,0:T(8,128)(2,1)S(1)}, u32[]{:S(2)}) copy-start(bf16[1,512,1024]{1,2,0:T(8,128)(2,1)S(1)} %get-tuple-element.35) | copy-start | bytes 3145732
  74.4 7.7 %collective-permute-start.3 = (bf16[2,128,1024]{1,2,0:T(8,128)(2,1)S(1)}, bf16[2,128,1024]{1,2,0:T(8,128)(2,1)S(1)}, u32[]{:S(2)}, u32[]{:S(2)}) collective-permute-start(bf16[2,128,1024]{1,2,0:T(8,128)(2,1)S(1)} %slice.92), channel_id=1, source_target_pairs={{0,4},{8,12},{16,20},{24,28},{32,36},{40,44},{48,52},{56,60},{64,6... | collective-permute-start | bytes 1572872 | tf_op jit(solution)/shard_map/ppermute | solution.py:98
  83.3 11.3 %copy-start.42 = (f32[8,128]{1,0:T(8,128)}, f32[8,128]{1,0:T(8,128)S(1)}, u32[]{:S(2)}) copy-start(f32[8,128]{1,0:T(8,128)S(1)} %get-tuple-element.30) | copy-start | bytes 12292
  87.0 6.0 %copy-start.2 = (f32[8,128,512]{2,1,0:T(8,128)S(1)}, f32[8,128,512]{2,1,0:T(8,128)}, u32[]{:S(2)}) copy-start(f32[8,128,512]{2,1,0:T(8,128)} %get-tuple-element.100) | copy-start | bytes 6291460
  87.0 6.0 %copy-start.26 = (pred[128,512]{1,0:T(8,128)(4,1)S(1)}, pred[128,512]{1,0:T(8,128)(4,1)}, u32[]{:S(2)}) copy-start(pred[128,512]{1,0:T(8,128)(4,1)} %copy-done.25) | copy-start | bytes 196612
  89.5 5.2 %copy-start.46 = (f32[8,128]{1,0:T(8,128)}, f32[8,128]{1,0:T(8,128)S(1)}, u32[]{:S(2)}) copy-start(f32[8,128]{1,0:T(8,128)S(1)} %get-tuple-element.111) | copy-start | bytes 12292
  101.3 5.9 %slice-start = ((s8[8388608]{0:T(1024)(128)(4,1)}), s8[4194304]{0:T(1024)(128)(4,1)S(1)}, s32[]{:S(2)}) async-start(s8[8388608]{0:T(1024)(128)(4,1)} %bitcast.333), calls=%async_computation | async-start | bytes 8388608
  102.1 5.3 %slice-start.1 = ((s8[8388608]{0:T(1024)(128)(4,1)}), s8[4194304]{0:T(1024)(128)(4,1)S(1)}, s32[]{:S(2)}) async-start(s8[8388608]{0:T(1024)(128)(4,1)} %bitcast.333), calls=%async_computation.1 | async-start | bytes 8388608
  108.8 14.9 %collective-permute-start.6 = (bf16[128,2048]{1,0:T(8,128)(2,1)S(1)}, bf16[128,2048]{1,0:T(8,128)(2,1)S(1)}, u32[]{:S(2)}, u32[]{:S(2)}) collective-permute-start(bf16[128,2048]{1,0:T(8,128)(2,1)S(1)} %get-tuple-element.46), channel_id=1, source_target_pairs={{0,3},{1,0},{2,1},{3,2},{4,7},{5,4},{6,5},{7,6},{8,11},{9,8},{10,9... | collective-permute-start | bytes 1572872 | tf_op jit(solution)/shard_map/ppermute | solution.py:19
  112.6 14.4 %collective-permute-start.4 = (bf16[128,2048]{1,0:T(8,128)(2,1)S(1)}, bf16[128,2048]{1,0:T(8,128)(2,1)S(1)}, u32[]{:S(2)}, u32[]{:S(2)}) collective-permute-start(bf16[128,2048]{1,0:T(8,128)(2,1)S(1)} %get-tuple-element.45), channel_id=1, source_target_pairs={{0,1},{1,2},{2,3},{3,0},{4,5},{5,6},{6,7},{7,4},{8,9},{9,10},{10,1... | collective-permute-start | bytes 1572872 | tf_op jit(solution)/shard_map/ppermute | solution.py:19
  124.0 24.2 %collective-permute-start.7 = (bf16[128,4096]{1,0:T(8,128)(2,1)S(1)}, bf16[128,4096]{1,0:T(8,128)(2,1)S(1)}, u32[]{:S(2)}, u32[]{:S(2)}) collective-permute-start(bf16[128,4096]{1,0:T(8,128)(2,1)S(1)} %pad_maximum_fusion.1), channel_id=1, source_target_pairs={{0,3},{1,0},{2,1},{3,2},{4,7},{5,4},{6,5},{7,6},{8,11},{9,8},{10,9... | collective-permute-start | bytes 3145736 | tf_op jit(solution)/shard_map/ppermute | solution.py:19
  127.2 24.6 %collective-permute-start.5 = (bf16[128,4096]{1,0:T(8,128)(2,1)S(1)}, bf16[128,4096]{1,0:T(8,128)(2,1)S(1)}, u32[]{:S(2)}, u32[]{:S(2)}) collective-permute-start(bf16[128,4096]{1,0:T(8,128)(2,1)S(1)} %pad_maximum_fusion), channel_id=1, source_target_pairs={{0,1},{1,2},{2,3},{3,0},{4,5},{5,6},{6,7},{7,4},{8,9},{9,10},{10,1... | collective-permute-start | bytes 3145736 | tf_op jit(solution)/shard_map/ppermute | solution.py:19
  (56 other events, 128.7 us)

commit v17 on v13

--- a/solution.py
+++ b/solution.py
@@ -68,8 +68,8 @@
                 summed = pv if summed is None else summed + pv
             return top, total, summed
 
-        near = list(zip(sources[2:], offsets[2:]))
-        far = list(zip(sources[:2], offsets[:2]))
+        near = list(zip(sources[1:], offsets[1:]))
+        far = list(zip(sources[:1], offsets[:1]))
         floor = jnp.full((heads, CHUNK, 1), -1e30, jnp.float32)
         top_a, total_a, summed_a = stage(near, floor)
         top, total_b, summed_b = stage(far, top_a)

time: 131 us -> 141 us (1.076)
  matrix products: 27.1 us -> 34.9 us
  waiting for transfers between devices: 48.9 us -> 52 us
  local copies, waits for them, and re-layouts: 22.2 us -> 20.3 us
    ppermute x4, waiting for transfers between devices: 20.8 us -> 25.1 us  [rotate(): return lax.ppermute(x, axis, [(i, (i + by) % peers) for i in range(peers)])]
    dot_general x16, matrix products: 9.78 us -> 14.1 us  [stage(): jnp.einsum('hqk,khd->qhd', probs, kv[1].reshape(n, heads, HD), preferred_...]
    dot_general x16, matrix products: 12.2 us -> 15.6 us  [scores(): jnp.einsum('qhd,khd->hqk', q, k, preferred_element_type=jnp.float32) * scale]
    unnamed x69 -> x105, local copies, waits for them, and re-layouts: 9.03 us -> 7.62 us
    reduce_sum x8 -> x6, other arithmetic: 8.44 us -> 7.83 us  [stage(): t = jnp.sum(weights, axis=2)]
  transfers between devices with their start and end apart: 8 -> 8, of which waited for: 6 -> 6; matrix products, arithmetic and copies ran while one was open for 32% -> 31% of each run, Pallas kernels for 0% -> 0%
where the time goes in v17:
time: 141 us; the launch traced here: 140 us
  waiting for transfers between devices  52 us (37%)
  matrix products  34.9 us (25%)
  local copies, waits for them, and re-layouts  20.3 us (14%)
  starting transfers between devices  17.5 us (12%)
  other arithmetic  14.4 us (10%)
    ppermute x2, waiting for transfers between devices, shift_up(): return lax.ppermute(x, axis, [(i, i + 1) for i in range(peers - 1)])  26.9 us
    ppermute x4, waiting for transfers between devices, rotate(): return lax.ppermute(x, axis, [(i, (i + by) % peers) for i in range(peers)])  25.1 us
    dot_general x16, matrix products, scores(): jnp.einsum('qhd,khd->hqk', q, k, preferred_element_type=jnp.float32) * scale  15.6 us
    dot_general x16, matrix products, stage(): jnp.einsum('hqk,khd->qhd', probs, kv[1].reshape(n, heads, HD), preferred_...  14.1 us
    reduce_sum x6, other arithmetic, stage(): t = jnp.sum(weights, axis=2)  7.83 us
    unnamed x105, local copies, waits for them, and re-layouts  7.62 us
    slice x5, local copies, waits for them, and re-layouts, stage(): kv[1].reshape(n, heads, HD)  7.49 us
    ppermute x4, starting transfers between devices, rotate(): return lax.ppermute(x, axis, [(i, (i + by) % peers) for i in range(peers)])  7.2 us
  transfers between devices with their start and end apart: 8, of which 6 were waited for; matrix products, arithmetic and copies ran while one was open for 31% of the time, Pallas kernels for 0%

profile of v17, /device:TPU:98, one launch (start us, length us, event | category | flops | bytes accessed | tf_op | source)
XLA Modules:
  0.0 140.1 jit_solution(1141242522913611776)
XLA Ops:
  0.0 3.9 %copy.14 = bf16[2,512,1024]{1,2,0:T(8,128)(2,1)} copy(bf16[2,512,1024]{2,1,0:T(8,128)(2,1)} %param.5) | data formatting | bytes 4194304 | tf_op args[1]
  4.0 2.0 %collective-permute-start = (bf16[2,512,1024]{1,2,0:T(8,128)(2,1)}, bf16[2,512,1024]{1,2,0:T(8,128)(2,1)}, u32[]{:S(2)}, u32[]{:S(2)}) collective-permute-start(bf16[2,512,1024]{1,2,0:T(8,128)(2,1)} %copy.14), channel_id=1, source_target_pairs={{0,4},{4,8},{8,12},{12,16},{16,20},{20,24},{24,28},{28,32},{32,36}... | collective-permute-start | bytes 6291464 | tf_op jit(solution)/shard_map/ppermute | solution.py:14
  11.1 1.9 %fusion.12 = (f32[8,128]{1,0:T(8,128)S(1)}, f32[8,128,512]{2,1,0:T(8,128)}) fusion(pred[128,512]{1,0:T(8,128)(4,1)S(1)} %get-tuple-element.67, bf16[128,8,128]{0,2,1:T(8,128)(2,1)S(1)} %bitcast.214, bf16[512,8,128]{0,2,1:T(8,128)(2,1)S(1)} %bitcast.186), kind=kOutput, calls=%fused_computation.41 | convolution fusion | flops 135789568 | bytes 3477504 | tf_op jit(solution)/shard_map/qhd,khd->hqk/dot_general | solution.py:52
  13.0 1.8 %fusion.9 = (f32[8,128]{1,0:T(8,128)S(1)}, f32[8,128,512]{2,1,0:T(8,128)}) fusion(pred[128,512]{1,0:T(8,128)(4,1)S(1)} %get-tuple-element.58, bf16[128,8,128]{0,2,1:T(8,128)(2,1)S(1)} %bitcast.210, bf16[512,8,128]{0,2,1:T(8,128)(2,1)S(1)} %bitcast.187), kind=kOutput, calls=%fused_computation.38 | convolution fusion | flops 135789568 | bytes 3477504 | tf_op jit(solution)/shard_map/qhd,khd->hqk/dot_general | solution.py:52
  16.1 15.6 %collective-permute-done = bf16[2,512,1024]{1,2,0:T(8,128)(2,1)} collective-permute-done((bf16[2,512,1024]{1,2,0:T(8,128)(2,1)}, bf16[2,512,1024]{1,2,0:T(8,128)(2,1)}, u32[]{:S(2)}, u32[]{:S(2)}) %collective-permute-start) | collective-permute-done | bytes 2097184 | tf_op jit(solution)/shard_map/ppermute | solution.py:14
  31.7 1.9 %collective-permute-start.1 = (bf16[2,512,1024]{1,2,0:T(8,128)(2,1)}, bf16[2,512,1024]{1,2,0:T(8,128)(2,1)}, u32[]{:S(2)}, u32[]{:S(2)}) collective-permute-start(bf16[2,512,1024]{1,2,0:T(8,128)(2,1)} %collective-permute-done), channel_id=1, source_target_pairs={{0,4},{4,8},{8,12},{12,16},{16,20},{20,24},{24,28},{28,32},{32,36}... | collective-permute-start | bytes 6291464 | tf_op jit(solution)/shard_map/ppermute | solution.py:14
  35.2 2.4 %copy.24 = bf16[1,512,1024]{1,2,0:T(8,128)(2,1)} copy(bf16[1,512,1024]{2,1,0:T(8,128)(2,1)} %slice.80) | data formatting | bytes 2097152 | tf_op jit(solution)/shard_map/slice | solution.py:66
  37.6 1.8 %copy.93 = bf16[128,1024]{0,1:T(8,128)(2,1)} copy(bf16[128,1024]{1,0:T(8,128)(2,1)} %get-tuple-element.29) | data formatting | bytes 524288
  40.2 2.2 %fusion.6 = (f32[8,128]{1,0:T(8,128)}, f32[8,128,512]{2,1,0:T(8,128)S(1)}) fusion(pred[128,512]{1,0:T(8,128)(4,1)} %get-tuple-element.57, bf16[128,8,128]{0,2,1:T(8,128)(2,1)} %bitcast.218, bf16[512,8,128]{0,2,1:T(8,128)(2,1)S(1)} %bitcast.189), kind=kOutput, calls=%fused_computation.35 | convolution fusion | flops 135789568 | bytes 3477504 | tf_op jit(solution)/shard_map/qhd,khd->hqk/dot_general | solution.py:52
  43.5 4.3 %collective-permute-start.2 = (bf16[2,128,1024]{1,2,0:T(8,128)(2,1)S(1)}, bf16[2,128,1024]{1,2,0:T(8,128)(2,1)S(1)}, u32[]{:S(2)}, u32[]{:S(2)}) collective-permute-start(bf16[2,128,1024]{1,2,0:T(8,128)(2,1)S(1)} %slice.91), channel_id=1, source_target_pairs={{0,8},{8,16},{16,24},{24,32},{32,40},{40,48},{48,56},{56,64},{64,7... | collective-permute-start | bytes 1572872 | tf_op jit(solution)/shard_map/ppermute | solution.py:33
  47.8 1.7 %fusion.202 = (bf16[1,512,1024]{1,2,0:T(8,128)(2,1)S(1)}, bf16[1,512,1024]{1,2,0:T(8,128)(2,1)S(1)}) fusion(bf16[2,512,1024]{1,2,0:T(8,128)(2,1)} %collective-permute-done), kind=kLoop, calls=%fused_computation.279 | loop fusion | bytes 4194304 | tf_op jit(solution)/shard_map/slice | solution.py:66
  53.7 11.3 %collective-permute-done.1 = bf16[2,512,1024]{1,2,0:T(8,128)(2,1)} collective-permute-done((bf16[2,512,1024]{1,2,0:T(8,128)(2,1)}, bf16[2,512,1024]{1,2,0:T(8,128)(2,1)}, u32[]{:S(2)}, u32[]{:S(2)}) %collective-permute-start.1) | collective-permute-done | bytes 2097184 | tf_op jit(solution)/shard_map/ppermute | solution.py:14
  66.1 2.1 %collective-permute-start.3 = (bf16[2,128,1024]{1,2,0:T(8,128)(2,1)S(1)}, bf16[2,128,1024]{1,2,0:T(8,128)(2,1)S(1)}, u32[]{:S(2)}, u32[]{:S(2)}) collective-permute-start(bf16[2,128,1024]{1,2,0:T(8,128)(2,1)S(1)} %slice.92), channel_id=1, source_target_pairs={{0,4},{8,12},{16,20},{24,28},{32,36},{40,44},{48,52},{56,60},{64,6... | collective-permute-start | bytes 1572872 | tf_op jit(solution)/shard_map/ppermute | solution.py:34
  68.2 1.7 %fusion.201 = (bf16[1,512,1024]{1,2,0:T(8,128)(2,1)S(1)}, bf16[1,512,1024]{1,2,0:T(8,128)(2,1)S(1)}) fusion(bf16[2,512,1024]{1,2,0:T(8,128)(2,1)} %collective-permute-done.1), kind=kLoop, calls=%fused_computation.278 | loop fusion | bytes 4194304 | tf_op jit(solution)/shard_map/slice | solution.py:66
  77.1 1.6 %fusion.65 = f32[8,128,128]{1,2,0:T(8,128)} fusion(bf16[512,8,128]{0,2,1:T(8,128)(2,1)S(1)} %bitcast.222, f32[8,128,512]{2,1,0:T(8,128)S(1)} %copy-done, f32[8,128]{1,0:T(8,128)S(1)} %get-tuple-element.24, pred[128,512]{1,0:T(8,128)(4,1)S(1)} %copy-done.24), kind=kOutput, calls=%fused_computation.106 | convolution fusion | flops 136314880 | bytes 3739648 | tf_op jit(solution)/shard_map/hqk,khd->qhd/dot_general | solution.py:66
  81.8 1.6 %fusion.72 = f32[8,128,128]{1,2,0:T(8,128)} fusion(bf16[512,8,128]{0,2,1:T(8,128)(2,1)S(1)} %bitcast.227, f32[8,128,512]{2,1,0:T(8,128)S(1)} %get-tuple-element.78, f32[8,128]{1,0:T(8,128)S(1)} %get-tuple-element.22, pred[128,512]{1,0:T(8,128)(4,1)S(1)} %copy-done.22), kind=kOutput, calls=%fused_computation.109 | convolution fusion | flops 136314880 | bytes 3739648 | tf_op jit(solution)/shard_map/hqk,khd->qhd/dot_general | solution.py:66
  84.0 3.7 %fusion.27 = (f32[8,128]{1,0:T(8,128)S(1)}, f32[8,128]{1,0:T(8,128)S(1)}, f32[8,128]{1,0:T(8,128)S(1)}, f32[8,128]{1,0:T(8,128)S(1)}, f32[8,128]{1,0:T(8,128)}, /*index=5*/f32[8,128]{1,0:T(8,128)}) fusion(f32[8,128,512]{2,1,0:T(8,128)S(1)} %get-tuple-element.78, f32[8,128]{1,0:T(8,128)S(1)} %get-tuple-element.22, pred[128,512]{1,0:T(8,128)(4,1)S(1)} %copy-done.22, ...), kind=kLoop, calls=%fused_computation.56 | loop fusion | flops 12576768 | bytes 13008896 | tf_op jit(solution)/shard_map/reduce_sum | solution.py:64
  87.7 1.9 %fusion.60 = f32[128,8,128]{0,2,1:T(8,128)S(1)} fusion(f32[8,128,128]{1,2,0:T(8,128)} %fusion.65, f32[8,128,128]{1,2,0:T(8,128)} %fusion.67, bf16[512,8,128]{0,2,1:T(8,128)(2,1)S(1)} %bitcast.190, f32[8,128,512]{2,1,0:T(8,128)S(1)} %get-tuple-element.88, f32[8,128]{1,0:T(8,128)S(1)} %get-tuple-element.24, pred[128,512]{1,0:T(8,128)(4,1)S(1)} %copy-done.9, ...), kind=kOutput, calls=%fused_computation.101 | convolution fusion | flops 136708096 | bytes 4792320 | tf_op jit(solution)/shard_map/hqk,khd->qhd/dot_general | solution.py:66
  94.0 3.3 %collective-permute-start.6 = (bf16[128,2048]{1,0:T(8,128)(2,1)S(1)}, bf16[128,2048]{1,0:T(8,128)(2,1)S(1)}, u32[]{:S(2)}, u32[]{:S(2)}) collective-permute-start(bf16[128,2048]{1,0:T(8,128)(2,1)S(1)} %get-tuple-element.34), channel_id=1, source_target_pairs={{0,3},{1,0},{2,1},{3,2},{4,7},{5,4},{6,5},{7,6},{8,11},{9,8},{10,9... | collective-permute-start | bytes 1572872 | tf_op jit(solution)/shard_map/ppermute | solution.py:19
  101.4 3.2 %fusion.15 = (f32[8,128]{1,0:T(8,128)S(1)}, f32[8,128]{1,0:T(8,128)S(1)}, f32[8,128]{1,0:T(8,128)S(1)}, f32[8,128]{1,0:T(8,128)S(1)}, f32[8,128]{1,0:T(8,128)S(1)}, /*index=5*/f32[8,128]{1,0:T(8,128)S(1)}) fusion(f32[8,128,512]{2,1,0:T(8,128)S(1)} %get-tuple-element.94, f32[8,128]{1,0:T(8,128)S(1)} %get-tuple-element.20, pred[128,512]{1,0:T(8,128)(4,1)S(1)} %copy-done.15, ...), kind=kLoop, calls=%fused_computation.44 | loop fusion | flops 12576768 | bytes 13008896 | tf_op jit(solution)/shard_map/reduce_sum | solution.py:64
  108.2 3.8 %collective-permute-start.7 = (bf16[128,4096]{1,0:T(8,128)(2,1)S(1)}, bf16[128,4096]{1,0:T(8,128)(2,1)S(1)}, u32[]{:S(2)}, u32[]{:S(2)}) collective-permute-start(bf16[128,4096]{1,0:T(8,128)(2,1)S(1)} %pad_maximum_fusion.1), channel_id=1, source_target_pairs={{0,3},{1,0},{2,1},{3,2},{4,7},{5,4},{6,5},{7,6},{8,11},{9,8},{10,9... | collective-permute-start | bytes 3145736 | tf_op jit(solution)/shard_map/ppermute | solution.py:19
  112.0 2.1 %collective-permute-done.4 = bf16[128,2048]{1,0:T(8,128)(2,1)S(1)} collective-permute-done((bf16[128,2048]{1,0:T(8,128)(2,1)S(1)}, bf16[128,2048]{1,0:T(8,128)(2,1)S(1)}, u32[]{:S(2)}, u32[]{:S(2)}) %collective-permute-start.4) | collective-permute-done | bytes 524320 | tf_op jit(solution)/shard_map/ppermute | solution.py:19
  116.0 17.0 %collective-permute-done.7 = bf16[128,4096]{1,0:T(8,128)(2,1)S(1)} collective-permute-done((bf16[128,4096]{1,0:T(8,128)(2,1)S(1)}, bf16[128,4096]{1,0:T(8,128)(2,1)S(1)}, u32[]{:S(2)}, u32[]{:S(2)}) %collective-permute-start.7) | collective-permute-done | bytes 1048608 | tf_op jit(solution)/shard_map/ppermute | solution.py:19
  133.0 5.8 %collective-permute-done.5 = bf16[128,4096]{1,0:T(8,128)(2,1)S(1)} collective-permute-done((bf16[128,4096]{1,0:T(8,128)(2,1)S(1)}, bf16[128,4096]{1,0:T(8,128)(2,1)S(1)}, u32[]{:S(2)}, u32[]{:S(2)}) %collective-permute-start.5) | collective-permute-done | bytes 1048608 | tf_op jit(solution)/shard_map/ppermute | solution.py:19
  (181 shorter events, 40.6 us)
Async XLA Ops:
  4.0 27.8 %collective-permute-start = (bf16[2,512,1024]{1,2,0:T(8,128)(2,1)}, bf16[2,512,1024]{1,2,0:T(8,128)(2,1)}, u32[]{:S(2)}, u32[]{:S(2)}) collective-permute-start(bf16[2,512,1024]{1,2,0:T(8,128)(2,1)} %copy.14), channel_id=1, source_target_pairs={{0,4},{4,8},{8,12},{12,16},{16,20},{20,24},{24,28},{28,32},{32,36}... | collective-permute-start | bytes 6291464 | tf_op jit(solution)/shard_map/ppermute | solution.py:14
  8.4 4.6 %copy-start.4 = (bf16[128,1024]{0,1:T(8,128)(2,1)}, bf16[128,1024]{0,1:T(8,128)(2,1)S(1)}, u32[]{:S(2)}) copy-start(bf16[128,1024]{0,1:T(8,128)(2,1)S(1)} %copy.95) | copy-start | bytes 786436
  8.6 4.4 %copy-start.2 = (bf16[128,1024]{0,1:T(8,128)(2,1)}, bf16[128,1024]{0,1:T(8,128)(2,1)S(1)}, u32[]{:S(2)}) copy-start(bf16[128,1024]{0,1:T(8,128)(2,1)S(1)} %copy.94) | copy-start | bytes 786436
  8.8 4.2 %copy-start.44 = (s32[128]{0:T(128)}, s32[128]{0:T(128)S(1)}, u32[]{:S(2)}) copy-start(s32[128]{0:T(128)S(1)} %iota_add_fusion.4) | copy-start | bytes 1540
  8.8 4.2 %copy-start.45 = (s32[128]{0:T(128)}, s32[128]{0:T(128)S(1)}, u32[]{:S(2)}) copy-start(s32[128]{0:T(128)S(1)} %iota_add_fusion.3) | copy-start | bytes 1540
  8.8 4.2 %copy-start.46 = (s32[128]{0:T(128)}, s32[128]{0:T(128)S(1)}, u32[]{:S(2)}) copy-start(s32[128]{0:T(128)S(1)} %iota_add_fusion.2) | copy-start | bytes 1540
  8.8 4.2 %copy-start.47 = (s32[128]{0:T(128)}, s32[128]{0:T(128)S(1)}, u32[]{:S(2)}) copy-start(s32[128]{0:T(128)S(1)} %iota_add_fusion.6) | copy-start | bytes 1540
  11.1 3.8 %copy-start.23 = (pred[128,512]{1,0:T(8,128)(4,1)}, pred[128,512]{1,0:T(8,128)(4,1)S(1)}, u32[]{:S(2)}) copy-start(pred[128,512]{1,0:T(8,128)(4,1)S(1)} %get-tuple-element.67) | copy-start | bytes 196612
  11.1 3.8 %copy-start.17 = (pred[128,512]{1,0:T(8,128)(4,1)}, pred[128,512]{1,0:T(8,128)(4,1)S(1)}, u32[]{:S(2)}) copy-start(pred[128,512]{1,0:T(8,128)(4,1)S(1)} %get-tuple-element.68) | copy-start | bytes 196612
  14.9 19.3 %copy-start.7 = (bf16[2,512,1024]{2,1,0:T(8,128)(2,1)S(1)}, bf16[2,512,1024]{2,1,0:T(8,128)(2,1)}, u32[]{:S(2)}) copy-start(bf16[2,512,1024]{2,1,0:T(8,128)(2,1)} %param.5) | copy-start | bytes 6291460
  31.7 33.3 %collective-permute-start.1 = (bf16[2,512,1024]{1,2,0:T(8,128)(2,1)}, bf16[2,512,1024]{1,2,0:T(8,128)(2,1)}, u32[]{:S(2)}, u32[]{:S(2)}) collective-permute-start(bf16[2,512,1024]{1,2,0:T(8,128)(2,1)} %collective-permute-done), channel_id=1, source_target_pairs={{0,4},{4,8},{8,12},{12,16},{16,20},{20,24},{24,28},{28,32},{32,36}... | collective-permute-start | bytes 6291464 | tf_op jit(solution)/shard_map/ppermute | solution.py:14
  43.5 6.0 %copy-start.5 = (bf16[128,1024]{0,1:T(8,128)(2,1)S(1)}, bf16[128,1024]{0,1:T(8,128)(2,1)}, u32[]{:S(2)}) copy-start(bf16[128,1024]{0,1:T(8,128)(2,1)} %copy-done.4) | copy-start | bytes 786436
  43.5 6.0 %copy-start.21 = (pred[128,512]{1,0:T(8,128)(4,1)S(1)}, pred[128,512]{1,0:T(8,128)(4,1)}, u32[]{:S(2)}) copy-start(pred[128,512]{1,0:T(8,128)(4,1)} %get-tuple-element.64) | copy-start | bytes 196612
  43.5 30.3 %collective-permute-start.2 = (bf16[2,128,1024]{1,2,0:T(8,128)(2,1)S(1)}, bf16[2,128,1024]{1,2,0:T(8,128)(2,1)S(1)}, u32[]{:S(2)}, u32[]{:S(2)}) collective-permute-start(bf16[2,128,1024]{1,2,0:T(8,128)(2,1)S(1)} %slice.91), channel_id=1, source_target_pairs={{0,8},{8,16},{16,24},{24,32},{32,40},{40,48},{48,56},{56,64},{64,7... | collective-permute-start | bytes 1572872 | tf_op jit(solution)/shard_map/ppermute | solution.py:33
  49.5 32.3 %copy-start.12 = (bf16[1,512,1024]{1,2,0:T(8,128)(2,1)}, bf16[1,512,1024]{1,2,0:T(8,128)(2,1)S(1)}, u32[]{:S(2)}) copy-start(bf16[1,512,1024]{1,2,0:T(8,128)(2,1)S(1)} %get-tuple-element.27) | copy-start | bytes 3145732
  66.1 3.8 %copy-start.9 = (pred[128,512]{1,0:T(8,128)(4,1)S(1)}, pred[128,512]{1,0:T(8,128)(4,1)}, u32[]{:S(2)}) copy-start(pred[128,512]{1,0:T(8,128)(4,1)} %get-tuple-element.61) | copy-start | bytes 196612
  66.1 7.7 %collective-permute-start.3 = (bf16[2,128,1024]{1,2,0:T(8,128)(2,1)S(1)}, bf16[2,128,1024]{1,2,0:T(8,128)(2,1)S(1)}, u32[]{:S(2)}, u32[]{:S(2)}) collective-permute-start(bf16[2,128,1024]{1,2,0:T(8,128)(2,1)S(1)} %slice.92), channel_id=1, source_target_pairs={{0,4},{8,12},{16,20},{24,28},{32,36},{40,44},{48,52},{56,60},{64,6... | collective-permute-start | bytes 1572872 | tf_op jit(solution)/shard_map/ppermute | solution.py:34
  75.0 8.3 %copy-start.40 = (f32[8,128]{1,0:T(8,128)}, f32[8,128]{1,0:T(8,128)S(1)}, u32[]{:S(2)}) copy-start(f32[8,128]{1,0:T(8,128)S(1)} %get-tuple-element.23) | copy-start | bytes 12292
  84.0 6.0 %slice-start = ((s8[8388608]{0:T(1024)(128)(4,1)}), s8[4194304]{0:T(1024)(128)(4,1)S(1)}, s32[]{:S(2)}) async-start(s8[8388608]{0:T(1024)(128)(4,1)} %bitcast.184), calls=%async_computation | async-start | bytes 8388608
  84.0 6.0 %slice-start.1 = ((s8[8388608]{0:T(1024)(128)(4,1)}), s8[4194304]{0:T(1024)(128)(4,1)S(1)}, s32[]{:S(2)}) async-start(s8[8388608]{0:T(1024)(128)(4,1)} %bitcast.184), calls=%async_computation.1 | async-start | bytes 8388608
  94.0 14.0 %collective-permute-start.6 = (bf16[128,2048]{1,0:T(8,128)(2,1)S(1)}, bf16[128,2048]{1,0:T(8,128)(2,1)S(1)}, u32[]{:S(2)}, u32[]{:S(2)}) collective-permute-start(bf16[128,2048]{1,0:T(8,128)(2,1)S(1)} %get-tuple-element.34), channel_id=1, source_target_pairs={{0,3},{1,0},{2,1},{3,2},{4,7},{5,4},{6,5},{7,6},{8,11},{9,8},{10,9... | collective-permute-start | bytes 1572872 | tf_op jit(solution)/shard_map/ppermute | solution.py:19
  99.8 14.2 %collective-permute-start.4 = (bf16[128,2048]{1,0:T(8,128)(2,1)S(1)}, bf16[128,2048]{1,0:T(8,128)(2,1)S(1)}, u32[]{:S(2)}, u32[]{:S(2)}) collective-permute-start(bf16[128,2048]{1,0:T(8,128)(2,1)S(1)} %get-tuple-element.33), channel_id=1, source_target_pairs={{0,1},{1,2},{2,3},{3,0},{4,5},{5,6},{6,7},{7,4},{8,9},{9,10},{10,1... | collective-permute-start | bytes 1572872 | tf_op jit(solution)/shard_map/ppermute | solution.py:19
  108.2 24.8 %collective-permute-start.7 = (bf16[128,4096]{1,0:T(8,128)(2,1)S(1)}, bf16[128,4096]{1,0:T(8,128)(2,1)S(1)}, u32[]{:S(2)}, u32[]{:S(2)}) collective-permute-start(bf16[128,4096]{1,0:T(8,128)(2,1)S(1)} %pad_maximum_fusion.1), channel_id=1, source_target_pairs={{0,3},{1,0},{2,1},{3,2},{4,7},{5,4},{6,5},{7,6},{8,11},{9,8},{10,9... | collective-permute-start | bytes 3145736 | tf_op jit(solution)/shard_map/ppermute | solution.py:19
  114.3 24.5 %collective-permute-start.5 = (bf16[128,4096]{1,0:T(8,128)(2,1)S(1)}, bf16[128,4096]{1,0:T(8,128)(2,1)S(1)}, u32[]{:S(2)}, u32[]{:S(2)}) collective-permute-start(bf16[128,4096]{1,0:T(8,128)(2,1)S(1)} %pad_maximum_fusion), channel_id=1, source_target_pairs={{0,1},{1,2},{2,3},{3,0},{4,5},{5,6},{6,7},{7,4},{8,9},{9,10},{10,1... | collective-permute-start | bytes 3145736 | tf_op jit(solution)/shard_map/ppermute | solution.py:19
  (34 other events, 71.2 us)

commit v18 on v13

--- a/solution.py
+++ b/solution.py
@@ -49,33 +49,33 @@
             k_docs = lax.dynamic_slice_in_dim(padded_docs, first_row + DOC_MOST + off, n)
             k_place = off + jnp.arange(n, dtype=jnp.int32)
             allowed = (k_docs[None, :] == q_docs[:, None]) & (k_place[None, :] <= q_place[:, None])
-            raw = jnp.einsum("qhd,khd->hqk", q, k, preferred_element_type=jnp.float32) * scale
-            return jnp.where(allowed[None], raw, jnp.float32(-1e30))
+            raw = jnp.einsum("khd,qhd->hkq", k, q, preferred_element_type=jnp.float32) * scale
+            return jnp.where(jnp.transpose(allowed)[None], raw, jnp.float32(-1e30))
 
         def stage(pairs, top):
             score_list = [scores(kv, off) for kv, off in pairs]
             for s in score_list:
-                top = jnp.maximum(top, s.max(axis=2, keepdims=True))
+                top = jnp.maximum(top, s.max(axis=1, keepdims=True))
             total = None
             summed = None
             for (kv, _), s in zip(pairs, score_list):
                 n = kv.shape[1]
                 weights = jnp.exp(s - top)
-                t = jnp.sum(weights, axis=2)
+                t = jnp.sum(weights, axis=1)
                 probs = weights.astype(jnp.bfloat16)
-                pv = jnp.einsum("hqk,khd->qhd", probs, kv[1].reshape(n, heads, HD), preferred_element_type=jnp.float32)
+                pv = jnp.einsum("hkq,khd->qhd", probs, kv[1].reshape(n, heads, HD), preferred_element_type=jnp.float32)
                 total = t if total is None else total + t
                 summed = pv if summed is None else summed + pv
             return top, total, summed
 
         near = list(zip(sources[2:], offsets[2:]))
         far = list(zip(sources[:2], offsets[:2]))
-        floor = jnp.full((heads, CHUNK, 1), -1e30, jnp.float32)
+        floor = jnp.full((heads, 1, CHUNK), -1e30, jnp.float32)
         top_a, total_a, summed_a = stage(near, floor)
         top, total_b, summed_b = stage(far, top_a)
         alpha = jnp.exp(top_a - top)
-        total = alpha[:, :, 0] * total_a + total_b
-        summed = jnp.transpose(alpha, (1, 0, 2)) * summed_a + summed_b
+        total = alpha[:, 0, :] * total_a + total_b
+        summed = jnp.transpose(alpha, (2, 0, 1)) * summed_a + summed_b
         attended = (summed / jnp.transpose(total)[:, :, None]).astype(jnp.bfloat16)
         attended = attended.reshape(CHUNK, heads * HD)
         return jnp.dot(attended, w_out, preferred_element_type=jnp.float32).astype(jnp.bfloat16)

time: 131 us -> 133 us (1.015)
  waiting for transfers between devices: 48.9 us -> 54 us
  local copies, waits for them, and re-layouts: 22.2 us -> 18.9 us
  starting transfers between devices: 17.5 us -> 19 us
  other arithmetic: 13.1 us -> 11.7 us
    ppermute x2, waiting for transfers between devices: 28.1 us -> 30.8 us  [shift_up(): return lax.ppermute(x, axis, [(i, i + 1) for i in range(peers - 1)])]
    ppermute x4, waiting for transfers between devices: 20.8 us -> 23.2 us  [rotate(): return lax.ppermute(x, axis, [(i, (i + by) % peers) for i in range(peers)])]
    reduce_sum x8 -> x12, other arithmetic: 8.44 us -> 6.69 us  [stage(): t = jnp.sum(weights, axis=1)]
    ppermute x4, starting transfers between devices: 7.13 us -> 8.65 us  [rotate(): return lax.ppermute(x, axis, [(i, (i + by) % peers) for i in range(peers)])]
    unnamed x69 -> x45, local copies, waits for them, and re-layouts: 9.03 us -> 8.07 us
  transfers between devices with their start and end apart: 8 -> 8, of which waited for: 6 -> 6; matrix products, arithmetic and copies ran while one was open for 32% -> 28% of each run, Pallas kernels for 0% -> 0%
where the time goes in v18:
time: 133 us; the launch traced here: 131 us
  waiting for transfers between devices  54 us (41%)
  matrix products  26.8 us (20%)
  starting transfers between devices  19 us (14%)
  local copies, waits for them, and re-layouts  18.9 us (14%)
  other arithmetic  11.7 us (9%)
    ppermute x2, waiting for transfers between devices, shift_up(): return lax.ppermute(x, axis, [(i, i + 1) for i in range(peers - 1)])  30.8 us
    ppermute x4, waiting for transfers between devices, rotate(): return lax.ppermute(x, axis, [(i, (i + by) % peers) for i in range(peers)])  23.2 us
    dot_general x16, matrix products, scores(): jnp.einsum('khd,qhd->hkq', k, q, preferred_element_type=jnp.float32) * scale  13.4 us
    ppermute x4, starting transfers between devices, rotate(): return lax.ppermute(x, axis, [(i, (i + by) % peers) for i in range(peers)])  8.65 us
    unnamed x45, local copies, waits for them, and re-layouts  8.07 us
    dot_general x16, matrix products, stage(): jnp.einsum('hkq,khd->qhd', probs, kv[1].reshape(n, heads, HD), preferred_...  7.96 us
    slice x5, local copies, waits for them, and re-layouts, stage(): kv[1].reshape(n, heads, HD)  7.15 us
    reduce_sum x12, other arithmetic, stage(): t = jnp.sum(weights, axis=1)  6.69 us
  transfers between devices with their start and end apart: 8, of which 6 were waited for; matrix products, arithmetic and copies ran while one was open for 28% of the time, Pallas kernels for 0%

profile of v18, /device:TPU:98, one launch (start us, length us, event | category | flops | bytes accessed | tf_op | source)
XLA Modules:
  0.0 131.0 jit_solution(13649380431455819472)
XLA Ops:
  0.0 3.9 %copy.22 = bf16[2,512,1024]{1,2,0:T(8,128)(2,1)} copy(bf16[2,512,1024]{2,1,0:T(8,128)(2,1)} %param.5) | data formatting | bytes 4194304 | tf_op args[1]
  4.0 2.0 %collective-permute-start = (bf16[2,512,1024]{1,2,0:T(8,128)(2,1)}, bf16[2,512,1024]{1,2,0:T(8,128)(2,1)}, u32[]{:S(2)}, u32[]{:S(2)}) collective-permute-start(bf16[2,512,1024]{1,2,0:T(8,128)(2,1)} %copy.22), channel_id=1, source_target_pairs={{0,4},{4,8},{8,12},{12,16},{16,20},{20,24},{24,28},{28,32},{32,36}... | collective-permute-start | bytes 6291464 | tf_op jit(solution)/shard_map/ppermute | solution.py:14
  8.9 1.5 %fusion.98 = (pred[512,128]{0,1:T(8,128)(4,1)S(1)}, pred[512,128]{0,1:T(8,128)(4,1)S(1)}, pred[512,128]{0,1:T(8,128)(4,1)}, pred[512,128]{0,1:T(8,128)(4,1)}, pr...) fusion(s32[512]{0:T(512)S(1)} %get-tuple-element.39, ...), kind=kLoop, calls=%fused_computation.140 | loop fusion | flops 2359296 | bytes 800768 | tf_op jit(solution)/shard_map/and | solution.py:51
  10.4 1.9 %fusion.140 = (f32[8,128]{1,0:T(8,128)S(1)}, f32[8,512,128]{1,2,0:T(8,128)}) fusion(bf16[128,8,128]{0,2,1:T(8,128)(2,1)S(1)} %bitcast.346, bf16[512,8,128]{0,2,1:T(8,128)(2,1)S(1)} %bitcast.318, pred[512,128]{0,1:T(8,128)(4,1)S(1)} %get-tuple-element.53), kind=kOutput, calls=%fused_computation.241 | convolution fusion | flops 135789568 | bytes 3477504 | tf_op jit(solution)/shard_map/khd,qhd->hkq/dot_general | solution.py:52
  12.3 1.8 %fusion.128 = (f32[8,128]{1,0:T(8,128)S(1)}, f32[8,512,128]{1,2,0:T(8,128)}) fusion(bf16[128,8,128]{0,2,1:T(8,128)(2,1)S(1)} %bitcast.350, bf16[512,8,128]{0,2,1:T(8,128)(2,1)S(1)} %bitcast.319, pred[512,128]{0,1:T(8,128)(4,1)S(1)} %get-tuple-element.54), kind=kOutput, calls=%fused_computation.229 | convolution fusion | flops 135789568 | bytes 3477504 | tf_op jit(solution)/shard_map/khd,qhd->hkq/dot_general | solution.py:52
  14.1 17.6 %collective-permute-done = bf16[2,512,1024]{1,2,0:T(8,128)(2,1)} collective-permute-done((bf16[2,512,1024]{1,2,0:T(8,128)(2,1)}, bf16[2,512,1024]{1,2,0:T(8,128)(2,1)}, u32[]{:S(2)}, u32[]{:S(2)}) %collective-permute-start) | collective-permute-done | bytes 2097184 | tf_op jit(solution)/shard_map/ppermute | solution.py:14
  31.7 1.9 %collective-permute-start.2 = (bf16[2,512,1024]{1,2,0:T(8,128)(2,1)}, bf16[2,512,1024]{1,2,0:T(8,128)(2,1)}, u32[]{:S(2)}, u32[]{:S(2)}) collective-permute-start(bf16[2,512,1024]{1,2,0:T(8,128)(2,1)} %collective-permute-done), channel_id=1, source_target_pairs={{0,4},{4,8},{8,12},{12,16},{16,20},{20,24},{24,28},{28,32},{32,36}... | collective-permute-start | bytes 6291464 | tf_op jit(solution)/shard_map/ppermute | solution.py:14
  33.7 1.9 %fusion.136 = (f32[8,128]{1,0:T(8,128)S(1)}, f32[8,512,128]{1,2,0:T(8,128)}) fusion(bf16[128,8,128]{0,2,1:T(8,128)(2,1)S(1)} %bitcast.342, bf16[512,8,128]{0,2,1:T(8,128)(2,1)S(1)} %bitcast.320, pred[512,128]{0,1:T(8,128)(4,1)S(1)} %get-tuple-element.64), kind=kOutput, calls=%fused_computation.237 | convolution fusion | flops 135789568 | bytes 3477504 | tf_op jit(solution)/shard_map/khd,qhd->hkq/dot_general | solution.py:52
  35.6 2.3 %slice.39 = bf16[1,512,1024]{2,1,0:T(8,128)(2,1)} slice(bf16[2,512,1024]{2,1,0:T(8,128)(2,1)} %param.5), slice={[1:2], [0:512], [0:1024]} | slice | bytes 2097152 | tf_op jit(solution)/shard_map/slice | solution.py:66
  37.8 1.5 %copy.33 = bf16[1,512,1024]{1,2,0:T(8,128)(2,1)S(1)} copy(bf16[1,512,1024]{2,1,0:T(8,128)(2,1)} %slice.39) | data formatting | bytes 2097152 | tf_op jit(solution)/shard_map/slice | solution.py:66
  40.3 1.5 %fusion.132 = (f32[8,128]{1,0:T(8,128)S(1)}, f32[8,512,128]{1,2,0:T(8,128)S(1)}) fusion(bf16[128,8,128]{0,2,1:T(8,128)(2,1)S(1)} %bitcast.354, bf16[512,8,128]{0,2,1:T(8,128)(2,1)S(1)} %bitcast.321, pred[512,128]{0,1:T(8,128)(4,1)} %get-tuple-element.63), kind=kOutput, calls=%fused_computation.233 | convolution fusion | flops 135789568 | bytes 3477504 | tf_op jit(solution)/shard_map/khd,qhd->hkq/dot_general | solution.py:52
  42.9 4.3 %collective-permute-start.1 = (bf16[2,128,1024]{1,2,0:T(8,128)(2,1)S(1)}, bf16[2,128,1024]{1,2,0:T(8,128)(2,1)S(1)}, u32[]{:S(2)}, u32[]{:S(2)}) collective-permute-start(bf16[2,128,1024]{1,2,0:T(8,128)(2,1)S(1)} %slice.90), channel_id=1, source_target_pairs={{0,8},{8,16},{16,24},{24,32},{32,40},{40,48},{48,56},{56,64},{64,7... | collective-permute-start | bytes 1572872 | tf_op jit(solution)/shard_map/ppermute | solution.py:33
  47.2 1.7 %fusion.122 = (bf16[1,512,1024]{1,2,0:T(8,128)(2,1)S(1)}, bf16[1,512,1024]{1,2,0:T(8,128)(2,1)S(1)}) fusion(bf16[2,512,1024]{1,2,0:T(8,128)(2,1)} %collective-permute-done), kind=kLoop, calls=%fused_computation.223 | loop fusion | bytes 4194304 | tf_op jit(solution)/shard_map/slice | solution.py:66
  51.8 13.2 %collective-permute-done.2 = bf16[2,512,1024]{1,2,0:T(8,128)(2,1)} collective-permute-done((bf16[2,512,1024]{1,2,0:T(8,128)(2,1)}, bf16[2,512,1024]{1,2,0:T(8,128)(2,1)}, u32[]{:S(2)}, u32[]{:S(2)}) %collective-permute-start.2) | collective-permute-done | bytes 2097184 | tf_op jit(solution)/shard_map/ppermute | solution.py:14
  66.1 2.1 %collective-permute-start.3 = (bf16[2,128,1024]{1,2,0:T(8,128)(2,1)S(1)}, bf16[2,128,1024]{1,2,0:T(8,128)(2,1)S(1)}, u32[]{:S(2)}, u32[]{:S(2)}) collective-permute-start(bf16[2,128,1024]{1,2,0:T(8,128)(2,1)S(1)} %slice.91), channel_id=1, source_target_pairs={{0,4},{8,12},{16,20},{24,28},{32,36},{40,44},{48,52},{56,60},{64,6... | collective-permute-start | bytes 1572872 | tf_op jit(solution)/shard_map/ppermute | solution.py:34
  68.2 1.7 %fusion.121 = (bf16[1,512,1024]{1,2,0:T(8,128)(2,1)S(1)}, bf16[1,512,1024]{1,2,0:T(8,128)(2,1)S(1)}) fusion(bf16[2,512,1024]{1,2,0:T(8,128)(2,1)} %collective-permute-done.2), kind=kLoop, calls=%fused_computation.222 | loop fusion | bytes 4194304 | tf_op jit(solution)/shard_map/slice | solution.py:66
  86.2 1.5 %convolution_convert_fusion.1 = bf16[128,4096]{1,0:T(8,128)(2,1)S(1)} fusion(bf16[128,1024]{0,1:T(8,128)(2,1)S(1)} %bitcast.363, bf16[1024,4096]{1,0:T(8,128)(2,1)S(1)} %bitcast.313), kind=kOutput, calls=%fused_computation.1 | convolution fusion | flops 1074266112 | bytes 9699328 | tf_op jit(solution)/shard_map/dot_general | solution.py:81
  87.8 1.6 %collective-permute-start.4 = (bf16[128,2048]{1,0:T(8,128)(2,1)S(1)}, bf16[128,2048]{1,0:T(8,128)(2,1)S(1)}, u32[]{:S(2)}, u32[]{:S(2)}) collective-permute-start(bf16[128,2048]{1,0:T(8,128)(2,1)S(1)} %get-tuple-element.29), channel_id=1, source_target_pairs={{0,1},{1,2},{2,3},{3,0},{4,5},{5,6},{6,7},{7,4},{8,9},{9,10},{10,1... | collective-permute-start | bytes 1572872 | tf_op jit(solution)/shard_map/ppermute | solution.py:19
  91.1 2.9 %collective-permute-start.6 = (bf16[128,2048]{1,0:T(8,128)(2,1)S(1)}, bf16[128,2048]{1,0:T(8,128)(2,1)S(1)}, u32[]{:S(2)}, u32[]{:S(2)}) collective-permute-start(bf16[128,2048]{1,0:T(8,128)(2,1)S(1)} %get-tuple-element.30), channel_id=1, source_target_pairs={{0,3},{1,0},{2,1},{3,2},{4,7},{5,4},{6,5},{7,6},{8,11},{9,8},{10,9... | collective-permute-start | bytes 1572872 | tf_op jit(solution)/shard_map/ppermute | solution.py:19
  100.0 2.3 %collective-permute-done.4 = bf16[128,2048]{1,0:T(8,128)(2,1)S(1)} collective-permute-done((bf16[128,2048]{1,0:T(8,128)(2,1)S(1)}, bf16[128,2048]{1,0:T(8,128)(2,1)S(1)}, u32[]{:S(2)}, u32[]{:S(2)}) %collective-permute-start.4) | collective-permute-done | bytes 524320 | tf_op jit(solution)/shard_map/ppermute | solution.py:19
  102.9 1.7 %collective-permute-done.6 = bf16[128,2048]{1,0:T(8,128)(2,1)S(1)} collective-permute-done((bf16[128,2048]{1,0:T(8,128)(2,1)S(1)}, bf16[128,2048]{1,0:T(8,128)(2,1)S(1)}, u32[]{:S(2)}, u32[]{:S(2)}) %collective-permute-start.6) | collective-permute-done | bytes 524320 | tf_op jit(solution)/shard_map/ppermute | solution.py:19
  104.9 3.8 %collective-permute-start.7 = (bf16[128,4096]{1,0:T(8,128)(2,1)S(1)}, bf16[128,4096]{1,0:T(8,128)(2,1)S(1)}, u32[]{:S(2)}, u32[]{:S(2)}) collective-permute-start(bf16[128,4096]{1,0:T(8,128)(2,1)S(1)} %pad_maximum_fusion.1), channel_id=1, source_target_pairs={{0,3},{1,0},{2,1},{3,2},{4,7},{5,4},{6,5},{7,6},{8,11},{9,8},{10,9... | collective-permute-start | bytes 3145736 | tf_op jit(solution)/shard_map/ppermute | solution.py:19
  110.5 16.9 %collective-permute-done.5 = bf16[128,4096]{1,0:T(8,128)(2,1)S(1)} collective-permute-done((bf16[128,4096]{1,0:T(8,128)(2,1)S(1)}, bf16[128,4096]{1,0:T(8,128)(2,1)S(1)}, u32[]{:S(2)}, u32[]{:S(2)}) %collective-permute-start.5) | collective-permute-done | bytes 1048608 | tf_op jit(solution)/shard_map/ppermute | solution.py:19
  127.4 2.2 %collective-permute-done.7 = bf16[128,4096]{1,0:T(8,128)(2,1)S(1)} collective-permute-done((bf16[128,4096]{1,0:T(8,128)(2,1)S(1)}, bf16[128,4096]{1,0:T(8,128)(2,1)S(1)}, u32[]{:S(2)}, u32[]{:S(2)}) %collective-permute-start.7) | collective-permute-done | bytes 1048608 | tf_op jit(solution)/shard_map/ppermute | solution.py:19
  (123 shorter events, 36.5 us)
Async XLA Ops:
  4.0 3.4 %copy-start.3 = (bf16[512,1024]{1,0:T(8,128)(2,1)S(1)}, bf16[512,1024]{1,0:T(8,128)(2,1)}, u32[]{:S(2)}) copy-start(bf16[512,1024]{1,0:T(8,128)(2,1)} %param.4) | copy-start | bytes 3145732
  4.0 27.8 %collective-permute-start = (bf16[2,512,1024]{1,2,0:T(8,128)(2,1)}, bf16[2,512,1024]{1,2,0:T(8,128)(2,1)}, u32[]{:S(2)}, u32[]{:S(2)}) collective-permute-start(bf16[2,512,1024]{1,2,0:T(8,128)(2,1)} %copy.22), channel_id=1, source_target_pairs={{0,4},{4,8},{8,12},{12,16},{16,20},{20,24},{24,28},{28,32},{32,36}... | collective-permute-start | bytes 6291464 | tf_op jit(solution)/shard_map/ppermute | solution.py:14
  8.1 4.2 %copy-start.14 = (s32[128]{0:T(128)}, s32[128]{0:T(128)S(1)}, u32[]{:S(2)}) copy-start(s32[128]{0:T(128)S(1)} %get-tuple-element.102) | copy-start | bytes 1540
  8.1 4.2 %copy-start.15 = (s32[128]{0:T(128)}, s32[128]{0:T(128)S(1)}, u32[]{:S(2)}) copy-start(s32[128]{0:T(128)S(1)} %get-tuple-element.103) | copy-start | bytes 1540
  8.1 4.2 %copy-start.16 = (s32[128]{0:T(128)}, s32[128]{0:T(128)S(1)}, u32[]{:S(2)}) copy-start(s32[128]{0:T(128)S(1)} %get-tuple-element.104) | copy-start | bytes 1540
  8.1 4.2 %copy-start.17 = (s32[128]{0:T(128)}, s32[128]{0:T(128)S(1)}, u32[]{:S(2)}) copy-start(s32[128]{0:T(128)S(1)} %get-tuple-element.105) | copy-start | bytes 1540
  8.8 3.5 %copy-start.11 = (s32[128]{0:T(128)}, s32[128]{0:T(128)S(1)}, u32[]{:S(2)}) copy-start(s32[128]{0:T(128)S(1)} %get-tuple-element.35) | copy-start | bytes 1540
  8.8 3.5 %copy-start.12 = (s32[128]{0:T(128)}, s32[128]{0:T(128)S(1)}, u32[]{:S(2)}) copy-start(s32[128]{0:T(128)S(1)} %get-tuple-element.36) | copy-start | bytes 1540
  8.8 3.5 %copy-start.13 = (s32[128]{0:T(128)}, s32[128]{0:T(128)S(1)}, u32[]{:S(2)}) copy-start(s32[128]{0:T(128)S(1)} %get-tuple-element.37) | copy-start | bytes 1540
  31.7 33.3 %collective-permute-start.2 = (bf16[2,512,1024]{1,2,0:T(8,128)(2,1)}, bf16[2,512,1024]{1,2,0:T(8,128)(2,1)}, u32[]{:S(2)}, u32[]{:S(2)}) collective-permute-start(bf16[2,512,1024]{1,2,0:T(8,128)(2,1)} %collective-permute-done), channel_id=1, source_target_pairs={{0,4},{4,8},{8,12},{12,16},{16,20},{20,24},{24,28},{28,32},{32,36}... | collective-permute-start | bytes 6291464 | tf_op jit(solution)/shard_map/ppermute | solution.py:14
  42.9 6.0 %copy-start.10 = (pred[512,128]{0,1:T(8,128)(4,1)S(1)}, pred[512,128]{0,1:T(8,128)(4,1)}, u32[]{:S(2)}) copy-start(pred[512,128]{0,1:T(8,128)(4,1)} %get-tuple-element.55) | copy-start | bytes 196612
  42.9 29.7 %collective-permute-start.1 = (bf16[2,128,1024]{1,2,0:T(8,128)(2,1)S(1)}, bf16[2,128,1024]{1,2,0:T(8,128)(2,1)S(1)}, u32[]{:S(2)}, u32[]{:S(2)}) collective-permute-start(bf16[2,128,1024]{1,2,0:T(8,128)(2,1)S(1)} %slice.90), channel_id=1, source_target_pairs={{0,8},{8,16},{16,24},{24,32},{32,40},{40,48},{48,56},{56,64},{64,7... | collective-permute-start | bytes 1572872 | tf_op jit(solution)/shard_map/ppermute | solution.py:33
  49.5 0.9 copy-start.8
  66.1 3.8 %copy-start.6 = (pred[512,128]{0,1:T(8,128)(4,1)S(1)}, pred[512,128]{0,1:T(8,128)(4,1)}, u32[]{:S(2)}) copy-start(pred[512,128]{0,1:T(8,128)(4,1)} %get-tuple-element.62) | copy-start | bytes 196612
  66.1 6.6 %collective-permute-start.3 = (bf16[2,128,1024]{1,2,0:T(8,128)(2,1)S(1)}, bf16[2,128,1024]{1,2,0:T(8,128)(2,1)S(1)}, u32[]{:S(2)}, u32[]{:S(2)}) collective-permute-start(bf16[2,128,1024]{1,2,0:T(8,128)(2,1)S(1)} %slice.91), channel_id=1, source_target_pairs={{0,4},{8,12},{16,20},{24,28},{32,36},{40,44},{48,52},{56,60},{64,6... | collective-permute-start | bytes 1572872 | tf_op jit(solution)/shard_map/ppermute | solution.py:34
  75.1 1.6 %copy-start.2 = (f32[8,512,128]{1,2,0:T(8,128)S(1)}, f32[8,512,128]{1,2,0:T(8,128)}, u32[]{:S(2)}) copy-start(f32[8,512,128]{1,2,0:T(8,128)} %get-tuple-element.98) | copy-start | bytes 6291460
  77.6 1.6 %copy-start.1 = (f32[8,512,128]{1,2,0:T(8,128)S(1)}, f32[8,512,128]{1,2,0:T(8,128)}, u32[]{:S(2)}) copy-start(f32[8,512,128]{1,2,0:T(8,128)} %get-tuple-element.74) | copy-start | bytes 6291460
  79.7 2.8 %slice-start = ((s8[8388608]{0:T(1024)(128)(4,1)}), s8[4194304]{0:T(1024)(128)(4,1)S(1)}, s32[]{:S(2)}) async-start(s8[8388608]{0:T(1024)(128)(4,1)} %bitcast.312), calls=%async_computation | async-start | bytes 8388608
  81.3 2.3 %slice-start.1 = ((s8[8388608]{0:T(1024)(128)(4,1)}), s8[4194304]{0:T(1024)(128)(4,1)S(1)}, s32[]{:S(2)}) async-start(s8[8388608]{0:T(1024)(128)(4,1)} %bitcast.312), calls=%async_computation.1 | async-start | bytes 8388608
  87.7 1.8 %copy-start = (f32[8,512,128]{1,2,0:T(8,128)S(1)}, f32[8,512,128]{1,2,0:T(8,128)}, u32[]{:S(2)}) copy-start(f32[8,512,128]{1,2,0:T(8,128)} %get-tuple-element.90) | copy-start | bytes 6291460
  87.8 14.5 %collective-permute-start.4 = (bf16[128,2048]{1,0:T(8,128)(2,1)S(1)}, bf16[128,2048]{1,0:T(8,128)(2,1)S(1)}, u32[]{:S(2)}, u32[]{:S(2)}) collective-permute-start(bf16[128,2048]{1,0:T(8,128)(2,1)S(1)} %get-tuple-element.29), channel_id=1, source_target_pairs={{0,1},{1,2},{2,3},{3,0},{4,5},{5,6},{6,7},{7,4},{8,9},{9,10},{10,1... | collective-permute-start | bytes 1572872 | tf_op jit(solution)/shard_map/ppermute | solution.py:19
  91.1 13.6 %collective-permute-start.6 = (bf16[128,2048]{1,0:T(8,128)(2,1)S(1)}, bf16[128,2048]{1,0:T(8,128)(2,1)S(1)}, u32[]{:S(2)}, u32[]{:S(2)}) collective-permute-start(bf16[128,2048]{1,0:T(8,128)(2,1)S(1)} %get-tuple-element.30), channel_id=1, source_target_pairs={{0,3},{1,0},{2,1},{3,2},{4,7},{5,4},{6,5},{7,6},{8,11},{9,8},{10,9... | collective-permute-start | bytes 1572872 | tf_op jit(solution)/shard_map/ppermute | solution.py:19
  102.6 24.9 %collective-permute-start.5 = (bf16[128,4096]{1,0:T(8,128)(2,1)S(1)}, bf16[128,4096]{1,0:T(8,128)(2,1)S(1)}, u32[]{:S(2)}, u32[]{:S(2)}) collective-permute-start(bf16[128,4096]{1,0:T(8,128)(2,1)S(1)} %pad_maximum_fusion), channel_id=1, source_target_pairs={{0,1},{1,2},{2,3},{3,0},{4,5},{5,6},{6,7},{7,4},{8,9},{9,10},{10,1... | collective-permute-start | bytes 3145736 | tf_op jit(solution)/shard_map/ppermute | solution.py:19
  104.9 24.8 %collective-permute-start.7 = (bf16[128,4096]{1,0:T(8,128)(2,1)S(1)}, bf16[128,4096]{1,0:T(8,128)(2,1)S(1)}, u32[]{:S(2)}, u32[]{:S(2)}) collective-permute-start(bf16[128,4096]{1,0:T(8,128)(2,1)S(1)} %pad_maximum_fusion.1), channel_id=1, source_target_pairs={{0,3},{1,0},{2,1},{3,2},{4,7},{5,4},{6,5},{7,6},{8,11},{9,8},{10,9... | collective-permute-start | bytes 3145736 | tf_op jit(solution)/shard_map/ppermute | solution.py:19
  (4 other events, 3.4 us)
